TPU v7x, 256 devices: a whole 4x4x8 slice. The times are simulated.
256 devices in a mesh: prow: 32 (over y, z), pcol: 8 (over x, core).
Axes of the slice: x: 4, y: 4, z: 8, core: 2. Of those that a mesh axis runs over, the one named last changes fastest.
Arguments:
- right_side: bfloat16 [32, 6, 128, 256], P('prow'), may hold values from -6 to 6
- lower_inverse: bfloat16 [32, 6, 256, 256], P('prow'), as said below
- upper_inverse: bfloat16 [32, 6, 256, 256], P('prow'), as said below
- lower_blocks: bfloat16 [32, 5, 48, 256, 256], P('prow', None, 'pcol'), may hold values from -0.0546875 to 0.0546875
- lower_sources: int32 [32, 5, 48], P('prow', None, 'pcol'), may hold values from 0 to 159, as said below
- lower_counts: int32 [32, 5, 8], P('prow', None, 'pcol'), may hold values from 1 to 6, as said below
- upper_blocks: bfloat16 [32, 5, 48, 256, 256], P('prow', None, 'pcol'), may hold values from -0.0546875 to 0.0546875
- upper_sources: int32 [32, 5, 48], P('prow', None, 'pcol'), may hold values from 32 to 191, as said below
- upper_counts: int32 [32, 5, 8], P('prow', None, 'pcol'), may hold values from 1 to 6, as said below
Outputs:
- solution: bfloat16 [32, 6, 128, 256], P('prow')
Inputs may be any that keep to these rules, and one draw needn't show every extreme that they name: `lower_sources`: entry [r, l, c] names supernode v * 32 + p of a level v below l + 1, with p % (8) == c // 6; entries may repeat. `upper_sources`: entry [r, l, c] names supernode v * 32 + p of a level v above l, with p % (8) == c // 6; entries may repeat. `lower_counts`: entry [r, l, g] is how many of the 6 slots of group g are live; the live ones come first. `upper_counts`: entry [r, l, g] is how many of the 6 slots of group g are live; the live ones come first. `lower_inverse`: each block is lower triangular. `upper_inverse`: each block is upper triangular.
All inputs are finite; a program needn't handle non-finite values.
Results may differ from a plain program's by a relative error of at most 0.02.
Values may be sent and summed in bfloat16 or wider, within the bound.
No kernel may reach another device: no remote copies, remote signals or barrier semaphores. Data moves between devices by JAX's collectives and lax.ppermute only.
A program may use at most 64 MiB of HBM per device.

v0:
```python
import jax
import jax.numpy as jnp
from jax import lax
from jax.sharding import PartitionSpec as P


def pick_sources(sources, count, store, width, ncol):
    group = store.shape[1]
    flat = store.reshape(store.shape[0] * group, store.shape[2], store.shape[3])
    position = sources // width * group + sources % width // ncol
    picked = flat[position]
    live = jnp.arange(sources.shape[0], dtype=jnp.int32) < count
    return jnp.where(live[:, None, None], picked, jnp.zeros_like(picked))


def contract(picked, blocks):
    return lax.dot_general(
        picked, blocks, (((0, 2), (0, 2)), ((), ())), preferred_element_type=jnp.float32
    )


def apply_inverse(residual, inverse):
    product = lax.dot_general(
        residual, inverse, (((1,), (1,)), ((), ())), preferred_element_type=jnp.float32
    )
    return product.astype(jnp.bfloat16)


def solve_level(right, inverse, blocks, sources, count, store):
    width = lax.axis_size("prow")
    ncol = lax.axis_size("pcol")
    picked = pick_sources(sources, count, store, width, ncol)
    total = lax.psum(contract(picked, blocks), "pcol")
    residual = (right.astype(jnp.float32) - total).astype(jnp.bfloat16)
    return apply_inverse(residual, inverse)


def spread(solved):
    ncol = lax.axis_size("pcol")
    column = lax.axis_index("pcol")
    whole = lax.all_gather(solved[None], "prow", axis=0, tiled=True)
    whole = whole.reshape(whole.shape[0] // ncol, ncol, whole.shape[1], whole.shape[2])
    return lax.dynamic_index_in_dim(whole, column, 1, keepdims=False)


def shards(
    right_side,
    lower_inverse,
    upper_inverse,
    lower_blocks,
    lower_sources,
    lower_counts,
    upper_blocks,
    upper_sources,
    upper_counts,
):
    group = lax.axis_size("prow") // lax.axis_size("pcol")
    levels = right_side.shape[1]
    shape = (levels, group, right_side.shape[2], right_side.shape[3])
    forward_store = jnp.zeros(shape, jnp.bfloat16)
    forward_own = []
    for level in range(levels):
        if level == 0:
            solved = apply_inverse(right_side[0, 0], lower_inverse[0, 0])
        else:
            solved = solve_level(
                right_side[0, level],
                lower_inverse[0, level],
                lower_blocks[0, level - 1],
                lower_sources[0, level - 1],
                lower_counts[0, level - 1, 0],
                forward_store,
            )
        forward_own.append(solved)
        if level + 1 < levels:
            forward_store = forward_store.at[level].set(spread(solved))
    backward_store = jnp.zeros(shape, jnp.bfloat16)
    backward_own = [None] * levels
    for level in range(levels - 1, -1, -1):
        if level == levels - 1:
            solved = apply_inverse(forward_own[level], upper_inverse[0, level])
        else:
            solved = solve_level(
                forward_own[level],
                upper_inverse[0, level],
                upper_blocks[0, level],
                upper_sources[0, level],
                upper_counts[0, level, 0],
                backward_store,
            )
        backward_own[level] = solved
        if level > 0:
            backward_store = backward_store.at[level].set(spread(solved))
    return jnp.stack(backward_own)[None]


def solution(mesh):
    in_specs = (
        P("prow", None, None, None),
        P("prow", None, None, None),
        P("prow", None, None, None),
        P("prow", None, "pcol", None, None),
        P("prow", None, "pcol"),
        P("prow", None, "pcol"),
        P("prow", None, "pcol", None, None),
        P("prow", None, "pcol"),
        P("prow", None, "pcol"),
    )
    out_specs = P("prow", None, None, None)
    return jax.shard_map(shards, mesh=mesh, in_specs=in_specs, out_specs=out_specs, check_vma=False)
```

profile of v0, /device:TPU:1, one launch (start us, length us, event | category | flops | bytes accessed | tf_op | source)
XLA Modules:
  0.0 1471.4 jit_solution(6980355928719453003)
XLA Ops:
  6.5 1.8 convolution_convert_fusion.11
  12.0 75.8 %all-gather.21.cloned.1.call-done = bf16[4096,256]{1,0:T(8,128)(2,1)} async-done(((bf16[128,256]{1,0:T(8,128)(2,1)}), bf16[4096,256]{1,0:T(8,128)(2,1)}) %all-gather.21.cloned.1.call-update) | async-done | bytes 2097168 | tf_op jit(solution)/shard_map/all_gather | solution.py:41
  89.6 2.2 convolution_bitcast_fusion.9
  91.8 63.4 %all-reduce.13.cloned.1.call-done = f32[128,256]{1,0:T(8,128)} async-done(((f32[128,256]{1,0:T(8,128)}), f32[128,256]{1,0:T(8,128)}) %all-reduce.13.cloned.1.call-update) | async-done | bytes 131088 | tf_op jit(solution)/shard_map/psum | solution.py:33
  157.8 75.7 %all-gather.23.cloned.1.call-done = bf16[4096,256]{1,0:T(8,128)(2,1)} async-done(((bf16[128,256]{1,0:T(8,128)(2,1)}), bf16[4096,256]{1,0:T(8,128)(2,1)}) %all-gather.23.cloned.1.call-update) | async-done | bytes 2097168 | tf_op jit(solution)/shard_map/all_gather | solution.py:41
  235.0 2.2 convolution_bitcast_fusion.8
  237.3 63.4 %all-reduce.15.cloned.1.call-done = f32[128,256]{1,0:T(8,128)} async-done(((f32[128,256]{1,0:T(8,128)}), f32[128,256]{1,0:T(8,128)}) %all-reduce.15.cloned.1.call-update) | async-done | bytes 131088 | tf_op jit(solution)/shard_map/psum | solution.py:33
  303.2 75.2 %all-gather.25.cloned.1.call-done = bf16[4096,256]{1,0:T(8,128)(2,1)} async-done(((bf16[128,256]{1,0:T(8,128)(2,1)}), bf16[4096,256]{1,0:T(8,128)(2,1)}) %all-gather.25.cloned.1.call-update) | async-done | bytes 2097168 | tf_op jit(solution)/shard_map/all_gather | solution.py:41
  379.9 2.2 convolution_bitcast_fusion.7
  382.2 63.4 %all-reduce.17.cloned.1.call-done = f32[128,256]{1,0:T(8,128)} async-done(((f32[128,256]{1,0:T(8,128)}), f32[128,256]{1,0:T(8,128)}) %all-reduce.17.cloned.1.call-update) | async-done | bytes 131088 | tf_op jit(solution)/shard_map/psum | solution.py:33
  448.1 75.7 %all-gather.27.cloned.1.call-done = bf16[4096,256]{1,0:T(8,128)(2,1)} async-done(((bf16[128,256]{1,0:T(8,128)(2,1)}), bf16[4096,256]{1,0:T(8,128)(2,1)}) %all-gather.27.cloned.1.call-update) | async-done | bytes 2097168 | tf_op jit(solution)/shard_map/all_gather | solution.py:41
  525.4 2.2 convolution_bitcast_fusion.6
  527.6 63.4 %all-reduce.19.cloned.1.call-done = f32[128,256]{1,0:T(8,128)} async-done(((f32[128,256]{1,0:T(8,128)}), f32[128,256]{1,0:T(8,128)}) %all-reduce.19.cloned.1.call-update) | async-done | bytes 131088 | tf_op jit(solution)/shard_map/psum | solution.py:33
  594.6 74.3 %all-gather.29.cloned.1.call-done = bf16[4096,256]{1,0:T(8,128)(2,1)} async-done(((bf16[128,256]{1,0:T(8,128)(2,1)}), bf16[4096,256]{1,0:T(8,128)(2,1)}) %all-gather.29.cloned.1.call-update) | async-done | bytes 2097168 | tf_op jit(solution)/shard_map/all_gather | solution.py:41
  670.5 2.2 convolution_bitcast_fusion.5
  672.7 63.4 %all-reduce.21.cloned.1.call-done = f32[128,256]{1,0:T(8,128)} async-done(((f32[128,256]{1,0:T(8,128)}), f32[128,256]{1,0:T(8,128)}) %all-reduce.21.cloned.1.call-update) | async-done | bytes 131088 | tf_op jit(solution)/shard_map/psum | solution.py:33
  736.2 1.9 convolution_convert_fusion.5
  740.1 74.3 %all-gather.31.cloned.1.call-done = bf16[4096,256]{1,0:T(8,128)(2,1)} async-done(((bf16[128,256]{1,0:T(8,128)(2,1)}), bf16[4096,256]{1,0:T(8,128)(2,1)}) %all-gather.31.cloned.1.call-update) | async-done | bytes 2097168 | tf_op jit(solution)/shard_map/all_gather | solution.py:41
  816.1 2.2 convolution_bitcast_fusion.4
  818.4 63.4 %all-reduce.23.cloned.1.call-done = f32[128,256]{1,0:T(8,128)} async-done(((f32[128,256]{1,0:T(8,128)}), f32[128,256]{1,0:T(8,128)}) %all-reduce.23.cloned.1.call-update) | async-done | bytes 131088 | tf_op jit(solution)/shard_map/psum | solution.py:33
  884.3 75.3 %all-gather.33.cloned.1.call-done = bf16[4096,256]{1,0:T(8,128)(2,1)} async-done(((bf16[128,256]{1,0:T(8,128)(2,1)}), bf16[4096,256]{1,0:T(8,128)(2,1)}) %all-gather.33.cloned.1.call-update) | async-done | bytes 2097168 | tf_op jit(solution)/shard_map/all_gather | solution.py:41
  961.2 2.2 convolution_bitcast_fusion.3
  963.5 63.4 %all-reduce.25.cloned.1.call-done = f32[128,256]{1,0:T(8,128)} async-done(((f32[128,256]{1,0:T(8,128)}), f32[128,256]{1,0:T(8,128)}) %all-reduce.25.cloned.1.call-update) | async-done | bytes 131088 | tf_op jit(solution)/shard_map/psum | solution.py:33
  1029.3 75.6 %all-gather.35.cloned.1.call-done = bf16[4096,256]{1,0:T(8,128)(2,1)} async-done(((bf16[128,256]{1,0:T(8,128)(2,1)}), bf16[4096,256]{1,0:T(8,128)(2,1)}) %all-gather.35.cloned.1.call-update) | async-done | bytes 2097168 | tf_op jit(solution)/shard_map/all_gather | solution.py:41
  1106.5 2.2 convolution_bitcast_fusion.2
  1108.8 63.4 %all-reduce.27.cloned.1.call-done = f32[128,256]{1,0:T(8,128)} async-done(((f32[128,256]{1,0:T(8,128)}), f32[128,256]{1,0:T(8,128)}) %all-reduce.27.cloned.1.call-update) | async-done | bytes 131088 | tf_op jit(solution)/shard_map/psum | solution.py:33
  1174.6 75.2 %all-gather.37.cloned.1.call-done = bf16[4096,256]{1,0:T(8,128)(2,1)} async-done(((bf16[128,256]{1,0:T(8,128)(2,1)}), bf16[4096,256]{1,0:T(8,128)(2,1)}) %all-gather.37.cloned.1.call-update) | async-done | bytes 2097168 | tf_op jit(solution)/shard_map/all_gather | solution.py:41
  1251.4 2.2 convolution_bitcast_fusion.1
  1253.7 63.4 %all-reduce.29.cloned.1.call-done = f32[128,256]{1,0:T(8,128)} async-done(((f32[128,256]{1,0:T(8,128)}), f32[128,256]{1,0:T(8,128)}) %all-reduce.29.cloned.1.call-update) | async-done | bytes 131088 | tf_op jit(solution)/shard_map/psum | solution.py:33
  1319.6 75.7 %all-gather.39.cloned.1.call-done = bf16[4096,256]{1,0:T(8,128)(2,1)} async-done(((bf16[128,256]{1,0:T(8,128)(2,1)}), bf16[4096,256]{1,0:T(8,128)(2,1)}) %all-gather.39.cloned.1.call-update) | async-done | bytes 2097168 | tf_op jit(solution)/shard_map/all_gather | solution.py:41
  1396.9 2.2 convolution_bitcast_fusion
  1399.1 63.5 %all-reduce.31.cloned.1.call-done = f32[128,256]{1,0:T(8,128)} async-done(((f32[128,256]{1,0:T(8,128)}), f32[128,256]{1,0:T(8,128)}) %all-reduce.31.cloned.1.call-update) | async-done | bytes 131088 | tf_op jit(solution)/shard_map/psum | solution.py:33
  (133 shorter events, 44.5 us)
Async XLA Ops:
  6.5 81.3 %all-gather.21.cloned.1.call-start = ((), (), s32[]{:S(2)}) async-start(), calls=%async_computation.10 | async-start | bytes 2162688 | tf_op jit(solution)/shard_map/all_gather | solution.py:41
  8.3 146.9 %all-reduce.13.cloned.1.call-start = ((), (), s32[]{:S(2)}) async-start(), calls=%async_computation | async-start | bytes 262144 | tf_op jit(solution)/shard_map/psum | solution.py:33
  91.8 141.7 %all-gather.23.cloned.1.call-start = ((), (), s32[]{:S(2)}) async-start(), calls=%async_computation.11 | async-start | bytes 2162688 | tf_op jit(solution)/shard_map/all_gather | solution.py:41
  157.0 143.7 %all-reduce.15.cloned.1.call-start = ((), (), s32[]{:S(2)}) async-start(), calls=%async_computation.1 | async-start | bytes 262144 | tf_op jit(solution)/shard_map/psum | solution.py:33
  237.2 141.2 %all-gather.25.cloned.1.call-start = ((), (), s32[]{:S(2)}) async-start(), calls=%async_computation.12 | async-start | bytes 2162688 | tf_op jit(solution)/shard_map/all_gather | solution.py:41
  302.4 143.2 %all-reduce.17.cloned.1.call-start = ((), (), s32[]{:S(2)}) async-start(), calls=%async_computation.2 | async-start | bytes 262144 | tf_op jit(solution)/shard_map/psum | solution.py:33
  382.1 141.7 %all-gather.27.cloned.1.call-start = ((), (), s32[]{:S(2)}) async-start(), calls=%async_computation.13 | async-start | bytes 2162688 | tf_op jit(solution)/shard_map/all_gather | solution.py:41
  447.4 143.7 %all-reduce.19.cloned.1.call-start = ((), (), s32[]{:S(2)}) async-start(), calls=%async_computation.3 | async-start | bytes 262144 | tf_op jit(solution)/shard_map/psum | solution.py:33
  527.6 208.6 %copy-start = (bf16[1,6,256,256]{3,2,1,0:T(8,128)(2,1)S(1)}, bf16[1,6,256,256]{3,2,1,0:T(8,128)(2,1)}, u32[]{:S(2)}) copy-start(bf16[1,6,256,256]{3,2,1,0:T(8,128)(2,1)} %param.31) | copy-start | bytes 2359300
  527.6 210.5 %copy-start.13 = (s32[1,5,1]{1,2,0:T(1,128)S(1)}, s32[1,5,1]{1,2,0:T(1,128)}, u32[]{:S(2)}) copy-start(s32[1,5,1]{1,2,0:T(1,128)} %param.37) | copy-start | bytes 64
  527.6 141.3 %all-gather.29.cloned.1.call-start = ((), (), s32[]{:S(2)}) async-start(), calls=%async_computation.14 | async-start | bytes 2162688 | tf_op jit(solution)/shard_map/all_gather | solution.py:41
  592.8 143.4 %all-reduce.21.cloned.1.call-start = ((), (), s32[]{:S(2)}) async-start(), calls=%async_computation.4 | async-start | bytes 262144 | tf_op jit(solution)/shard_map/psum | solution.py:33
  672.7 141.7 %all-gather.31.cloned.1.call-start = ((), (), s32[]{:S(2)}) async-start(), calls=%async_computation.15 | async-start | bytes 2162688 | tf_op jit(solution)/shard_map/all_gather | solution.py:41
  738.1 143.7 %all-reduce.23.cloned.1.call-start = ((), (), s32[]{:S(2)}) async-start(), calls=%async_computation.5 | async-start | bytes 262144 | tf_op jit(solution)/shard_map/psum | solution.py:33
  818.3 208.6 %copy-start.9 = (bf16[128,256]{1,0:T(8,128)(2,1)S(1)}, bf16[128,256]{1,0:T(8,128)(2,1)}, u32[]{:S(2)}) copy-start(bf16[128,256]{1,0:T(8,128)(2,1)} %convolution_convert_fusion.8) | copy-start | bytes 196612
  818.3 211.0 %copy-start.15 = (s32[6]{0:T(128)S(1)}, s32[6]{0:T(128)}, u32[]{:S(2)}) copy-start(s32[6]{0:T(128)} %get-tuple-element.148) | copy-start | bytes 76
  818.3 141.3 %all-gather.33.cloned.1.call-start = ((), (), s32[]{:S(2)}) async-start(), calls=%async_computation.16 | async-start | bytes 2162688 | tf_op jit(solution)/shard_map/all_gather | solution.py:41
  883.6 143.3 %all-reduce.25.cloned.1.call-start = ((), (), s32[]{:S(2)}) async-start(), calls=%async_computation.6 | async-start | bytes 262144 | tf_op jit(solution)/shard_map/psum | solution.py:33
  963.4 208.8 %copy-start.8 = (bf16[128,256]{1,0:T(8,128)(2,1)S(1)}, bf16[128,256]{1,0:T(8,128)(2,1)}, u32[]{:S(2)}) copy-start(bf16[128,256]{1,0:T(8,128)(2,1)} %convolution_convert_fusion.9) | copy-start | bytes 196612
  963.4 141.5 %all-gather.35.cloned.1.call-start = ((), (), s32[]{:S(2)}) async-start(), calls=%async_computation.17 | async-start | bytes 2162688 | tf_op jit(solution)/shard_map/all_gather | solution.py:41
  1028.7 143.5 %all-reduce.27.cloned.1.call-start = ((), (), s32[]{:S(2)}) async-start(), calls=%async_computation.7 | async-start | bytes 262144 | tf_op jit(solution)/shard_map/psum | solution.py:33
  1108.7 208.5 %copy-start.7 = (bf16[128,256]{1,0:T(8,128)(2,1)S(1)}, bf16[128,256]{1,0:T(8,128)(2,1)}, u32[]{:S(2)}) copy-start(bf16[128,256]{1,0:T(8,128)(2,1)} %convolution_convert_fusion.10) | copy-start | bytes 196612
  1108.7 141.2 %all-gather.37.cloned.1.call-start = ((), (), s32[]{:S(2)}) async-start(), calls=%async_computation.18 | async-start | bytes 2162688 | tf_op jit(solution)/shard_map/all_gather | solution.py:41
  1174.0 143.2 %all-reduce.29.cloned.1.call-start = ((), (), s32[]{:S(2)}) async-start(), calls=%async_computation.8 | async-start | bytes 262144 | tf_op jit(solution)/shard_map/psum | solution.py:33
  1253.6 208.9 %copy-start.6 = (bf16[128,256]{1,0:T(8,128)(2,1)S(1)}, bf16[128,256]{1,0:T(8,128)(2,1)}, u32[]{:S(2)}) copy-start(bf16[128,256]{1,0:T(8,128)(2,1)} %convolution_convert_fusion.11) | copy-start | bytes 196612
  1253.7 210.0 %copy-start.4 = (bf16[128,256]{1,0:T(8,128)(2,1)S(1)}, bf16[128,256]{1,0:T(8,128)(2,1)}, u32[]{:S(2)}) copy-start(bf16[128,256]{1,0:T(8,128)(2,1)} %convolution_convert_fusion.2) | copy-start | bytes 196612
  1253.7 210.0 %copy-start.3 = (bf16[128,256]{1,0:T(8,128)(2,1)S(1)}, bf16[128,256]{1,0:T(8,128)(2,1)}, u32[]{:S(2)}) copy-start(bf16[128,256]{1,0:T(8,128)(2,1)} %convolution_convert_fusion.3) | copy-start | bytes 196612
  1253.7 141.6 %all-gather.39.cloned.1.call-start = ((), (), s32[]{:S(2)}) async-start(), calls=%async_computation.19 | async-start | bytes 2162688 | tf_op jit(solution)/shard_map/all_gather | solution.py:41
  1318.9 144.8 %copy-start.5 = (bf16[128,256]{1,0:T(8,128)(2,1)S(1)}, bf16[128,256]{1,0:T(8,128)(2,1)}, u32[]{:S(2)}) copy-start(bf16[128,256]{1,0:T(8,128)(2,1)} %convolution_convert_fusion.1) | copy-start | bytes 196612
  1318.9 144.9 %copy-start.2 = (bf16[128,256]{1,0:T(8,128)(2,1)S(1)}, bf16[128,256]{1,0:T(8,128)(2,1)}, u32[]{:S(2)}) copy-start(bf16[128,256]{1,0:T(8,128)(2,1)} %convolution_convert_fusion.4) | copy-start | bytes 196612
  1318.9 144.9 %copy-start.11 = (bf16[128,256]{1,0:T(8,128)(2,1)S(1)}, bf16[128,256]{1,0:T(8,128)(2,1)}, u32[]{:S(2)}) copy-start(bf16[128,256]{1,0:T(8,128)(2,1)} %convolution_convert_fusion.5) | copy-start | bytes 196612
  1318.9 143.6 %all-reduce.31.cloned.1.call-start = ((), (), s32[]{:S(2)}) async-start(), calls=%async_computation.9 | async-start | bytes 262144 | tf_op jit(solution)/shard_map/psum | solution.py:33
  (5 other events, 269.1 us)
Sparse Core Ops, SparseCore 0:
  9.9 77.8 all-gather.20
  91.9 63.3 all-reduce.12
  158.2 75.2 all-gather.22
  237.3 63.2 all-reduce.14
  303.1 75.2 all-gather.24
  382.3 63.3 all-reduce.16
  448.6 75.2 all-gather.26
  527.7 63.3 all-reduce.18
  593.7 75.2 all-gather.28
  672.8 63.3 all-reduce.20
  739.1 75.2 all-gather.30
  818.4 63.3 all-reduce.22
  884.4 75.2 all-gather.32
  963.5 63.3 all-reduce.24
  1029.7 75.2 all-gather.34
  1108.8 63.3 all-reduce.26
  1174.6 75.2 all-gather.36
  1253.8 63.3 all-reduce.28
  1320.1 75.2 all-gather.38
  1399.2 63.2 all-reduce.30
where the time goes:
time: 1470 us
  waiting for transfers between devices  1390 us (95%)
  matrix products  40.5 us (3%)
  local copies, waits for them, and re-layouts  18.7 us (1%)
    all_gather x10, waiting for transfers between devices, spread(): whole = lax.all_gather(solved[None], 'prow', axis=0, tiled=True)  753 us
    psum x10, waiting for transfers between devices, solve_level(): total = lax.psum(contract(picked, blocks), 'pcol')  634 us
  transfers between devices with their start and end apart: 20, of which 20 were waited for; matrix products, arithmetic and copies ran while one was open for 1% of the time, Pallas kernels for 0%

commit v1 on v0

v1 whole, which is shorter than its diff:
```python
import functools

import jax
import jax.numpy as jnp
from jax import lax
from jax.experimental import pallas as pl
from jax.experimental.pallas import tpu as pltpu
from jax.sharding import PartitionSpec as P

BF = jnp.bfloat16
F32 = jnp.float32
NT = (((1,), (1,)), ((), ()))


def update_kernel(low, levels, width, ncol, level, sources, counts, blocks, *rest):
    stores = rest[:levels]
    out, held, sems = rest[levels:]
    slots = held.shape[0]
    count = counts[level]

    def copy(slot):
        return pltpu.make_async_copy(blocks.at[0, level, slot], held.at[slot], sems.at[slot])

    for slot in range(slots):

        @pl.when(slot < count)
        def _():
            copy(slot).start()

    out[...] = jnp.zeros_like(out)
    for slot in range(slots):

        @pl.when(slot < count)
        def _():
            copy(slot).wait()
            source = sources[level, slot]
            step = source // width - low
            place = source % width // ncol
            for v in range(levels):

                @pl.when(step == v)
                def _():
                    out[...] += lax.dot_general(stores[v][place], held[slot], NT, preferred_element_type=F32)


def update(low, stores, level, sources, counts, blocks, width, ncol):
    slots, size = blocks.shape[2], blocks.shape[3]
    nrhs = stores[0].shape[1]
    smem = pl.BlockSpec(memory_space=pltpu.SMEM)
    vmem = pl.BlockSpec(memory_space=pltpu.VMEM)
    return pl.pallas_call(
        functools.partial(update_kernel, low, len(stores), width, ncol, level),
        out_shape=jax.ShapeDtypeStruct((nrhs, size), F32),
        in_specs=[smem, smem, pl.BlockSpec(memory_space=pl.ANY)] + [vmem] * len(stores),
        out_specs=vmem,
        scratch_shapes=[pltpu.VMEM((slots, size, size), BF), pltpu.SemaphoreType.DMA((slots,))],
        name="update",
    )(sources, counts, blocks, *stores)


def finish_kernel(right, parts, inverse, out):
    total = parts[0]
    for i in range(1, parts.shape[0]):
        total = total + parts[i]
    residual = (right[...].astype(F32) - total).astype(BF)
    out[...] = lax.dot_general(residual, inverse[...], NT, preferred_element_type=F32).astype(BF)


def finish(right, parts, inverse):
    vmem = pl.BlockSpec(memory_space=pltpu.VMEM)
    return pl.pallas_call(
        finish_kernel,
        out_shape=jax.ShapeDtypeStruct(right.shape, BF),
        in_specs=[vmem] * 3,
        out_specs=vmem,
        name="finish",
    )(right, parts, inverse)


def apply_inverse(residual, inverse):
    return lax.dot_general(residual, inverse, NT, preferred_element_type=F32).astype(BF)


def shards(
    right_side,
    lower_inverse,
    upper_inverse,
    lower_blocks,
    lower_sources,
    lower_counts,
    upper_blocks,
    upper_sources,
    upper_counts,
):
    width = lax.axis_size("prow")
    ncol = lax.axis_size("pcol")
    group = width // ncol
    column = lax.axis_index("pcol")
    levels, nrhs, size = right_side.shape[1:]
    part = nrhs // ncol
    turn = [
        ((g * ncol + z) * ncol + c, (g * ncol + c) * ncol + z)
        for g in range(group)
        for z in range(ncol)
        for c in range(ncol)
    ]
    right = lax.dynamic_slice_in_dim(right_side[0], column * part, part, 1)

    def spread(solved):
        solved = lax.ppermute(solved, ("prow", "pcol"), turn)
        solved = jnp.broadcast_to(solved[None], (width, part, size))
        whole = lax.all_to_all(solved, "prow", 0, 0, tiled=True)
        return whole.reshape(group, nrhs, size)

    def reduce(partial):
        return lax.all_to_all(partial.reshape(ncol, part, size), "pcol", 0, 0, tiled=True)

    lower_args = (lower_sources[0], lower_counts[0, :, 0], lower_blocks, width, ncol)
    upper_args = (upper_sources[0], upper_counts[0, :, 0], upper_blocks, width, ncol)
    own = []
    stores = []
    for level in range(levels):
        if level == 0:
            solved = apply_inverse(right[0], lower_inverse[0, 0])
        else:
            partial = update(0, stores, level - 1, *lower_args)
            solved = finish(right[level], reduce(partial), lower_inverse[0, level])
        own.append(solved)
        if level + 1 < levels:
            stores.append(spread(solved))
    result = [None] * levels
    stores = []
    for level in range(levels - 1, -1, -1):
        if level == levels - 1:
            solved = apply_inverse(own[level], upper_inverse[0, level])
        else:
            partial = update(level + 1, stores, level, *upper_args)
            solved = finish(own[level], reduce(partial), upper_inverse[0, level])
        result[level] = solved
        if level > 0:
            stores.insert(0, spread(solved))
    whole = jnp.broadcast_to(jnp.stack(result)[None], (ncol, levels, part, size))
    whole = lax.all_to_all(whole, "pcol", 0, 0, tiled=True)
    return jnp.transpose(whole, (1, 0, 2, 3)).reshape(1, levels, nrhs, size)


def solution(mesh):
    in_specs = (
        P("prow", None, None, None),
        P("prow", None, None, None),
        P("prow", None, None, None),
        P("prow", None, "pcol", None, None),
        P("prow", None, "pcol"),
        P("prow", None, "pcol"),
        P("prow", None, "pcol", None, None),
        P("prow", None, "pcol"),
        P("prow", None, "pcol"),
    )
    out_specs = P("prow", None, None, None)
    return jax.shard_map(shards, mesh=mesh, in_specs=in_specs, out_specs=out_specs, check_vma=False)
```

time: 1470 us -> 459 us (0.31)
  waiting for transfers between devices: 1390 us -> 42.5 us
  blocking collectives: 0 us -> 272 us
  starting transfers between devices: 0.8 us -> 77.8 us
  Pallas kernels: 0 us -> 50.1 us
  matrix products: 40.5 us -> 1.98 us
    all_gather x10 -> x0, waiting for transfers between devices: 753 us -> none  [spread(): whole = lax.all_gather(solved[None], 'prow', axis=0, tiled=True)]
    psum x10 -> x0, waiting for transfers between devices: 634 us -> none  [solve_level(): total = lax.psum(contract(picked, blocks), 'pcol')]
    all_to_all x0 -> x17, blocking collectives: none -> 272 us  [the longest x8 147 us: spread(): whole = lax.all_to_all(solved, 'prow', 0, 0, tiled=True)]
    pallas_call x0 -> x20, Pallas kernels: none -> 50.1 us  [the longest x10 32.5 us: update(): pl.pallas_call(functools.partial(update_kernel, low, len(stores), width,...]
    all_to_all x0 -> x4, starting transfers between devices: none -> 42.5 us  [the longest x2 25.7 us: spread(): whole = lax.all_to_all(solved, 'prow', 0, 0, tiled=True)]
    dot_general x21 -> x2, matrix products: 40.5 us -> 1.98 us  [apply_inverse(): lax.dot_general(residual, inverse, NT, preferred_element_type=F32)]
    ppermute x0 -> x10, starting transfers between devices: none -> 35.3 us  [spread(): solved = lax.ppermute(solved, ('prow', 'pcol'), turn)]
    all_to_all x0 -> x4, waiting for transfers between devices: none -> 24.9 us  [the longest x2 17.4 us: spread(): whole = lax.all_to_all(solved, 'prow', 0, 0, tiled=True)]
  transfers between devices with their start and end apart: 20 -> 14, of which waited for: 20 -> 14; matrix products, arithmetic and copies ran while one was open for 1% -> 1% of each run, Pallas kernels for 0% -> 0%
where the time goes in v1:
time: 459 us; the launch traced here: 456 us
  blocking collectives  272 us (59%)
  starting transfers between devices  77.8 us (17%)
  Pallas kernels  50.1 us (11%)
  waiting for transfers between devices  42.5 us (9%)
  local copies, waits for them, and re-layouts  10.8 us (2%)
    all_to_all x8, blocking collectives, spread(): whole = lax.all_to_all(solved, 'prow', 0, 0, tiled=True)  147 us
    all_to_all x8, blocking collectives, reduce(): lax.all_to_all(partial.reshape(ncol, part, size), 'pcol', 0, 0, tiled=True)  113 us
    ppermute x10, starting transfers between devices, spread(): solved = lax.ppermute(solved, ('prow', 'pcol'), turn)  35.3 us
    pallas_call x10, Pallas kernels, update(): pl.pallas_call(functools.partial(update_kernel, low, len(stores), width,...  32.5 us
    all_to_all x2, starting transfers between devices, spread(): whole = lax.all_to_all(solved, 'prow', 0, 0, tiled=True)  25.7 us
    pallas_call x10, Pallas kernels, finish(): pl.pallas_call(finish_kernel, out_shape=jax.ShapeDtypeStruct(right.shape,...  17.6 us
    ppermute x10, waiting for transfers between devices, spread(): solved = lax.ppermute(solved, ('prow', 'pcol'), turn)  17.5 us
    all_to_all x2, waiting for transfers between devices, spread(): whole = lax.all_to_all(solved, 'prow', 0, 0, tiled=True)  17.4 us
  transfers between devices with their start and end apart: 14, of which 14 were waited for; matrix products, arithmetic and copies ran while one was open for 1% of the time, Pallas kernels for 0%

profile of v1, /device:TPU:1, one launch (start us, length us, event | category | flops | bytes accessed | tf_op | source)
XLA Modules:
  0.0 455.6 jit_solution(12520021675710095637)
XLA Ops:
  1.1 5.0 %collective-permute-start = (bf16[16,256]{1,0:T(8,128)(2,1)S(1)}, bf16[16,256]{1,0:T(8,128)(2,1)S(1)}, u32[]{:S(2)}, u32[]{:S(2)}) collective-permute-start(bf16[16,256]{1,0:T(8,128)(2,1)S(1)} %convolution_convert_fusion.1.right), channel_id=1, source_target_pairs={{0,0},{1,8},{2,16},{3,24},{4,32},{5,40},{6,48},{7,56},{8,1},{9,9},... | collective-permute-start | bytes 24584 | tf_op jit(solution)/shard_map/ppermute | solution.py:110
  8.2 16.2 %all-to-all-start = ((bf16[32,16,256]{2,1,0:T(8,128)(2,1)}), bf16[32,16,256]{2,1,0:T(8,128)(2,1)S(1)}, u32[]{:S(2)}, u32[]{:S(2)}) async-start(bf16[32,16,256]{2,1,0:T(8,128)(2,1)} %broadcast_in_dim.22), calls=%async_computation | async-start | bytes 524288 | tf_op jit(solution)/shard_map/all_to_all | solution.py:112
  25.6 8.4 %all-to-all-done = bf16[32,16,256]{2,1,0:T(8,128)(2,1)S(1)} async-done(((bf16[32,16,256]{2,1,0:T(8,128)(2,1)}), bf16[32,16,256]{2,1,0:T(8,128)(2,1)S(1)}, u32[]{:S(2)}, u32[]{:S(2)}) %all-to-all-start) | async-done | bytes 262176 | tf_op jit(solution)/shard_map/all_to_all | solution.py:112
  37.5 8.8 %all-to-all-start.1 = ((f32[8,16,256]{2,1,0:T(8,128)}), f32[8,16,256]{2,1,0:T(8,128)S(1)}, u32[]{:S(2)}, u32[]{:S(2)}) async-start(f32[8,16,256]{2,1,0:T(8,128)} %bitcast.121), calls=%async_computation.1 | async-start | bytes 262144 | tf_op jit(solution)/shard_map/all_to_all | solution.py:116
  59.2 18.1 %all_to_all.105 = bf16[32,16,256]{2,1,0:T(8,128)(2,1)} all-to-all(bf16[32,16,256]{2,1,0:T(8,128)(2,1)S(1)} %broadcast_in_dim.23), channel_id=1, replica_groups=mesh['prow'=32,'pcol'=8] {'prow'}, dimensions={0} | all-to-all | bytes 524288 | tf_op jit(solution)/shard_map/all_to_all | solution.py:112
  80.2 14.8 %all_to_all.106.parts = f32[8,16,256]{2,1,0:T(8,128)} all-to-all(f32[8,16,256]{2,1,0:T(8,128)} %bitcast.115), channel_id=1, replica_groups=mesh['prow'=32,'pcol'=8] {'pcol'}, dimensions={0} | all-to-all | bytes 262144 | tf_op jit(solution)/shard_map/all_to_all | solution.py:116
  96.8 3.4 collective-permute-start.2
  102.0 18.5 %all_to_all.107 = bf16[32,16,256]{2,1,0:T(8,128)(2,1)} all-to-all(bf16[32,16,256]{2,1,0:T(8,128)(2,1)S(1)} %broadcast_in_dim.24), channel_id=1, replica_groups=mesh['prow'=32,'pcol'=8] {'prow'}, dimensions={0} | all-to-all | bytes 524288 | tf_op jit(solution)/shard_map/all_to_all | solution.py:112
  123.7 13.9 %all_to_all.108.parts = f32[8,16,256]{2,1,0:T(8,128)} all-to-all(f32[8,16,256]{2,1,0:T(8,128)} %bitcast.116), channel_id=1, replica_groups=mesh['prow'=32,'pcol'=8] {'pcol'}, dimensions={0} | all-to-all | bytes 262144 | tf_op jit(solution)/shard_map/all_to_all | solution.py:116
  139.4 3.5 collective-permute-start.3
  144.5 18.3 %all_to_all.109 = bf16[32,16,256]{2,1,0:T(8,128)(2,1)} all-to-all(bf16[32,16,256]{2,1,0:T(8,128)(2,1)S(1)} %broadcast_in_dim.25), channel_id=1, replica_groups=mesh['prow'=32,'pcol'=8] {'prow'}, dimensions={0} | all-to-all | bytes 524288 | tf_op jit(solution)/shard_map/all_to_all | solution.py:112
  166.1 14.8 %all_to_all.110.parts = f32[8,16,256]{2,1,0:T(8,128)} all-to-all(f32[8,16,256]{2,1,0:T(8,128)} %bitcast.117), channel_id=1, replica_groups=mesh['prow'=32,'pcol'=8] {'pcol'}, dimensions={0} | all-to-all | bytes 262144 | tf_op jit(solution)/shard_map/all_to_all | solution.py:116
  182.7 3.4 collective-permute-start.4
  187.9 18.2 %all_to_all.111 = bf16[32,16,256]{2,1,0:T(8,128)(2,1)} all-to-all(bf16[32,16,256]{2,1,0:T(8,128)(2,1)S(1)} %broadcast_in_dim.26), channel_id=1, replica_groups=mesh['prow'=32,'pcol'=8] {'prow'}, dimensions={0} | all-to-all | bytes 524288 | tf_op jit(solution)/shard_map/all_to_all | solution.py:112
  206.1 4.0 update.14
  210.1 13.1 %all_to_all.112.parts = f32[8,16,256]{2,1,0:T(8,128)} all-to-all(f32[8,16,256]{2,1,0:T(8,128)} %bitcast.113), channel_id=1, replica_groups=mesh['prow'=32,'pcol'=8] {'pcol'}, dimensions={0} | all-to-all | bytes 262144 | tf_op jit(solution)/shard_map/all_to_all | solution.py:116
  231.5 9.5 %all-to-all-start.10 = ((bf16[32,16,256]{2,1,0:T(8,128)(2,1)}), bf16[32,16,256]{2,1,0:T(8,128)(2,1)S(1)}, u32[]{:S(2)}, u32[]{:S(2)}) async-start(bf16[32,16,256]{2,1,0:T(8,128)(2,1)} %broadcast_in_dim.27), calls=%async_computation.10 | async-start | bytes 524288 | tf_op jit(solution)/shard_map/all_to_all | solution.py:112
  241.7 9.1 %all-to-all-done.10 = bf16[32,16,256]{2,1,0:T(8,128)(2,1)S(1)} async-done(((bf16[32,16,256]{2,1,0:T(8,128)(2,1)}), bf16[32,16,256]{2,1,0:T(8,128)(2,1)S(1)}, u32[]{:S(2)}, u32[]{:S(2)}) %all-to-all-start.10) | async-done | bytes 262176 | tf_op jit(solution)/shard_map/all_to_all | solution.py:112
  254.4 8.0 %all-to-all-start.11 = ((f32[8,16,256]{2,1,0:T(8,128)}), f32[8,16,256]{2,1,0:T(8,128)S(1)}, u32[]{:S(2)}, u32[]{:S(2)}) async-start(f32[8,16,256]{2,1,0:T(8,128)} %bitcast.122), calls=%async_computation.11 | async-start | bytes 262144 | tf_op jit(solution)/shard_map/all_to_all | solution.py:116
  263.3 4.4 all-to-all-done.11.parts
  270.2 3.8 collective-permute-start.6
  275.5 18.7 %all_to_all.113 = bf16[32,16,256]{2,1,0:T(8,128)(2,1)} all-to-all(bf16[32,16,256]{2,1,0:T(8,128)(2,1)S(1)} %broadcast_in_dim.28), channel_id=1, replica_groups=mesh['prow'=32,'pcol'=8] {'prow'}, dimensions={0} | all-to-all | bytes 524288 | tf_op jit(solution)/shard_map/all_to_all | solution.py:112
  297.0 14.0 %all_to_all.114.parts = f32[8,16,256]{2,1,0:T(8,128)} all-to-all(f32[8,16,256]{2,1,0:T(8,128)} %bitcast.118), channel_id=1, replica_groups=mesh['prow'=32,'pcol'=8] {'pcol'}, dimensions={0} | all-to-all | bytes 262144 | tf_op jit(solution)/shard_map/all_to_all | solution.py:116
  318.0 18.8 %all_to_all.115 = bf16[32,16,256]{2,1,0:T(8,128)(2,1)} all-to-all(bf16[32,16,256]{2,1,0:T(8,128)(2,1)S(1)} %broadcast_in_dim.29), channel_id=1, replica_groups=mesh['prow'=32,'pcol'=8] {'prow'}, dimensions={0} | all-to-all | bytes 524288 | tf_op jit(solution)/shard_map/all_to_all | solution.py:112
  336.8 4.0 update.17
  340.8 14.0 %all_to_all.116.parts = f32[8,16,256]{2,1,0:T(8,128)} all-to-all(f32[8,16,256]{2,1,0:T(8,128)} %bitcast.119), channel_id=1, replica_groups=mesh['prow'=32,'pcol'=8] {'pcol'}, dimensions={0} | all-to-all | bytes 262144 | tf_op jit(solution)/shard_map/all_to_all | solution.py:116
  361.7 18.0 %all_to_all.117 = bf16[32,16,256]{2,1,0:T(8,128)(2,1)} all-to-all(bf16[32,16,256]{2,1,0:T(8,128)(2,1)S(1)} %broadcast_in_dim.30), channel_id=1, replica_groups=mesh['prow'=32,'pcol'=8] {'prow'}, dimensions={0} | all-to-all | bytes 524288 | tf_op jit(solution)/shard_map/all_to_all | solution.py:112
  383.0 14.0 %all_to_all.118.parts = f32[8,16,256]{2,1,0:T(8,128)} all-to-all(f32[8,16,256]{2,1,0:T(8,128)} %bitcast.120), channel_id=1, replica_groups=mesh['prow'=32,'pcol'=8] {'pcol'}, dimensions={0} | all-to-all | bytes 262144 | tf_op jit(solution)/shard_map/all_to_all | solution.py:116
  398.8 3.4 collective-permute-start.9
  404.1 18.8 %all_to_all.119 = bf16[32,16,256]{2,1,0:T(8,128)(2,1)} all-to-all(bf16[32,16,256]{2,1,0:T(8,128)(2,1)S(1)} %broadcast_in_dim.31), channel_id=1, replica_groups=mesh['prow'=32,'pcol'=8] {'prow'}, dimensions={0} | all-to-all | bytes 524288 | tf_op jit(solution)/shard_map/all_to_all | solution.py:112
  426.3 14.7 %all_to_all.120.parts = f32[8,16,256]{2,1,0:T(8,128)} all-to-all(f32[8,16,256]{2,1,0:T(8,128)} %bitcast.114), channel_id=1, replica_groups=mesh['prow'=32,'pcol'=8] {'pcol'}, dimensions={0} | all-to-all | bytes 262144 | tf_op jit(solution)/shard_map/all_to_all | solution.py:116
  443.5 11.3 %all_to_all.121 = bf16[8,6,16,256]{3,2,1,0:T(8,128)(2,1)S(1)} all-to-all(bf16[8,6,16,256]{3,2,1,0:T(8,128)(2,1)S(1)} %broadcast_in_dim.32), channel_id=1, replica_groups=mesh['prow'=32,'pcol'=8] {'pcol'}, dimensions={0} | all-to-all | bytes 786432 | tf_op jit(solution)/shard_map/all_to_all | solution.py:143
  (82 shorter events, 88.3 us)
Async XLA Ops:
  0.0 46.3 %copy-start.2 = (bf16[1,6,256,256]{3,2,1,0:T(8,128)(2,1)S(1)}, bf16[1,6,256,256]{3,2,1,0:T(8,128)(2,1)}, u32[]{:S(2)}) copy-start(bf16[1,6,256,256]{3,2,1,0:T(8,128)(2,1)} %param.10) | copy-start | bytes 2359300
  1.1 76.2 %copy-start.6 = (bf16[16,256]{1,0:T(8,128)(2,1)}, bf16[16,256]{1,0:T(8,128)(2,1)S(1)}, u32[]{:S(2)}) copy-start(bf16[16,256]{1,0:T(8,128)(2,1)S(1)} %convolution_convert_fusion.1.right) | copy-start | bytes 24580
  1.1 6.3 %collective-permute-start = (bf16[16,256]{1,0:T(8,128)(2,1)S(1)}, bf16[16,256]{1,0:T(8,128)(2,1)S(1)}, u32[]{:S(2)}, u32[]{:S(2)}) collective-permute-start(bf16[16,256]{1,0:T(8,128)(2,1)S(1)} %convolution_convert_fusion.1.right), channel_id=1, source_target_pairs={{0,0},{1,8},{2,16},{3,24},{4,32},{5,40},{6,48},{7,56},{8,1},{9,9},... | collective-permute-start | bytes 24584 | tf_op jit(solution)/shard_map/ppermute | solution.py:110
  8.2 25.8 %all-to-all-start = ((bf16[32,16,256]{2,1,0:T(8,128)(2,1)}), bf16[32,16,256]{2,1,0:T(8,128)(2,1)S(1)}, u32[]{:S(2)}, u32[]{:S(2)}) async-start(bf16[32,16,256]{2,1,0:T(8,128)(2,1)} %broadcast_in_dim.22), calls=%async_computation | async-start | bytes 524288 | tf_op jit(solution)/shard_map/all_to_all | solution.py:112
  34.0 0.7 copy-start
  37.5 14.1 %all-to-all-start.1 = ((f32[8,16,256]{2,1,0:T(8,128)}), f32[8,16,256]{2,1,0:T(8,128)S(1)}, u32[]{:S(2)}, u32[]{:S(2)}) async-start(f32[8,16,256]{2,1,0:T(8,128)} %bitcast.121), calls=%async_computation.1 | async-start | bytes 262144 | tf_op jit(solution)/shard_map/all_to_all | solution.py:116
  51.6 0.7 copy-start.4
  54.0 5.2 %collective-permute-start.1 = (bf16[16,256]{1,0:T(8,128)(2,1)}, bf16[16,256]{1,0:T(8,128)(2,1)S(1)}, u32[]{:S(2)}, u32[]{:S(2)}) collective-permute-start(bf16[16,256]{1,0:T(8,128)(2,1)} %finish.10.right), channel_id=1, source_target_pairs={{0,0},{1,8},{2,16},{3,24},{4,32},{5,40},{6,48},{7,56},{8,1},{9,9},... | collective-permute-start | bytes 24584 | tf_op jit(solution)/shard_map/ppermute | solution.py:110
  96.8 5.2 %collective-permute-start.2 = (bf16[16,256]{1,0:T(8,128)(2,1)}, bf16[16,256]{1,0:T(8,128)(2,1)S(1)}, u32[]{:S(2)}, u32[]{:S(2)}) collective-permute-start(bf16[16,256]{1,0:T(8,128)(2,1)} %finish.11.right), channel_id=1, source_target_pairs={{0,0},{1,8},{2,16},{3,24},{4,32},{5,40},{6,48},{7,56},{8,1},{9,9},... | collective-permute-start | bytes 24584 | tf_op jit(solution)/shard_map/ppermute | solution.py:110
  139.4 5.2 %collective-permute-start.3 = (bf16[16,256]{1,0:T(8,128)(2,1)}, bf16[16,256]{1,0:T(8,128)(2,1)S(1)}, u32[]{:S(2)}, u32[]{:S(2)}) collective-permute-start(bf16[16,256]{1,0:T(8,128)(2,1)} %finish.12.right), channel_id=1, source_target_pairs={{0,0},{1,8},{2,16},{3,24},{4,32},{5,40},{6,48},{7,56},{8,1},{9,9},... | collective-permute-start | bytes 24584 | tf_op jit(solution)/shard_map/ppermute | solution.py:110
  166.1 58.8 %copy-start.3 = (bf16[1,6,256,256]{3,2,1,0:T(8,128)(2,1)S(1)}, bf16[1,6,256,256]{3,2,1,0:T(8,128)(2,1)}, u32[]{:S(2)}) copy-start(bf16[1,6,256,256]{3,2,1,0:T(8,128)(2,1)} %param.11) | copy-start | bytes 2359300
  180.9 60.2 %copy-start.11 = (s32[1,5,6]{2,0,1:T(1,128)S(1)}, s32[1,5,6]{2,0,1:T(1,128)}, u32[]{:S(2)}) copy-start(s32[1,5,6]{2,0,1:T(1,128)} %param.16) | copy-start | bytes 364
  182.7 5.2 %collective-permute-start.4 = (bf16[16,256]{1,0:T(8,128)(2,1)}, bf16[16,256]{1,0:T(8,128)(2,1)S(1)}, u32[]{:S(2)}, u32[]{:S(2)}) collective-permute-start(bf16[16,256]{1,0:T(8,128)(2,1)} %finish.13.right), channel_id=1, source_target_pairs={{0,0},{1,8},{2,16},{3,24},{4,32},{5,40},{6,48},{7,56},{8,1},{9,9},... | collective-permute-start | bytes 24584 | tf_op jit(solution)/shard_map/ppermute | solution.py:110
  225.8 5.0 %collective-permute-start.5 = (bf16[16,256]{1,0:T(8,128)(2,1)S(1)}, bf16[16,256]{1,0:T(8,128)(2,1)S(1)}, u32[]{:S(2)}, u32[]{:S(2)}) collective-permute-start(bf16[16,256]{1,0:T(8,128)(2,1)S(1)} %convolution_convert_fusion), channel_id=1, source_target_pairs={{0,0},{1,8},{2,16},{3,24},{4,32},{5,40},{6,48},{7,56},{8,1},{9,9},... | collective-permute-start | bytes 24584 | tf_op jit(solution)/shard_map/ppermute | solution.py:110
  231.5 19.2 %all-to-all-start.10 = ((bf16[32,16,256]{2,1,0:T(8,128)(2,1)}), bf16[32,16,256]{2,1,0:T(8,128)(2,1)S(1)}, u32[]{:S(2)}, u32[]{:S(2)}) async-start(bf16[32,16,256]{2,1,0:T(8,128)(2,1)} %broadcast_in_dim.27), calls=%async_computation.10 | async-start | bytes 524288 | tf_op jit(solution)/shard_map/all_to_all | solution.py:112
  250.7 0.7 copy-start.1
  254.4 13.3 %all-to-all-start.11 = ((f32[8,16,256]{2,1,0:T(8,128)}), f32[8,16,256]{2,1,0:T(8,128)S(1)}, u32[]{:S(2)}, u32[]{:S(2)}) async-start(f32[8,16,256]{2,1,0:T(8,128)} %bitcast.122), calls=%async_computation.11 | async-start | bytes 262144 | tf_op jit(solution)/shard_map/all_to_all | solution.py:116
  267.7 0.7 copy-start.5
  270.2 5.3 %collective-permute-start.6 = (bf16[16,256]{1,0:T(8,128)(2,1)}, bf16[16,256]{1,0:T(8,128)(2,1)S(1)}, u32[]{:S(2)}, u32[]{:S(2)}) collective-permute-start(bf16[16,256]{1,0:T(8,128)(2,1)} %finish.15), channel_id=1, source_target_pairs={{0,0},{1,8},{2,16},{3,24},{4,32},{5,40},{6,48},{7,56},{8,1},{9,9},... | collective-permute-start | bytes 24584 | tf_op jit(solution)/shard_map/ppermute | solution.py:110
  312.8 5.2 %collective-permute-start.7 = (bf16[16,256]{1,0:T(8,128)(2,1)}, bf16[16,256]{1,0:T(8,128)(2,1)S(1)}, u32[]{:S(2)}, u32[]{:S(2)}) collective-permute-start(bf16[16,256]{1,0:T(8,128)(2,1)} %finish.16), channel_id=1, source_target_pairs={{0,0},{1,8},{2,16},{3,24},{4,32},{5,40},{6,48},{7,56},{8,1},{9,9},... | collective-permute-start | bytes 24584 | tf_op jit(solution)/shard_map/ppermute | solution.py:110
  356.5 5.2 %collective-permute-start.8 = (bf16[16,256]{1,0:T(8,128)(2,1)}, bf16[16,256]{1,0:T(8,128)(2,1)S(1)}, u32[]{:S(2)}, u32[]{:S(2)}) collective-permute-start(bf16[16,256]{1,0:T(8,128)(2,1)} %finish.17), channel_id=1, source_target_pairs={{0,0},{1,8},{2,16},{3,24},{4,32},{5,40},{6,48},{7,56},{8,1},{9,9},... | collective-permute-start | bytes 24584 | tf_op jit(solution)/shard_map/ppermute | solution.py:110
  383.0 60.4 %copy-start.9 = (bf16[16,256]{1,0:T(8,128)(2,1)S(1)}, bf16[16,256]{1,0:T(8,128)(2,1)}, u32[]{:S(2)}) copy-start(bf16[16,256]{1,0:T(8,128)(2,1)} %finish.17) | copy-start | bytes 24580
  383.0 60.4 %copy-start.8 = (bf16[16,256]{1,0:T(8,128)(2,1)S(1)}, bf16[16,256]{1,0:T(8,128)(2,1)}, u32[]{:S(2)}) copy-start(bf16[16,256]{1,0:T(8,128)(2,1)} %finish.16) | copy-start | bytes 24580
  383.0 60.4 %copy-start.7 = (bf16[16,256]{1,0:T(8,128)(2,1)S(1)}, bf16[16,256]{1,0:T(8,128)(2,1)}, u32[]{:S(2)}) copy-start(bf16[16,256]{1,0:T(8,128)(2,1)} %finish.15) | copy-start | bytes 24580
  398.8 44.6 %copy-start.10 = (bf16[16,256]{1,0:T(8,128)(2,1)S(1)}, bf16[16,256]{1,0:T(8,128)(2,1)}, u32[]{:S(2)}) copy-start(bf16[16,256]{1,0:T(8,128)(2,1)} %finish.18) | copy-start | bytes 24580
  398.8 5.3 %collective-permute-start.9 = (bf16[16,256]{1,0:T(8,128)(2,1)}, bf16[16,256]{1,0:T(8,128)(2,1)S(1)}, u32[]{:S(2)}, u32[]{:S(2)}) collective-permute-start(bf16[16,256]{1,0:T(8,128)(2,1)} %finish.18), channel_id=1, source_target_pairs={{0,0},{1,8},{2,16},{3,24},{4,32},{5,40},{6,48},{7,56},{8,1},{9,9},... | collective-permute-start | bytes 24584 | tf_op jit(solution)/shard_map/ppermute | solution.py:110

commit v2 on v0

v2 whole, which is shorter than its diff:
```python
import functools

import jax
import jax.numpy as jnp
from jax import lax
from jax.experimental import pallas as pl
from jax.experimental.pallas import tpu as pltpu
from jax.sharding import Mesh
from jax.sharding import PartitionSpec as P

BF = jnp.bfloat16
F32 = jnp.float32
I32 = jnp.int32
NT = (((1,), (1,)), ((), ()))
ROW = ("g", "z")
TURNED = ("z", "g")
COL = ("x", "core")
SMEM = pl.BlockSpec(memory_space=pltpu.SMEM)
VMEM = pl.BlockSpec(memory_space=pltpu.VMEM)
ANY = pl.BlockSpec(memory_space=pl.ANY)
HBM = pl.BlockSpec(memory_space=pltpu.HBM)
LAST_SPLIT = 4


def dot(x, y):
    return lax.dot_general(x, y, NT, preferred_element_type=F32)


def run(copies):
    for copy in copies:
        copy.start()
    return copies


def update_kernel(level, table, blocks, *rest):
    *stores, out, held, known, sems = rest
    slots = held.shape[0]
    inputs = run([pltpu.make_async_copy(ref, known.at[i], sems.at[i]) for i, ref in enumerate(stores)])
    weights = run(
        [pltpu.make_async_copy(blocks.at[0, level, i], held.at[i], sems.at[len(stores) + i]) for i in range(slots)]
    )
    for copy in inputs:
        copy.wait()
    total = jnp.zeros(out.shape, F32)
    for slot in range(slots):
        place = table[level, slot]
        at = jnp.maximum(place, 0)
        group = known.shape[2]
        picked = known[at // group, :, at % group].reshape(out.shape)
        picked = jnp.where(place >= 0, picked, jnp.zeros_like(picked))
        weights[slot].wait()
        total += dot(picked, held[slot])
    out[...] = total


def update(level, table, blocks, stores):
    slots, size = blocks.shape[2], blocks.shape[3]
    ncol, group, part, _ = stores[0].shape
    n = len(stores)
    return pl.pallas_call(
        functools.partial(update_kernel, level),
        out_shape=jax.ShapeDtypeStruct((ncol * part, size), F32),
        in_specs=[SMEM, HBM] + [ANY] * n,
        out_specs=VMEM,
        scratch_shapes=[
            pltpu.VMEM((slots, size, size), BF),
            pltpu.VMEM((n, ncol, group, part, size), BF),
            pltpu.SemaphoreType.DMA((n + slots,)),
        ],
        compiler_params=pltpu.CompilerParams(vmem_limit_bytes=6 << 20),
        cost_estimate=pl.CostEstimate(flops=2 * slots * ncol * part * size * size, bytes_accessed=1 << 20, transcendentals=0),
        name="update",
    )(table, blocks, *stores)


def finish_kernel(level, parts, right, inverse, out, spread, held, sem):
    copy = pltpu.make_async_copy(inverse.at[0, level], held, sem)
    copy.start()
    residual = right[level]
    if parts is not None:
        total = parts[0]
        for i in range(1, parts.shape[0]):
            total = total + parts[i]
        residual = (residual.astype(F32) - total).astype(BF)
    copy.wait()
    solved = dot(residual, held[...]).astype(BF)
    out[...] = solved
    for i in range(spread.shape[0]):
        spread[i] = solved


def finish(level, parts, right, inverse, width):
    part, size = right.shape[1:]
    body = functools.partial(finish_kernel, level)
    if parts is None:
        body = functools.partial(finish_kernel, level, None)
    return pl.pallas_call(
        body,
        out_shape=[jax.ShapeDtypeStruct((part, size), BF), jax.ShapeDtypeStruct((width, part, size), BF)],
        in_specs=([] if parts is None else [VMEM]) + [VMEM, ANY],
        out_specs=[VMEM, VMEM],
        scratch_shapes=[pltpu.VMEM((size, size), BF), pltpu.SemaphoreType.DMA(())],
        compiler_params=pltpu.CompilerParams(vmem_limit_bytes=4 << 20),
        cost_estimate=pl.CostEstimate(flops=2 * part * size * size, bytes_accessed=1 << 19, transcendentals=0),
        name="finish",
    )(*([] if parts is None else [parts]), right, inverse)


def solve_kernel(n, low, row, at, levels, table, blocks, right, *rest):
    m = len(levels)
    inverses, rest = rest[:m], rest[m:]
    stores, (out, spread, held, known, diag, sems) = rest[:n], rest[n:]
    ncol, slots = held.shape[:2]
    inputs = run(
        [pltpu.make_async_copy(ref, known.at[pl.ds(i * ref.shape[0], ref.shape[0])], sems.at[i]) for i, ref in enumerate(stores)]
    )
    weights = run([pltpu.make_async_copy(blocks.at[c, at], held.at[c], sems.at[n + c]) for c in range(ncol)])
    ends = run([pltpu.make_async_copy(ref.at[0, k], diag.at[i], sems.at[n + ncol + i]) for i, (ref, k) in enumerate(zip(inverses, levels))])
    for copy in inputs:
        copy.wait()
    total = jnp.zeros(out.shape, F32)
    first = low * spread.shape[0]
    for c in range(ncol):
        weights[c].wait()
        for slot in range(slots):
            place = table[c, row * slots + slot]
            picked = known[jnp.maximum(place - first, 0)]
            picked = jnp.where(place >= 0, picked, jnp.zeros_like(picked))
            total += dot(picked, held[c, slot])
    solved = (right[...].astype(F32) - total).astype(BF)
    for i in range(m):
        ends[i].wait()
        solved = dot(solved, diag[i]).astype(BF)
    out[...] = solved
    for i in range(spread.shape[0]):
        spread[i] = solved


def solve(low, row, at, levels, table, blocks, right, inverses, stores):
    part, size = right.shape
    ncol, slots = blocks.shape[0], blocks.shape[2]
    n, m, width = len(stores), len(inverses), stores[0].shape[0]
    return pl.pallas_call(
        functools.partial(solve_kernel, n, low, row, at, levels),
        out_shape=[jax.ShapeDtypeStruct((part, size), BF), jax.ShapeDtypeStruct((width, part, size), BF)],
        in_specs=[SMEM, HBM, VMEM] + [ANY] * (m + n),
        out_specs=[VMEM, VMEM],
        scratch_shapes=[
            pltpu.VMEM((ncol, slots, size, size), BF),
            pltpu.VMEM((n * width, part, size), BF),
            pltpu.VMEM((m, size, size), BF),
            pltpu.SemaphoreType.DMA((n + ncol + m,)),
        ],
        compiler_params=pltpu.CompilerParams(vmem_limit_bytes=48 << 20),
        cost_estimate=pl.CostEstimate(flops=2 * ncol * slots * part * size * size, bytes_accessed=7 << 20, transcendentals=0),
        name="solve",
    )(table, blocks, right, *inverses, *stores)


def shards(
    right_side,
    lower_inverse,
    upper_inverse,
    lower_blocks,
    lower_sources,
    lower_counts,
    upper_blocks,
    upper_sources,
    upper_counts,
):
    width = lax.axis_size(ROW)
    ncol = lax.axis_size(COL)
    group = width // ncol
    column = lax.axis_index(COL)
    levels, nrhs, size = right_side.shape[1:]
    slots = lower_blocks.shape[2]
    part = nrhs // ncol
    right = lax.dynamic_slice_in_dim(right_side[0], column * part, part, 1)

    last = LAST_SPLIT
    low_part = lower_blocks[0, last:]
    cut = levels - 1 - (levels - 1 - low_part.shape[0] + 1) // 2
    first = jnp.concatenate([low_part, upper_blocks[0, cut:]])
    second = upper_blocks[0, :cut]
    gathered = lax.all_gather(first, COL, axis=0)
    gathered_low = lax.all_gather(second, COL, axis=0)

    def places(sources, counts, by_column):
        s, n = sources[0], counts[0]
        live = jnp.arange(slots, dtype=I32)[None] < n
        g = s % width // ncol
        place = s // width * group + g
        if by_column:
            place = (s // width * ncol + s % ncol) * group + g
        return jnp.where(live, place, -1)

    own_table = places(lower_sources, lower_counts, False)
    late = jnp.concatenate(
        [places(lower_sources, lower_counts, True)[last:], places(upper_sources, upper_counts, True)]
    ).reshape(-1)
    table = lax.all_to_all(jnp.broadcast_to(late[None], (ncol, late.shape[0])), COL, 0, 0, tiled=True)

    def spread(copies):
        return lax.all_to_all(copies, TURNED, 0, 0, tiled=True)

    def by_column(whole):
        return lax.all_to_all(whole.reshape(ncol, group, part, size), COL, 0, 0, tiled=True)

    stores, halves = [], []
    for level in range(last + 1):
        parts = None
        if level > 0:
            partial = update(level - 1, own_table, lower_blocks, halves)
            parts = lax.all_to_all(partial.reshape(ncol, part, size), COL, 0, 0, tiled=True)
        solved, copies = finish(level, parts, right, lower_inverse, width)
        if level == 0:
            own = []
        own.append(solved)
        stores.append(spread(copies))
        if level < last:
            halves.append(by_column(stores[-1]))
    nlow = low_part.shape[0]
    for level in range(last + 1, levels):
        ends = [lower_inverse], [level]
        if level == levels - 1:
            ends = [lower_inverse, upper_inverse], [level, level]
        at = level - last - 1
        solved, copies = solve(0, at, at, ends[1], table, gathered, right[level], ends[0], stores)
        own.append(solved)
        stores.append(spread(copies))
    stores = stores[-1:]
    result = [own[-1]]
    for level in range(levels - 2, -1, -1):
        blocks, at = (gathered, nlow + level - cut) if level >= cut else (gathered_low, level)
        solved, copies = solve(
            level + 1, nlow + level, at, [level], table, blocks, own[level], [upper_inverse], stores
        )
        result.insert(0, solved)
        if level > 0:
            stores.insert(0, spread(copies))
    whole = jnp.broadcast_to(jnp.stack(result)[None], (ncol, levels, part, size))
    whole = lax.all_to_all(whole, COL, 0, 0, tiled=True)
    return jnp.transpose(whole, (1, 0, 2, 3)).reshape(1, levels, nrhs, size)


def solution(mesh):
    width, ncol = mesh.devices.shape
    grid = Mesh(mesh.devices.reshape(width // ncol, ncol, ncol // 2, 2), ROW + COL)
    in_specs = (
        P(ROW, None, None, None),
        P(ROW, None, None, None),
        P(ROW, None, None, None),
        P(ROW, None, COL, None, None),
        P(ROW, None, COL),
        P(ROW, None, COL),
        P(ROW, None, COL, None, None),
        P(ROW, None, COL),
        P(ROW, None, COL),
    )
    out_specs = P(ROW, None, None, None)
    return jax.shard_map(shards, mesh=grid, in_specs=in_specs, out_specs=out_specs, check_vma=False)
```

time: 1470 us -> 355 us (0.24)
  waiting for transfers between devices: 1390 us -> 41.5 us
  blocking collectives: 0 us -> 214 us
  Pallas kernels: 0 us -> 48.2 us
  matrix products: 40.5 us -> 0 us
  starting transfers between devices: 0.8 us -> 23.3 us
    all_gather x10 -> x2, waiting for transfers between devices: 753 us -> 0.02 us  [the longest x1 0.02 us: shards(): gathered_low = lax.all_gather(second, COL, axis=0)]
    psum x10 -> x0, waiting for transfers between devices: 634 us -> none  [solve_level(): total = lax.psum(contract(picked, blocks), 'pcol')]
    all_to_all x0 -> x15, blocking collectives: none -> 214 us  [the longest x8 122 us: spread(): return lax.all_to_all(copies, TURNED, 0, 0, tiled=True)]
    pallas_call x0 -> x15, Pallas kernels: none -> 48.2 us  [the longest x6 34.7 us: solve(): pl.pallas_call(functools.partial(solve_kernel, n, low, row, at, levels),...]
    all_to_all x0 -> x5, waiting for transfers between devices: none -> 41.4 us  [the longest x2 21.7 us: spread(): return lax.all_to_all(copies, TURNED, 0, 0, tiled=True)]
    dot_general x21 -> x0, matrix products: 40.5 us -> none  [the longest x10 21.9 us: contract(): lax.dot_general(picked, blocks, (((0, 2), (0, 2)), ((), ())), preferred_e...]
    all_to_all x0 -> x5, starting transfers between devices: none -> 23.3 us  [the longest x2 7.94 us: spread(): return lax.all_to_all(copies, TURNED, 0, 0, tiled=True)]
  transfers between devices with their start and end apart: 20 -> 7, of which waited for: 20 -> 5; matrix products, arithmetic and copies ran while one was open for 1% -> 1% of each run, Pallas kernels for 0% -> 9%
where the time goes in v2:
time: 355 us; the launch traced here: 354 us
  blocking collectives  214 us (60%)
  Pallas kernels  48.2 us (14%)
  waiting for transfers between devices  41.5 us (12%)
  starting transfers between devices  23.3 us (7%)
  between operations  13.7 us (4%)
  local copies, waits for them, and re-layouts  10.9 us (3%)
    all_to_all x8, blocking collectives, spread(): return lax.all_to_all(copies, TURNED, 0, 0, tiled=True)  122 us
    all_to_all x3, blocking collectives, by_column(): lax.all_to_all(whole.reshape(ncol, group, part, size), COL, 0, 0, tiled=T...  43.2 us
    pallas_call x6, Pallas kernels, solve(): pl.pallas_call(functools.partial(solve_kernel, n, low, row, at, levels),...  34.7 us
    all_to_all x3, blocking collectives, shards(): lax.all_to_all(partial.reshape(ncol, part, size), COL, 0, 0, tiled=True)  30.1 us
    all_to_all x2, waiting for transfers between devices, spread(): return lax.all_to_all(copies, TURNED, 0, 0, tiled=True)  21.7 us
    all_to_all x1, blocking collectives, shards(): whole = lax.all_to_all(whole, COL, 0, 0, tiled=True)  18.4 us
    pallas_call x4, Pallas kernels, update(): pl.pallas_call(functools.partial(update_kernel, level), out_shape=jax.Sha...  11 us
    all_to_all x1, waiting for transfers between devices, by_column(): lax.all_to_all(whole.reshape(ncol, group, part, size), COL, 0, 0, tiled=T...  9.67 us
  transfers between devices with their start and end apart: 7, of which 5 were waited for; matrix products, arithmetic and copies ran while one was open for 1% of the time, Pallas kernels for 9%

profile of v2, /device:TPU:1, one launch (start us, length us, event | category | flops | bytes accessed | tf_op | source)
XLA Modules:
  0.0 353.6 jit_solution(1854331078913034945)
XLA Ops:
  11.0 3.3 slice.17
  15.8 23.1 %all_to_all.103.rest_2_ = bf16[32,16,256]{2,1,0:T(8,128)(2,1)} all-to-all(bf16[32,16,256]{2,1,0:T(8,128)(2,1)S(1)} %get-tuple-element.27), channel_id=1, replica_groups=mesh['g'=4,'z'=8,'x'=4,'core'=2] {'z','g'}, dimensions={0} | all-to-all | bytes 524288 | tf_op jit(solution)/shard_map/all_to_all | solution.py:204
  38.9 6.7 %all-to-all-start.2 = ((bf16[8,4,16,256]{3,2,1,0:T(8,128)(2,1)}), bf16[8,4,16,256]{3,2,1,0:T(8,128)(2,1)S(1)}, u32[]{:S(2)}, u32[]{:S(2)}) async-start(bf16[8,4,16,256]{3,2,1,0:T(8,128)(2,1)} %bitcast.4), calls=%async_computation.2 | async-start | bytes 524288 | tf_op jit(solution)/shard_map/all_to_all | solution.py:207
  45.7 9.7 %all-to-all-done.2.rest_0_ = bf16[8,4,16,256]{3,2,1,0:T(8,128)(2,1)S(1)} async-done(((bf16[8,4,16,256]{3,2,1,0:T(8,128)(2,1)}), bf16[8,4,16,256]{3,2,1,0:T(8,128)(2,1)S(1)}, u32[]{:S(2)}, u32[]{:S(2)}) %all-to-all-start.2) | async-done | bytes 262176 | tf_op jit(solution)/shard_map/all_to_all | solution.py:207
  60.2 10.0 %all_to_all.104.parts = f32[8,16,256]{2,1,0:T(8,128)S(1)} all-to-all(f32[8,16,256]{2,1,0:T(8,128)S(1)} %bitcast.100), channel_id=1, replica_groups=mesh['g'=4,'z'=8,'x'=4,'core'=2] {'x','core'}, dimensions={0} | all-to-all | bytes 262144 | tf_op jit(solution)/shard_map/all_to_all | solution.py:214
  70.6 14.0 %all_to_all.105.rest_3_ = bf16[32,16,256]{2,1,0:T(8,128)(2,1)S(1)} all-to-all(bf16[32,16,256]{2,1,0:T(8,128)(2,1)S(1)} %get-tuple-element.29), channel_id=1, replica_groups=mesh['g'=4,'z'=8,'x'=4,'core'=2] {'z','g'}, dimensions={0} | all-to-all | bytes 524288 | tf_op jit(solution)/shard_map/all_to_all | solution.py:204
  84.6 15.5 %all_to_all.106.rest_1_ = bf16[8,4,16,256]{3,2,1,0:T(8,128)(2,1)S(1)} all-to-all(bf16[8,4,16,256]{3,2,1,0:T(8,128)(2,1)S(1)} %bitcast.97), channel_id=1, replica_groups=mesh['g'=4,'z'=8,'x'=4,'core'=2] {'x','core'}, dimensions={0} | all-to-all | bytes 524288 | tf_op jit(solution)/shard_map/all_to_all | solution.py:207
  102.6 10.0 %all_to_all.107.parts = f32[8,16,256]{2,1,0:T(8,128)S(1)} all-to-all(f32[8,16,256]{2,1,0:T(8,128)S(1)} %bitcast.102), channel_id=1, replica_groups=mesh['g'=4,'z'=8,'x'=4,'core'=2] {'x','core'}, dimensions={0} | all-to-all | bytes 262144 | tf_op jit(solution)/shard_map/all_to_all | solution.py:214
  113.0 13.9 %all_to_all.108.rest_4_ = bf16[32,16,256]{2,1,0:T(8,128)(2,1)S(1)} all-to-all(bf16[32,16,256]{2,1,0:T(8,128)(2,1)S(1)} %get-tuple-element.31), channel_id=1, replica_groups=mesh['g'=4,'z'=8,'x'=4,'core'=2] {'z','g'}, dimensions={0} | all-to-all | bytes 524288 | tf_op jit(solution)/shard_map/all_to_all | solution.py:204
  126.9 12.2 %all_to_all.109.rest_2_ = bf16[8,4,16,256]{3,2,1,0:T(8,128)(2,1)S(1)} all-to-all(bf16[8,4,16,256]{3,2,1,0:T(8,128)(2,1)S(1)} %bitcast.98), channel_id=1, replica_groups=mesh['g'=4,'z'=8,'x'=4,'core'=2] {'x','core'}, dimensions={0} | all-to-all | bytes 524288 | tf_op jit(solution)/shard_map/all_to_all | solution.py:207
  141.8 10.1 %all_to_all.110.parts = f32[8,16,256]{2,1,0:T(8,128)S(1)} all-to-all(f32[8,16,256]{2,1,0:T(8,128)S(1)} %bitcast.101), channel_id=1, replica_groups=mesh['g'=4,'z'=8,'x'=4,'core'=2] {'x','core'}, dimensions={0} | all-to-all | bytes 262144 | tf_op jit(solution)/shard_map/all_to_all | solution.py:214
  152.2 13.9 %all_to_all.111.rest_5_ = bf16[32,16,256]{2,1,0:T(8,128)(2,1)S(1)} all-to-all(bf16[32,16,256]{2,1,0:T(8,128)(2,1)S(1)} %get-tuple-element.33), channel_id=1, replica_groups=mesh['g'=4,'z'=8,'x'=4,'core'=2] {'z','g'}, dimensions={0} | all-to-all | bytes 524288 | tf_op jit(solution)/shard_map/all_to_all | solution.py:204
  166.1 15.5 %all_to_all.112.rest_3_ = bf16[8,4,16,256]{3,2,1,0:T(8,128)(2,1)S(1)} all-to-all(bf16[8,4,16,256]{3,2,1,0:T(8,128)(2,1)S(1)} %bitcast.99), channel_id=1, replica_groups=mesh['g'=4,'z'=8,'x'=4,'core'=2] {'x','core'}, dimensions={0} | all-to-all | bytes 524288 | tf_op jit(solution)/shard_map/all_to_all | solution.py:207
  184.9 4.2 %all-to-all-start.12 = ((f32[8,16,256]{2,1,0:T(8,128)}), f32[8,16,256]{2,1,0:T(8,128)S(1)}, u32[]{:S(2)}, u32[]{:S(2)}) async-start(f32[8,16,256]{2,1,0:T(8,128)} %bitcast.14), calls=%async_computation.12 | async-start | bytes 262144 | tf_op jit(solution)/shard_map/all_to_all | solution.py:214
  189.3 6.5 %all-to-all-done.12.parts = f32[8,16,256]{2,1,0:T(8,128)S(1)} async-done(((f32[8,16,256]{2,1,0:T(8,128)}), f32[8,16,256]{2,1,0:T(8,128)S(1)}, u32[]{:S(2)}, u32[]{:S(2)}) %all-to-all-start.12) | async-done | bytes 131104 | tf_op jit(solution)/shard_map/all_to_all | solution.py:214
  196.4 4.4 %all-to-all-start = ((s32[8,1,36]{2,1,0:T(1,128)}), s32[8,1,36]{2,1,0:T(1,128)S(1)}, u32[]{:S(2)}, u32[]{:S(2)}) async-start(s32[8,1,36]{2,1,0:T(1,128)} %broadcast_in_dim.11), calls=%async_computation | async-start | bytes 8192 | tf_op jit(solution)/shard_map/all_to_all | solution.py:201
  201.9 3.5 %all-to-all-done = s32[8,1,36]{2,1,0:T(1,128)S(1)} async-done(((s32[8,1,36]{2,1,0:T(1,128)}), s32[8,1,36]{2,1,0:T(1,128)S(1)}, u32[]{:S(2)}, u32[]{:S(2)}) %all-to-all-start) | async-done | bytes 1184 | tf_op jit(solution)/shard_map/all_to_all | solution.py:201
  205.4 3.9 %all-to-all-start.13 = ((bf16[32,16,256]{2,1,0:T(8,128)(2,1)}), bf16[32,16,256]{2,1,0:T(8,128)(2,1)S(1)}, u32[]{:S(2)}, u32[]{:S(2)}) async-start(bf16[32,16,256]{2,1,0:T(8,128)(2,1)} %get-tuple-element.35), calls=%async_computation.13 | async-start | bytes 524288 | tf_op jit(solution)/shard_map/all_to_all | solution.py:204
  209.3 11.5 %all-to-all-done.13.rest_6_ = bf16[32,16,256]{2,1,0:T(8,128)(2,1)S(1)} async-done(((bf16[32,16,256]{2,1,0:T(8,128)(2,1)}), bf16[32,16,256]{2,1,0:T(8,128)(2,1)S(1)}, u32[]{:S(2)}, u32[]{:S(2)}) %all-to-all-start.13) | async-done | bytes 262176 | tf_op jit(solution)/shard_map/all_to_all | solution.py:204
  220.8 5.8 %solve.6 = (bf16[16,256]{1,0:T(8,128)(2,1)S(1)}, bf16[32,16,256]{2,1,0:T(8,128)(2,1)S(1)}) custom-call(s32[8,36]{1,0:T(8,128)S(1)} %bitcast.103, bf16[8,3,6,256,256]{4,3,2,1,0:T(8,128)(2,1)} %bitcast.109, bf16[16,256]{1,0:T(8,128)(2,1)S(1)} %dynamic-slice_bitcast_fusion.1.right, bf16[1,6,256,256]{3,2,1,0:T(8,128)(2,1)S(1)} %copy-done.2, ...), custom_call_target="tpu_custom_call" | custom-call | flops 100663296 | bytes 7340032 | tf_op jit(solution)/shard_map/solve/pallas_call | solution.py:143
  226.6 14.7 %all_to_all.113.rest_1_.rest_2_.rest_3_.rest_4_.rest_5_ = bf16[32,16,256]{2,1,0:T(8,128)(2,1)S(1)} all-to-all(bf16[32,16,256]{2,1,0:T(8,128)(2,1)S(1)} %get-tuple-element.36), channel_id=1, replica_groups=mesh['g'=4,'z'=8,'x'=4,'core'=2] {'z','g'}, dimensions={0} | all-to-all | bytes 524288 | tf_op jit(solution)/shard_map/all_to_all | solution.py:204
  241.3 5.5 %solve.7 = (bf16[16,256]{1,0:T(8,128)(2,1)S(1)}, bf16[32,16,256]{2,1,0:T(8,128)(2,1)S(1)}) custom-call(s32[8,36]{1,0:T(8,128)S(1)} %bitcast.104, bf16[8,3,6,256,256]{4,3,2,1,0:T(8,128)(2,1)} %bitcast.110, bf16[16,256]{1,0:T(8,128)(2,1)S(1)} %get-tuple-element.34.right, bf16[1,6,256,256]{3,2,1,0:T(8,128)(2,1)S(1)} %copy-done.3, ...), custom_call_target="tpu_custom_call" | custom-call | flops 100663296 | bytes 7340032 | tf_op jit(solution)/shard_map/solve/pallas_call | solution.py:143
  246.8 15.1 %all_to_all.114.rest_1_.rest_2_.rest_3_.rest_4_ = bf16[32,16,256]{2,1,0:T(8,128)(2,1)S(1)} all-to-all(bf16[32,16,256]{2,1,0:T(8,128)(2,1)S(1)} %get-tuple-element.37), channel_id=1, replica_groups=mesh['g'=4,'z'=8,'x'=4,'core'=2] {'z','g'}, dimensions={0} | all-to-all | bytes 524288 | tf_op jit(solution)/shard_map/all_to_all | solution.py:204
  261.9 6.2 %solve.8 = (bf16[16,256]{1,0:T(8,128)(2,1)S(1)}, bf16[32,16,256]{2,1,0:T(8,128)(2,1)}) custom-call(s32[8,36]{1,0:T(8,128)S(1)} %bitcast.105, bf16[8,3,6,256,256]{4,3,2,1,0:T(8,128)(2,1)} %bitcast.111, bf16[16,256]{1,0:T(8,128)(2,1)S(1)} %get-tuple-element.32.right, bf16[1,6,256,256]{3,2,1,0:T(8,128)(2,1)S(1)} %copy-done.3, ...), custom_call_target="tpu_custom_call" | custom-call | flops 100663296 | bytes 7340032 | tf_op jit(solution)/shard_map/solve/pallas_call | solution.py:143
  268.1 4.1 %all-to-all-start.16 = ((bf16[32,16,256]{2,1,0:T(8,128)(2,1)}), bf16[32,16,256]{2,1,0:T(8,128)(2,1)S(1)}, u32[]{:S(2)}, u32[]{:S(2)}) async-start(bf16[32,16,256]{2,1,0:T(8,128)(2,1)} %get-tuple-element.38), calls=%async_computation.16 | async-start | bytes 524288 | tf_op jit(solution)/shard_map/all_to_all | solution.py:204
  272.2 10.2 %all-to-all-done.16.rest_1_.rest_2_.rest_3_ = bf16[32,16,256]{2,1,0:T(8,128)(2,1)S(1)} async-done(((bf16[32,16,256]{2,1,0:T(8,128)(2,1)}), bf16[32,16,256]{2,1,0:T(8,128)(2,1)S(1)}, u32[]{:S(2)}, u32[]{:S(2)}) %all-to-all-start.16) | async-done | bytes 262176 | tf_op jit(solution)/shard_map/all_to_all | solution.py:204
  282.4 5.5 %solve.9 = (bf16[16,256]{1,0:T(8,128)(2,1)S(1)}, bf16[32,16,256]{2,1,0:T(8,128)(2,1)S(1)}) custom-call(s32[8,36]{1,0:T(8,128)S(1)} %bitcast.106, bf16[8,3,6,256,256]{4,3,2,1,0:T(8,128)(2,1)} %all-gather.4.cloned.1.call-done.blocks, bf16[16,256]{1,0:T(8,128)(2,1)S(1)} %get-tuple-element.30.right, bf16[1,6,256,256]{3,2,1,0:T(8,128)(2,1)S(1)} %copy-done.3, ...), custom_call_target="tpu_custom_call" | custom-call | flops 100663296 | bytes 7340032 | tf_op jit(solution)/shard_map/solve/pallas_call | solution.py:143
  287.9 13.8 %all_to_all.115.rest_1_.rest_2_ = bf16[32,16,256]{2,1,0:T(8,128)(2,1)S(1)} all-to-all(bf16[32,16,256]{2,1,0:T(8,128)(2,1)S(1)} %get-tuple-element.39), channel_id=1, replica_groups=mesh['g'=4,'z'=8,'x'=4,'core'=2] {'z','g'}, dimensions={0} | all-to-all | bytes 524288 | tf_op jit(solution)/shard_map/all_to_all | solution.py:204
  301.7 5.5 %solve.10 = (bf16[16,256]{1,0:T(8,128)(2,1)S(1)}, bf16[32,16,256]{2,1,0:T(8,128)(2,1)S(1)}) custom-call(s32[8,36]{1,0:T(8,128)S(1)} %bitcast.107, bf16[8,3,6,256,256]{4,3,2,1,0:T(8,128)(2,1)} %all-gather.4.cloned.1.call-done.blocks, bf16[16,256]{1,0:T(8,128)(2,1)S(1)} %get-tuple-element.28.right, bf16[1,6,256,256]{3,2,1,0:T(8,128)(2,1)S(1)} %copy-done.3, ...), custom_call_target="tpu_custom_call" | custom-call | flops 100663296 | bytes 7340032 | tf_op jit(solution)/shard_map/solve/pallas_call | solution.py:143
  307.3 13.9 %all_to_all.116.rest_1_ = bf16[32,16,256]{2,1,0:T(8,128)(2,1)S(1)} all-to-all(bf16[32,16,256]{2,1,0:T(8,128)(2,1)S(1)} %get-tuple-element.40), channel_id=1, replica_groups=mesh['g'=4,'z'=8,'x'=4,'core'=2] {'z','g'}, dimensions={0} | all-to-all | bytes 524288 | tf_op jit(solution)/shard_map/all_to_all | solution.py:204
  321.1 6.3 %solve.11 = (bf16[16,256]{1,0:T(8,128)(2,1)S(1)}, bf16[32,16,256]{2,1,0:T(8,128)(2,1)}) custom-call(s32[8,36]{1,0:T(8,128)S(1)} %bitcast.108, bf16[8,3,6,256,256]{4,3,2,1,0:T(8,128)(2,1)} %all-gather.4.cloned.1.call-done.blocks, bf16[16,256]{1,0:T(8,128)(2,1)S(1)} %get-tuple-element.26.right, bf16[1,6,256,256]{3,2,1,0:T(8,128)(2,1)S(1)} %copy-done.3, ...), custom_call_target="tpu_custom_call" | custom-call | flops 100663296 | bytes 7340032 | tf_op jit(solution)/shard_map/solve/pallas_call | solution.py:143
  327.5 18.4 %all_to_all.117 = bf16[8,6,16,256]{3,2,1,0:T(8,128)(2,1)S(1)} all-to-all(bf16[8,6,16,256]{3,2,1,0:T(8,128)(2,1)S(1)} %broadcast_in_dim.22), channel_id=1, replica_groups=mesh['g'=4,'z'=8,'x'=4,'core'=2] {'x','core'}, dimensions={0} | all-to-all | bytes 786432 | tf_op jit(solution)/shard_map/all_to_all | solution.py:242
  (50 shorter events, 23.0 us)
Async XLA Ops:
  6.5 7.8 %copy-start = (bf16[1,6,128,256]{3,2,1,0:T(8,128)(2,1)S(1)}, bf16[1,6,128,256]{3,2,1,0:T(8,128)(2,1)}, u32[]{:S(2)}) copy-start(bf16[1,6,128,256]{3,2,1,0:T(8,128)(2,1)} %param.9) | copy-start | bytes 1179652
  6.5 214.2 %all-gather.6.cloned.1.call-start = ((), (), s32[]{:S(2)}) async-start(), calls=%async_computation.21 | async-start | bytes 21233664 | tf_op jit(solution)/shard_map/all_gather | solution.py:185
  11.0 261.2 %all-gather.4.cloned.1.call-start = ((), (), s32[]{:S(2)}) async-start(), calls=%async_computation.20 | async-start | bytes 21233664 | tf_op jit(solution)/shard_map/all_gather | solution.py:186
  14.3 1.1 copy-start.2
  14.3 31.4 %copy-start.5 = (s32[1,5,6]{2,0,1:T(1,128)S(1)}, s32[1,5,6]{2,0,1:T(1,128)}, u32[]{:S(2)}) copy-start(s32[1,5,6]{2,0,1:T(1,128)} %param.13) | copy-start | bytes 364
  14.3 31.4 %copy-start.7 = (s32[1,5,1]{1,2,0:T(1,128)S(1)}, s32[1,5,1]{1,2,0:T(1,128)}, u32[]{:S(2)}) copy-start(s32[1,5,1]{1,2,0:T(1,128)} %param.14) | copy-start | bytes 64
  38.9 16.5 %all-to-all-start.2 = ((bf16[8,4,16,256]{3,2,1,0:T(8,128)(2,1)}), bf16[8,4,16,256]{3,2,1,0:T(8,128)(2,1)S(1)}, u32[]{:S(2)}, u32[]{:S(2)}) async-start(bf16[8,4,16,256]{3,2,1,0:T(8,128)(2,1)} %bitcast.4), calls=%async_computation.2 | async-start | bytes 524288 | tf_op jit(solution)/shard_map/all_to_all | solution.py:207
  55.4 2.3 copy-start.1
  181.6 7.5 %copy-start.4 = (s32[1,5,6]{2,0,1:T(1,128)S(1)}, s32[1,5,6]{2,0,1:T(1,128)}, u32[]{:S(2)}) copy-start(s32[1,5,6]{2,0,1:T(1,128)} %param.16) | copy-start | bytes 364
  181.6 7.5 %copy-start.6 = (s32[1,5,1]{1,2,0:T(1,128)S(1)}, s32[1,5,1]{1,2,0:T(1,128)}, u32[]{:S(2)}) copy-start(s32[1,5,1]{1,2,0:T(1,128)} %param.17) | copy-start | bytes 64
  181.6 39.2 %copy-start.3 = (bf16[1,6,256,256]{3,2,1,0:T(8,128)(2,1)S(1)}, bf16[1,6,256,256]{3,2,1,0:T(8,128)(2,1)}, u32[]{:S(2)}) copy-start(bf16[1,6,256,256]{3,2,1,0:T(8,128)(2,1)} %rest_0_.11) | copy-start | bytes 2359300
  184.9 10.9 %all-to-all-start.12 = ((f32[8,16,256]{2,1,0:T(8,128)}), f32[8,16,256]{2,1,0:T(8,128)S(1)}, u32[]{:S(2)}, u32[]{:S(2)}) async-start(f32[8,16,256]{2,1,0:T(8,128)} %bitcast.14), calls=%async_computation.12 | async-start | bytes 262144 | tf_op jit(solution)/shard_map/all_to_all | solution.py:214
  196.4 9.0 %all-to-all-start = ((s32[8,1,36]{2,1,0:T(1,128)}), s32[8,1,36]{2,1,0:T(1,128)S(1)}, u32[]{:S(2)}, u32[]{:S(2)}) async-start(s32[8,1,36]{2,1,0:T(1,128)} %broadcast_in_dim.11), calls=%async_computation | async-start | bytes 8192 | tf_op jit(solution)/shard_map/all_to_all | solution.py:201
  205.4 15.4 %all-to-all-start.13 = ((bf16[32,16,256]{2,1,0:T(8,128)(2,1)}), bf16[32,16,256]{2,1,0:T(8,128)(2,1)S(1)}, u32[]{:S(2)}, u32[]{:S(2)}) async-start(bf16[32,16,256]{2,1,0:T(8,128)(2,1)} %get-tuple-element.35), calls=%async_computation.13 | async-start | bytes 524288 | tf_op jit(solution)/shard_map/all_to_all | solution.py:204
  268.1 14.3 %all-to-all-start.16 = ((bf16[32,16,256]{2,1,0:T(8,128)(2,1)}), bf16[32,16,256]{2,1,0:T(8,128)(2,1)S(1)}, u32[]{:S(2)}, u32[]{:S(2)}) async-start(bf16[32,16,256]{2,1,0:T(8,128)(2,1)} %get-tuple-element.38), calls=%async_computation.16 | async-start | bytes 524288 | tf_op jit(solution)/shard_map/all_to_all | solution.py:204
Sparse Core Ops, SparseCore 0:
  11.1 108.9 all-gather.5
  121.9 102.6 all-gather.3

commit v3 on v2

v3 whole, which is shorter than its diff:
```python
import functools

import jax
import jax.numpy as jnp
from jax import lax
from jax.experimental import pallas as pl
from jax.experimental.pallas import tpu as pltpu
from jax.sharding import Mesh
from jax.sharding import PartitionSpec as P

BF = jnp.bfloat16
F32 = jnp.float32
I32 = jnp.int32
NT = (((1,), (1,)), ((), ()))
ROW = ("g", "z")
TURNED = ("z", "g")
COL = ("x", "core")
SMEM = pl.BlockSpec(memory_space=pltpu.SMEM)
VMEM = pl.BlockSpec(memory_space=pltpu.VMEM)
ANY = pl.BlockSpec(memory_space=pl.ANY)
HBM = pl.BlockSpec(memory_space=pltpu.HBM)
LAST_SPLIT = 4
HEAD = 3


def dot(x, y):
    return lax.dot_general(x, y, NT, preferred_element_type=F32)


def run(copies):
    for copy in copies:
        copy.start()
    return copies


def params(mib):
    return pltpu.CompilerParams(vmem_limit_bytes=mib << 20)


def join_kernel(cut, low_blocks, high_blocks, out, sems):
    n = low_blocks.shape[1]
    last = n - (out.shape[0] - (high_blocks.shape[1] - cut))
    copies = [
        pltpu.make_async_copy(low_blocks.at[0, pl.ds(last, n - last)], out.at[pl.ds(0, n - last)], sems.at[0]),
        pltpu.make_async_copy(high_blocks.at[0, pl.ds(cut, n - cut)], out.at[pl.ds(n - last, n - cut)], sems.at[1]),
    ]
    for copy in run(copies):
        copy.wait()


def join(count, cut, low_blocks, high_blocks):
    return pl.pallas_call(
        functools.partial(join_kernel, cut),
        out_shape=jax.ShapeDtypeStruct((count,) + low_blocks.shape[2:], BF),
        in_specs=[ANY, ANY],
        out_specs=ANY,
        scratch_shapes=[pltpu.SemaphoreType.DMA((2,))],
        compiler_params=params(60),
        name="join",
    )(low_blocks, high_blocks)


def head_kernel(count, blocks, out, sem):
    copy = pltpu.make_async_copy(blocks.at[0, pl.ds(0, count)], out, sem)
    copy.start()
    copy.wait()


def head(count, blocks):
    return pl.pallas_call(
        functools.partial(head_kernel, count),
        out_shape=jax.ShapeDtypeStruct((count,) + blocks.shape[2:], BF),
        in_specs=[ANY],
        out_specs=ANY,
        scratch_shapes=[pltpu.SemaphoreType.DMA(())],
        compiler_params=params(60),
        name="head",
    )(blocks)


def pick(stores, first, place, load):
    width = 32
    at = jnp.maximum(place, 0)
    level, index = at // width - first, at % width
    picked = load(stores[0], index)
    for i in range(1, len(stores)):
        picked = jnp.where(level == i, load(stores[i], index), picked)
    return jnp.where(place >= 0, picked, jnp.zeros_like(picked))


def update_kernel(level, n, extra, table, blocks, *rest):
    stores, rest = rest[:n], rest[n:]
    out = rest[-1]
    ncol, group, part, size = stores[0].shape

    def load(store, index):
        return store[:, index % group].reshape(ncol * part, size)

    total = jnp.zeros((ncol * part, size), F32)
    for slot in range(blocks.shape[2]):
        total += dot(pick(stores, 0, table[level, slot], load), blocks[0, level, slot])
    out[:, :part] = total.reshape(ncol, part, size)
    if extra:
        out[:, part:] = jnp.broadcast_to(rest[0][...][None], (ncol, extra, size))


def update(level, table, blocks, stores, late=None):
    slots, size = blocks.shape[2], blocks.shape[3]
    ncol, group, part, _ = stores[0].shape
    n = len(stores)
    extra = 0 if late is None else late.shape[0]
    return pl.pallas_call(
        functools.partial(update_kernel, level, n, extra),
        out_shape=jax.ShapeDtypeStruct((ncol, part + extra, size), F32),
        in_specs=[SMEM, VMEM] + [VMEM] * (n + (late is not None)),
        out_specs=VMEM,
        compiler_params=params(4),
        cost_estimate=pl.CostEstimate(flops=2 * slots * ncol * part * size * size, bytes_accessed=1 << 20, transcendentals=0),
        name="update",
    )(table, blocks, *stores, *([] if late is None else [late]))


def finish_kernel(level, parts, right, inverse, out, spread, *table):
    residual = right[level]
    part = residual.shape[0]
    if parts is not None:
        total = parts[0, :part]
        for i in range(1, parts.shape[0]):
            total = total + parts[i, :part]
        residual = (residual.astype(F32) - total).astype(BF)
    solved = dot(residual, inverse[0, level]).astype(BF)
    out[...] = solved
    for i in range(spread.shape[0]):
        spread[i] = solved
    if table:
        for i in range(parts.shape[0]):
            table[0][i : i + 1] = parts[i, part : part + 1, :128].astype(I32)


def finish(level, parts, right, inverse, width):
    part, size = right.shape[1:]
    body = functools.partial(finish_kernel, level)
    out_shape = [jax.ShapeDtypeStruct((part, size), BF), jax.ShapeDtypeStruct((width, part, size), BF)]
    if parts is None:
        body = functools.partial(finish_kernel, level, None)
    elif parts.shape[1] > part:
        out_shape.append(jax.ShapeDtypeStruct((parts.shape[0], 128), I32))
    return pl.pallas_call(
        body,
        out_shape=out_shape,
        in_specs=([] if parts is None else [VMEM]) + [VMEM, VMEM],
        out_specs=[VMEM] * len(out_shape),
        compiler_params=params(4),
        cost_estimate=pl.CostEstimate(flops=2 * part * size * size, bytes_accessed=1 << 19, transcendentals=0),
        name="finish",
    )(*([] if parts is None else [parts]), right, inverse)


def solve_kernel(n, low, row, at, levels, held, table, blocks, right, *rest):
    m = len(levels)
    inverses, stores, rest = rest[:m], rest[m : m + n], rest[m + n :]
    ncol, _, slots = blocks.shape[:3]
    part = right.shape[0]
    copies = []
    if held:
        *rest, room, sems = rest
        copies = run([pltpu.make_async_copy(blocks.at[c, at], room.at[c], sems.at[c]) for c in range(ncol)])
    total = jnp.zeros(right.shape, F32)
    for c in range(ncol):
        if held:
            copies[c].wait()
        for slot in range(slots):
            picked = pick(stores, low, table[c, row * slots + slot], lambda store, index: store[index])
            total += dot(picked, room[c, slot] if held else blocks[c, at, slot])
    solved = (right[...].astype(F32) - total).astype(BF)
    for i, level in enumerate(levels):
        solved = dot(solved, inverses[i][0, level]).astype(BF)
    if len(rest) > 2:
        *done, out = rest
        for i in range(ncol):
            out[i, 0] = solved
            for j, ref in enumerate(done):
                out[i, j + 1] = ref[...]
    else:
        out, spread = rest
        out[...] = solved
        for i in range(spread.shape[0]):
            spread[i] = solved


def solve(low, row, at, levels, held, table, blocks, right, inverses, stores, done=()):
    part, size = right.shape
    ncol, slots = blocks.shape[0], blocks.shape[2]
    n, m, width = len(stores), len(inverses), stores[0].shape[0]
    if done:
        out_shape = jax.ShapeDtypeStruct((ncol, len(done) + 1, part, size), BF)
        out_specs = VMEM
    else:
        out_shape = [jax.ShapeDtypeStruct((part, size), BF), jax.ShapeDtypeStruct((width, part, size), BF)]
        out_specs = [VMEM, VMEM]
    scratch = [pltpu.VMEM((ncol, slots, size, size), BF), pltpu.SemaphoreType.DMA((ncol,))]
    return pl.pallas_call(
        functools.partial(solve_kernel, n, low, row, at, levels, held),
        out_shape=out_shape,
        in_specs=[SMEM, ANY if held else VMEM] + [VMEM] * (1 + m + n + len(done)),
        out_specs=out_specs,
        scratch_shapes=scratch if held else [],
        compiler_params=params(48 if held else 6),
        cost_estimate=pl.CostEstimate(flops=2 * ncol * slots * part * size * size, bytes_accessed=7 << 20, transcendentals=0),
        name="solve",
    )(table, blocks, right, *inverses, *stores, *done)


def shards(
    right_side,
    lower_inverse,
    upper_inverse,
    lower_blocks,
    lower_sources,
    lower_counts,
    upper_blocks,
    upper_sources,
    upper_counts,
):
    width = lax.axis_size(ROW)
    ncol = lax.axis_size(COL)
    group = width // ncol
    column = lax.axis_index(COL)
    levels, nrhs, size = right_side.shape[1:]
    slots = lower_blocks.shape[2]
    part = nrhs // ncol
    right = lax.dynamic_slice_in_dim(right_side[0], column * part, part, 1)

    last = LAST_SPLIT
    nlow = levels - 1 - last
    cut = HEAD
    first = join(nlow + levels - 1 - cut, cut, lower_blocks, upper_blocks)
    second = head(cut, upper_blocks)
    gathered = lax.all_gather(first, COL, axis=0)
    gathered_low = lax.all_gather(second, COL, axis=0)

    def places(sources, counts, by_column):
        s, n = sources[0], counts[0]
        live = jnp.arange(slots, dtype=I32)[None] < n
        g = s % width // ncol
        place = s // width * width + g
        if by_column:
            place = (s // width * ncol + s % ncol) * group + g
        return jnp.where(live, place, -1)

    own_table = places(lower_sources, lower_counts, False)
    late = jnp.concatenate(
        [places(lower_sources, lower_counts, True)[last:], places(upper_sources, upper_counts, True)]
    ).reshape(-1)
    late = jnp.pad(late.astype(F32)[None], ((0, 7), (0, size - late.shape[0])))

    def spread(copies):
        return lax.all_to_all(copies, TURNED, 0, 0, tiled=True)

    def by_column(whole):
        return lax.all_to_all(whole.reshape(ncol, group, part, size), COL, 0, 0, tiled=True)

    stores, halves, own = [], [], []
    for level in range(last + 1):
        parts = None
        if level > 0:
            partial = update(level - 1, own_table, lower_blocks, halves, late if level == 1 else None)
            parts = lax.all_to_all(partial, COL, 0, 0, tiled=True)
        solved, copies, *rest = finish(level, parts, right, lower_inverse, width)
        if rest:
            table = rest[0]
        own.append(solved)
        if level == last:
            copies, gathered = lax.optimization_barrier((copies, gathered))
        stores.append(spread(copies))
        if level < last:
            halves.append(by_column(stores[-1]))
    for level in range(last + 1, levels):
        ends = [lower_inverse], [level]
        if level == levels - 1:
            ends = [lower_inverse, upper_inverse], [level, level]
        at = level - last - 1
        solved, copies = solve(0, at, at, ends[1], True, table, gathered, right[level], ends[0], stores)
        own.append(solved)
        stores.append(spread(copies))
    stores = stores[-1:]
    result = [own[-1]]
    for level in range(levels - 2, -1, -1):
        blocks, at = (gathered, nlow + level - cut) if level >= cut else (gathered_low, level)
        args = (level + 1, nlow + level, at, [level], True, table, blocks, own[level], [upper_inverse], stores)
        if level > 0:
            solved, copies = solve(*args)
            result.insert(0, solved)
            stores.insert(0, spread(copies))
    whole = lax.all_to_all(solve(*args, result), COL, 0, 0, tiled=True)
    return jnp.transpose(whole, (1, 0, 2, 3)).reshape(1, levels, nrhs, size)


def solution(mesh):
    width, ncol = mesh.devices.shape
    grid = Mesh(mesh.devices.reshape(width // ncol, ncol, ncol // 2, 2), ROW + COL)
    in_specs = (
        P(ROW, None, None, None),
        P(ROW, None, None, None),
        P(ROW, None, None, None),
        P(ROW, None, COL, None, None),
        P(ROW, None, COL),
        P(ROW, None, COL),
        P(ROW, None, COL, None, None),
        P(ROW, None, COL),
        P(ROW, None, COL),
    )
    out_specs = P(ROW, None, None, None)
    return jax.shard_map(shards, mesh=grid, in_specs=in_specs, out_specs=out_specs, check_vma=False)
```

time: 355 us -> 468 us (1.32)
  Pallas kernels: 48.2 us -> 185 us
  blocking collectives: 214 us -> 200 us
  local copies, waits for them, and re-layouts: 10.9 us -> 3.06 us
    pallas_call x15 -> x17, Pallas kernels: 48.2 us -> 185 us  [the longest x1 72.6 us: join(): pl.pallas_call(functools.partial(join_kernel, cut), out_shape=jax.ShapeDt...]
    all_to_all x8 -> x7, blocking collectives: 122 us -> 98.6 us  [spread(): return lax.all_to_all(copies, TURNED, 0, 0, tiled=True)]
    all_to_all x2 -> x3, starting transfers between devices: 7.94 us -> 19.9 us  [spread(): return lax.all_to_all(copies, TURNED, 0, 0, tiled=True)]
    all_to_all x2 -> x3, waiting for transfers between devices: 21.7 us -> 32.7 us  [spread(): return lax.all_to_all(copies, TURNED, 0, 0, tiled=True)]
    all_to_all x2 -> x0, waiting for transfers between devices: 10.1 us -> none  [the longest x1 6.54 us: shards(): lax.all_to_all(partial.reshape(ncol, part, size), COL, 0, 0, tiled=True)]
    all_to_all x4 -> x5, blocking collectives: 48.6 us -> 57.8 us  [the longest x4 39.6 us: shards(): parts = lax.all_to_all(partial, COL, 0, 0, tiled=True)]
    all_to_all x2 -> x0, starting transfers between devices: 8.62 us -> none  [the longest x1 4.4 us: shards(): lax.all_to_all(jnp.broadcast_to(late[None], (ncol, late.shape[0])), COL,...]
  transfers between devices with their start and end apart: 7 -> 6, of which waited for: 5 -> 4; matrix products, arithmetic and copies ran while one was open for 1% -> 0% of each run, Pallas kernels for 9% -> 21%
where the time goes in v3:
time: 468 us; the launch traced here: 467 us
  blocking collectives  200 us (43%)
  Pallas kernels  185 us (40%)
  waiting for transfers between devices  39.1 us (8%)
  starting transfers between devices  26.7 us (6%)
  between operations  13.7 us (3%)
    all_to_all x7, blocking collectives, spread(): return lax.all_to_all(copies, TURNED, 0, 0, tiled=True)  98.6 us
    pallas_call x1, Pallas kernels, join(): pl.pallas_call(functools.partial(join_kernel, cut), out_shape=jax.ShapeDt...  72.6 us
    pallas_call x1, Pallas kernels, head(): pl.pallas_call(functools.partial(head_kernel, count), out_shape=jax.Shape...  72.6 us
    all_to_all x3, blocking collectives, by_column(): lax.all_to_all(whole.reshape(ncol, group, part, size), COL, 0, 0, tiled=T...  43.5 us
    all_to_all x4, blocking collectives, shards(): parts = lax.all_to_all(partial, COL, 0, 0, tiled=True)  39.6 us
    pallas_call x6, Pallas kernels, solve(): pl.pallas_call(functools.partial(solve_kernel, n, low, row, at, levels, h...  33.3 us
    all_to_all x3, waiting for transfers between devices, spread(): return lax.all_to_all(copies, TURNED, 0, 0, tiled=True)  32.7 us
    all_to_all x3, starting transfers between devices, spread(): return lax.all_to_all(copies, TURNED, 0, 0, tiled=True)  19.9 us
  transfers between devices with their start and end apart: 6, of which 4 were waited for; matrix products, arithmetic and copies ran while one was open for 0% of the time, Pallas kernels for 21%

profile of v3, /device:TPU:1, one launch (start us, length us, event | category | flops | bytes accessed | tf_op | source)
XLA Modules:
  0.0 467.4 jit_solution(15925533094187415623)
XLA Ops:
  6.5 72.6 %join.1 = bf16[3,6,256,256]{3,2,1,0:T(8,128)(2,1)} custom-call(bf16[1,5,6,256,256]{4,3,2,1,0:T(8,128)(2,1)} %low_blocks.1, bf16[1,5,6,256,256]{4,3,2,1,0:T(8,128)(2,1)} %high_blocks.1), custom_call_target="tpu_custom_call" | custom-call | tf_op jit(solution)/shard_map/join/pallas_call | solution.py:52
  79.3 72.6 %head.1 = bf16[3,6,256,256]{3,2,1,0:T(8,128)(2,1)} custom-call(bf16[1,5,6,256,256]{4,3,2,1,0:T(8,128)(2,1)} %high_blocks.1), custom_call_target="tpu_custom_call" | custom-call | tf_op jit(solution)/shard_map/head/pallas_call | solution.py:70
  152.8 12.2 %all-to-all-start = ((bf16[32,16,256]{2,1,0:T(8,128)(2,1)}), bf16[32,16,256]{2,1,0:T(8,128)(2,1)}, u32[]{:S(2)}, u32[]{:S(2)}) async-start(bf16[32,16,256]{2,1,0:T(8,128)(2,1)} %get-tuple-element.28), calls=%async_computation | async-start | bytes 524288 | tf_op jit(solution)/shard_map/all_to_all | solution.py:258
  165.1 11.1 %all-to-all-done.rest_2_ = bf16[32,16,256]{2,1,0:T(8,128)(2,1)} async-done(((bf16[32,16,256]{2,1,0:T(8,128)(2,1)}), bf16[32,16,256]{2,1,0:T(8,128)(2,1)}, u32[]{:S(2)}, u32[]{:S(2)}) %all-to-all-start) | async-done | bytes 262176 | tf_op jit(solution)/shard_map/all_to_all | solution.py:258
  176.2 6.7 %all-to-all-start.1 = ((bf16[8,4,16,256]{3,2,1,0:T(8,128)(2,1)}), bf16[8,4,16,256]{3,2,1,0:T(8,128)(2,1)S(1)}, u32[]{:S(2)}, u32[]{:S(2)}) async-start(bf16[8,4,16,256]{3,2,1,0:T(8,128)(2,1)} %bitcast.2), calls=%async_computation.1 | async-start | bytes 524288 | tf_op jit(solution)/shard_map/all_to_all | solution.py:261
  183.1 6.3 %all-to-all-done.1.rest_0_ = bf16[8,4,16,256]{3,2,1,0:T(8,128)(2,1)S(1)} async-done(((bf16[8,4,16,256]{3,2,1,0:T(8,128)(2,1)}), bf16[8,4,16,256]{3,2,1,0:T(8,128)(2,1)S(1)}, u32[]{:S(2)}, u32[]{:S(2)}) %all-to-all-start.1) | async-done | bytes 262176 | tf_op jit(solution)/shard_map/all_to_all | solution.py:261
  189.4 2.1 copy-done.1
  192.5 11.0 %all_to_all.95.parts = f32[8,24,256]{2,1,0:T(8,128)S(1)} all-to-all(f32[8,24,256]{2,1,0:T(8,128)S(1)} %update.4), channel_id=1, replica_groups=mesh['g'=4,'z'=8,'x'=4,'core'=2] {'x','core'}, dimensions={0} | all-to-all | bytes 393216 | tf_op jit(solution)/shard_map/all_to_all | solution.py:268
  203.8 13.4 %all_to_all.96.rest_3_ = bf16[32,16,256]{2,1,0:T(8,128)(2,1)S(1)} all-to-all(bf16[32,16,256]{2,1,0:T(8,128)(2,1)S(1)} %get-tuple-element.32), channel_id=1, replica_groups=mesh['g'=4,'z'=8,'x'=4,'core'=2] {'z','g'}, dimensions={0} | all-to-all | bytes 524288 | tf_op jit(solution)/shard_map/all_to_all | solution.py:258
  217.2 15.7 %all_to_all.97.rest_1_ = bf16[8,4,16,256]{3,2,1,0:T(8,128)(2,1)S(1)} all-to-all(bf16[8,4,16,256]{3,2,1,0:T(8,128)(2,1)S(1)} %bitcast.76), channel_id=1, replica_groups=mesh['g'=4,'z'=8,'x'=4,'core'=2] {'x','core'}, dimensions={0} | all-to-all | bytes 524288 | tf_op jit(solution)/shard_map/all_to_all | solution.py:261
  234.0 10.0 %all_to_all.98.parts = f32[8,16,256]{2,1,0:T(8,128)S(1)} all-to-all(f32[8,16,256]{2,1,0:T(8,128)S(1)} %update.5), channel_id=1, replica_groups=mesh['g'=4,'z'=8,'x'=4,'core'=2] {'x','core'}, dimensions={0} | all-to-all | bytes 262144 | tf_op jit(solution)/shard_map/all_to_all | solution.py:268
  244.1 13.7 %all_to_all.99.rest_4_ = bf16[32,16,256]{2,1,0:T(8,128)(2,1)S(1)} all-to-all(bf16[32,16,256]{2,1,0:T(8,128)(2,1)S(1)} %get-tuple-element.34), channel_id=1, replica_groups=mesh['g'=4,'z'=8,'x'=4,'core'=2] {'z','g'}, dimensions={0} | all-to-all | bytes 524288 | tf_op jit(solution)/shard_map/all_to_all | solution.py:258
  257.9 15.5 %all_to_all.100.rest_2_ = bf16[8,4,16,256]{3,2,1,0:T(8,128)(2,1)S(1)} all-to-all(bf16[8,4,16,256]{3,2,1,0:T(8,128)(2,1)S(1)} %bitcast.77), channel_id=1, replica_groups=mesh['g'=4,'z'=8,'x'=4,'core'=2] {'x','core'}, dimensions={0} | all-to-all | bytes 524288 | tf_op jit(solution)/shard_map/all_to_all | solution.py:261
  274.4 10.0 %all_to_all.101.parts = f32[8,16,256]{2,1,0:T(8,128)S(1)} all-to-all(f32[8,16,256]{2,1,0:T(8,128)S(1)} %update.6), channel_id=1, replica_groups=mesh['g'=4,'z'=8,'x'=4,'core'=2] {'x','core'}, dimensions={0} | all-to-all | bytes 262144 | tf_op jit(solution)/shard_map/all_to_all | solution.py:268
  284.5 14.1 %all_to_all.102.rest_5_ = bf16[32,16,256]{2,1,0:T(8,128)(2,1)S(1)} all-to-all(bf16[32,16,256]{2,1,0:T(8,128)(2,1)S(1)} %get-tuple-element.35), channel_id=1, replica_groups=mesh['g'=4,'z'=8,'x'=4,'core'=2] {'z','g'}, dimensions={0} | all-to-all | bytes 524288 | tf_op jit(solution)/shard_map/all_to_all | solution.py:258
  298.6 12.2 %all_to_all.103.rest_3_ = bf16[8,4,16,256]{3,2,1,0:T(8,128)(2,1)S(1)} all-to-all(bf16[8,4,16,256]{3,2,1,0:T(8,128)(2,1)S(1)} %bitcast.78), channel_id=1, replica_groups=mesh['g'=4,'z'=8,'x'=4,'core'=2] {'x','core'}, dimensions={0} | all-to-all | bytes 524288 | tf_op jit(solution)/shard_map/all_to_all | solution.py:261
  311.9 8.7 %all_to_all.104.parts = f32[8,16,256]{2,1,0:T(8,128)S(1)} all-to-all(f32[8,16,256]{2,1,0:T(8,128)S(1)} %update.7), channel_id=1, replica_groups=mesh['g'=4,'z'=8,'x'=4,'core'=2] {'x','core'}, dimensions={0} | all-to-all | bytes 262144 | tf_op jit(solution)/shard_map/all_to_all | solution.py:268
  321.5 3.9 all-to-all-start.12
  325.4 11.1 %all-to-all-done.12.rest_6_ = bf16[32,16,256]{2,1,0:T(8,128)(2,1)S(1)} async-done(((bf16[32,16,256]{2,1,0:T(8,128)(2,1)}), bf16[32,16,256]{2,1,0:T(8,128)(2,1)S(1)}, u32[]{:S(2)}, u32[]{:S(2)}) %all-to-all-start.12) | async-done | bytes 262176 | tf_op jit(solution)/shard_map/all_to_all | solution.py:258
  336.5 5.8 %solve.6 = (bf16[16,256]{1,0:T(8,128)(2,1)S(1)}, bf16[32,16,256]{2,1,0:T(8,128)(2,1)S(1)}) custom-call(s32[8,128]{1,0:T(8,128)S(1)} %get-tuple-element.29.table, bf16[8,3,6,256,256]{4,3,2,1,0:T(8,128)(2,1)} %bitcast.79, bf16[16,256]{1,0:T(8,128)(2,1)S(1)} %dynamic-slice_bitcast_fusion.1.right, bf16[1,6,256,256]{3,2,1,0:T(8,128)(2,1)S(1)} %copy-done.4, ...), custom_call_target="tpu_custom_call" | custom-call | flops 100663296 | bytes 7340032 | tf_op jit(solution)/shard_map/solve/pallas_call | solution.py:202
  342.3 14.9 %all_to_all.105.rest_1_.rest_2_.rest_3_.rest_4_.rest_5_ = bf16[32,16,256]{2,1,0:T(8,128)(2,1)S(1)} all-to-all(bf16[32,16,256]{2,1,0:T(8,128)(2,1)S(1)} %get-tuple-element.41), channel_id=1, replica_groups=mesh['g'=4,'z'=8,'x'=4,'core'=2] {'z','g'}, dimensions={0} | all-to-all | bytes 524288 | tf_op jit(solution)/shard_map/all_to_all | solution.py:258
  357.2 5.4 %solve.7 = (bf16[16,256]{1,0:T(8,128)(2,1)S(1)}, bf16[32,16,256]{2,1,0:T(8,128)(2,1)S(1)}) custom-call(s32[8,128]{1,0:T(8,128)S(1)} %get-tuple-element.29.table, bf16[8,3,6,256,256]{4,3,2,1,0:T(8,128)(2,1)} %bitcast.80, bf16[16,256]{1,0:T(8,128)(2,1)S(1)} %get-tuple-element.39.right, bf16[1,6,256,256]{3,2,1,0:T(8,128)(2,1)S(1)} %copy-done.3, ...), custom_call_target="tpu_custom_call" | custom-call | flops 100663296 | bytes 7340032 | tf_op jit(solution)/shard_map/solve/pallas_call | solution.py:202
  362.6 14.9 %all_to_all.106.rest_1_.rest_2_.rest_3_.rest_4_ = bf16[32,16,256]{2,1,0:T(8,128)(2,1)S(1)} all-to-all(bf16[32,16,256]{2,1,0:T(8,128)(2,1)S(1)} %get-tuple-element.42), channel_id=1, replica_groups=mesh['g'=4,'z'=8,'x'=4,'core'=2] {'z','g'}, dimensions={0} | all-to-all | bytes 524288 | tf_op jit(solution)/shard_map/all_to_all | solution.py:258
  377.5 6.1 %solve.8 = (bf16[16,256]{1,0:T(8,128)(2,1)S(1)}, bf16[32,16,256]{2,1,0:T(8,128)(2,1)}) custom-call(s32[8,128]{1,0:T(8,128)S(1)} %get-tuple-element.29.table, bf16[8,3,6,256,256]{4,3,2,1,0:T(8,128)(2,1)} %bitcast.81, bf16[16,256]{1,0:T(8,128)(2,1)S(1)} %get-tuple-element.38.right, bf16[1,6,256,256]{3,2,1,0:T(8,128)(2,1)S(1)} %copy-done.3, ...), custom_call_target="tpu_custom_call" | custom-call | flops 100663296 | bytes 7340032 | tf_op jit(solution)/shard_map/solve/pallas_call | solution.py:202
  383.5 3.9 all-to-all-start.15
  387.4 10.5 %all-to-all-done.15.rest_1_.rest_2_.rest_3_ = bf16[32,16,256]{2,1,0:T(8,128)(2,1)S(1)} async-done(((bf16[32,16,256]{2,1,0:T(8,128)(2,1)}), bf16[32,16,256]{2,1,0:T(8,128)(2,1)S(1)}, u32[]{:S(2)}, u32[]{:S(2)}) %all-to-all-start.15) | async-done | bytes 262176 | tf_op jit(solution)/shard_map/all_to_all | solution.py:258
  398.0 5.4 %solve.9 = (bf16[16,256]{1,0:T(8,128)(2,1)S(1)}, bf16[32,16,256]{2,1,0:T(8,128)(2,1)S(1)}) custom-call(s32[8,128]{1,0:T(8,128)S(1)} %get-tuple-element.29.table, bf16[8,3,6,256,256]{4,3,2,1,0:T(8,128)(2,1)} %bitcast.82, bf16[16,256]{1,0:T(8,128)(2,1)S(1)} %get-tuple-element.33.right, bf16[1,6,256,256]{3,2,1,0:T(8,128)(2,1)S(1)} %copy-done.3, ...), custom_call_target="tpu_custom_call" | custom-call | flops 100663296 | bytes 7340032 | tf_op jit(solution)/shard_map/solve/pallas_call | solution.py:202
  403.4 13.7 %all_to_all.107.rest_1_.rest_2_ = bf16[32,16,256]{2,1,0:T(8,128)(2,1)S(1)} all-to-all(bf16[32,16,256]{2,1,0:T(8,128)(2,1)S(1)} %get-tuple-element.44), channel_id=1, replica_groups=mesh['g'=4,'z'=8,'x'=4,'core'=2] {'z','g'}, dimensions={0} | all-to-all | bytes 524288 | tf_op jit(solution)/shard_map/all_to_all | solution.py:258
  417.1 5.4 %solve.10 = (bf16[16,256]{1,0:T(8,128)(2,1)S(1)}, bf16[32,16,256]{2,1,0:T(8,128)(2,1)S(1)}) custom-call(s32[8,128]{1,0:T(8,128)S(1)} %get-tuple-element.29.table, bf16[8,3,6,256,256]{4,3,2,1,0:T(8,128)(2,1)} %bitcast.83, bf16[16,256]{1,0:T(8,128)(2,1)S(1)} %get-tuple-element.31.right, bf16[1,6,256,256]{3,2,1,0:T(8,128)(2,1)S(1)} %copy-done.3, ...), custom_call_target="tpu_custom_call" | custom-call | flops 100663296 | bytes 7340032 | tf_op jit(solution)/shard_map/solve/pallas_call | solution.py:202
  422.5 13.9 %all_to_all.108.rest_1_ = bf16[32,16,256]{2,1,0:T(8,128)(2,1)S(1)} all-to-all(bf16[32,16,256]{2,1,0:T(8,128)(2,1)S(1)} %get-tuple-element.45), channel_id=1, replica_groups=mesh['g'=4,'z'=8,'x'=4,'core'=2] {'z','g'}, dimensions={0} | all-to-all | bytes 524288 | tf_op jit(solution)/shard_map/all_to_all | solution.py:258
  436.3 5.3 %solve.11 = bf16[8,6,16,256]{3,2,1,0:T(8,128)(2,1)S(1)} custom-call(s32[8,128]{1,0:T(8,128)S(1)} %get-tuple-element.29.table, bf16[8,3,6,256,256]{4,3,2,1,0:T(8,128)(2,1)} %bitcast.84, bf16[16,256]{1,0:T(8,128)(2,1)S(1)} %get-tuple-element.30.right, bf16[1,6,256,256]{3,2,1,0:T(8,128)(2,1)S(1)} %copy-done.3, bf16[32,16,256]{2,1,0:T(8,128)(2,1)S(1)} %all_to_all.108.rest_1_, ...), custom_call_target="tpu_custom_call" | custom-call | flops 100663296 | bytes 7340032 | tf_op jit(solution)/shard_map/solve/pallas_call | solution.py:202
  441.7 18.1 %all_to_all.109 = bf16[8,6,16,256]{3,2,1,0:T(8,128)(2,1)S(1)} all-to-all(bf16[8,6,16,256]{3,2,1,0:T(8,128)(2,1)S(1)} %solve.11), channel_id=1, replica_groups=mesh['g'=4,'z'=8,'x'=4,'core'=2] {'x','core'}, dimensions={0} | all-to-all | bytes 786432 | tf_op jit(solution)/shard_map/all_to_all | solution.py:295
  (41 shorter events, 7.6 us)
Async XLA Ops:
  6.5 145.4 %copy-start = (bf16[1,6,128,256]{3,2,1,0:T(8,128)(2,1)S(1)}, bf16[1,6,128,256]{3,2,1,0:T(8,128)(2,1)}, u32[]{:S(2)}) copy-start(bf16[1,6,128,256]{3,2,1,0:T(8,128)(2,1)} %param.9) | copy-start | bytes 1179652
  6.5 314.9 %all-gather.7.cloned.1.call-start = ((), (), s32[]{:S(2)}) async-start(), calls=%async_computation.20 | async-start | bytes 21233664 | tf_op jit(solution)/shard_map/all_gather | solution.py:239
  79.2 72.8 %copy-start.4 = (bf16[1,6,256,256]{3,2,1,0:T(8,128)(2,1)S(1)}, bf16[1,6,256,256]{3,2,1,0:T(8,128)(2,1)}, u32[]{:S(2)}) copy-start(bf16[1,6,256,256]{3,2,1,0:T(8,128)(2,1)} %rest_0_.6) | copy-start | bytes 2359300
  79.2 85.8 %copy-start.6 = (s32[1,5,6]{2,0,1:T(1,128)S(1)}, s32[1,5,6]{2,0,1:T(1,128)}, u32[]{:S(2)}) copy-start(s32[1,5,6]{2,0,1:T(1,128)} %param.13) | copy-start | bytes 364
  79.2 85.8 %copy-start.8 = (s32[1,5,1]{1,2,0:T(1,128)S(1)}, s32[1,5,1]{1,2,0:T(1,128)}, u32[]{:S(2)}) copy-start(s32[1,5,1]{1,2,0:T(1,128)} %param.14) | copy-start | bytes 64
  79.2 103.7 %copy-start.5 = (s32[1,5,6]{2,0,1:T(1,128)S(1)}, s32[1,5,6]{2,0,1:T(1,128)}, u32[]{:S(2)}) copy-start(s32[1,5,6]{2,0,1:T(1,128)} %param.16) | copy-start | bytes 364
  79.2 103.7 %copy-start.7 = (s32[1,5,1]{1,2,0:T(1,128)S(1)}, s32[1,5,1]{1,2,0:T(1,128)}, u32[]{:S(2)}) copy-start(s32[1,5,1]{1,2,0:T(1,128)} %param.17) | copy-start | bytes 64
  79.2 308.2 %all-gather.5.cloned.1.call-start = ((), (), s32[]{:S(2)}) async-start(), calls=%async_computation.19 | async-start | bytes 21233664 | tf_op jit(solution)/shard_map/all_gather | solution.py:240
  152.8 23.3 %all-to-all-start = ((bf16[32,16,256]{2,1,0:T(8,128)(2,1)}), bf16[32,16,256]{2,1,0:T(8,128)(2,1)}, u32[]{:S(2)}, u32[]{:S(2)}) async-start(bf16[32,16,256]{2,1,0:T(8,128)(2,1)} %get-tuple-element.28), calls=%async_computation | async-start | bytes 524288 | tf_op jit(solution)/shard_map/all_to_all | solution.py:258
  176.2 13.3 %all-to-all-start.1 = ((bf16[8,4,16,256]{3,2,1,0:T(8,128)(2,1)}), bf16[8,4,16,256]{3,2,1,0:T(8,128)(2,1)S(1)}, u32[]{:S(2)}, u32[]{:S(2)}) async-start(bf16[8,4,16,256]{3,2,1,0:T(8,128)(2,1)} %bitcast.2), calls=%async_computation.1 | async-start | bytes 524288 | tf_op jit(solution)/shard_map/all_to_all | solution.py:261
  189.4 2.1 copy-start.1
  191.5 41.4 %copy-start.2 = (bf16[1,5,6,256,256]{4,3,2,1,0:T(8,128)(2,1)S(1)}, bf16[1,5,6,256,256]{4,3,2,1,0:T(8,128)(2,1)}, u32[]{:S(2)}) copy-start(bf16[1,5,6,256,256]{4,3,2,1,0:T(8,128)(2,1)} %low_blocks.1) | copy-start | bytes 11796484
  284.5 52.0 %copy-start.3 = (bf16[1,6,256,256]{3,2,1,0:T(8,128)(2,1)S(1)}, bf16[1,6,256,256]{3,2,1,0:T(8,128)(2,1)}, u32[]{:S(2)}) copy-start(bf16[1,6,256,256]{3,2,1,0:T(8,128)(2,1)} %rest_0_.11) | copy-start | bytes 2359300
  321.5 15.0 %all-to-all-start.12 = ((bf16[32,16,256]{2,1,0:T(8,128)(2,1)}), bf16[32,16,256]{2,1,0:T(8,128)(2,1)S(1)}, u32[]{:S(2)}, u32[]{:S(2)}) async-start(bf16[32,16,256]{2,1,0:T(8,128)(2,1)} %get-tuple-element.40), calls=%async_computation.12 | async-start | bytes 524288 | tf_op jit(solution)/shard_map/all_to_all | solution.py:258
  383.5 14.5 %all-to-all-start.15 = ((bf16[32,16,256]{2,1,0:T(8,128)(2,1)}), bf16[32,16,256]{2,1,0:T(8,128)(2,1)S(1)}, u32[]{:S(2)}, u32[]{:S(2)}) async-start(bf16[32,16,256]{2,1,0:T(8,128)(2,1)} %get-tuple-element.43), calls=%async_computation.15 | async-start | bytes 524288 | tf_op jit(solution)/shard_map/all_to_all | solution.py:258
Sparse Core Ops, SparseCore 0:
  79.3 100.5 all-gather.6
  181.7 107.2 all-gather.4

commit v4 on v3

--- a/solution.py
+++ b/solution.py
@@ -37,45 +37,42 @@
     return pltpu.CompilerParams(vmem_limit_bytes=mib << 20)
 
 
-def join_kernel(cut, low_blocks, high_blocks, out, sems):
-    n = low_blocks.shape[1]
-    last = n - (out.shape[0] - (high_blocks.shape[1] - cut))
-    copies = [
-        pltpu.make_async_copy(low_blocks.at[0, pl.ds(last, n - last)], out.at[pl.ds(0, n - last)], sems.at[0]),
-        pltpu.make_async_copy(high_blocks.at[0, pl.ds(cut, n - cut)], out.at[pl.ds(n - last, n - cut)], sems.at[1]),
-    ]
-    for copy in run(copies):
-        copy.wait()
-
-
-def join(count, cut, low_blocks, high_blocks):
+def select_kernel(parts, out, room, *sems):
+    loads, stores, n = [], [], 0
+    for source, low, high in parts:
+        for row in range(low, high):
+            loads.append(pltpu.make_async_copy(source.at[0, row], room.at[n], sems[0].at[n]))
+            stores.append(pltpu.make_async_copy(room.at[n], out.at[n], sems[1].at[n]))
+            n += 1
+    run(loads)
+    for load, store in zip(loads, stores):
+        load.wait()
+        store.start()
+    for store in stores:
+        store.wait()
+
+
+def select(*parts):
+    count = sum(high - low for _, low, high in parts)
+    shape = parts[0][0].shape[2:]
+
+    def body(*refs):
+        n = len(parts)
+        select_kernel([(ref, low, high) for ref, (_, low, high) in zip(refs, parts)], *refs[n:])
+
     return pl.pallas_call(
-        functools.partial(join_kernel, cut),
-        out_shape=jax.ShapeDtypeStruct((count,) + low_blocks.shape[2:], BF),
-        in_specs=[ANY, ANY],
+        body,
+        out_shape=jax.ShapeDtypeStruct((count,) + shape, BF),
+        in_specs=[ANY] * len(parts),
         out_specs=ANY,
-        scratch_shapes=[pltpu.SemaphoreType.DMA((2,))],
-        compiler_params=params(60),
-        name="join",
-    )(low_blocks, high_blocks)
-
-
-def head_kernel(count, blocks, out, sem):
-    copy = pltpu.make_async_copy(blocks.at[0, pl.ds(0, count)], out, sem)
-    copy.start()
-    copy.wait()
-
-
-def head(count, blocks):
-    return pl.pallas_call(
-        functools.partial(head_kernel, count),
-        out_shape=jax.ShapeDtypeStruct((count,) + blocks.shape[2:], BF),
-        in_specs=[ANY],
-        out_specs=ANY,
-        scratch_shapes=[pltpu.SemaphoreType.DMA(())],
-        compiler_params=params(60),
-        name="head",
-    )(blocks)
+        scratch_shapes=[
+            pltpu.VMEM((count,) + shape, BF),
+            pltpu.SemaphoreType.DMA((count,)),
+            pltpu.SemaphoreType.DMA((count,)),
+        ],
+        compiler_params=params(62),
+        name="select",
+    )(*[source for source, _, _ in parts])
 
 
 def pick(stores, first, place, load):
@@ -234,8 +231,8 @@
     last = LAST_SPLIT
     nlow = levels - 1 - last
     cut = HEAD
-    first = join(nlow + levels - 1 - cut, cut, lower_blocks, upper_blocks)
-    second = head(cut, upper_blocks)
+    first = select((lower_blocks, last, levels - 1), (upper_blocks, cut, levels - 1))
+    second = select((upper_blocks, 0, cut))
     gathered = lax.all_gather(first, COL, axis=0)
     gathered_low = lax.all_gather(second, COL, axis=0)
 

time: 468 us -> 334 us (0.71)
  Pallas kernels: 185 us -> 45 us
    pallas_call x2, Pallas kernels: 145 us -> 5.3 us  [select(): pl.pallas_call(body, out_shape=jax.ShapeDtypeStruct((count,) + shape, BF)...]
  transfers between devices with their start and end apart: 6 -> 6, of which waited for: 4 -> 4; matrix products, arithmetic and copies ran while one was open for 0% -> 0% of each run, Pallas kernels for 21% -> 8%
where the time goes in v4:
time: 334 us; the launch traced here: 333 us
  blocking collectives  203 us (61%)
  Pallas kernels  45 us (13%)
  waiting for transfers between devices  41.5 us (12%)
  starting transfers between devices  26.7 us (8%)
  between operations  13.7 us (4%)
    all_to_all x7, blocking collectives, spread(): return lax.all_to_all(copies, TURNED, 0, 0, tiled=True)  100 us
    all_to_all x3, blocking collectives, by_column(): lax.all_to_all(whole.reshape(ncol, group, part, size), COL, 0, 0, tiled=T...  41.9 us
    all_to_all x4, blocking collectives, shards(): parts = lax.all_to_all(partial, COL, 0, 0, tiled=True)  41.9 us
    pallas_call x6, Pallas kernels, solve(): pl.pallas_call(functools.partial(solve_kernel, n, low, row, at, levels, h...  33.3 us
    all_to_all x3, waiting for transfers between devices, spread(): return lax.all_to_all(copies, TURNED, 0, 0, tiled=True)  31.8 us
    all_to_all x3, starting transfers between devices, spread(): return lax.all_to_all(copies, TURNED, 0, 0, tiled=True)  19.9 us
    all_to_all x1, blocking collectives, shards(): whole = lax.all_to_all(solve(*args, result), COL, 0, 0, tiled=True)  18.9 us
    all_to_all x1, waiting for transfers between devices, by_column(): lax.all_to_all(whole.reshape(ncol, group, part, size), COL, 0, 0, tiled=T...  9.56 us
  transfers between devices with their start and end apart: 6, of which 4 were waited for; matrix products, arithmetic and copies ran while one was open for 0% of the time, Pallas kernels for 8%

profile of v4, /device:TPU:1, one launch (start us, length us, event | category | flops | bytes accessed | tf_op | source)
XLA Modules:
  0.0 333.3 jit_solution(10618348873347964384)
XLA Ops:
  6.5 2.7 select.28
  9.3 2.6 select.27
  13.0 12.2 %all-to-all-start = ((bf16[32,16,256]{2,1,0:T(8,128)(2,1)}), bf16[32,16,256]{2,1,0:T(8,128)(2,1)}, u32[]{:S(2)}, u32[]{:S(2)}) async-start(bf16[32,16,256]{2,1,0:T(8,128)(2,1)} %get-tuple-element.28), calls=%async_computation | async-start | bytes 524288 | tf_op jit(solution)/shard_map/all_to_all | solution.py:255
  25.2 11.1 %all-to-all-done.rest_2_ = bf16[32,16,256]{2,1,0:T(8,128)(2,1)} async-done(((bf16[32,16,256]{2,1,0:T(8,128)(2,1)}), bf16[32,16,256]{2,1,0:T(8,128)(2,1)}, u32[]{:S(2)}, u32[]{:S(2)}) %all-to-all-start) | async-done | bytes 262176 | tf_op jit(solution)/shard_map/all_to_all | solution.py:255
  36.3 6.7 %all-to-all-start.1 = ((bf16[8,4,16,256]{3,2,1,0:T(8,128)(2,1)}), bf16[8,4,16,256]{3,2,1,0:T(8,128)(2,1)S(1)}, u32[]{:S(2)}, u32[]{:S(2)}) async-start(bf16[8,4,16,256]{3,2,1,0:T(8,128)(2,1)} %bitcast.2), calls=%async_computation.1 | async-start | bytes 524288 | tf_op jit(solution)/shard_map/all_to_all | solution.py:258
  43.2 9.6 %all-to-all-done.1.rest_0_ = bf16[8,4,16,256]{3,2,1,0:T(8,128)(2,1)S(1)} async-done(((bf16[8,4,16,256]{3,2,1,0:T(8,128)(2,1)}), bf16[8,4,16,256]{3,2,1,0:T(8,128)(2,1)S(1)}, u32[]{:S(2)}, u32[]{:S(2)}) %all-to-all-start.1) | async-done | bytes 262176 | tf_op jit(solution)/shard_map/all_to_all | solution.py:258
  52.8 2.4 copy-done.1
  56.2 11.8 %all_to_all.95.parts = f32[8,24,256]{2,1,0:T(8,128)S(1)} all-to-all(f32[8,24,256]{2,1,0:T(8,128)S(1)} %update.4), channel_id=1, replica_groups=mesh['g'=4,'z'=8,'x'=4,'core'=2] {'x','core'}, dimensions={0} | all-to-all | bytes 393216 | tf_op jit(solution)/shard_map/all_to_all | solution.py:265
  68.2 14.3 %all_to_all.96.rest_3_ = bf16[32,16,256]{2,1,0:T(8,128)(2,1)S(1)} all-to-all(bf16[32,16,256]{2,1,0:T(8,128)(2,1)S(1)} %get-tuple-element.32), channel_id=1, replica_groups=mesh['g'=4,'z'=8,'x'=4,'core'=2] {'z','g'}, dimensions={0} | all-to-all | bytes 524288 | tf_op jit(solution)/shard_map/all_to_all | solution.py:255
  82.5 15.1 %all_to_all.97.rest_1_ = bf16[8,4,16,256]{3,2,1,0:T(8,128)(2,1)S(1)} all-to-all(bf16[8,4,16,256]{3,2,1,0:T(8,128)(2,1)S(1)} %bitcast.76), channel_id=1, replica_groups=mesh['g'=4,'z'=8,'x'=4,'core'=2] {'x','core'}, dimensions={0} | all-to-all | bytes 524288 | tf_op jit(solution)/shard_map/all_to_all | solution.py:258
  98.6 10.0 %all_to_all.98.parts = f32[8,16,256]{2,1,0:T(8,128)S(1)} all-to-all(f32[8,16,256]{2,1,0:T(8,128)S(1)} %update.5), channel_id=1, replica_groups=mesh['g'=4,'z'=8,'x'=4,'core'=2] {'x','core'}, dimensions={0} | all-to-all | bytes 262144 | tf_op jit(solution)/shard_map/all_to_all | solution.py:265
  108.8 14.1 %all_to_all.99.rest_4_ = bf16[32,16,256]{2,1,0:T(8,128)(2,1)S(1)} all-to-all(bf16[32,16,256]{2,1,0:T(8,128)(2,1)S(1)} %get-tuple-element.34), channel_id=1, replica_groups=mesh['g'=4,'z'=8,'x'=4,'core'=2] {'z','g'}, dimensions={0} | all-to-all | bytes 524288 | tf_op jit(solution)/shard_map/all_to_all | solution.py:255
  122.9 12.2 %all_to_all.100.rest_2_ = bf16[8,4,16,256]{3,2,1,0:T(8,128)(2,1)S(1)} all-to-all(bf16[8,4,16,256]{3,2,1,0:T(8,128)(2,1)S(1)} %bitcast.77), channel_id=1, replica_groups=mesh['g'=4,'z'=8,'x'=4,'core'=2] {'x','core'}, dimensions={0} | all-to-all | bytes 524288 | tf_op jit(solution)/shard_map/all_to_all | solution.py:258
  136.2 10.1 %all_to_all.101.parts = f32[8,16,256]{2,1,0:T(8,128)S(1)} all-to-all(f32[8,16,256]{2,1,0:T(8,128)S(1)} %update.6), channel_id=1, replica_groups=mesh['g'=4,'z'=8,'x'=4,'core'=2] {'x','core'}, dimensions={0} | all-to-all | bytes 262144 | tf_op jit(solution)/shard_map/all_to_all | solution.py:265
  146.5 14.7 %all_to_all.102.rest_5_ = bf16[32,16,256]{2,1,0:T(8,128)(2,1)S(1)} all-to-all(bf16[32,16,256]{2,1,0:T(8,128)(2,1)S(1)} %get-tuple-element.35), channel_id=1, replica_groups=mesh['g'=4,'z'=8,'x'=4,'core'=2] {'z','g'}, dimensions={0} | all-to-all | bytes 524288 | tf_op jit(solution)/shard_map/all_to_all | solution.py:255
  161.2 14.6 %all_to_all.103.rest_3_ = bf16[8,4,16,256]{3,2,1,0:T(8,128)(2,1)S(1)} all-to-all(bf16[8,4,16,256]{3,2,1,0:T(8,128)(2,1)S(1)} %bitcast.78), channel_id=1, replica_groups=mesh['g'=4,'z'=8,'x'=4,'core'=2] {'x','core'}, dimensions={0} | all-to-all | bytes 524288 | tf_op jit(solution)/shard_map/all_to_all | solution.py:258
  176.7 10.0 %all_to_all.104.parts = f32[8,16,256]{2,1,0:T(8,128)S(1)} all-to-all(f32[8,16,256]{2,1,0:T(8,128)S(1)} %update.7), channel_id=1, replica_groups=mesh['g'=4,'z'=8,'x'=4,'core'=2] {'x','core'}, dimensions={0} | all-to-all | bytes 262144 | tf_op jit(solution)/shard_map/all_to_all | solution.py:265
  187.6 3.9 %all-to-all-start.12 = ((bf16[32,16,256]{2,1,0:T(8,128)(2,1)}), bf16[32,16,256]{2,1,0:T(8,128)(2,1)S(1)}, u32[]{:S(2)}, u32[]{:S(2)}) async-start(bf16[32,16,256]{2,1,0:T(8,128)(2,1)} %get-tuple-element.40), calls=%async_computation.12 | async-start | bytes 524288 | tf_op jit(solution)/shard_map/all_to_all | solution.py:255
  191.6 10.4 %all-to-all-done.12.rest_6_ = bf16[32,16,256]{2,1,0:T(8,128)(2,1)S(1)} async-done(((bf16[32,16,256]{2,1,0:T(8,128)(2,1)}), bf16[32,16,256]{2,1,0:T(8,128)(2,1)S(1)}, u32[]{:S(2)}, u32[]{:S(2)}) %all-to-all-start.12) | async-done | bytes 262176 | tf_op jit(solution)/shard_map/all_to_all | solution.py:255
  202.0 5.8 %solve.6 = (bf16[16,256]{1,0:T(8,128)(2,1)S(1)}, bf16[32,16,256]{2,1,0:T(8,128)(2,1)S(1)}) custom-call(s32[8,128]{1,0:T(8,128)S(1)} %get-tuple-element.29.table, bf16[8,3,6,256,256]{4,3,2,1,0:T(8,128)(2,1)} %bitcast.79, bf16[16,256]{1,0:T(8,128)(2,1)S(1)} %dynamic-slice_bitcast_fusion.1.right, bf16[1,6,256,256]{3,2,1,0:T(8,128)(2,1)S(1)} %copy-done.4, ...), custom_call_target="tpu_custom_call" | custom-call | flops 100663296 | bytes 7340032 | tf_op jit(solution)/shard_map/solve/pallas_call | solution.py:199
  207.8 15.4 %all_to_all.105.rest_1_.rest_2_.rest_3_.rest_4_.rest_5_ = bf16[32,16,256]{2,1,0:T(8,128)(2,1)S(1)} all-to-all(bf16[32,16,256]{2,1,0:T(8,128)(2,1)S(1)} %get-tuple-element.41), channel_id=1, replica_groups=mesh['g'=4,'z'=8,'x'=4,'core'=2] {'z','g'}, dimensions={0} | all-to-all | bytes 524288 | tf_op jit(solution)/shard_map/all_to_all | solution.py:255
  223.3 5.4 %solve.7 = (bf16[16,256]{1,0:T(8,128)(2,1)S(1)}, bf16[32,16,256]{2,1,0:T(8,128)(2,1)S(1)}) custom-call(s32[8,128]{1,0:T(8,128)S(1)} %get-tuple-element.29.table, bf16[8,3,6,256,256]{4,3,2,1,0:T(8,128)(2,1)} %bitcast.80, bf16[16,256]{1,0:T(8,128)(2,1)S(1)} %get-tuple-element.39.right, bf16[1,6,256,256]{3,2,1,0:T(8,128)(2,1)S(1)} %copy-done.3, ...), custom_call_target="tpu_custom_call" | custom-call | flops 100663296 | bytes 7340032 | tf_op jit(solution)/shard_map/solve/pallas_call | solution.py:199
  228.6 14.2 %all_to_all.106.rest_1_.rest_2_.rest_3_.rest_4_ = bf16[32,16,256]{2,1,0:T(8,128)(2,1)S(1)} all-to-all(bf16[32,16,256]{2,1,0:T(8,128)(2,1)S(1)} %get-tuple-element.42), channel_id=1, replica_groups=mesh['g'=4,'z'=8,'x'=4,'core'=2] {'z','g'}, dimensions={0} | all-to-all | bytes 524288 | tf_op jit(solution)/shard_map/all_to_all | solution.py:255
  242.8 6.1 %solve.8 = (bf16[16,256]{1,0:T(8,128)(2,1)S(1)}, bf16[32,16,256]{2,1,0:T(8,128)(2,1)}) custom-call(s32[8,128]{1,0:T(8,128)S(1)} %get-tuple-element.29.table, bf16[8,3,6,256,256]{4,3,2,1,0:T(8,128)(2,1)} %bitcast.81, bf16[16,256]{1,0:T(8,128)(2,1)S(1)} %get-tuple-element.38.right, bf16[1,6,256,256]{3,2,1,0:T(8,128)(2,1)S(1)} %copy-done.3, ...), custom_call_target="tpu_custom_call" | custom-call | flops 100663296 | bytes 7340032 | tf_op jit(solution)/shard_map/solve/pallas_call | solution.py:199
  248.9 3.9 %all-to-all-start.15 = ((bf16[32,16,256]{2,1,0:T(8,128)(2,1)}), bf16[32,16,256]{2,1,0:T(8,128)(2,1)S(1)}, u32[]{:S(2)}, u32[]{:S(2)}) async-start(bf16[32,16,256]{2,1,0:T(8,128)(2,1)} %get-tuple-element.43), calls=%async_computation.15 | async-start | bytes 524288 | tf_op jit(solution)/shard_map/all_to_all | solution.py:255
  252.8 10.3 %all-to-all-done.15.rest_1_.rest_2_.rest_3_ = bf16[32,16,256]{2,1,0:T(8,128)(2,1)S(1)} async-done(((bf16[32,16,256]{2,1,0:T(8,128)(2,1)}), bf16[32,16,256]{2,1,0:T(8,128)(2,1)S(1)}, u32[]{:S(2)}, u32[]{:S(2)}) %all-to-all-start.15) | async-done | bytes 262176 | tf_op jit(solution)/shard_map/all_to_all | solution.py:255
  263.2 5.4 %solve.9 = (bf16[16,256]{1,0:T(8,128)(2,1)S(1)}, bf16[32,16,256]{2,1,0:T(8,128)(2,1)S(1)}) custom-call(s32[8,128]{1,0:T(8,128)S(1)} %get-tuple-element.29.table, bf16[8,3,6,256,256]{4,3,2,1,0:T(8,128)(2,1)} %bitcast.82, bf16[16,256]{1,0:T(8,128)(2,1)S(1)} %get-tuple-element.33.right, bf16[1,6,256,256]{3,2,1,0:T(8,128)(2,1)S(1)} %copy-done.3, ...), custom_call_target="tpu_custom_call" | custom-call | flops 100663296 | bytes 7340032 | tf_op jit(solution)/shard_map/solve/pallas_call | solution.py:199
  268.5 13.9 %all_to_all.107.rest_1_.rest_2_ = bf16[32,16,256]{2,1,0:T(8,128)(2,1)S(1)} all-to-all(bf16[32,16,256]{2,1,0:T(8,128)(2,1)S(1)} %get-tuple-element.44), channel_id=1, replica_groups=mesh['g'=4,'z'=8,'x'=4,'core'=2] {'z','g'}, dimensions={0} | all-to-all | bytes 524288 | tf_op jit(solution)/shard_map/all_to_all | solution.py:255
  282.4 5.4 %solve.10 = (bf16[16,256]{1,0:T(8,128)(2,1)S(1)}, bf16[32,16,256]{2,1,0:T(8,128)(2,1)S(1)}) custom-call(s32[8,128]{1,0:T(8,128)S(1)} %get-tuple-element.29.table, bf16[8,3,6,256,256]{4,3,2,1,0:T(8,128)(2,1)} %bitcast.83, bf16[16,256]{1,0:T(8,128)(2,1)S(1)} %get-tuple-element.31.right, bf16[1,6,256,256]{3,2,1,0:T(8,128)(2,1)S(1)} %copy-done.3, ...), custom_call_target="tpu_custom_call" | custom-call | flops 100663296 | bytes 7340032 | tf_op jit(solution)/shard_map/solve/pallas_call | solution.py:199
  287.8 13.8 %all_to_all.108.rest_1_ = bf16[32,16,256]{2,1,0:T(8,128)(2,1)S(1)} all-to-all(bf16[32,16,256]{2,1,0:T(8,128)(2,1)S(1)} %get-tuple-element.45), channel_id=1, replica_groups=mesh['g'=4,'z'=8,'x'=4,'core'=2] {'z','g'}, dimensions={0} | all-to-all | bytes 524288 | tf_op jit(solution)/shard_map/all_to_all | solution.py:255
  301.5 5.3 %solve.11 = bf16[8,6,16,256]{3,2,1,0:T(8,128)(2,1)S(1)} custom-call(s32[8,128]{1,0:T(8,128)S(1)} %get-tuple-element.29.table, bf16[8,3,6,256,256]{4,3,2,1,0:T(8,128)(2,1)} %bitcast.84, bf16[16,256]{1,0:T(8,128)(2,1)S(1)} %get-tuple-element.30.right, bf16[1,6,256,256]{3,2,1,0:T(8,128)(2,1)S(1)} %copy-done.3, bf16[32,16,256]{2,1,0:T(8,128)(2,1)S(1)} %all_to_all.108.rest_1_, ...), custom_call_target="tpu_custom_call" | custom-call | flops 100663296 | bytes 7340032 | tf_op jit(solution)/shard_map/solve/pallas_call | solution.py:199
  306.9 18.9 %all_to_all.109 = bf16[8,6,16,256]{3,2,1,0:T(8,128)(2,1)S(1)} all-to-all(bf16[8,6,16,256]{3,2,1,0:T(8,128)(2,1)S(1)} %solve.11), channel_id=1, replica_groups=mesh['g'=4,'z'=8,'x'=4,'core'=2] {'x','core'}, dimensions={0} | all-to-all | bytes 786432 | tf_op jit(solution)/shard_map/all_to_all | solution.py:292
  (41 shorter events, 7.6 us)
Async XLA Ops:
  6.5 5.5 %copy-start = (bf16[1,6,128,256]{3,2,1,0:T(8,128)(2,1)S(1)}, bf16[1,6,128,256]{3,2,1,0:T(8,128)(2,1)}, u32[]{:S(2)}) copy-start(bf16[1,6,128,256]{3,2,1,0:T(8,128)(2,1)} %param.9) | copy-start | bytes 1179652
  6.5 181.1 %all-gather.7.cloned.1.call-start = ((), (), s32[]{:S(2)}) async-start(), calls=%async_computation.20 | async-start | bytes 21233664 | tf_op jit(solution)/shard_map/all_gather | solution.py:236
  9.2 2.8 copy-start.4
  9.2 15.9 %copy-start.6 = (s32[1,5,6]{2,0,1:T(1,128)S(1)}, s32[1,5,6]{2,0,1:T(1,128)}, u32[]{:S(2)}) copy-start(s32[1,5,6]{2,0,1:T(1,128)} %param.13) | copy-start | bytes 364
  9.3 15.9 %copy-start.8 = (s32[1,5,1]{1,2,0:T(1,128)S(1)}, s32[1,5,1]{1,2,0:T(1,128)}, u32[]{:S(2)}) copy-start(s32[1,5,1]{1,2,0:T(1,128)} %param.14) | copy-start | bytes 64
  9.3 33.8 %copy-start.5 = (s32[1,5,6]{2,0,1:T(1,128)S(1)}, s32[1,5,6]{2,0,1:T(1,128)}, u32[]{:S(2)}) copy-start(s32[1,5,6]{2,0,1:T(1,128)} %param.16) | copy-start | bytes 364
  9.3 33.8 %copy-start.7 = (s32[1,5,1]{1,2,0:T(1,128)S(1)}, s32[1,5,1]{1,2,0:T(1,128)}, u32[]{:S(2)}) copy-start(s32[1,5,1]{1,2,0:T(1,128)} %param.17) | copy-start | bytes 64
  9.3 243.5 %all-gather.5.cloned.1.call-start = ((), (), s32[]{:S(2)}) async-start(), calls=%async_computation.19 | async-start | bytes 21233664 | tf_op jit(solution)/shard_map/all_gather | solution.py:237
  13.0 23.3 %all-to-all-start = ((bf16[32,16,256]{2,1,0:T(8,128)(2,1)}), bf16[32,16,256]{2,1,0:T(8,128)(2,1)}, u32[]{:S(2)}, u32[]{:S(2)}) async-start(bf16[32,16,256]{2,1,0:T(8,128)(2,1)} %get-tuple-element.28), calls=%async_computation | async-start | bytes 524288 | tf_op jit(solution)/shard_map/all_to_all | solution.py:255
  36.3 16.5 %all-to-all-start.1 = ((bf16[8,4,16,256]{3,2,1,0:T(8,128)(2,1)}), bf16[8,4,16,256]{3,2,1,0:T(8,128)(2,1)S(1)}, u32[]{:S(2)}, u32[]{:S(2)}) async-start(bf16[8,4,16,256]{3,2,1,0:T(8,128)(2,1)} %bitcast.2), calls=%async_computation.1 | async-start | bytes 524288 | tf_op jit(solution)/shard_map/all_to_all | solution.py:258
  52.8 2.4 copy-start.1
  55.2 42.4 %copy-start.2 = (bf16[1,5,6,256,256]{4,3,2,1,0:T(8,128)(2,1)S(1)}, bf16[1,5,6,256,256]{4,3,2,1,0:T(8,128)(2,1)}, u32[]{:S(2)}) copy-start(bf16[1,5,6,256,256]{4,3,2,1,0:T(8,128)(2,1)} %refs_0_.3) | copy-start | bytes 11796484
  146.5 55.5 %copy-start.3 = (bf16[1,6,256,256]{3,2,1,0:T(8,128)(2,1)S(1)}, bf16[1,6,256,256]{3,2,1,0:T(8,128)(2,1)}, u32[]{:S(2)}) copy-start(bf16[1,6,256,256]{3,2,1,0:T(8,128)(2,1)} %rest_0_.11) | copy-start | bytes 2359300
  187.6 14.3 %all-to-all-start.12 = ((bf16[32,16,256]{2,1,0:T(8,128)(2,1)}), bf16[32,16,256]{2,1,0:T(8,128)(2,1)S(1)}, u32[]{:S(2)}, u32[]{:S(2)}) async-start(bf16[32,16,256]{2,1,0:T(8,128)(2,1)} %get-tuple-element.40), calls=%async_computation.12 | async-start | bytes 524288 | tf_op jit(solution)/shard_map/all_to_all | solution.py:255
  248.9 14.3 %all-to-all-start.15 = ((bf16[32,16,256]{2,1,0:T(8,128)(2,1)}), bf16[32,16,256]{2,1,0:T(8,128)(2,1)S(1)}, u32[]{:S(2)}, u32[]{:S(2)}) async-start(bf16[32,16,256]{2,1,0:T(8,128)(2,1)} %get-tuple-element.43), calls=%async_computation.15 | async-start | bytes 524288 | tf_op jit(solution)/shard_map/all_to_all | solution.py:255
Sparse Core Ops, SparseCore 0:
  9.3 109.6 all-gather.6
  120.9 102.6 all-gather.4

commit v5 on v4

--- a/solution.py
+++ b/solution.py
@@ -19,8 +19,8 @@
 VMEM = pl.BlockSpec(memory_space=pltpu.VMEM)
 ANY = pl.BlockSpec(memory_space=pl.ANY)
 HBM = pl.BlockSpec(memory_space=pltpu.HBM)
-LAST_SPLIT = 4
-HEAD = 3
+LAST_SPLIT = 3
+RUNS = (4, 2, 1)
 
 
 def dot(x, y):
@@ -82,7 +82,8 @@
     picked = load(stores[0], index)
     for i in range(1, len(stores)):
         picked = jnp.where(level == i, load(stores[i], index), picked)
-    return jnp.where(place >= 0, picked, jnp.zeros_like(picked))
+    live = (place >= first * width) & (place < (first + len(stores)) * width)
+    return jnp.where(live, picked, jnp.zeros_like(picked))
 
 
 def update_kernel(level, n, extra, table, blocks, *rest):
@@ -153,22 +154,69 @@
     )(*([] if parts is None else [parts]), right, inverse)
 
 
-def solve_kernel(n, low, row, at, levels, held, table, blocks, right, *rest):
+def row(store, index):
+    return store[index]
+
+
+def hbm(blocks):
+    return pltpu.with_memory_space_constraint(blocks, pltpu.HBM)
+
+
+def older_kernel(first, line, at, table, blocks, *rest):
+    *stores, out, room, sems = rest
+    ncol, slots = room.shape[:2]
+    copies = run([pltpu.make_async_copy(blocks.at[c, at], room.at[c], sems.at[c]) for c in range(ncol)])
+    total = jnp.zeros(out.shape, F32)
+    for c in range(ncol):
+        copies[c].wait()
+        for slot in range(slots):
+            total += dot(pick(stores, first, table[c, line * slots + slot], row), room[c, slot])
+    out[...] = total
+
+
+def older(first, line, at, table, blocks, stores):
+    ncol, _, slots, size, _ = blocks.shape
+    part = stores[0].shape[1]
+    return pl.pallas_call(
+        functools.partial(older_kernel, first, line, at),
+        out_shape=jax.ShapeDtypeStruct((part, size), F32),
+        in_specs=[SMEM, ANY] + [VMEM] * len(stores),
+        out_specs=VMEM,
+        scratch_shapes=[pltpu.VMEM((ncol, slots, size, size), BF), pltpu.SemaphoreType.DMA((ncol,))],
+        compiler_params=params(10),
+        cost_estimate=pl.CostEstimate(flops=2 * ncol * slots * part * size * size, bytes_accessed=13 << 20, transcendentals=0),
+        name="older",
+    )(table, hbm(blocks), *stores)
+
+
+def solve_kernel(newest, line, at, levels, olds, table, blocks, store, right, *rest):
     m = len(levels)
-    inverses, stores, rest = rest[:m], rest[m : m + n], rest[m + n :]
-    ncol, _, slots = blocks.shape[:3]
-    part = right.shape[0]
-    copies = []
-    if held:
-        *rest, room, sems = rest
-        copies = run([pltpu.make_async_copy(blocks.at[c, at], room.at[c], sems.at[c]) for c in range(ncol)])
-    total = jnp.zeros(right.shape, F32)
-    for c in range(ncol):
-        if held:
-            copies[c].wait()
-        for slot in range(slots):
-            picked = pick(stores, low, table[c, row * slots + slot], lambda store, index: store[index])
-            total += dot(picked, room[c, slot] if held else blocks[c, at, slot])
+    before, rest = rest[:olds], rest[olds:]
+    inverses, rest = rest[:m], rest[m:]
+    *rest, found, room, sems = rest
+    ncol, slots = blocks.shape[0], blocks.shape[2]
+
+    def fetch(code, j):
+        i = code // 32
+        return pltpu.make_async_copy(blocks.at[i // slots, at, i % slots], room.at[j], sems.at[j])
+
+    n = jnp.int32(0)
+    for i in range(ncol * slots):
+        place = table[i // slots, line * slots + i % slots]
+        found[n] = i * 32 + place % 32
+        n = n + jnp.where((place >= newest * 32) & (place < newest * 32 + 32), 1, 0)
+
+    @pl.loop(0, n)
+    def _(j):
+        fetch(found[j], j).start()
+
+    def one(j, total):
+        code = found[j]
+        fetch(code, j).wait()
+        return total + dot(store[code % 32], room[j])
+
+    total = before[0][...] if olds else jnp.zeros(right.shape, F32)
+    total = lax.fori_loop(0, n, one, total)
     solved = (right[...].astype(F32) - total).astype(BF)
     for i, level in enumerate(levels):
         solved = dot(solved, inverses[i][0, level]).astype(BF)
@@ -185,27 +233,30 @@
             spread[i] = solved
 
 
-def solve(low, row, at, levels, held, table, blocks, right, inverses, stores, done=()):
+def solve(newest, line, at, levels, table, blocks, store, right, before, inverses, done=()):
     part, size = right.shape
     ncol, slots = blocks.shape[0], blocks.shape[2]
-    n, m, width = len(stores), len(inverses), stores[0].shape[0]
+    width = store.shape[0]
     if done:
         out_shape = jax.ShapeDtypeStruct((ncol, len(done) + 1, part, size), BF)
         out_specs = VMEM
     else:
         out_shape = [jax.ShapeDtypeStruct((part, size), BF), jax.ShapeDtypeStruct((width, part, size), BF)]
         out_specs = [VMEM, VMEM]
-    scratch = [pltpu.VMEM((ncol, slots, size, size), BF), pltpu.SemaphoreType.DMA((ncol,))]
-    return pl.pallas_call(
-        functools.partial(solve_kernel, n, low, row, at, levels, held),
+    return pl.pallas_call(
+        functools.partial(solve_kernel, newest, line, at, levels, len(before)),
         out_shape=out_shape,
-        in_specs=[SMEM, ANY if held else VMEM] + [VMEM] * (1 + m + n + len(done)),
+        in_specs=[SMEM, ANY] + [VMEM] * (2 + len(before) + len(inverses) + len(done)),
         out_specs=out_specs,
-        scratch_shapes=scratch if held else [],
-        compiler_params=params(48 if held else 6),
-        cost_estimate=pl.CostEstimate(flops=2 * ncol * slots * part * size * size, bytes_accessed=7 << 20, transcendentals=0),
+        scratch_shapes=[
+            pltpu.SMEM((ncol * slots + 1,), I32),
+            pltpu.VMEM((ncol * slots, size, size), BF),
+            pltpu.SemaphoreType.DMA((ncol * slots,)),
+        ],
+        compiler_params=params(10),
+        cost_estimate=pl.CostEstimate(flops=2 * ncol * slots * part * size * size, bytes_accessed=4 << 20, transcendentals=0),
         name="solve",
-    )(table, blocks, right, *inverses, *stores, *done)
+    )(table, hbm(blocks), store, right, *before, *inverses, *done)
 
 
 def shards(
@@ -229,12 +280,14 @@
     right = lax.dynamic_slice_in_dim(right_side[0], column * part, part, 1)
 
     last = LAST_SPLIT
-    nlow = levels - 1 - last
-    cut = HEAD
-    first = select((lower_blocks, last, levels - 1), (upper_blocks, cut, levels - 1))
-    second = select((upper_blocks, 0, cut))
-    gathered = lax.all_gather(first, COL, axis=0)
-    gathered_low = lax.all_gather(second, COL, axis=0)
+    late_rows = [(lower_blocks, level - 1) for level in range(last + 1, levels)]
+    late_rows += [(upper_blocks, level) for level in range(levels - 2, -1, -1)]
+    gathered, begin = [], 0
+    for count in RUNS:
+        rows = select(*[(source, k, k + 1) for source, k in late_rows[begin : begin + count]])
+        whole = lax.all_gather(rows, COL, axis=0)
+        gathered += [(whole, i) for i in range(count)]
+        begin += count
 
     def places(sources, counts, by_column):
         s, n = sources[0], counts[0]
@@ -247,7 +300,10 @@
 
     own_table = places(lower_sources, lower_counts, False)
     late = jnp.concatenate(
-        [places(lower_sources, lower_counts, True)[last:], places(upper_sources, upper_counts, True)]
+        [
+            places(lower_sources, lower_counts, True)[last:],
+            places(upper_sources, upper_counts, True)[::-1],
+        ]
     ).reshape(-1)
     late = jnp.pad(late.astype(F32)[None], ((0, 7), (0, size - late.shape[0])))
 
@@ -267,29 +323,39 @@
         if rest:
             table = rest[0]
         own.append(solved)
-        if level == last:
-            copies, gathered = lax.optimization_barrier((copies, gathered))
-        stores.append(spread(copies))
         if level < last:
+            stores.append(spread(copies))
             halves.append(by_column(stores[-1]))
+
+    def step(line, olds, first, copies):
+        blocks, at = gathered[line]
+        copies, tied = lax.optimization_barrier((copies, table))
+        before = [older(first, line, at, tied, blocks, olds)] if olds else []
+        return spread(copies), before
+
+    line = 0
     for level in range(last + 1, levels):
+        newest, before = step(line, stores, 0, copies)
         ends = [lower_inverse], [level]
         if level == levels - 1:
             ends = [lower_inverse, upper_inverse], [level, level]
-        at = level - last - 1
-        solved, copies = solve(0, at, at, ends[1], True, table, gathered, right[level], ends[0], stores)
+        blocks, at = gathered[line]
+        solved, copies = solve(level - 1, line, at, ends[1], table, blocks, newest, right[level], before, ends[0])
         own.append(solved)
-        stores.append(spread(copies))
-    stores = stores[-1:]
-    result = [own[-1]]
+        stores.append(newest)
+        line += 1
+    result, stores = [solved], []
     for level in range(levels - 2, -1, -1):
-        blocks, at = (gathered, nlow + level - cut) if level >= cut else (gathered_low, level)
-        args = (level + 1, nlow + level, at, [level], True, table, blocks, own[level], [upper_inverse], stores)
+        newest, before = step(line, stores, level + 2, copies)
+        blocks, at = gathered[line]
+        done = result if level == 0 else ()
+        solved = solve(level + 1, line, at, [level], table, blocks, newest, own[level], before, [upper_inverse], done)
         if level > 0:
-            solved, copies = solve(*args)
+            solved, copies = solved
             result.insert(0, solved)
-            stores.insert(0, spread(copies))
-    whole = lax.all_to_all(solve(*args, result), COL, 0, 0, tiled=True)
+            stores.insert(0, newest)
+        line += 1
+    whole = lax.all_to_all(solved, COL, 0, 0, tiled=True)
     return jnp.transpose(whole, (1, 0, 2, 3)).reshape(1, levels, nrhs, size)
 
 

time: 334 us -> 321 us (0.961)
  blocking collectives: 203 us -> 123 us
  Pallas kernels: 45 us -> 78.9 us
  starting transfers between devices: 26.7 us -> 48.4 us
  waiting for transfers between devices: 41.5 us -> 49.6 us
    all_to_all x7 -> x3, blocking collectives: 100 us -> 43.7 us  [spread(): return lax.all_to_all(copies, TURNED, 0, 0, tiled=True)]
    pallas_call x6 -> x13, Pallas kernels: 33.3 us -> 66.3 us  [the longest x7 33.6 us: solve(): pl.pallas_call(functools.partial(solve_kernel, newest, line, at, levels,...]
    all_to_all x3 -> x7, starting transfers between devices: 19.9 us -> 41.6 us  [spread(): return lax.all_to_all(copies, TURNED, 0, 0, tiled=True)]
    all_to_all x4 -> x3, blocking collectives: 41.9 us -> 30.4 us  [shards(): parts = lax.all_to_all(partial, COL, 0, 0, tiled=True)]
    all_to_all x3 -> x2, blocking collectives: 41.9 us -> 30.5 us  [by_column(): lax.all_to_all(whole.reshape(ncol, group, part, size), COL, 0, 0, tiled=T...]
    all_to_all x3 -> x7, waiting for transfers between devices: 31.8 us -> 40 us  [spread(): return lax.all_to_all(copies, TURNED, 0, 0, tiled=True)]
    pallas_call x2 -> x3, Pallas kernels: 5.3 us -> 7.42 us  [select(): pl.pallas_call(body, out_shape=jax.ShapeDtypeStruct((count,) + shape, BF)...]
  transfers between devices with their start and end apart: 6 -> 11, of which waited for: 4 -> 8; matrix products, arithmetic and copies ran while one was open for 0% -> 1% of each run, Pallas kernels for 8% -> 23%
where the time goes in v5:
time: 321 us; the launch traced here: 318 us
  blocking collectives  123 us (38%)
  Pallas kernels  78.9 us (25%)
  waiting for transfers between devices  49.6 us (15%)
  starting transfers between devices  48.4 us (15%)
  between operations  13.4 us (4%)
  local copies, waits for them, and re-layouts  4.59 us (1%)
    all_to_all x3, blocking collectives, spread(): return lax.all_to_all(copies, TURNED, 0, 0, tiled=True)  43.7 us
    all_to_all x7, starting transfers between devices, spread(): return lax.all_to_all(copies, TURNED, 0, 0, tiled=True)  41.6 us
    all_to_all x7, waiting for transfers between devices, spread(): return lax.all_to_all(copies, TURNED, 0, 0, tiled=True)  40 us
    pallas_call x7, Pallas kernels, solve(): pl.pallas_call(functools.partial(solve_kernel, newest, line, at, levels,...  33.6 us
    pallas_call x6, Pallas kernels, older(): pl.pallas_call(functools.partial(older_kernel, first, line, at), out_shap...  32.8 us
    all_to_all x2, blocking collectives, by_column(): lax.all_to_all(whole.reshape(ncol, group, part, size), COL, 0, 0, tiled=T...  30.5 us
    all_to_all x3, blocking collectives, shards(): parts = lax.all_to_all(partial, COL, 0, 0, tiled=True)  30.4 us
    all_to_all x1, blocking collectives, shards(): whole = lax.all_to_all(solved, COL, 0, 0, tiled=True)  18.6 us
  transfers between devices with their start and end apart: 11, of which 8 were waited for; matrix products, arithmetic and copies ran while one was open for 1% of the time, Pallas kernels for 23%

profile of v5, /device:TPU:1, one launch (start us, length us, event | category | flops | bytes accessed | tf_op | source)
XLA Modules:
  0.0 318.4 jit_solution(6715974183743594141)
XLA Ops:
  15.9 12.2 %all-to-all-start = ((bf16[32,16,256]{2,1,0:T(8,128)(2,1)}), bf16[32,16,256]{2,1,0:T(8,128)(2,1)}, u32[]{:S(2)}, u32[]{:S(2)}) async-start(bf16[32,16,256]{2,1,0:T(8,128)(2,1)} %get-tuple-element.39), calls=%async_computation | async-start | bytes 524288 | tf_op jit(solution)/shard_map/all_to_all | solution.py:311
  28.2 11.1 %all-to-all-done.rest_0_ = bf16[32,16,256]{2,1,0:T(8,128)(2,1)} async-done(((bf16[32,16,256]{2,1,0:T(8,128)(2,1)}), bf16[32,16,256]{2,1,0:T(8,128)(2,1)}, u32[]{:S(2)}, u32[]{:S(2)}) %all-to-all-start) | async-done | bytes 262176 | tf_op jit(solution)/shard_map/all_to_all | solution.py:311
  39.3 6.7 %all-to-all-start.1 = ((bf16[8,4,16,256]{3,2,1,0:T(8,128)(2,1)}), bf16[8,4,16,256]{3,2,1,0:T(8,128)(2,1)S(1)}, u32[]{:S(2)}, u32[]{:S(2)}) async-start(bf16[8,4,16,256]{3,2,1,0:T(8,128)(2,1)} %bitcast.2), calls=%async_computation.1 | async-start | bytes 524288 | tf_op jit(solution)/shard_map/all_to_all | solution.py:314
  46.2 9.5 %all-to-all-done.1.rest_0_ = bf16[8,4,16,256]{3,2,1,0:T(8,128)(2,1)S(1)} async-done(((bf16[8,4,16,256]{3,2,1,0:T(8,128)(2,1)}), bf16[8,4,16,256]{3,2,1,0:T(8,128)(2,1)S(1)}, u32[]{:S(2)}, u32[]{:S(2)}) %all-to-all-start.1) | async-done | bytes 262176 | tf_op jit(solution)/shard_map/all_to_all | solution.py:314
  58.9 11.8 %all_to_all.85.parts = f32[8,24,256]{2,1,0:T(8,128)S(1)} all-to-all(f32[8,24,256]{2,1,0:T(8,128)S(1)} %update.3), channel_id=1, replica_groups=mesh['g'=4,'z'=8,'x'=4,'core'=2] {'x','core'}, dimensions={0} | all-to-all | bytes 393216 | tf_op jit(solution)/shard_map/all_to_all | solution.py:321
  70.9 14.4 %all_to_all.86.rest_1_ = bf16[32,16,256]{2,1,0:T(8,128)(2,1)S(1)} all-to-all(bf16[32,16,256]{2,1,0:T(8,128)(2,1)S(1)} %get-tuple-element.41), channel_id=1, replica_groups=mesh['g'=4,'z'=8,'x'=4,'core'=2] {'z','g'}, dimensions={0} | all-to-all | bytes 524288 | tf_op jit(solution)/shard_map/all_to_all | solution.py:311
  85.3 15.1 %all_to_all.87.rest_1_ = bf16[8,4,16,256]{3,2,1,0:T(8,128)(2,1)S(1)} all-to-all(bf16[8,4,16,256]{3,2,1,0:T(8,128)(2,1)S(1)} %bitcast.78), channel_id=1, replica_groups=mesh['g'=4,'z'=8,'x'=4,'core'=2] {'x','core'}, dimensions={0} | all-to-all | bytes 524288 | tf_op jit(solution)/shard_map/all_to_all | solution.py:314
  101.4 10.0 %all_to_all.88.parts = f32[8,16,256]{2,1,0:T(8,128)S(1)} all-to-all(f32[8,16,256]{2,1,0:T(8,128)S(1)} %update.4), channel_id=1, replica_groups=mesh['g'=4,'z'=8,'x'=4,'core'=2] {'x','core'}, dimensions={0} | all-to-all | bytes 262144 | tf_op jit(solution)/shard_map/all_to_all | solution.py:321
  111.6 14.1 %all_to_all.89.rest_2_ = bf16[32,16,256]{2,1,0:T(8,128)(2,1)S(1)} all-to-all(bf16[32,16,256]{2,1,0:T(8,128)(2,1)S(1)} %get-tuple-element.42), channel_id=1, replica_groups=mesh['g'=4,'z'=8,'x'=4,'core'=2] {'z','g'}, dimensions={0} | all-to-all | bytes 524288 | tf_op jit(solution)/shard_map/all_to_all | solution.py:311
  125.8 15.5 %all_to_all.90.rest_2_ = bf16[8,4,16,256]{3,2,1,0:T(8,128)(2,1)S(1)} all-to-all(bf16[8,4,16,256]{3,2,1,0:T(8,128)(2,1)S(1)} %bitcast.79), channel_id=1, replica_groups=mesh['g'=4,'z'=8,'x'=4,'core'=2] {'x','core'}, dimensions={0} | all-to-all | bytes 524288 | tf_op jit(solution)/shard_map/all_to_all | solution.py:314
  142.2 8.6 %all_to_all.91.parts = f32[8,16,256]{2,1,0:T(8,128)S(1)} all-to-all(f32[8,16,256]{2,1,0:T(8,128)S(1)} %update.5), channel_id=1, replica_groups=mesh['g'=4,'z'=8,'x'=4,'core'=2] {'x','core'}, dimensions={0} | all-to-all | bytes 262144 | tf_op jit(solution)/shard_map/all_to_all | solution.py:321
  151.7 5.0 %all-to-all-start.9 = ((bf16[32,16,256]{2,1,0:T(8,128)(2,1)}), bf16[32,16,256]{2,1,0:T(8,128)(2,1)S(1)}, u32[]{:S(2)}, u32[]{:S(2)}) async-start(bf16[32,16,256]{2,1,0:T(8,128)(2,1)} %get-tuple-element.44), calls=%async_computation.9 | async-start | bytes 524288 | tf_op jit(solution)/shard_map/all_to_all | solution.py:311
  157.4 5.6 %older.6.rest_0_ = f32[16,256]{1,0:T(8,128)S(1)} custom-call(s32[8,128]{1,0:T(8,128)S(1)} %get-tuple-element.67.table, bf16[8,4,6,256,256]{4,3,2,1,0:T(8,128)(2,1)} %bitcast.80, bf16[32,16,256]{2,1,0:T(8,128)(2,1)} %all-to-all-done.rest_0_, bf16[32,16,256]{2,1,0:T(8,128)(2,1)S(1)} %all_to_all.86.rest_1_, bf16[32,16,256]{2,1,0:T(8,128)(2,1)S(1)} %all_to_all.89.rest_2_), custom_call_target="tpu_custom_call" | custom-call | flops 100663296 | bytes 13631488 | tf_op jit(solution)/shard_map/older/pallas_call | solution.py:180
  167.2 5.0 %solve.7 = (bf16[16,256]{1,0:T(8,128)(2,1)S(1)}, bf16[32,16,256]{2,1,0:T(8,128)(2,1)}) custom-call(s32[8,128]{1,0:T(8,128)S(1)} %get-tuple-element.67.table, bf16[8,4,6,256,256]{4,3,2,1,0:T(8,128)(2,1)} %bitcast.81, bf16[32,16,256]{2,1,0:T(8,128)(2,1)S(1)} %all-to-all-done.9.store.rest_3_, bf16[16,256]{1,0:T(8,128)(2,1)S(1)} %get-tuple-element.74.right, ...), custom_call_target="tpu_custom_call" | custom-call | flops 100663296 | bytes 4194304 | tf_op jit(solution)/shard_map/solve/pallas_call | solution.py:246
  172.2 5.3 %all-to-all-start.10 = ((bf16[32,16,256]{2,1,0:T(8,128)(2,1)}), bf16[32,16,256]{2,1,0:T(8,128)(2,1)S(1)}, u32[]{:S(2)}, u32[]{:S(2)}) async-start(bf16[32,16,256]{2,1,0:T(8,128)(2,1)} %get-tuple-element.47), calls=%async_computation.10 | async-start | bytes 524288 | tf_op jit(solution)/shard_map/all_to_all | solution.py:311
  177.5 5.8 %older.7.rest_0_ = f32[16,256]{1,0:T(8,128)S(1)} custom-call(s32[8,128]{1,0:T(8,128)S(1)} %get-tuple-element.67.table, bf16[8,4,6,256,256]{4,3,2,1,0:T(8,128)(2,1)} %bitcast.82, bf16[32,16,256]{2,1,0:T(8,128)(2,1)} %all-to-all-done.rest_0_, bf16[32,16,256]{2,1,0:T(8,128)(2,1)S(1)} %all_to_all.86.rest_1_, bf16[32,16,256]{2,1,0:T(8,128)(2,1)S(1)} %all_to_all.89.rest_2_, ...), custom_call_target="tpu_custom_call" | custom-call | flops 100663296 | bytes 13631488 | tf_op jit(solution)/shard_map/older/pallas_call | solution.py:180
  183.4 4.5 %all-to-all-done.10.store = bf16[32,16,256]{2,1,0:T(8,128)(2,1)S(1)} async-done(((bf16[32,16,256]{2,1,0:T(8,128)(2,1)}), bf16[32,16,256]{2,1,0:T(8,128)(2,1)S(1)}, u32[]{:S(2)}, u32[]{:S(2)}) %all-to-all-start.10) | async-done | bytes 262176 | tf_op jit(solution)/shard_map/all_to_all | solution.py:311
  191.5 15.1 %all_to_all.92.store.rest_0_.rest_1_.rest_2_.rest_3_ = bf16[32,16,256]{2,1,0:T(8,128)(2,1)S(1)} all-to-all(bf16[32,16,256]{2,1,0:T(8,128)(2,1)S(1)} %get-tuple-element.50), channel_id=1, replica_groups=mesh['g'=4,'z'=8,'x'=4,'core'=2] {'z','g'}, dimensions={0} | all-to-all | bytes 524288 | tf_op jit(solution)/shard_map/all_to_all | solution.py:311
  206.7 7.5 %solve.9 = (bf16[16,256]{1,0:T(8,128)(2,1)S(1)}, bf16[32,16,256]{2,1,0:T(8,128)(2,1)}) custom-call(s32[8,128]{1,0:T(8,128)S(1)} %get-tuple-element.67.table, bf16[8,4,6,256,256]{4,3,2,1,0:T(8,128)(2,1)} %bitcast.84, bf16[32,16,256]{2,1,0:T(8,128)(2,1)S(1)} %all_to_all.92.store.rest_0_.rest_1_.rest_2_.rest_3_, bf16[16,256]{1,0:T(8,128)(2,1)S(1)} %get-tuple-element.51.right, ...), custom_call_target="tpu_custom_call" | custom-call | flops 100663296 | bytes 4194304 | tf_op jit(solution)/shard_map/solve/pallas_call | solution.py:246
  214.2 5.7 %all-to-all-start.12 = ((bf16[32,16,256]{2,1,0:T(8,128)(2,1)}), bf16[32,16,256]{2,1,0:T(8,128)(2,1)S(1)}, u32[]{:S(2)}, u32[]{:S(2)}) async-start(bf16[32,16,256]{2,1,0:T(8,128)(2,1)} %get-tuple-element.53), calls=%async_computation.12 | async-start | bytes 524288 | tf_op jit(solution)/shard_map/all_to_all | solution.py:311
  220.0 5.3 %older.8.rest_0_ = f32[16,256]{1,0:T(8,128)S(1)} custom-call(s32[8,128]{1,0:T(8,128)S(1)} %get-tuple-element.67.table, bf16[8,4,6,256,256]{4,3,2,1,0:T(8,128)(2,1)} %bitcast.85, bf16[32,16,256]{2,1,0:T(8,128)(2,1)S(1)} %all_to_all.92.store.rest_0_.rest_1_.rest_2_.rest_3_), custom_call_target="tpu_custom_call" | custom-call | flops 100663296 | bytes 13631488 | tf_op jit(solution)/shard_map/older/pallas_call | solution.py:180
  225.3 5.1 %all-to-all-done.12.store.rest_0_.rest_1_.rest_2_ = bf16[32,16,256]{2,1,0:T(8,128)(2,1)S(1)} async-done(((bf16[32,16,256]{2,1,0:T(8,128)(2,1)}), bf16[32,16,256]{2,1,0:T(8,128)(2,1)S(1)}, u32[]{:S(2)}, u32[]{:S(2)}) %all-to-all-start.12) | async-done | bytes 262176 | tf_op jit(solution)/shard_map/all_to_all | solution.py:311
  230.4 4.9 %solve.10 = (bf16[16,256]{1,0:T(8,128)(2,1)S(1)}, bf16[32,16,256]{2,1,0:T(8,128)(2,1)}) custom-call(s32[8,128]{1,0:T(8,128)S(1)} %get-tuple-element.67.table, bf16[8,4,6,256,256]{4,3,2,1,0:T(8,128)(2,1)} %bitcast.86, bf16[32,16,256]{2,1,0:T(8,128)(2,1)S(1)} %all-to-all-done.12.store.rest_0_.rest_1_.rest_2_, bf16[16,256]{1,0:T(8,128)(2,1)S(1)} %get-tuple-element.54.right, ...), custom_call_target="tpu_custom_call" | custom-call | flops 100663296 | bytes 4194304 | tf_op jit(solution)/shard_map/solve/pallas_call | solution.py:246
  235.4 5.0 %all-to-all-start.13 = ((bf16[32,16,256]{2,1,0:T(8,128)(2,1)}), bf16[32,16,256]{2,1,0:T(8,128)(2,1)S(1)}, u32[]{:S(2)}, u32[]{:S(2)}) async-start(bf16[32,16,256]{2,1,0:T(8,128)(2,1)} %get-tuple-element.57), calls=%async_computation.13 | async-start | bytes 524288 | tf_op jit(solution)/shard_map/all_to_all | solution.py:311
  240.5 5.3 %older.9.rest_0_ = f32[16,256]{1,0:T(8,128)S(1)} custom-call(s32[8,128]{1,0:T(8,128)S(1)} %get-tuple-element.67.table, bf16[8,2,6,256,256]{4,3,2,1,0:T(8,128)(2,1)} %bitcast.87, bf16[32,16,256]{2,1,0:T(8,128)(2,1)S(1)} %all-to-all-done.12.store.rest_0_.rest_1_.rest_2_, bf16[32,16,256]{2,1,0:T(8,128)(2,1)S(1)} %all_to_all.92.store.rest_0_.rest_1_.rest_2_.rest_3_), custom_call_target="tpu_custom_call" | custom-call | flops 100663296 | bytes 13631488 | tf_op jit(solution)/shard_map/older/pallas_call | solution.py:180
  245.8 4.9 %all-to-all-done.13.store.rest_0_.rest_1_ = bf16[32,16,256]{2,1,0:T(8,128)(2,1)S(1)} async-done(((bf16[32,16,256]{2,1,0:T(8,128)(2,1)}), bf16[32,16,256]{2,1,0:T(8,128)(2,1)S(1)}, u32[]{:S(2)}, u32[]{:S(2)}) %all-to-all-start.13) | async-done | bytes 262176 | tf_op jit(solution)/shard_map/all_to_all | solution.py:311
  250.7 4.8 %solve.11 = (bf16[16,256]{1,0:T(8,128)(2,1)S(1)}, bf16[32,16,256]{2,1,0:T(8,128)(2,1)}) custom-call(s32[8,128]{1,0:T(8,128)S(1)} %get-tuple-element.67.table, bf16[8,2,6,256,256]{4,3,2,1,0:T(8,128)(2,1)} %bitcast.88, bf16[32,16,256]{2,1,0:T(8,128)(2,1)S(1)} %all-to-all-done.13.store.rest_0_.rest_1_, bf16[16,256]{1,0:T(8,128)(2,1)S(1)} %get-tuple-element.58.right, ...), custom_call_target="tpu_custom_call" | custom-call | flops 100663296 | bytes 4194304 | tf_op jit(solution)/shard_map/solve/pallas_call | solution.py:246
  259.6 5.3 %older.10.rest_0_ = f32[16,256]{1,0:T(8,128)S(1)} custom-call(s32[8,128]{1,0:T(8,128)S(1)} %get-tuple-element.67.table, bf16[8,2,6,256,256]{4,3,2,1,0:T(8,128)(2,1)} %bitcast.89, bf16[32,16,256]{2,1,0:T(8,128)(2,1)S(1)} %all-to-all-done.13.store.rest_0_.rest_1_, bf16[32,16,256]{2,1,0:T(8,128)(2,1)S(1)} %all-to-all-done.12.store.rest_0_.rest_1_.rest_2_, ...), custom_call_target="tpu_custom_call" | custom-call | flops 100663296 | bytes 13631488 | tf_op jit(solution)/shard_map/older/pallas_call | solution.py:180
  265.0 5.1 %all-to-all-done.14.store.rest_0_ = bf16[32,16,256]{2,1,0:T(8,128)(2,1)S(1)} async-done(((bf16[32,16,256]{2,1,0:T(8,128)(2,1)}), bf16[32,16,256]{2,1,0:T(8,128)(2,1)S(1)}, u32[]{:S(2)}, u32[]{:S(2)}) %all-to-all-start.14) | async-done | bytes 262176 | tf_op jit(solution)/shard_map/all_to_all | solution.py:311
  278.8 5.3 %older.11.rest_0_ = f32[16,256]{1,0:T(8,128)S(1)} custom-call(s32[8,128]{1,0:T(8,128)S(1)} %get-tuple-element.67.table, bf16[8,1,6,256,256]{4,3,2,1,0:T(8,128)(2,1)} %bitcast.91, bf16[32,16,256]{2,1,0:T(8,128)(2,1)S(1)} %all-to-all-done.14.store.rest_0_, bf16[32,16,256]{2,1,0:T(8,128)(2,1)S(1)} %all-to-all-done.13.store.rest_0_.rest_1_, ...), custom_call_target="tpu_custom_call" | custom-call | flops 100663296 | bytes 13631488 | tf_op jit(solution)/shard_map/older/pallas_call | solution.py:180
  284.1 5.1 %all-to-all-done.15.store = bf16[32,16,256]{2,1,0:T(8,128)(2,1)S(1)} async-done(((bf16[32,16,256]{2,1,0:T(8,128)(2,1)}), bf16[32,16,256]{2,1,0:T(8,128)(2,1)S(1)}, u32[]{:S(2)}, u32[]{:S(2)}) %all-to-all-start.15) | async-done | bytes 262176 | tf_op jit(solution)/shard_map/all_to_all | solution.py:311
  292.5 18.6 %all_to_all.93 = bf16[8,6,16,256]{3,2,1,0:T(8,128)(2,1)S(1)} all-to-all(bf16[8,6,16,256]{3,2,1,0:T(8,128)(2,1)S(1)} %solve.13), channel_id=1, replica_groups=mesh['g'=4,'z'=8,'x'=4,'core'=2] {'x','core'}, dimensions={0} | all-to-all | bytes 786432 | tf_op jit(solution)/shard_map/all_to_all | solution.py:358
  (51 shorter events, 41.5 us)
Async XLA Ops:
  6.5 150.9 %all-gather.11.cloned.1.call-start = ((), (), s32[]{:S(2)}) async-start(), calls=%async_computation.19 | async-start | bytes 28311552 | tf_op jit(solution)/shard_map/all_gather | solution.py:288
  9.5 230.9 %all-gather.9.cloned.1.call-start = ((), (), s32[]{:S(2)}) async-start(), calls=%async_computation.18 | async-start | bytes 14155776 | tf_op jit(solution)/shard_map/all_gather | solution.py:288
  11.9 3.1 copy-start.3
  11.9 16.2 %copy-start.5 = (s32[1,5,6]{2,0,1:T(1,128)S(1)}, s32[1,5,6]{2,0,1:T(1,128)}, u32[]{:S(2)}) copy-start(s32[1,5,6]{2,0,1:T(1,128)} %param.13) | copy-start | bytes 364
  11.9 16.2 %copy-start.7 = (s32[1,5,1]{1,2,0:T(1,128)S(1)}, s32[1,5,1]{1,2,0:T(1,128)}, u32[]{:S(2)}) copy-start(s32[1,5,1]{1,2,0:T(1,128)} %param.14) | copy-start | bytes 64
  12.0 34.1 %copy-start.4 = (s32[1,5,6]{2,0,1:T(1,128)S(1)}, s32[1,5,6]{2,0,1:T(1,128)}, u32[]{:S(2)}) copy-start(s32[1,5,6]{2,0,1:T(1,128)} %param.16) | copy-start | bytes 364
  12.0 34.0 %copy-start.6 = (s32[1,5,1]{1,2,0:T(1,128)S(1)}, s32[1,5,1]{1,2,0:T(1,128)}, u32[]{:S(2)}) copy-start(s32[1,5,1]{1,2,0:T(1,128)} %param.17) | copy-start | bytes 64
  12.0 266.8 %all-gather.7.cloned.1.call-start = ((), (), s32[]{:S(2)}) async-start(), calls=%async_computation.17 | async-start | bytes 7077888 | tf_op jit(solution)/shard_map/all_gather | solution.py:288
  15.9 23.3 %all-to-all-start = ((bf16[32,16,256]{2,1,0:T(8,128)(2,1)}), bf16[32,16,256]{2,1,0:T(8,128)(2,1)}, u32[]{:S(2)}, u32[]{:S(2)}) async-start(bf16[32,16,256]{2,1,0:T(8,128)(2,1)} %get-tuple-element.39), calls=%async_computation | async-start | bytes 524288 | tf_op jit(solution)/shard_map/all_to_all | solution.py:311
  39.3 16.5 %all-to-all-start.1 = ((bf16[8,4,16,256]{3,2,1,0:T(8,128)(2,1)}), bf16[8,4,16,256]{3,2,1,0:T(8,128)(2,1)S(1)}, u32[]{:S(2)}, u32[]{:S(2)}) async-start(bf16[8,4,16,256]{3,2,1,0:T(8,128)(2,1)} %bitcast.2), calls=%async_computation.1 | async-start | bytes 524288 | tf_op jit(solution)/shard_map/all_to_all | solution.py:314
  55.8 2.1 copy-start
  57.9 42.5 %copy-start.1 = (bf16[1,5,6,256,256]{4,3,2,1,0:T(8,128)(2,1)S(1)}, bf16[1,5,6,256,256]{4,3,2,1,0:T(8,128)(2,1)}, u32[]{:S(2)}) copy-start(bf16[1,5,6,256,256]{4,3,2,1,0:T(8,128)(2,1)} %blocks.5) | copy-start | bytes 11796484
  151.7 15.5 %all-to-all-start.9 = ((bf16[32,16,256]{2,1,0:T(8,128)(2,1)}), bf16[32,16,256]{2,1,0:T(8,128)(2,1)S(1)}, u32[]{:S(2)}, u32[]{:S(2)}) async-start(bf16[32,16,256]{2,1,0:T(8,128)(2,1)} %get-tuple-element.44), calls=%async_computation.9 | async-start | bytes 524288 | tf_op jit(solution)/shard_map/all_to_all | solution.py:311
  172.2 15.7 %all-to-all-start.10 = ((bf16[32,16,256]{2,1,0:T(8,128)(2,1)}), bf16[32,16,256]{2,1,0:T(8,128)(2,1)S(1)}, u32[]{:S(2)}, u32[]{:S(2)}) async-start(bf16[32,16,256]{2,1,0:T(8,128)(2,1)} %get-tuple-element.47), calls=%async_computation.10 | async-start | bytes 524288 | tf_op jit(solution)/shard_map/all_to_all | solution.py:311
  177.5 10.4 %copy-start.2 = (bf16[1,6,256,256]{3,2,1,0:T(8,128)(2,1)S(1)}, bf16[1,6,256,256]{3,2,1,0:T(8,128)(2,1)}, u32[]{:S(2)}) copy-start(bf16[1,6,256,256]{3,2,1,0:T(8,128)(2,1)} %rest_1_.11) | copy-start | bytes 2359300
  214.2 16.2 %all-to-all-start.12 = ((bf16[32,16,256]{2,1,0:T(8,128)(2,1)}), bf16[32,16,256]{2,1,0:T(8,128)(2,1)S(1)}, u32[]{:S(2)}, u32[]{:S(2)}) async-start(bf16[32,16,256]{2,1,0:T(8,128)(2,1)} %get-tuple-element.53), calls=%async_computation.12 | async-start | bytes 524288 | tf_op jit(solution)/shard_map/all_to_all | solution.py:311
  235.4 15.3 %all-to-all-start.13 = ((bf16[32,16,256]{2,1,0:T(8,128)(2,1)}), bf16[32,16,256]{2,1,0:T(8,128)(2,1)S(1)}, u32[]{:S(2)}, u32[]{:S(2)}) async-start(bf16[32,16,256]{2,1,0:T(8,128)(2,1)} %get-tuple-element.57), calls=%async_computation.13 | async-start | bytes 524288 | tf_op jit(solution)/shard_map/all_to_all | solution.py:311
  255.4 14.7 %all-to-all-start.14 = ((bf16[32,16,256]{2,1,0:T(8,128)(2,1)}), bf16[32,16,256]{2,1,0:T(8,128)(2,1)S(1)}, u32[]{:S(2)}, u32[]{:S(2)}) async-start(bf16[32,16,256]{2,1,0:T(8,128)(2,1)} %get-tuple-element.61), calls=%async_computation.14 | async-start | bytes 524288 | tf_op jit(solution)/shard_map/all_to_all | solution.py:311
  274.5 14.7 %all-to-all-start.15 = ((bf16[32,16,256]{2,1,0:T(8,128)(2,1)}), bf16[32,16,256]{2,1,0:T(8,128)(2,1)S(1)}, u32[]{:S(2)}, u32[]{:S(2)}) async-start(bf16[32,16,256]{2,1,0:T(8,128)(2,1)} %get-tuple-element.65), calls=%async_computation.15 | async-start | bytes 524288 | tf_op jit(solution)/shard_map/all_to_all | solution.py:311
Sparse Core Ops, SparseCore 0:
  9.7 138.9 all-gather.10
  150.5 72.2 all-gather.8
  224.6 43.9 all-gather.6

commit v6 on v5

--- a/solution.py
+++ b/solution.py
@@ -21,6 +21,7 @@
 HBM = pl.BlockSpec(memory_space=pltpu.HBM)
 LAST_SPLIT = 3
 RUNS = (4, 2, 1)
+STEP = 4
 
 
 def dot(x, y):
@@ -195,28 +196,52 @@
     inverses, rest = rest[:m], rest[m:]
     *rest, found, room, sems = rest
     ncol, slots = blocks.shape[0], blocks.shape[2]
-
-    def fetch(code, j):
-        i = code // 32
-        return pltpu.make_async_copy(blocks.at[i // slots, at, i % slots], room.at[j], sems.at[j])
-
-    n = jnp.int32(0)
-    for i in range(ncol * slots):
-        place = table[i // slots, line * slots + i % slots]
-        found[n] = i * 32 + place % 32
-        n = n + jnp.where((place >= newest * 32) & (place < newest * 32 + 32), 1, 0)
-
-    @pl.loop(0, n)
-    def _(j):
-        fetch(found[j], j).start()
-
-    def one(j, total):
-        code = found[j]
-        fetch(code, j).wait()
-        return total + dot(store[code % 32], room[j])
-
-    total = before[0][...] if olds else jnp.zeros(right.shape, F32)
-    total = lax.fori_loop(0, n, one, total)
+    if olds:
+        n = jnp.int32(0)
+        for i in range(ncol * slots):
+            place = table[i // slots, line * slots + i % slots]
+            hit = (place >= newest * 32) & (place < newest * 32 + 32)
+
+            @pl.when(hit)
+            def _():
+                pltpu.make_async_copy(blocks.at[i // slots, at, i % slots], room.at[n], sems.at[n]).start()
+                found[n] = place - newest * 32
+
+            n = n + jnp.where(hit, 1, 0)
+
+        def some(k, total):
+            for u in range(STEP):
+                j = k * STEP + u
+
+                @pl.when(j < n)
+                def _():
+                    pltpu.make_async_copy(blocks.at[0, at, 0], room.at[j], sems.at[j]).wait()
+
+            terms = []
+            for u in range(STEP):
+                j = k * STEP + u
+                to = jnp.minimum(j, n - 1)
+                picked = store[found[to]]
+                picked = jnp.where(j < n, picked, jnp.zeros_like(picked))
+                terms.append(dot(picked, room[to]))
+            while len(terms) > 1:
+                terms = [x + y for x, y in zip(terms[::2], terms[1::2])]
+            return total + terms[0]
+
+        total = lax.fori_loop(0, (n + STEP - 1) // STEP, some, before[0][...])
+    else:
+        copies = run(
+            [
+                pltpu.make_async_copy(blocks.at[c, at], room.at[pl.ds(c * slots, slots)], sems.at[c])
+                for c in range(ncol)
+            ]
+        )
+        total = jnp.zeros(right.shape, F32)
+        for c in range(ncol):
+            copies[c].wait()
+            for slot in range(slots):
+                picked = pick([store], newest, table[c, line * slots + slot], row)
+                total += dot(picked, room[c * slots + slot])
     solved = (right[...].astype(F32) - total).astype(BF)
     for i, level in enumerate(levels):
         solved = dot(solved, inverses[i][0, level]).astype(BF)
@@ -282,12 +307,18 @@
     last = LAST_SPLIT
     late_rows = [(lower_blocks, level - 1) for level in range(last + 1, levels)]
     late_rows += [(upper_blocks, level) for level in range(levels - 2, -1, -1)]
-    gathered, begin = [], 0
-    for count in RUNS:
-        rows = select(*[(source, k, k + 1) for source, k in late_rows[begin : begin + count]])
-        whole = lax.all_gather(rows, COL, axis=0)
-        gathered += [(whole, i) for i in range(count)]
-        begin += count
+    gathered = []
+
+    def gather(count, tie=None):
+        rows = late_rows[len(gathered) : len(gathered) + count]
+        if tie is not None:
+            tie, high = lax.optimization_barrier((tie, upper_blocks))
+            rows = [(high, k) for _, k in rows]
+        whole = lax.all_gather(select(*[(source, k, k + 1) for source, k in rows]), COL, axis=0)
+        gathered.extend((whole, i) for i in range(count))
+        return tie
+
+    gather(RUNS[0])
 
     def places(sources, counts, by_column):
         s, n = sources[0], counts[0]
@@ -323,6 +354,9 @@
         if rest:
             table = rest[0]
         own.append(solved)
+        if level == 0:
+            for count in RUNS[1:]:
+                copies = gather(count, copies)
         if level < last:
             stores.append(spread(copies))
             halves.append(by_column(stores[-1]))

time: 321 us -> 310 us (0.966)
  Pallas kernels: 78.9 us -> 72.4 us
  starting transfers between devices: 48.4 us -> 45.1 us
    pallas_call x7, Pallas kernels: 33.6 us -> 27.2 us  [solve(): pl.pallas_call(functools.partial(solve_kernel, newest, line, at, levels,...]
    all_to_all x7, starting transfers between devices: 41.6 us -> 38.2 us  [spread(): return lax.all_to_all(copies, TURNED, 0, 0, tiled=True)]
  transfers between devices with their start and end apart: 11 -> 11, of which waited for: 8 -> 8; matrix products, arithmetic and copies ran while one was open for 1% -> 1% of each run, Pallas kernels for 23% -> 22%
where the time goes in v6:
time: 310 us
  blocking collectives  124 us (40%)
  Pallas kernels  72.4 us (23%)
  waiting for transfers between devices  50 us (16%)
  starting transfers between devices  45.1 us (15%)
  between operations  13.4 us (4%)
  local copies, waits for them, and re-layouts  4.59 us (1%)
    all_to_all x3, blocking collectives, spread(): return lax.all_to_all(copies, TURNED, 0, 0, tiled=True)  43.9 us
    all_to_all x7, waiting for transfers between devices, spread(): return lax.all_to_all(copies, TURNED, 0, 0, tiled=True)  40.4 us
    all_to_all x7, starting transfers between devices, spread(): return lax.all_to_all(copies, TURNED, 0, 0, tiled=True)  38.2 us
    pallas_call x6, Pallas kernels, older(): pl.pallas_call(functools.partial(older_kernel, first, line, at), out_shap...  32.5 us
    all_to_all x2, blocking collectives, by_column(): lax.all_to_all(whole.reshape(ncol, group, part, size), COL, 0, 0, tiled=T...  30.5 us
    all_to_all x3, blocking collectives, shards(): parts = lax.all_to_all(partial, COL, 0, 0, tiled=True)  30.4 us
    pallas_call x7, Pallas kernels, solve(): pl.pallas_call(functools.partial(solve_kernel, newest, line, at, levels,...  27.2 us
    all_to_all x1, blocking collectives, shards(): whole = lax.all_to_all(solved, COL, 0, 0, tiled=True)  19.1 us
  transfers between devices with their start and end apart: 11, of which 8 were waited for; matrix products, arithmetic and copies ran while one was open for 1% of the time, Pallas kernels for 22%

profile of v6, /device:TPU:1, one launch (start us, length us, event | category | flops | bytes accessed | tf_op | source)
XLA Modules:
  0.0 309.6 jit_solution(11008096869119695622)
XLA Ops:
  15.9 12.2 %all-to-all-start = ((bf16[32,16,256]{2,1,0:T(8,128)(2,1)}), bf16[32,16,256]{2,1,0:T(8,128)(2,1)}, u32[]{:S(2)}, u32[]{:S(2)}) async-start(bf16[32,16,256]{2,1,0:T(8,128)(2,1)} %get-tuple-element.45), calls=%async_computation | async-start | bytes 524288 | tf_op jit(solution)/shard_map/all_to_all | solution.py:342
  28.2 11.1 %all-to-all-done.rest_0_ = bf16[32,16,256]{2,1,0:T(8,128)(2,1)} async-done(((bf16[32,16,256]{2,1,0:T(8,128)(2,1)}), bf16[32,16,256]{2,1,0:T(8,128)(2,1)}, u32[]{:S(2)}, u32[]{:S(2)}) %all-to-all-start) | async-done | bytes 262176 | tf_op jit(solution)/shard_map/all_to_all | solution.py:342
  39.3 6.7 %all-to-all-start.1 = ((bf16[8,4,16,256]{3,2,1,0:T(8,128)(2,1)}), bf16[8,4,16,256]{3,2,1,0:T(8,128)(2,1)S(1)}, u32[]{:S(2)}, u32[]{:S(2)}) async-start(bf16[8,4,16,256]{3,2,1,0:T(8,128)(2,1)} %bitcast.2), calls=%async_computation.1 | async-start | bytes 524288 | tf_op jit(solution)/shard_map/all_to_all | solution.py:345
  46.2 9.5 %all-to-all-done.1.rest_0_ = bf16[8,4,16,256]{3,2,1,0:T(8,128)(2,1)S(1)} async-done(((bf16[8,4,16,256]{3,2,1,0:T(8,128)(2,1)}), bf16[8,4,16,256]{3,2,1,0:T(8,128)(2,1)S(1)}, u32[]{:S(2)}, u32[]{:S(2)}) %all-to-all-start.1) | async-done | bytes 262176 | tf_op jit(solution)/shard_map/all_to_all | solution.py:345
  58.9 11.8 %all_to_all.85.parts = f32[8,24,256]{2,1,0:T(8,128)S(1)} all-to-all(f32[8,24,256]{2,1,0:T(8,128)S(1)} %update.3), channel_id=1, replica_groups=mesh['g'=4,'z'=8,'x'=4,'core'=2] {'x','core'}, dimensions={0} | all-to-all | bytes 393216 | tf_op jit(solution)/shard_map/all_to_all | solution.py:352
  70.9 14.4 %all_to_all.86.rest_1_ = bf16[32,16,256]{2,1,0:T(8,128)(2,1)S(1)} all-to-all(bf16[32,16,256]{2,1,0:T(8,128)(2,1)S(1)} %get-tuple-element.49), channel_id=1, replica_groups=mesh['g'=4,'z'=8,'x'=4,'core'=2] {'z','g'}, dimensions={0} | all-to-all | bytes 524288 | tf_op jit(solution)/shard_map/all_to_all | solution.py:342
  85.3 15.1 %all_to_all.87.rest_1_ = bf16[8,4,16,256]{3,2,1,0:T(8,128)(2,1)S(1)} all-to-all(bf16[8,4,16,256]{3,2,1,0:T(8,128)(2,1)S(1)} %bitcast.78), channel_id=1, replica_groups=mesh['g'=4,'z'=8,'x'=4,'core'=2] {'x','core'}, dimensions={0} | all-to-all | bytes 524288 | tf_op jit(solution)/shard_map/all_to_all | solution.py:345
  101.4 10.0 %all_to_all.88.parts = f32[8,16,256]{2,1,0:T(8,128)S(1)} all-to-all(f32[8,16,256]{2,1,0:T(8,128)S(1)} %update.4), channel_id=1, replica_groups=mesh['g'=4,'z'=8,'x'=4,'core'=2] {'x','core'}, dimensions={0} | all-to-all | bytes 262144 | tf_op jit(solution)/shard_map/all_to_all | solution.py:352
  111.6 14.1 %all_to_all.89.rest_2_ = bf16[32,16,256]{2,1,0:T(8,128)(2,1)S(1)} all-to-all(bf16[32,16,256]{2,1,0:T(8,128)(2,1)S(1)} %get-tuple-element.50), channel_id=1, replica_groups=mesh['g'=4,'z'=8,'x'=4,'core'=2] {'z','g'}, dimensions={0} | all-to-all | bytes 524288 | tf_op jit(solution)/shard_map/all_to_all | solution.py:342
  125.7 15.5 %all_to_all.90.rest_2_ = bf16[8,4,16,256]{3,2,1,0:T(8,128)(2,1)S(1)} all-to-all(bf16[8,4,16,256]{3,2,1,0:T(8,128)(2,1)S(1)} %bitcast.79), channel_id=1, replica_groups=mesh['g'=4,'z'=8,'x'=4,'core'=2] {'x','core'}, dimensions={0} | all-to-all | bytes 524288 | tf_op jit(solution)/shard_map/all_to_all | solution.py:345
  142.2 8.6 %all_to_all.91.parts = f32[8,16,256]{2,1,0:T(8,128)S(1)} all-to-all(f32[8,16,256]{2,1,0:T(8,128)S(1)} %update.5), channel_id=1, replica_groups=mesh['g'=4,'z'=8,'x'=4,'core'=2] {'x','core'}, dimensions={0} | all-to-all | bytes 262144 | tf_op jit(solution)/shard_map/all_to_all | solution.py:352
  151.7 5.0 %all-to-all-start.9 = ((bf16[32,16,256]{2,1,0:T(8,128)(2,1)}), bf16[32,16,256]{2,1,0:T(8,128)(2,1)S(1)}, u32[]{:S(2)}, u32[]{:S(2)}) async-start(bf16[32,16,256]{2,1,0:T(8,128)(2,1)} %get-tuple-element.52), calls=%async_computation.9 | async-start | bytes 524288 | tf_op jit(solution)/shard_map/all_to_all | solution.py:342
  157.4 5.7 %older.6.rest_0_ = f32[16,256]{1,0:T(8,128)S(1)} custom-call(s32[8,128]{1,0:T(8,128)S(1)} %get-tuple-element.75.table, bf16[8,4,6,256,256]{4,3,2,1,0:T(8,128)(2,1)} %bitcast.80, bf16[32,16,256]{2,1,0:T(8,128)(2,1)} %all-to-all-done.rest_0_, bf16[32,16,256]{2,1,0:T(8,128)(2,1)S(1)} %all_to_all.86.rest_1_, bf16[32,16,256]{2,1,0:T(8,128)(2,1)S(1)} %all_to_all.89.rest_2_), custom_call_target="tpu_custom_call" | custom-call | flops 100663296 | bytes 13631488 | tf_op jit(solution)/shard_map/older/pallas_call | solution.py:181
  163.1 4.2 %all-to-all-done.9.store.rest_3_ = bf16[32,16,256]{2,1,0:T(8,128)(2,1)S(1)} async-done(((bf16[32,16,256]{2,1,0:T(8,128)(2,1)}), bf16[32,16,256]{2,1,0:T(8,128)(2,1)S(1)}, u32[]{:S(2)}, u32[]{:S(2)}) %all-to-all-start.9) | async-done | bytes 262176 | tf_op jit(solution)/shard_map/all_to_all | solution.py:342
  171.1 5.2 %all-to-all-start.10 = ((bf16[32,16,256]{2,1,0:T(8,128)(2,1)}), bf16[32,16,256]{2,1,0:T(8,128)(2,1)S(1)}, u32[]{:S(2)}, u32[]{:S(2)}) async-start(bf16[32,16,256]{2,1,0:T(8,128)(2,1)} %get-tuple-element.55), calls=%async_computation.10 | async-start | bytes 524288 | tf_op jit(solution)/shard_map/all_to_all | solution.py:342
  176.3 5.7 %older.7.rest_0_ = f32[16,256]{1,0:T(8,128)S(1)} custom-call(s32[8,128]{1,0:T(8,128)S(1)} %get-tuple-element.75.table, bf16[8,4,6,256,256]{4,3,2,1,0:T(8,128)(2,1)} %bitcast.82, bf16[32,16,256]{2,1,0:T(8,128)(2,1)} %all-to-all-done.rest_0_, bf16[32,16,256]{2,1,0:T(8,128)(2,1)S(1)} %all_to_all.86.rest_1_, bf16[32,16,256]{2,1,0:T(8,128)(2,1)S(1)} %all_to_all.89.rest_2_, ...), custom_call_target="tpu_custom_call" | custom-call | flops 100663296 | bytes 13631488 | tf_op jit(solution)/shard_map/older/pallas_call | solution.py:181
  182.1 4.7 %all-to-all-done.10.store = bf16[32,16,256]{2,1,0:T(8,128)(2,1)S(1)} async-done(((bf16[32,16,256]{2,1,0:T(8,128)(2,1)}), bf16[32,16,256]{2,1,0:T(8,128)(2,1)S(1)}, u32[]{:S(2)}, u32[]{:S(2)}) %all-to-all-start.10) | async-done | bytes 262176 | tf_op jit(solution)/shard_map/all_to_all | solution.py:342
  189.4 15.4 %all_to_all.92.store.rest_0_.rest_1_.rest_2_.rest_3_ = bf16[32,16,256]{2,1,0:T(8,128)(2,1)S(1)} all-to-all(bf16[32,16,256]{2,1,0:T(8,128)(2,1)S(1)} %get-tuple-element.58), channel_id=1, replica_groups=mesh['g'=4,'z'=8,'x'=4,'core'=2] {'z','g'}, dimensions={0} | all-to-all | bytes 524288 | tf_op jit(solution)/shard_map/all_to_all | solution.py:342
  204.8 6.4 %solve.9 = (bf16[16,256]{1,0:T(8,128)(2,1)S(1)}, bf16[32,16,256]{2,1,0:T(8,128)(2,1)}) custom-call(s32[8,128]{1,0:T(8,128)S(1)} %get-tuple-element.75.table, bf16[8,4,6,256,256]{4,3,2,1,0:T(8,128)(2,1)} %bitcast.84, bf16[32,16,256]{2,1,0:T(8,128)(2,1)S(1)} %all_to_all.92.store.rest_0_.rest_1_.rest_2_.rest_3_, bf16[16,256]{1,0:T(8,128)(2,1)S(1)} %get-tuple-element.59.right, ...), custom_call_target="tpu_custom_call" | custom-call | flops 100663296 | bytes 4194304 | tf_op jit(solution)/shard_map/solve/pallas_call | solution.py:271
  215.1 5.3 %older.8.rest_0_ = f32[16,256]{1,0:T(8,128)S(1)} custom-call(s32[8,128]{1,0:T(8,128)S(1)} %get-tuple-element.75.table, bf16[8,4,6,256,256]{4,3,2,1,0:T(8,128)(2,1)} %bitcast.85, bf16[32,16,256]{2,1,0:T(8,128)(2,1)S(1)} %all_to_all.92.store.rest_0_.rest_1_.rest_2_.rest_3_), custom_call_target="tpu_custom_call" | custom-call | flops 100663296 | bytes 13631488 | tf_op jit(solution)/shard_map/older/pallas_call | solution.py:181
  220.4 5.3 %all-to-all-done.12.store.rest_0_.rest_1_.rest_2_ = bf16[32,16,256]{2,1,0:T(8,128)(2,1)S(1)} async-done(((bf16[32,16,256]{2,1,0:T(8,128)(2,1)}), bf16[32,16,256]{2,1,0:T(8,128)(2,1)S(1)}, u32[]{:S(2)}, u32[]{:S(2)}) %all-to-all-start.12) | async-done | bytes 262176 | tf_op jit(solution)/shard_map/all_to_all | solution.py:342
  225.7 4.3 %solve.10 = (bf16[16,256]{1,0:T(8,128)(2,1)S(1)}, bf16[32,16,256]{2,1,0:T(8,128)(2,1)}) custom-call(s32[8,128]{1,0:T(8,128)S(1)} %get-tuple-element.75.table, bf16[8,4,6,256,256]{4,3,2,1,0:T(8,128)(2,1)} %bitcast.86, bf16[32,16,256]{2,1,0:T(8,128)(2,1)S(1)} %all-to-all-done.12.store.rest_0_.rest_1_.rest_2_, bf16[16,256]{1,0:T(8,128)(2,1)S(1)} %get-tuple-element.62.right, ...), custom_call_target="tpu_custom_call" | custom-call | flops 100663296 | bytes 4194304 | tf_op jit(solution)/shard_map/solve/pallas_call | solution.py:271
  230.0 4.0 %all-to-all-start.13 = ((bf16[32,16,256]{2,1,0:T(8,128)(2,1)}), bf16[32,16,256]{2,1,0:T(8,128)(2,1)S(1)}, u32[]{:S(2)}, u32[]{:S(2)}) async-start(bf16[32,16,256]{2,1,0:T(8,128)(2,1)} %get-tuple-element.65), calls=%async_computation.13 | async-start | bytes 524288 | tf_op jit(solution)/shard_map/all_to_all | solution.py:342
  234.1 5.3 %older.9.rest_0_ = f32[16,256]{1,0:T(8,128)S(1)} custom-call(s32[8,128]{1,0:T(8,128)S(1)} %get-tuple-element.75.table, bf16[8,2,6,256,256]{4,3,2,1,0:T(8,128)(2,1)} %bitcast.87, bf16[32,16,256]{2,1,0:T(8,128)(2,1)S(1)} %all-to-all-done.12.store.rest_0_.rest_1_.rest_2_, bf16[32,16,256]{2,1,0:T(8,128)(2,1)S(1)} %all_to_all.92.store.rest_0_.rest_1_.rest_2_.rest_3_), custom_call_target="tpu_custom_call" | custom-call | flops 100663296 | bytes 13631488 | tf_op jit(solution)/shard_map/older/pallas_call | solution.py:181
  239.4 5.1 %all-to-all-done.13.store.rest_0_.rest_1_ = bf16[32,16,256]{2,1,0:T(8,128)(2,1)S(1)} async-done(((bf16[32,16,256]{2,1,0:T(8,128)(2,1)}), bf16[32,16,256]{2,1,0:T(8,128)(2,1)S(1)}, u32[]{:S(2)}, u32[]{:S(2)}) %all-to-all-start.13) | async-done | bytes 262176 | tf_op jit(solution)/shard_map/all_to_all | solution.py:342
  248.3 3.9 %all-to-all-start.14 = ((bf16[32,16,256]{2,1,0:T(8,128)(2,1)}), bf16[32,16,256]{2,1,0:T(8,128)(2,1)S(1)}, u32[]{:S(2)}, u32[]{:S(2)}) async-start(bf16[32,16,256]{2,1,0:T(8,128)(2,1)} %get-tuple-element.69), calls=%async_computation.14 | async-start | bytes 524288 | tf_op jit(solution)/shard_map/all_to_all | solution.py:342
  252.2 5.3 %older.10.rest_0_ = f32[16,256]{1,0:T(8,128)S(1)} custom-call(s32[8,128]{1,0:T(8,128)S(1)} %get-tuple-element.75.table, bf16[8,2,6,256,256]{4,3,2,1,0:T(8,128)(2,1)} %bitcast.89, bf16[32,16,256]{2,1,0:T(8,128)(2,1)S(1)} %all-to-all-done.13.store.rest_0_.rest_1_, bf16[32,16,256]{2,1,0:T(8,128)(2,1)S(1)} %all-to-all-done.12.store.rest_0_.rest_1_.rest_2_, ...), custom_call_target="tpu_custom_call" | custom-call | flops 100663296 | bytes 13631488 | tf_op jit(solution)/shard_map/older/pallas_call | solution.py:181
  257.6 5.1 %all-to-all-done.14.store.rest_0_ = bf16[32,16,256]{2,1,0:T(8,128)(2,1)S(1)} async-done(((bf16[32,16,256]{2,1,0:T(8,128)(2,1)}), bf16[32,16,256]{2,1,0:T(8,128)(2,1)S(1)}, u32[]{:S(2)}, u32[]{:S(2)}) %all-to-all-start.14) | async-done | bytes 262176 | tf_op jit(solution)/shard_map/all_to_all | solution.py:342
  266.2 4.1 %all-to-all-start.15 = ((bf16[32,16,256]{2,1,0:T(8,128)(2,1)}), bf16[32,16,256]{2,1,0:T(8,128)(2,1)S(1)}, u32[]{:S(2)}, u32[]{:S(2)}) async-start(bf16[32,16,256]{2,1,0:T(8,128)(2,1)} %get-tuple-element.73), calls=%async_computation.15 | async-start | bytes 524288 | tf_op jit(solution)/shard_map/all_to_all | solution.py:342
  270.3 5.3 %older.11.rest_0_ = f32[16,256]{1,0:T(8,128)S(1)} custom-call(s32[8,128]{1,0:T(8,128)S(1)} %get-tuple-element.75.table, bf16[8,1,6,256,256]{4,3,2,1,0:T(8,128)(2,1)} %bitcast.91, bf16[32,16,256]{2,1,0:T(8,128)(2,1)S(1)} %all-to-all-done.14.store.rest_0_, bf16[32,16,256]{2,1,0:T(8,128)(2,1)S(1)} %all-to-all-done.13.store.rest_0_.rest_1_, ...), custom_call_target="tpu_custom_call" | custom-call | flops 100663296 | bytes 13631488 | tf_op jit(solution)/shard_map/older/pallas_call | solution.py:181
  275.6 5.1 %all-to-all-done.15.store = bf16[32,16,256]{2,1,0:T(8,128)(2,1)S(1)} async-done(((bf16[32,16,256]{2,1,0:T(8,128)(2,1)}), bf16[32,16,256]{2,1,0:T(8,128)(2,1)S(1)}, u32[]{:S(2)}, u32[]{:S(2)}) %all-to-all-start.15) | async-done | bytes 262176 | tf_op jit(solution)/shard_map/all_to_all | solution.py:342
  283.2 19.1 %all_to_all.93 = bf16[8,6,16,256]{3,2,1,0:T(8,128)(2,1)S(1)} all-to-all(bf16[8,6,16,256]{3,2,1,0:T(8,128)(2,1)S(1)} %solve.13), channel_id=1, replica_groups=mesh['g'=4,'z'=8,'x'=4,'core'=2] {'x','core'}, dimensions={0} | all-to-all | bytes 786432 | tf_op jit(solution)/shard_map/all_to_all | solution.py:392
  (51 shorter events, 37.9 us)
Async XLA Ops:
  6.5 3.9 %copy-start.3 = (bf16[1,6,256,256]{3,2,1,0:T(8,128)(2,1)S(1)}, bf16[1,6,256,256]{3,2,1,0:T(8,128)(2,1)}, u32[]{:S(2)}) copy-start(bf16[1,6,256,256]{3,2,1,0:T(8,128)(2,1)} %rest_1_.7) | copy-start | bytes 2359300
  6.5 150.9 %all-gather.11.cloned.1.call-start = ((), (), s32[]{:S(2)}) async-start(), calls=%async_computation.19 | async-start | bytes 28311552 | tf_op jit(solution)/shard_map/all_gather | solution.py:317
  9.6 224.5 %all-gather.9.cloned.1.call-start = ((), (), s32[]{:S(2)}) async-start(), calls=%async_computation.18 | async-start | bytes 14155776 | tf_op jit(solution)/shard_map/all_gather | solution.py:317
  13.7 14.4 %copy-start.5 = (s32[1,5,6]{2,0,1:T(1,128)S(1)}, s32[1,5,6]{2,0,1:T(1,128)}, u32[]{:S(2)}) copy-start(s32[1,5,6]{2,0,1:T(1,128)} %param.13) | copy-start | bytes 364
  13.7 14.4 %copy-start.7 = (s32[1,5,1]{1,2,0:T(1,128)S(1)}, s32[1,5,1]{1,2,0:T(1,128)}, u32[]{:S(2)}) copy-start(s32[1,5,1]{1,2,0:T(1,128)} %param.14) | copy-start | bytes 64
  13.7 32.3 %copy-start.4 = (s32[1,5,6]{2,0,1:T(1,128)S(1)}, s32[1,5,6]{2,0,1:T(1,128)}, u32[]{:S(2)}) copy-start(s32[1,5,6]{2,0,1:T(1,128)} %param.16) | copy-start | bytes 364
  13.7 32.3 %copy-start.6 = (s32[1,5,1]{1,2,0:T(1,128)S(1)}, s32[1,5,1]{1,2,0:T(1,128)}, u32[]{:S(2)}) copy-start(s32[1,5,1]{1,2,0:T(1,128)} %param.17) | copy-start | bytes 64
  13.8 256.5 %all-gather.7.cloned.1.call-start = ((), (), s32[]{:S(2)}) async-start(), calls=%async_computation.17 | async-start | bytes 7077888 | tf_op jit(solution)/shard_map/all_gather | solution.py:317
  15.9 23.3 %all-to-all-start = ((bf16[32,16,256]{2,1,0:T(8,128)(2,1)}), bf16[32,16,256]{2,1,0:T(8,128)(2,1)}, u32[]{:S(2)}, u32[]{:S(2)}) async-start(bf16[32,16,256]{2,1,0:T(8,128)(2,1)} %get-tuple-element.45), calls=%async_computation | async-start | bytes 524288 | tf_op jit(solution)/shard_map/all_to_all | solution.py:342
  39.3 16.5 %all-to-all-start.1 = ((bf16[8,4,16,256]{3,2,1,0:T(8,128)(2,1)}), bf16[8,4,16,256]{3,2,1,0:T(8,128)(2,1)S(1)}, u32[]{:S(2)}, u32[]{:S(2)}) async-start(bf16[8,4,16,256]{3,2,1,0:T(8,128)(2,1)} %bitcast.2), calls=%async_computation.1 | async-start | bytes 524288 | tf_op jit(solution)/shard_map/all_to_all | solution.py:345
  55.8 2.1 copy-start
  57.9 42.5 %copy-start.1 = (bf16[1,5,6,256,256]{4,3,2,1,0:T(8,128)(2,1)S(1)}, bf16[1,5,6,256,256]{4,3,2,1,0:T(8,128)(2,1)}, u32[]{:S(2)}) copy-start(bf16[1,5,6,256,256]{4,3,2,1,0:T(8,128)(2,1)} %blocks.5) | copy-start | bytes 11796484
  151.7 15.5 %all-to-all-start.9 = ((bf16[32,16,256]{2,1,0:T(8,128)(2,1)}), bf16[32,16,256]{2,1,0:T(8,128)(2,1)S(1)}, u32[]{:S(2)}, u32[]{:S(2)}) async-start(bf16[32,16,256]{2,1,0:T(8,128)(2,1)} %get-tuple-element.52), calls=%async_computation.9 | async-start | bytes 524288 | tf_op jit(solution)/shard_map/all_to_all | solution.py:342
  171.1 15.6 %all-to-all-start.10 = ((bf16[32,16,256]{2,1,0:T(8,128)(2,1)}), bf16[32,16,256]{2,1,0:T(8,128)(2,1)S(1)}, u32[]{:S(2)}, u32[]{:S(2)}) async-start(bf16[32,16,256]{2,1,0:T(8,128)(2,1)} %get-tuple-element.55), calls=%async_computation.10 | async-start | bytes 524288 | tf_op jit(solution)/shard_map/all_to_all | solution.py:342
  176.3 10.4 %copy-start.2 = (bf16[1,6,256,256]{3,2,1,0:T(8,128)(2,1)S(1)}, bf16[1,6,256,256]{3,2,1,0:T(8,128)(2,1)}, u32[]{:S(2)}) copy-start(bf16[1,6,256,256]{3,2,1,0:T(8,128)(2,1)} %rest_1_.11) | copy-start | bytes 2359300
  211.2 14.5 %all-to-all-start.12 = ((bf16[32,16,256]{2,1,0:T(8,128)(2,1)}), bf16[32,16,256]{2,1,0:T(8,128)(2,1)S(1)}, u32[]{:S(2)}, u32[]{:S(2)}) async-start(bf16[32,16,256]{2,1,0:T(8,128)(2,1)} %get-tuple-element.61), calls=%async_computation.12 | async-start | bytes 524288 | tf_op jit(solution)/shard_map/all_to_all | solution.py:342
  230.0 14.4 %all-to-all-start.13 = ((bf16[32,16,256]{2,1,0:T(8,128)(2,1)}), bf16[32,16,256]{2,1,0:T(8,128)(2,1)S(1)}, u32[]{:S(2)}, u32[]{:S(2)}) async-start(bf16[32,16,256]{2,1,0:T(8,128)(2,1)} %get-tuple-element.65), calls=%async_computation.13 | async-start | bytes 524288 | tf_op jit(solution)/shard_map/all_to_all | solution.py:342
  248.3 14.3 %all-to-all-start.14 = ((bf16[32,16,256]{2,1,0:T(8,128)(2,1)}), bf16[32,16,256]{2,1,0:T(8,128)(2,1)S(1)}, u32[]{:S(2)}, u32[]{:S(2)}) async-start(bf16[32,16,256]{2,1,0:T(8,128)(2,1)} %get-tuple-element.69), calls=%async_computation.14 | async-start | bytes 524288 | tf_op jit(solution)/shard_map/all_to_all | solution.py:342
  266.2 14.5 %all-to-all-start.15 = ((bf16[32,16,256]{2,1,0:T(8,128)(2,1)}), bf16[32,16,256]{2,1,0:T(8,128)(2,1)S(1)}, u32[]{:S(2)}, u32[]{:S(2)}) async-start(bf16[32,16,256]{2,1,0:T(8,128)(2,1)} %get-tuple-element.73), calls=%async_computation.15 | async-start | bytes 524288 | tf_op jit(solution)/shard_map/all_to_all | solution.py:342
Sparse Core Ops, SparseCore 0:
  9.7 138.9 all-gather.10
  150.6 72.2 all-gather.8
  224.7 43.8 all-gather.6

commit v7 on v5

--- a/solution.py
+++ b/solution.py
@@ -21,6 +21,8 @@
 HBM = pl.BlockSpec(memory_space=pltpu.HBM)
 LAST_SPLIT = 3
 RUNS = (4, 2, 1)
+STEP = 4
+READY = (6, 10)
 
 
 def dot(x, y):
@@ -37,42 +39,61 @@
     return pltpu.CompilerParams(vmem_limit_bytes=mib << 20)
 
 
-def select_kernel(parts, out, room, *sems):
-    loads, stores, n = [], [], 0
-    for source, low, high in parts:
-        for row in range(low, high):
-            loads.append(pltpu.make_async_copy(source.at[0, row], room.at[n], sems[0].at[n]))
-            stores.append(pltpu.make_async_copy(room.at[n], out.at[n], sems[1].at[n]))
-            n += 1
-    run(loads)
-    for load, store in zip(loads, stores):
-        load.wait()
-        store.start()
-    for store in stores:
-        store.wait()
-
-
-def select(*parts):
-    count = sum(high - low for _, low, high in parts)
-    shape = parts[0][0].shape[2:]
-
-    def body(*refs):
-        n = len(parts)
-        select_kernel([(ref, low, high) for ref, (_, low, high) in zip(refs, parts)], *refs[n:])
-
+def hbm(blocks):
+    return pltpu.with_memory_space_constraint(blocks, pltpu.HBM)
+
+
+def begin_kernel(lines, runs, column, low_blocks, high_blocks, right_side, inverse, *rest):
+    outs, rest = rest[: len(runs)], rest[len(runs) :]
+    right, out, spread, diag, room, loads, stores, sems = rest
+    part = right.shape[1]
+    start = pl.multiple_of(column[0] * part, part)
+    small = run(
+        [
+            pltpu.make_async_copy(right_side.at[0, :, pl.ds(start, part)], right, sems.at[0]),
+            pltpu.make_async_copy(inverse.at[0, 0], diag, sems.at[1]),
+        ]
+    )
+    sources = (low_blocks, high_blocks)
+    reads = run(
+        [pltpu.make_async_copy(sources[which].at[0, k], room.at[i], loads.at[i]) for i, (which, k) in enumerate(lines)]
+    )
+    places = [(j, i) for j, count in enumerate(runs) for i in range(count)]
+    writes = [pltpu.make_async_copy(room.at[n], outs[j].at[i], stores.at[n]) for n, (j, i) in enumerate(places)]
+    for copy in small:
+        copy.wait()
+    solved = dot(right[0], diag[...]).astype(BF)
+    out[...] = solved
+    for i in range(spread.shape[0]):
+        spread[i] = solved
+    for read, write in zip(reads, writes):
+        read.wait()
+        write.start()
+    for write in writes:
+        write.wait()
+
+
+def begin(lines, runs, column, low_blocks, high_blocks, right_side, inverse, ncol, width):
+    block = low_blocks.shape[2:]
+    levels, nrhs, size = right_side.shape[1:]
+    part = nrhs // ncol
+    n = len(lines)
     return pl.pallas_call(
-        body,
-        out_shape=jax.ShapeDtypeStruct((count,) + shape, BF),
-        in_specs=[ANY] * len(parts),
-        out_specs=ANY,
+        functools.partial(begin_kernel, lines, runs),
+        out_shape=[pltpu.HBM((count,) + block, BF) for count in runs]
+        + [jax.ShapeDtypeStruct(shape, BF) for shape in ((levels, part, size), (part, size), (width, part, size))],
+        in_specs=[SMEM] + [ANY] * 4,
+        out_specs=[ANY] * len(runs) + [VMEM] * 3,
         scratch_shapes=[
-            pltpu.VMEM((count,) + shape, BF),
-            pltpu.SemaphoreType.DMA((count,)),
-            pltpu.SemaphoreType.DMA((count,)),
+            pltpu.VMEM((size, size), BF),
+            pltpu.VMEM((n,) + block, BF),
+            pltpu.SemaphoreType.DMA((n,)),
+            pltpu.SemaphoreType.DMA((n,)),
+            pltpu.SemaphoreType.DMA((2,)),
         ],
-        compiler_params=params(62),
-        name="select",
-    )(*[source for source, _, _ in parts])
+        compiler_params=params(10),
+        name="begin",
+    )(column, hbm(low_blocks), hbm(high_blocks), hbm(right_side), hbm(inverse))
 
 
 def pick(stores, first, place, load):
@@ -158,14 +179,22 @@
     return store[index]
 
 
-def hbm(blocks):
-    return pltpu.with_memory_space_constraint(blocks, pltpu.HBM)
-
-
-def older_kernel(first, line, at, table, blocks, *rest):
-    *stores, out, room, sems = rest
+def older_kernel(first, line, at, newest, table, blocks, *rest):
+    *stores, out, found, ready, room, sems, ready_sems = rest
     ncol, slots = room.shape[:2]
+    cap = ready.shape[0]
     copies = run([pltpu.make_async_copy(blocks.at[c, at], room.at[c], sems.at[c]) for c in range(ncol)])
+    n = jnp.int32(0)
+    for i in range(ncol * slots):
+        place = table[i // slots, line * slots + i % slots]
+        hit = (place >= newest * 32) & (place < newest * 32 + 32)
+
+        @pl.when(hit)
+        def _():
+            found[n] = i * 32 + place - newest * 32
+
+        n = n + jnp.where(hit, 1, 0)
+    found[ncol * slots] = n
     total = jnp.zeros(out.shape, F32)
     for c in range(ncol):
         copies[c].wait()
@@ -173,56 +202,50 @@
             total += dot(pick(stores, first, table[c, line * slots + slot], row), room[c, slot])
     out[...] = total
 
-
-def older(first, line, at, table, blocks, stores):
+    def keep(j, _):
+        i = found[j] // 32
+        copy = pltpu.make_async_copy(room.at[i // slots, i % slots], ready.at[j], ready_sems.at[j])
+        copy.start()
+        return _
+
+    def kept(j, _):
+        pltpu.make_async_copy(room.at[0, 0], ready.at[j], ready_sems.at[j]).wait()
+        return _
+
+    lax.fori_loop(0, jnp.minimum(n, cap), keep, 0)
+    lax.fori_loop(0, jnp.minimum(n, cap), kept, 0)
+
+
+def older(ready, first, line, at, newest, table, blocks, stores):
     ncol, _, slots, size, _ = blocks.shape
     part = stores[0].shape[1]
     return pl.pallas_call(
-        functools.partial(older_kernel, first, line, at),
-        out_shape=jax.ShapeDtypeStruct((part, size), F32),
+        functools.partial(older_kernel, first, line, at, newest),
+        out_shape=[
+            pltpu.VMEM((part, size), F32),
+            jax.ShapeDtypeStruct((64,), I32),
+            pltpu.VMEM((ready, size, size), BF),
+        ],
         in_specs=[SMEM, ANY] + [VMEM] * len(stores),
-        out_specs=VMEM,
-        scratch_shapes=[pltpu.VMEM((ncol, slots, size, size), BF), pltpu.SemaphoreType.DMA((ncol,))],
+        out_specs=[VMEM, SMEM, VMEM],
+        scratch_shapes=[
+            pltpu.VMEM((ncol, slots, size, size), BF),
+            pltpu.SemaphoreType.DMA((ncol,)),
+            pltpu.SemaphoreType.DMA((ready,)),
+        ],
         compiler_params=params(10),
         cost_estimate=pl.CostEstimate(flops=2 * ncol * slots * part * size * size, bytes_accessed=13 << 20, transcendentals=0),
         name="older",
     )(table, hbm(blocks), *stores)
 
 
-def solve_kernel(newest, line, at, levels, olds, table, blocks, store, right, *rest):
-    m = len(levels)
-    before, rest = rest[:olds], rest[olds:]
-    inverses, rest = rest[:m], rest[m:]
-    *rest, found, room, sems = rest
-    ncol, slots = blocks.shape[0], blocks.shape[2]
-
-    def fetch(code, j):
-        i = code // 32
-        return pltpu.make_async_copy(blocks.at[i // slots, at, i % slots], room.at[j], sems.at[j])
-
-    n = jnp.int32(0)
-    for i in range(ncol * slots):
-        place = table[i // slots, line * slots + i % slots]
-        found[n] = i * 32 + place % 32
-        n = n + jnp.where((place >= newest * 32) & (place < newest * 32 + 32), 1, 0)
-
-    @pl.loop(0, n)
-    def _(j):
-        fetch(found[j], j).start()
-
-    def one(j, total):
-        code = found[j]
-        fetch(code, j).wait()
-        return total + dot(store[code % 32], room[j])
-
-    total = before[0][...] if olds else jnp.zeros(right.shape, F32)
-    total = lax.fori_loop(0, n, one, total)
-    solved = (right[...].astype(F32) - total).astype(BF)
+def finish_row(total, right, level, inverses, levels, rest):
+    solved = ((right[level] if len(right.shape) > 2 else right[...]).astype(F32) - total).astype(BF)
     for i, level in enumerate(levels):
         solved = dot(solved, inverses[i][0, level]).astype(BF)
     if len(rest) > 2:
         *done, out = rest
-        for i in range(ncol):
+        for i in range(out.shape[0]):
             out[i, 0] = solved
             for j, ref in enumerate(done):
                 out[i, j + 1] = ref[...]
@@ -233,8 +256,64 @@
             spread[i] = solved
 
 
+def dense_kernel(newest, line, at, levels, blocks, store, right, table, *rest):
+    m = len(levels)
+    inverses, (*rest, room, sems) = rest[:m], rest[m:]
+    ncol, slots = blocks.shape[0], blocks.shape[2]
+    copies = run([pltpu.make_async_copy(blocks.at[c, at], room.at[c], sems.at[c]) for c in range(ncol)])
+    total = jnp.zeros(store.shape[1:], F32)
+    for c in range(ncol):
+        copies[c].wait()
+        for slot in range(slots):
+            total += dot(pick([store], newest, table[c, line * slots + slot], row), room[c, slot])
+    finish_row(total, right, levels[0], inverses, levels, rest)
+
+
+def sparse_kernel(newest, line, at, levels, blocks, store, right, before, found, ready, *rest):
+    m = len(levels)
+    inverses, (*rest, room, sems) = rest[:m], rest[m:]
+    ncol, slots = blocks.shape[0], blocks.shape[2]
+    cap = ready.shape[0]
+    n = found[ncol * slots]
+
+    def fetch(j):
+        i = found[j] // 32
+        return pltpu.make_async_copy(blocks.at[i // slots, at, i % slots], room.at[j - cap], sems.at[j - cap])
+
+    @pl.loop(cap, jnp.maximum(n, cap))
+    def _(j):
+        fetch(j).start()
+
+    def some(low, high, load, k, total):
+        terms = []
+        for u in range(STEP):
+            j = low + k * STEP + u
+            to = jnp.minimum(j, high - 1)
+            picked = store[found[to] % 32]
+            picked = jnp.where(j < high, picked, jnp.zeros_like(picked))
+            terms.append(dot(picked, load(to)))
+        while len(terms) > 1:
+            terms = [x + y for x, y in zip(terms[::2], terms[1::2])]
+        return total + terms[0]
+
+    held = jnp.minimum(n, cap)
+    total = lax.fori_loop(
+        0, (held + STEP - 1) // STEP, lambda k, total: some(0, held, lambda j: ready[j], k, total), before[...]
+    )
+
+    @pl.loop(cap, jnp.maximum(n, cap))
+    def _(j):
+        fetch(j).wait()
+
+    more = jnp.maximum(n - cap, 0)
+    total = lax.fori_loop(
+        0, (more + STEP - 1) // STEP, lambda k, total: some(cap, n, lambda j: room[j - cap], k, total), total
+    )
+    finish_row(total, right, levels[0], inverses, levels, rest)
+
+
 def solve(newest, line, at, levels, table, blocks, store, right, before, inverses, done=()):
-    part, size = right.shape
+    part, size = right.shape[-2:]
     ncol, slots = blocks.shape[0], blocks.shape[2]
     width = store.shape[0]
     if done:
@@ -243,20 +322,24 @@
     else:
         out_shape = [jax.ShapeDtypeStruct((part, size), BF), jax.ShapeDtypeStruct((width, part, size), BF)]
         out_specs = [VMEM, VMEM]
+    if before:
+        body, own, own_specs = sparse_kernel, before, [VMEM, SMEM, VMEM]
+        copies = ncol * slots - before[2].shape[0]
+        room = (copies, size, size)
+    else:
+        body, own, own_specs = dense_kernel, [table], [SMEM]
+        room = (ncol, slots, size, size)
+        copies = ncol
     return pl.pallas_call(
-        functools.partial(solve_kernel, newest, line, at, levels, len(before)),
+        functools.partial(body, newest, line, at, levels),
         out_shape=out_shape,
-        in_specs=[SMEM, ANY] + [VMEM] * (2 + len(before) + len(inverses) + len(done)),
+        in_specs=[ANY, VMEM, VMEM] + own_specs + [VMEM] * (len(inverses) + len(done)),
         out_specs=out_specs,
-        scratch_shapes=[
-            pltpu.SMEM((ncol * slots + 1,), I32),
-            pltpu.VMEM((ncol * slots, size, size), BF),
-            pltpu.SemaphoreType.DMA((ncol * slots,)),
-        ],
+        scratch_shapes=[pltpu.VMEM(room, BF), pltpu.SemaphoreType.DMA((copies,))],
         compiler_params=params(10),
         cost_estimate=pl.CostEstimate(flops=2 * ncol * slots * part * size * size, bytes_accessed=4 << 20, transcendentals=0),
         name="solve",
-    )(table, hbm(blocks), store, right, *before, *inverses, *done)
+    )(hbm(blocks), store, right, *own, *inverses, *done)
 
 
 def shards(
@@ -277,17 +360,16 @@
     levels, nrhs, size = right_side.shape[1:]
     slots = lower_blocks.shape[2]
     part = nrhs // ncol
-    right = lax.dynamic_slice_in_dim(right_side[0], column * part, part, 1)
 
     last = LAST_SPLIT
-    late_rows = [(lower_blocks, level - 1) for level in range(last + 1, levels)]
-    late_rows += [(upper_blocks, level) for level in range(levels - 2, -1, -1)]
-    gathered, begin = [], 0
-    for count in RUNS:
-        rows = select(*[(source, k, k + 1) for source, k in late_rows[begin : begin + count]])
-        whole = lax.all_gather(rows, COL, axis=0)
-        gathered += [(whole, i) for i in range(count)]
-        begin += count
+    lines = [(0, level - 1) for level in range(last + 1, levels)] + [(1, level) for level in range(levels - 2, -1, -1)]
+    *rows, right, first, copies = begin(
+        lines, RUNS, jnp.full((1,), column, I32), lower_blocks, upper_blocks, right_side, lower_inverse, ncol, width
+    )
+    gathered = []
+    for count, part_rows in zip(RUNS, rows):
+        whole = lax.all_gather(part_rows, COL, axis=0)
+        gathered.extend((whole, i) for i in range(count))
 
     def places(sources, counts, by_column):
         s, n = sources[0], counts[0]
@@ -313,40 +395,38 @@
     def by_column(whole):
         return lax.all_to_all(whole.reshape(ncol, group, part, size), COL, 0, 0, tiled=True)
 
-    stores, halves, own = [], [], []
-    for level in range(last + 1):
-        parts = None
-        if level > 0:
-            partial = update(level - 1, own_table, lower_blocks, halves, late if level == 1 else None)
-            parts = lax.all_to_all(partial, COL, 0, 0, tiled=True)
+    stores, halves, own = [spread(copies)], [], [first]
+    for level in range(1, last + 1):
+        halves.append(by_column(stores[-1]))
+        partial = update(level - 1, own_table, lower_blocks, halves, late if level == 1 else None)
+        parts = lax.all_to_all(partial, COL, 0, 0, tiled=True)
         solved, copies, *rest = finish(level, parts, right, lower_inverse, width)
         if rest:
             table = rest[0]
         own.append(solved)
         if level < last:
             stores.append(spread(copies))
-            halves.append(by_column(stores[-1]))
-
-    def step(line, olds, first, copies):
+
+    def step(ready, line, olds, first, newest, copies):
         blocks, at = gathered[line]
         copies, tied = lax.optimization_barrier((copies, table))
-        before = [older(first, line, at, tied, blocks, olds)] if olds else []
+        before = older(READY[ready], first, line, at, newest, tied, blocks, olds) if olds else []
         return spread(copies), before
 
     line = 0
     for level in range(last + 1, levels):
-        newest, before = step(line, stores, 0, copies)
+        newest, before = step(0, line, stores, 0, level - 1, copies)
         ends = [lower_inverse], [level]
         if level == levels - 1:
             ends = [lower_inverse, upper_inverse], [level, level]
         blocks, at = gathered[line]
-        solved, copies = solve(level - 1, line, at, ends[1], table, blocks, newest, right[level], before, ends[0])
+        solved, copies = solve(level - 1, line, at, ends[1], table, blocks, newest, right, before, ends[0])
         own.append(solved)
         stores.append(newest)
         line += 1
     result, stores = [solved], []
     for level in range(levels - 2, -1, -1):
-        newest, before = step(line, stores, level + 2, copies)
+        newest, before = step(1, line, stores, level + 2, level + 1, copies)
         blocks, at = gathered[line]
         done = result if level == 0 else ()
         solved = solve(level + 1, line, at, [level], table, blocks, newest, own[level], before, [upper_inverse], done)

time: 321 us -> 312 us (0.972)
  waiting for transfers between devices: 49.6 us -> 39.2 us
  starting transfers between devices: 48.4 us -> 53 us
    all_to_all x7, waiting for transfers between devices: 40 us -> 28.2 us  [spread(): return lax.all_to_all(copies, TURNED, 0, 0, tiled=True)]
    all_to_all x7, starting transfers between devices: 41.6 us -> 46.2 us  [spread(): return lax.all_to_all(copies, TURNED, 0, 0, tiled=True)]
    pallas_call x16 -> x14, Pallas kernels: 73.7 us -> 72.4 us  [the longest x6 45.4 us: older(): pl.pallas_call(functools.partial(older_kernel, first, line, at, newest),...]
  transfers between devices with their start and end apart: 11 -> 11, of which waited for: 8 -> 8; matrix products, arithmetic and copies ran while one was open for 1% -> 0% of each run, Pallas kernels for 23% -> 22%
where the time goes in v7:
time: 312 us; the launch traced here: 310 us
  blocking collectives  124 us (40%)
  Pallas kernels  76.7 us (25%)
  starting transfers between devices  53 us (17%)
  waiting for transfers between devices  39.2 us (13%)
  between operations  13.4 us (4%)
    all_to_all x7, starting transfers between devices, spread(): return lax.all_to_all(copies, TURNED, 0, 0, tiled=True)  46.2 us
    pallas_call x6, Pallas kernels, older(): pl.pallas_call(functools.partial(older_kernel, first, line, at, newest),...  45.4 us
    all_to_all x3, blocking collectives, spread(): return lax.all_to_all(copies, TURNED, 0, 0, tiled=True)  45.2 us
    all_to_all x3, blocking collectives, shards(): parts = lax.all_to_all(partial, COL, 0, 0, tiled=True)  31.4 us
    all_to_all x2, blocking collectives, by_column(): lax.all_to_all(whole.reshape(ncol, group, part, size), COL, 0, 0, tiled=T...  30.5 us
    all_to_all x7, waiting for transfers between devices, spread(): return lax.all_to_all(copies, TURNED, 0, 0, tiled=True)  28.2 us
    pallas_call x7, Pallas kernels, solve(): pl.pallas_call(functools.partial(body, newest, line, at, levels), out_sha...  21.3 us
    all_to_all x1, blocking collectives, shards(): whole = lax.all_to_all(solved, COL, 0, 0, tiled=True)  17.2 us
  transfers between devices with their start and end apart: 11, of which 8 were waited for; matrix products, arithmetic and copies ran while one was open for 0% of the time, Pallas kernels for 22%

profile of v7, /device:TPU:1, one launch (start us, length us, event | category | flops | bytes accessed | tf_op | source)
XLA Modules:
  0.0 310.0 jit_solution(11705816846634263158)
XLA Ops:
  6.5 5.7 %begin.1 = (bf16[4,6,256,256]{3,2,1,0:T(8,128)(2,1)}, bf16[2,6,256,256]{3,2,1,0:T(8,128)(2,1)}, bf16[1,6,256,256]{3,2,1,0:T(8,128)(2,1)}, bf16[6,16,256]{2,1,0:T...) custom-call(s32[1]{0:T(128)} %bitcast.column, bf16[1,5,6,256,256]{4,3,2,1,0:T(8,128)(2,1)} %blocks.5, ...), custom_call_target="tpu_custom_call" | custom-call | tf_op jit(solution)/shard_map/begin/pallas_call | solution.py:81
  13.8 12.3 %all-to-all-start = ((bf16[32,16,256]{2,1,0:T(8,128)(2,1)}), bf16[32,16,256]{2,1,0:T(8,128)(2,1)}, u32[]{:S(2)}, u32[]{:S(2)}) async-start(bf16[32,16,256]{2,1,0:T(8,128)(2,1)} %get-tuple-element.64), calls=%async_computation | async-start | bytes 524288 | tf_op jit(solution)/shard_map/all_to_all | solution.py:393
  26.3 11.1 %all-to-all-done.rest_0_ = bf16[32,16,256]{2,1,0:T(8,128)(2,1)} async-done(((bf16[32,16,256]{2,1,0:T(8,128)(2,1)}), bf16[32,16,256]{2,1,0:T(8,128)(2,1)}, u32[]{:S(2)}, u32[]{:S(2)}) %all-to-all-start) | async-done | bytes 262176 | tf_op jit(solution)/shard_map/all_to_all | solution.py:393
  37.3 6.7 %all-to-all-start.1 = ((bf16[8,4,16,256]{3,2,1,0:T(8,128)(2,1)}), bf16[8,4,16,256]{3,2,1,0:T(8,128)(2,1)S(1)}, u32[]{:S(2)}, u32[]{:S(2)}) async-start(bf16[8,4,16,256]{3,2,1,0:T(8,128)(2,1)} %bitcast.5), calls=%async_computation.1 | async-start | bytes 524288 | tf_op jit(solution)/shard_map/all_to_all | solution.py:396
  44.3 9.5 %all-to-all-done.1.rest_0_ = bf16[8,4,16,256]{3,2,1,0:T(8,128)(2,1)S(1)} async-done(((bf16[8,4,16,256]{3,2,1,0:T(8,128)(2,1)}), bf16[8,4,16,256]{3,2,1,0:T(8,128)(2,1)S(1)}, u32[]{:S(2)}, u32[]{:S(2)}) %all-to-all-start.1) | async-done | bytes 262176 | tf_op jit(solution)/shard_map/all_to_all | solution.py:396
  56.9 11.8 %all_to_all.85.parts = f32[8,24,256]{2,1,0:T(8,128)S(1)} all-to-all(f32[8,24,256]{2,1,0:T(8,128)S(1)} %update.3), channel_id=1, replica_groups=mesh['g'=4,'z'=8,'x'=4,'core'=2] {'x','core'}, dimensions={0} | all-to-all | bytes 393216 | tf_op jit(solution)/shard_map/all_to_all | solution.py:402
  68.9 14.4 %all_to_all.86.rest_1_ = bf16[32,16,256]{2,1,0:T(8,128)(2,1)S(1)} all-to-all(bf16[32,16,256]{2,1,0:T(8,128)(2,1)S(1)} %get-tuple-element.66), channel_id=1, replica_groups=mesh['g'=4,'z'=8,'x'=4,'core'=2] {'z','g'}, dimensions={0} | all-to-all | bytes 524288 | tf_op jit(solution)/shard_map/all_to_all | solution.py:393
  83.3 15.1 %all_to_all.87.rest_1_ = bf16[8,4,16,256]{3,2,1,0:T(8,128)(2,1)S(1)} all-to-all(bf16[8,4,16,256]{3,2,1,0:T(8,128)(2,1)S(1)} %bitcast.73), channel_id=1, replica_groups=mesh['g'=4,'z'=8,'x'=4,'core'=2] {'x','core'}, dimensions={0} | all-to-all | bytes 524288 | tf_op jit(solution)/shard_map/all_to_all | solution.py:396
  99.4 10.0 %all_to_all.88.parts = f32[8,16,256]{2,1,0:T(8,128)S(1)} all-to-all(f32[8,16,256]{2,1,0:T(8,128)S(1)} %update.4), channel_id=1, replica_groups=mesh['g'=4,'z'=8,'x'=4,'core'=2] {'x','core'}, dimensions={0} | all-to-all | bytes 262144 | tf_op jit(solution)/shard_map/all_to_all | solution.py:402
  109.6 14.2 %all_to_all.89.rest_2_ = bf16[32,16,256]{2,1,0:T(8,128)(2,1)S(1)} all-to-all(bf16[32,16,256]{2,1,0:T(8,128)(2,1)S(1)} %get-tuple-element.67), channel_id=1, replica_groups=mesh['g'=4,'z'=8,'x'=4,'core'=2] {'z','g'}, dimensions={0} | all-to-all | bytes 524288 | tf_op jit(solution)/shard_map/all_to_all | solution.py:393
  123.8 15.5 %all_to_all.90.rest_2_ = bf16[8,4,16,256]{3,2,1,0:T(8,128)(2,1)S(1)} all-to-all(bf16[8,4,16,256]{3,2,1,0:T(8,128)(2,1)S(1)} %bitcast.74), channel_id=1, replica_groups=mesh['g'=4,'z'=8,'x'=4,'core'=2] {'x','core'}, dimensions={0} | all-to-all | bytes 524288 | tf_op jit(solution)/shard_map/all_to_all | solution.py:396
  140.2 9.6 %all_to_all.91.parts = f32[8,16,256]{2,1,0:T(8,128)S(1)} all-to-all(f32[8,16,256]{2,1,0:T(8,128)S(1)} %update.5), channel_id=1, replica_groups=mesh['g'=4,'z'=8,'x'=4,'core'=2] {'x','core'}, dimensions={0} | all-to-all | bytes 262144 | tf_op jit(solution)/shard_map/all_to_all | solution.py:402
  150.8 3.9 %all-to-all-start.9 = ((bf16[32,16,256]{2,1,0:T(8,128)(2,1)}), bf16[32,16,256]{2,1,0:T(8,128)(2,1)S(1)}, u32[]{:S(2)}, u32[]{:S(2)}) async-start(bf16[32,16,256]{2,1,0:T(8,128)(2,1)} %get-tuple-element.70), calls=%async_computation.9 | async-start | bytes 524288 | tf_op jit(solution)/shard_map/all_to_all | solution.py:393
  154.7 6.6 %older.6 = (f32[16,256]{1,0:T(8,128)S(1)}, s32[64]{0:T(128)S(1)}, bf16[6,256,256]{2,1,0:T(8,128)(2,1)S(1)}) custom-call(s32[8,128]{1,0:T(8,128)S(1)} %get-tuple-element.108.table, bf16[8,4,6,256,256]{4,3,2,1,0:T(8,128)(2,1)} %bitcast.75, bf16[32,16,256]{2,1,0:T(8,128)(2,1)} %all-to-all-done.rest_0_, bf16[32,16,256]{2,1,0:T(8,128)(2,1)S(1)} %all_to_all.86.rest_1_, ...), custom_call_target="tpu_custom_call" | custom-call | flops 100663296 | bytes 13631488 | tf_op jit(solution)/shard_map/older/pallas_call | solution.py:222
  161.4 3.9 %all-to-all-done.9.store.rest_3_ = bf16[32,16,256]{2,1,0:T(8,128)(2,1)S(1)} async-done(((bf16[32,16,256]{2,1,0:T(8,128)(2,1)}), bf16[32,16,256]{2,1,0:T(8,128)(2,1)S(1)}, u32[]{:S(2)}, u32[]{:S(2)}) %all-to-all-start.9) | async-done | bytes 262176 | tf_op jit(solution)/shard_map/all_to_all | solution.py:393
  167.3 7.6 %all-to-all-start.10 = ((bf16[32,16,256]{2,1,0:T(8,128)(2,1)}), bf16[32,16,256]{2,1,0:T(8,128)(2,1)S(1)}, u32[]{:S(2)}, u32[]{:S(2)}) async-start(bf16[32,16,256]{2,1,0:T(8,128)(2,1)} %get-tuple-element.76), calls=%async_computation.10 | async-start | bytes 524288 | tf_op jit(solution)/shard_map/all_to_all | solution.py:393
  175.0 7.5 %older.7 = (f32[16,256]{1,0:T(8,128)S(1)}, s32[64]{0:T(128)S(1)}, bf16[6,256,256]{2,1,0:T(8,128)(2,1)S(1)}) custom-call(s32[8,128]{1,0:T(8,128)S(1)} %get-tuple-element.108.table, bf16[8,4,6,256,256]{4,3,2,1,0:T(8,128)(2,1)} %bitcast.77, bf16[32,16,256]{2,1,0:T(8,128)(2,1)} %all-to-all-done.rest_0_, bf16[32,16,256]{2,1,0:T(8,128)(2,1)S(1)} %all_to_all.86.rest_1_, ...), custom_call_target="tpu_custom_call" | custom-call | flops 100663296 | bytes 13631488 | tf_op jit(solution)/shard_map/older/pallas_call | solution.py:222
  182.5 2.9 all-to-all-done.10.store
  187.8 16.7 %all_to_all.92.store.rest_0_.rest_1_.rest_2_.rest_3_ = bf16[32,16,256]{2,1,0:T(8,128)(2,1)S(1)} all-to-all(bf16[32,16,256]{2,1,0:T(8,128)(2,1)S(1)} %get-tuple-element.82), channel_id=1, replica_groups=mesh['g'=4,'z'=8,'x'=4,'core'=2] {'z','g'}, dimensions={0} | all-to-all | bytes 524288 | tf_op jit(solution)/shard_map/all_to_all | solution.py:393
  204.5 6.1 %solve.9 = (bf16[16,256]{1,0:T(8,128)(2,1)S(1)}, bf16[32,16,256]{2,1,0:T(8,128)(2,1)}) custom-call(bf16[8,4,6,256,256]{4,3,2,1,0:T(8,128)(2,1)} %bitcast.79, bf16[32,16,256]{2,1,0:T(8,128)(2,1)S(1)} %all_to_all.92.store.rest_0_.rest_1_.rest_2_.rest_3_, bf16[16,256]{1,0:T(8,128)(2,1)S(1)} %get-tuple-element.83.right, s32[8,128]{1,0:T(8,128)S(1)} %get-tuple-element.108.table, ...), custom_call_target="tpu_custom_call" | custom-call | flops 100663296 | bytes 4194304 | tf_op jit(solution)/shard_map/solve/pallas_call | solution.py:333
  210.5 3.9 %all-to-all-start.12 = ((bf16[32,16,256]{2,1,0:T(8,128)(2,1)}), bf16[32,16,256]{2,1,0:T(8,128)(2,1)S(1)}, u32[]{:S(2)}, u32[]{:S(2)}) async-start(bf16[32,16,256]{2,1,0:T(8,128)(2,1)} %get-tuple-element.85), calls=%async_computation.12 | async-start | bytes 524288 | tf_op jit(solution)/shard_map/all_to_all | solution.py:393
  214.4 8.0 %older.8 = (f32[16,256]{1,0:T(8,128)S(1)}, s32[64]{0:T(128)S(1)}, bf16[10,256,256]{2,1,0:T(8,128)(2,1)S(1)}) custom-call(s32[8,128]{1,0:T(8,128)S(1)} %get-tuple-element.108.table, bf16[8,4,6,256,256]{4,3,2,1,0:T(8,128)(2,1)} %bitcast.80, bf16[32,16,256]{2,1,0:T(8,128)(2,1)S(1)} %all_to_all.92.store.rest_0_.rest_1_.rest_2_.rest_3_), custom_call_target="tpu_custom_call" | custom-call | flops 100663296 | bytes 13631488 | tf_op jit(solution)/shard_map/older/pallas_call | solution.py:222
  225.0 3.5 %solve.10 = (bf16[16,256]{1,0:T(8,128)(2,1)S(1)}, bf16[32,16,256]{2,1,0:T(8,128)(2,1)}) custom-call(bf16[8,4,6,256,256]{4,3,2,1,0:T(8,128)(2,1)} %bitcast.81, bf16[32,16,256]{2,1,0:T(8,128)(2,1)S(1)} %all-to-all-done.12.store.rest_0_.rest_1_.rest_2_, bf16[16,256]{1,0:T(8,128)(2,1)S(1)} %get-tuple-element.86.right, f32[16,256]{1,0:T(8,128)S(1)} %get-tuple-element.88.before, ...), custom_call_target="tpu_custom_call" | custom-call | flops 100663296 | bytes 4194304 | tf_op jit(solution)/shard_map/solve/pallas_call | solution.py:333
  228.5 5.7 %all-to-all-start.13 = ((bf16[32,16,256]{2,1,0:T(8,128)(2,1)}), bf16[32,16,256]{2,1,0:T(8,128)(2,1)S(1)}, u32[]{:S(2)}, u32[]{:S(2)}) async-start(bf16[32,16,256]{2,1,0:T(8,128)(2,1)} %get-tuple-element.92), calls=%async_computation.13 | async-start | bytes 524288 | tf_op jit(solution)/shard_map/all_to_all | solution.py:393
  234.3 7.9 %older.9 = (f32[16,256]{1,0:T(8,128)S(1)}, s32[64]{0:T(128)S(1)}, bf16[10,256,256]{2,1,0:T(8,128)(2,1)S(1)}) custom-call(s32[8,128]{1,0:T(8,128)S(1)} %get-tuple-element.108.table, bf16[8,2,6,256,256]{4,3,2,1,0:T(8,128)(2,1)} %bitcast.82, bf16[32,16,256]{2,1,0:T(8,128)(2,1)S(1)} %all-to-all-done.12.store.rest_0_.rest_1_.rest_2_, ...), custom_call_target="tpu_custom_call" | custom-call | flops 100663296 | bytes 13631488 | tf_op jit(solution)/shard_map/older/pallas_call | solution.py:222
  244.7 3.0 solve.11
  247.7 6.8 %all-to-all-start.14 = ((bf16[32,16,256]{2,1,0:T(8,128)(2,1)}), bf16[32,16,256]{2,1,0:T(8,128)(2,1)S(1)}, u32[]{:S(2)}, u32[]{:S(2)}) async-start(bf16[32,16,256]{2,1,0:T(8,128)(2,1)} %get-tuple-element.99), calls=%async_computation.14 | async-start | bytes 524288 | tf_op jit(solution)/shard_map/all_to_all | solution.py:393
  254.5 7.3 %older.10 = (f32[16,256]{1,0:T(8,128)S(1)}, s32[64]{0:T(128)S(1)}, bf16[10,256,256]{2,1,0:T(8,128)(2,1)S(1)}) custom-call(s32[8,128]{1,0:T(8,128)S(1)} %get-tuple-element.108.table, bf16[8,2,6,256,256]{4,3,2,1,0:T(8,128)(2,1)} %bitcast.84, bf16[32,16,256]{2,1,0:T(8,128)(2,1)S(1)} %all-to-all-done.13.store.rest_0_.rest_1_, ...), custom_call_target="tpu_custom_call" | custom-call | flops 100663296 | bytes 13631488 | tf_op jit(solution)/shard_map/older/pallas_call | solution.py:222
  261.8 3.1 all-to-all-done.14.store.rest_0_
  267.2 6.0 %all-to-all-start.15 = ((bf16[32,16,256]{2,1,0:T(8,128)(2,1)}), bf16[32,16,256]{2,1,0:T(8,128)(2,1)S(1)}, u32[]{:S(2)}, u32[]{:S(2)}) async-start(bf16[32,16,256]{2,1,0:T(8,128)(2,1)} %get-tuple-element.106), calls=%async_computation.15 | async-start | bytes 524288 | tf_op jit(solution)/shard_map/all_to_all | solution.py:393
  273.2 7.9 %older.11 = (f32[16,256]{1,0:T(8,128)S(1)}, s32[64]{0:T(128)S(1)}, bf16[10,256,256]{2,1,0:T(8,128)(2,1)S(1)}) custom-call(s32[8,128]{1,0:T(8,128)S(1)} %get-tuple-element.108.table, bf16[8,1,6,256,256]{4,3,2,1,0:T(8,128)(2,1)} %bitcast.86, bf16[32,16,256]{2,1,0:T(8,128)(2,1)S(1)} %all-to-all-done.14.store.rest_0_, ...), custom_call_target="tpu_custom_call" | custom-call | flops 100663296 | bytes 13631488 | tf_op jit(solution)/shard_map/older/pallas_call | solution.py:222
  285.4 17.2 %all_to_all.93 = bf16[8,6,16,256]{3,2,1,0:T(8,128)(2,1)S(1)} all-to-all(bf16[8,6,16,256]{3,2,1,0:T(8,128)(2,1)S(1)} %solve.13), channel_id=1, replica_groups=mesh['g'=4,'z'=8,'x'=4,'core'=2] {'x','core'}, dimensions={0} | all-to-all | bytes 786432 | tf_op jit(solution)/shard_map/all_to_all | solution.py:438
  (46 shorter events, 25.1 us)
Async XLA Ops:
  6.5 148.2 %all-gather.11.cloned.1.call-start = ((), (), s32[]{:S(2)}) async-start(), calls=%async_computation.19 | async-start | bytes 28311552 | tf_op jit(solution)/shard_map/all_gather | solution.py:371
  12.3 13.9 %copy-start.5 = (s32[1,5,6]{2,0,1:T(1,128)S(1)}, s32[1,5,6]{2,0,1:T(1,128)}, u32[]{:S(2)}) copy-start(s32[1,5,6]{2,0,1:T(1,128)} %param.13) | copy-start | bytes 364
  12.3 13.9 %copy-start.7 = (s32[1,5,1]{1,2,0:T(1,128)S(1)}, s32[1,5,1]{1,2,0:T(1,128)}, u32[]{:S(2)}) copy-start(s32[1,5,1]{1,2,0:T(1,128)} %param.14) | copy-start | bytes 64
  12.3 31.8 %copy-start.4 = (s32[1,5,6]{2,0,1:T(1,128)S(1)}, s32[1,5,6]{2,0,1:T(1,128)}, u32[]{:S(2)}) copy-start(s32[1,5,6]{2,0,1:T(1,128)} %param.16) | copy-start | bytes 364
  12.3 31.8 %copy-start.6 = (s32[1,5,1]{1,2,0:T(1,128)S(1)}, s32[1,5,1]{1,2,0:T(1,128)}, u32[]{:S(2)}) copy-start(s32[1,5,1]{1,2,0:T(1,128)} %param.17) | copy-start | bytes 64
  12.3 222.0 %all-gather.9.cloned.1.call-start = ((), (), s32[]{:S(2)}) async-start(), calls=%async_computation.18 | async-start | bytes 14155776 | tf_op jit(solution)/shard_map/all_gather | solution.py:371
  13.1 260.1 %all-gather.7.cloned.1.call-start = ((), (), s32[]{:S(2)}) async-start(), calls=%async_computation.17 | async-start | bytes 7077888 | tf_op jit(solution)/shard_map/all_gather | solution.py:371
  13.8 54.9 %copy-start.3 = (bf16[1,6,256,256]{3,2,1,0:T(8,128)(2,1)S(1)}, bf16[1,6,256,256]{3,2,1,0:T(8,128)(2,1)}, u32[]{:S(2)}) copy-start(bf16[1,6,256,256]{3,2,1,0:T(8,128)(2,1)} %rest_0_.8) | copy-start | bytes 2359300
  13.8 23.5 %all-to-all-start = ((bf16[32,16,256]{2,1,0:T(8,128)(2,1)}), bf16[32,16,256]{2,1,0:T(8,128)(2,1)}, u32[]{:S(2)}, u32[]{:S(2)}) async-start(bf16[32,16,256]{2,1,0:T(8,128)(2,1)} %get-tuple-element.64), calls=%async_computation | async-start | bytes 524288 | tf_op jit(solution)/shard_map/all_to_all | solution.py:393
  37.3 16.5 %all-to-all-start.1 = ((bf16[8,4,16,256]{3,2,1,0:T(8,128)(2,1)}), bf16[8,4,16,256]{3,2,1,0:T(8,128)(2,1)S(1)}, u32[]{:S(2)}, u32[]{:S(2)}) async-start(bf16[8,4,16,256]{3,2,1,0:T(8,128)(2,1)} %bitcast.5), calls=%async_computation.1 | async-start | bytes 524288 | tf_op jit(solution)/shard_map/all_to_all | solution.py:396
  53.8 2.1 copy-start
  55.9 42.5 %copy-start.1 = (bf16[1,5,6,256,256]{4,3,2,1,0:T(8,128)(2,1)S(1)}, bf16[1,5,6,256,256]{4,3,2,1,0:T(8,128)(2,1)}, u32[]{:S(2)}) copy-start(bf16[1,5,6,256,256]{4,3,2,1,0:T(8,128)(2,1)} %blocks.5) | copy-start | bytes 11796484
  150.8 14.5 %all-to-all-start.9 = ((bf16[32,16,256]{2,1,0:T(8,128)(2,1)}), bf16[32,16,256]{2,1,0:T(8,128)(2,1)S(1)}, u32[]{:S(2)}, u32[]{:S(2)}) async-start(bf16[32,16,256]{2,1,0:T(8,128)(2,1)} %get-tuple-element.70), calls=%async_computation.9 | async-start | bytes 524288 | tf_op jit(solution)/shard_map/all_to_all | solution.py:393
  167.3 18.0 %all-to-all-start.10 = ((bf16[32,16,256]{2,1,0:T(8,128)(2,1)}), bf16[32,16,256]{2,1,0:T(8,128)(2,1)S(1)}, u32[]{:S(2)}, u32[]{:S(2)}) async-start(bf16[32,16,256]{2,1,0:T(8,128)(2,1)} %get-tuple-element.76), calls=%async_computation.10 | async-start | bytes 524288 | tf_op jit(solution)/shard_map/all_to_all | solution.py:393
  175.0 10.4 %copy-start.2 = (bf16[1,6,256,256]{3,2,1,0:T(8,128)(2,1)S(1)}, bf16[1,6,256,256]{3,2,1,0:T(8,128)(2,1)}, u32[]{:S(2)}) copy-start(bf16[1,6,256,256]{3,2,1,0:T(8,128)(2,1)} %rest_0_.13) | copy-start | bytes 2359300
  210.5 14.5 %all-to-all-start.12 = ((bf16[32,16,256]{2,1,0:T(8,128)(2,1)}), bf16[32,16,256]{2,1,0:T(8,128)(2,1)S(1)}, u32[]{:S(2)}, u32[]{:S(2)}) async-start(bf16[32,16,256]{2,1,0:T(8,128)(2,1)} %get-tuple-element.85), calls=%async_computation.12 | async-start | bytes 524288 | tf_op jit(solution)/shard_map/all_to_all | solution.py:393
  228.5 16.1 %all-to-all-start.13 = ((bf16[32,16,256]{2,1,0:T(8,128)(2,1)}), bf16[32,16,256]{2,1,0:T(8,128)(2,1)S(1)}, u32[]{:S(2)}, u32[]{:S(2)}) async-start(bf16[32,16,256]{2,1,0:T(8,128)(2,1)} %get-tuple-element.92), calls=%async_computation.13 | async-start | bytes 524288 | tf_op jit(solution)/shard_map/all_to_all | solution.py:393
  247.7 17.2 %all-to-all-start.14 = ((bf16[32,16,256]{2,1,0:T(8,128)(2,1)}), bf16[32,16,256]{2,1,0:T(8,128)(2,1)S(1)}, u32[]{:S(2)}, u32[]{:S(2)}) async-start(bf16[32,16,256]{2,1,0:T(8,128)(2,1)} %get-tuple-element.99), calls=%async_computation.14 | async-start | bytes 524288 | tf_op jit(solution)/shard_map/all_to_all | solution.py:393
  267.2 16.4 %all-to-all-start.15 = ((bf16[32,16,256]{2,1,0:T(8,128)(2,1)}), bf16[32,16,256]{2,1,0:T(8,128)(2,1)S(1)}, u32[]{:S(2)}, u32[]{:S(2)}) async-start(bf16[32,16,256]{2,1,0:T(8,128)(2,1)} %get-tuple-element.106), calls=%async_computation.15 | async-start | bytes 524288 | tf_op jit(solution)/shard_map/all_to_all | solution.py:393
Sparse Core Ops, SparseCore 0:
  12.5 140.3 all-gather.10
  154.7 70.8 all-gather.8
  227.4 43.8 all-gather.6

commit v8 on v7

--- a/solution.py
+++ b/solution.py
@@ -43,6 +43,37 @@
     return pltpu.with_memory_space_constraint(blocks, pltpu.HBM)
 
 
+def first_kernel(lines, low_blocks, high_blocks, out, room, loads, stores):
+    sources = (low_blocks, high_blocks)
+    reads = run(
+        [pltpu.make_async_copy(sources[which].at[0, k], room.at[i], loads.at[i]) for i, (which, k) in enumerate(lines)]
+    )
+    writes = [pltpu.make_async_copy(room.at[i], out.at[i], stores.at[i]) for i in range(len(lines))]
+    for read, write in zip(reads, writes):
+        read.wait()
+        write.start()
+    for write in writes:
+        write.wait()
+
+
+def first_run(lines, low_blocks, high_blocks):
+    block = low_blocks.shape[2:]
+    n = len(lines)
+    return pl.pallas_call(
+        functools.partial(first_kernel, lines),
+        out_shape=pltpu.HBM((n,) + block, BF),
+        in_specs=[ANY] * 2,
+        out_specs=ANY,
+        scratch_shapes=[
+            pltpu.VMEM((n,) + block, BF),
+            pltpu.SemaphoreType.DMA((n,)),
+            pltpu.SemaphoreType.DMA((n,)),
+        ],
+        compiler_params=params(10),
+        name="first",
+    )(hbm(low_blocks), hbm(high_blocks))
+
+
 def begin_kernel(lines, runs, column, low_blocks, high_blocks, right_side, inverse, *rest):
     outs, rest = rest[: len(runs)], rest[len(runs) :]
     right, out, spread, diag, room, loads, stores, sems = rest
@@ -193,6 +224,10 @@
         def _():
             found[n] = i * 32 + place - newest * 32
 
+        @pl.when(hit & (n < cap))
+        def _():
+            pltpu.make_async_copy(blocks.at[i // slots, at, i % slots], ready.at[n], ready_sems.at[n]).start()
+
         n = n + jnp.where(hit, 1, 0)
     found[ncol * slots] = n
     total = jnp.zeros(out.shape, F32)
@@ -202,18 +237,9 @@
             total += dot(pick(stores, first, table[c, line * slots + slot], row), room[c, slot])
     out[...] = total
 
-    def keep(j, _):
-        i = found[j] // 32
-        copy = pltpu.make_async_copy(room.at[i // slots, i % slots], ready.at[j], ready_sems.at[j])
-        copy.start()
-        return _
-
-    def kept(j, _):
-        pltpu.make_async_copy(room.at[0, 0], ready.at[j], ready_sems.at[j]).wait()
-        return _
-
-    lax.fori_loop(0, jnp.minimum(n, cap), keep, 0)
-    lax.fori_loop(0, jnp.minimum(n, cap), kept, 0)
+    @pl.loop(0, jnp.minimum(n, cap))
+    def _(j):
+        pltpu.make_async_copy(blocks.at[0, at, 0], ready.at[j], ready_sems.at[j]).wait()
 
 
 def older(ready, first, line, at, newest, table, blocks, stores):
@@ -363,11 +389,20 @@
 
     last = LAST_SPLIT
     lines = [(0, level - 1) for level in range(last + 1, levels)] + [(1, level) for level in range(levels - 2, -1, -1)]
+    head = first_run(lines[: RUNS[0]], lower_blocks, upper_blocks)
     *rows, right, first, copies = begin(
-        lines, RUNS, jnp.full((1,), column, I32), lower_blocks, upper_blocks, right_side, lower_inverse, ncol, width
+        lines[RUNS[0] :],
+        RUNS[1:],
+        jnp.full((1,), column, I32),
+        lower_blocks,
+        upper_blocks,
+        right_side,
+        lower_inverse,
+        ncol,
+        width,
     )
     gathered = []
-    for count, part_rows in zip(RUNS, rows):
+    for count, part_rows in zip(RUNS, [head] + rows):
         whole = lax.all_gather(part_rows, COL, axis=0)
         gathered.extend((whole, i) for i in range(count))
 

time: 312 us -> 306 us (0.981)
  waiting for transfers between devices: 39.2 us -> 43.9 us
  starting transfers between devices: 53 us -> 48.6 us
  Pallas kernels: 76.7 us -> 72.8 us
    pallas_call x6, Pallas kernels: 45.4 us -> 39.9 us  [older(): pl.pallas_call(functools.partial(older_kernel, first, line, at, newest),...]
    all_to_all x7, waiting for transfers between devices: 28.2 us -> 33.2 us  [spread(): return lax.all_to_all(copies, TURNED, 0, 0, tiled=True)]
    all_to_all x7, starting transfers between devices: 46.2 us -> 41.7 us  [spread(): return lax.all_to_all(copies, TURNED, 0, 0, tiled=True)]
  transfers between devices with their start and end apart: 11 -> 11, of which waited for: 8 -> 9; matrix products, arithmetic and copies ran while one was open for 0% -> 0% of each run, Pallas kernels for 22% -> 22%
where the time goes in v8:
time: 306 us; the launch traced here: 305 us
  blocking collectives  123 us (40%)
  Pallas kernels  72.8 us (24%)
  starting transfers between devices  48.6 us (16%)
  waiting for transfers between devices  43.9 us (14%)
  between operations  13.4 us (4%)
  local copies, waits for them, and re-layouts  3.12 us (1%)
    all_to_all x3, blocking collectives, spread(): return lax.all_to_all(copies, TURNED, 0, 0, tiled=True)  44.5 us
    all_to_all x7, starting transfers between devices, spread(): return lax.all_to_all(copies, TURNED, 0, 0, tiled=True)  41.7 us
    pallas_call x6, Pallas kernels, older(): pl.pallas_call(functools.partial(older_kernel, first, line, at, newest),...  39.9 us
    all_to_all x7, waiting for transfers between devices, spread(): return lax.all_to_all(copies, TURNED, 0, 0, tiled=True)  33.2 us
    all_to_all x2, blocking collectives, by_column(): lax.all_to_all(whole.reshape(ncol, group, part, size), COL, 0, 0, tiled=T...  30.5 us
    all_to_all x3, blocking collectives, shards(): parts = lax.all_to_all(partial, COL, 0, 0, tiled=True)  30.4 us
    pallas_call x7, Pallas kernels, solve(): pl.pallas_call(functools.partial(body, newest, line, at, levels), out_sha...  21.9 us
    all_to_all x1, blocking collectives, shards(): whole = lax.all_to_all(solved, COL, 0, 0, tiled=True)  17.2 us
  transfers between devices with their start and end apart: 11, of which 9 were waited for; matrix products, arithmetic and copies ran while one was open for 0% of the time, Pallas kernels for 22%

profile of v8, /device:TPU:1, one launch (start us, length us, event | category | flops | bytes accessed | tf_op | source)
XLA Modules:
  0.0 304.6 jit_solution(6759513539117626711)
XLA Ops:
  9.6 3.8 %begin.1 = (bf16[2,6,256,256]{3,2,1,0:T(8,128)(2,1)}, bf16[1,6,256,256]{3,2,1,0:T(8,128)(2,1)}, bf16[6,16,256]{2,1,0:T(8,128)(2,1)S(1)}, bf16[16,256]{1,0:T(8,128)(2,1)S(1)}, bf16[32,16,256]{2,1,0:T(8,128)(2,1)}) custom-call(s32[1]{0:T(128)} %bitcast.column, bf16[1,5,6,256,256]{4,3,2,1,0:T(8,128)(2,1)} %blocks.5, bf16[1,5,6,256,256]{4,3,2,1,0:T(8,128)(2,1)} %high_blocks.3, ...), custom_call_target="tpu_custom_call" | custom-call | tf_op jit(solution)/shard_map/begin/pallas_call | solution.py:112
  14.2 12.3 %all-to-all-start = ((bf16[32,16,256]{2,1,0:T(8,128)(2,1)}), bf16[32,16,256]{2,1,0:T(8,128)(2,1)}, u32[]{:S(2)}, u32[]{:S(2)}) async-start(bf16[32,16,256]{2,1,0:T(8,128)(2,1)} %get-tuple-element.62), calls=%async_computation | async-start | bytes 524288 | tf_op jit(solution)/shard_map/all_to_all | solution.py:428
  26.6 11.1 %all-to-all-done.rest_0_ = bf16[32,16,256]{2,1,0:T(8,128)(2,1)} async-done(((bf16[32,16,256]{2,1,0:T(8,128)(2,1)}), bf16[32,16,256]{2,1,0:T(8,128)(2,1)}, u32[]{:S(2)}, u32[]{:S(2)}) %all-to-all-start) | async-done | bytes 262176 | tf_op jit(solution)/shard_map/all_to_all | solution.py:428
  37.7 6.7 %all-to-all-start.1 = ((bf16[8,4,16,256]{3,2,1,0:T(8,128)(2,1)}), bf16[8,4,16,256]{3,2,1,0:T(8,128)(2,1)S(1)}, u32[]{:S(2)}, u32[]{:S(2)}) async-start(bf16[8,4,16,256]{3,2,1,0:T(8,128)(2,1)} %bitcast.5), calls=%async_computation.1 | async-start | bytes 524288 | tf_op jit(solution)/shard_map/all_to_all | solution.py:431
  44.6 9.5 %all-to-all-done.1.rest_0_ = bf16[8,4,16,256]{3,2,1,0:T(8,128)(2,1)S(1)} async-done(((bf16[8,4,16,256]{3,2,1,0:T(8,128)(2,1)}), bf16[8,4,16,256]{3,2,1,0:T(8,128)(2,1)S(1)}, u32[]{:S(2)}, u32[]{:S(2)}) %all-to-all-start.1) | async-done | bytes 262176 | tf_op jit(solution)/shard_map/all_to_all | solution.py:431
  57.4 11.8 %all_to_all.85.parts = f32[8,24,256]{2,1,0:T(8,128)S(1)} all-to-all(f32[8,24,256]{2,1,0:T(8,128)S(1)} %update.3), channel_id=1, replica_groups=mesh['g'=4,'z'=8,'x'=4,'core'=2] {'x','core'}, dimensions={0} | all-to-all | bytes 393216 | tf_op jit(solution)/shard_map/all_to_all | solution.py:437
  69.4 14.2 %all_to_all.86.rest_1_ = bf16[32,16,256]{2,1,0:T(8,128)(2,1)S(1)} all-to-all(bf16[32,16,256]{2,1,0:T(8,128)(2,1)S(1)} %get-tuple-element.64), channel_id=1, replica_groups=mesh['g'=4,'z'=8,'x'=4,'core'=2] {'z','g'}, dimensions={0} | all-to-all | bytes 524288 | tf_op jit(solution)/shard_map/all_to_all | solution.py:428
  83.6 15.1 %all_to_all.87.rest_1_ = bf16[8,4,16,256]{3,2,1,0:T(8,128)(2,1)S(1)} all-to-all(bf16[8,4,16,256]{3,2,1,0:T(8,128)(2,1)S(1)} %bitcast.73), channel_id=1, replica_groups=mesh['g'=4,'z'=8,'x'=4,'core'=2] {'x','core'}, dimensions={0} | all-to-all | bytes 524288 | tf_op jit(solution)/shard_map/all_to_all | solution.py:431
  99.7 10.0 %all_to_all.88.parts = f32[8,16,256]{2,1,0:T(8,128)S(1)} all-to-all(f32[8,16,256]{2,1,0:T(8,128)S(1)} %update.4), channel_id=1, replica_groups=mesh['g'=4,'z'=8,'x'=4,'core'=2] {'x','core'}, dimensions={0} | all-to-all | bytes 262144 | tf_op jit(solution)/shard_map/all_to_all | solution.py:437
  109.9 14.1 %all_to_all.89.rest_2_ = bf16[32,16,256]{2,1,0:T(8,128)(2,1)S(1)} all-to-all(bf16[32,16,256]{2,1,0:T(8,128)(2,1)S(1)} %get-tuple-element.65), channel_id=1, replica_groups=mesh['g'=4,'z'=8,'x'=4,'core'=2] {'z','g'}, dimensions={0} | all-to-all | bytes 524288 | tf_op jit(solution)/shard_map/all_to_all | solution.py:428
  124.0 15.5 %all_to_all.90.rest_2_ = bf16[8,4,16,256]{3,2,1,0:T(8,128)(2,1)S(1)} all-to-all(bf16[8,4,16,256]{3,2,1,0:T(8,128)(2,1)S(1)} %bitcast.74), channel_id=1, replica_groups=mesh['g'=4,'z'=8,'x'=4,'core'=2] {'x','core'}, dimensions={0} | all-to-all | bytes 524288 | tf_op jit(solution)/shard_map/all_to_all | solution.py:431
  140.5 8.6 %all_to_all.91.parts = f32[8,16,256]{2,1,0:T(8,128)S(1)} all-to-all(f32[8,16,256]{2,1,0:T(8,128)S(1)} %update.5), channel_id=1, replica_groups=mesh['g'=4,'z'=8,'x'=4,'core'=2] {'x','core'}, dimensions={0} | all-to-all | bytes 262144 | tf_op jit(solution)/shard_map/all_to_all | solution.py:437
  150.0 5.0 %all-to-all-start.9 = ((bf16[32,16,256]{2,1,0:T(8,128)(2,1)}), bf16[32,16,256]{2,1,0:T(8,128)(2,1)S(1)}, u32[]{:S(2)}, u32[]{:S(2)}) async-start(bf16[32,16,256]{2,1,0:T(8,128)(2,1)} %get-tuple-element.68), calls=%async_computation.9 | async-start | bytes 524288 | tf_op jit(solution)/shard_map/all_to_all | solution.py:428
  155.0 6.7 %older.6 = (f32[16,256]{1,0:T(8,128)S(1)}, s32[64]{0:T(128)S(1)}, bf16[6,256,256]{2,1,0:T(8,128)(2,1)S(1)}) custom-call(s32[8,128]{1,0:T(8,128)S(1)} %get-tuple-element.106.table, bf16[8,4,6,256,256]{4,3,2,1,0:T(8,128)(2,1)} %bitcast.75, bf16[32,16,256]{2,1,0:T(8,128)(2,1)} %all-to-all-done.rest_0_, bf16[32,16,256]{2,1,0:T(8,128)(2,1)S(1)} %all_to_all.86.rest_1_, ...), custom_call_target="tpu_custom_call" | custom-call | flops 100663296 | bytes 13631488 | tf_op jit(solution)/shard_map/older/pallas_call | solution.py:248
  161.7 3.8 %all-to-all-done.9.store.rest_3_ = bf16[32,16,256]{2,1,0:T(8,128)(2,1)S(1)} async-done(((bf16[32,16,256]{2,1,0:T(8,128)(2,1)}), bf16[32,16,256]{2,1,0:T(8,128)(2,1)S(1)}, u32[]{:S(2)}, u32[]{:S(2)}) %all-to-all-start.9) | async-done | bytes 262176 | tf_op jit(solution)/shard_map/all_to_all | solution.py:428
  168.5 5.4 %all-to-all-start.10 = ((bf16[32,16,256]{2,1,0:T(8,128)(2,1)}), bf16[32,16,256]{2,1,0:T(8,128)(2,1)S(1)}, u32[]{:S(2)}, u32[]{:S(2)}) async-start(bf16[32,16,256]{2,1,0:T(8,128)(2,1)} %get-tuple-element.74), calls=%async_computation.10 | async-start | bytes 524288 | tf_op jit(solution)/shard_map/all_to_all | solution.py:428
  173.9 7.0 %older.7 = (f32[16,256]{1,0:T(8,128)S(1)}, s32[64]{0:T(128)S(1)}, bf16[6,256,256]{2,1,0:T(8,128)(2,1)S(1)}) custom-call(s32[8,128]{1,0:T(8,128)S(1)} %get-tuple-element.106.table, bf16[8,4,6,256,256]{4,3,2,1,0:T(8,128)(2,1)} %bitcast.77, bf16[32,16,256]{2,1,0:T(8,128)(2,1)} %all-to-all-done.rest_0_, bf16[32,16,256]{2,1,0:T(8,128)(2,1)S(1)} %all_to_all.86.rest_1_, ...), custom_call_target="tpu_custom_call" | custom-call | flops 100663296 | bytes 13631488 | tf_op jit(solution)/shard_map/older/pallas_call | solution.py:248
  186.7 16.2 %all_to_all.92.store.rest_0_.rest_1_.rest_2_.rest_3_ = bf16[32,16,256]{2,1,0:T(8,128)(2,1)S(1)} all-to-all(bf16[32,16,256]{2,1,0:T(8,128)(2,1)S(1)} %get-tuple-element.80), channel_id=1, replica_groups=mesh['g'=4,'z'=8,'x'=4,'core'=2] {'z','g'}, dimensions={0} | all-to-all | bytes 524288 | tf_op jit(solution)/shard_map/all_to_all | solution.py:428
  202.9 6.1 %solve.9 = (bf16[16,256]{1,0:T(8,128)(2,1)S(1)}, bf16[32,16,256]{2,1,0:T(8,128)(2,1)}) custom-call(bf16[8,4,6,256,256]{4,3,2,1,0:T(8,128)(2,1)} %bitcast.79, bf16[32,16,256]{2,1,0:T(8,128)(2,1)S(1)} %all_to_all.92.store.rest_0_.rest_1_.rest_2_.rest_3_, bf16[16,256]{1,0:T(8,128)(2,1)S(1)} %get-tuple-element.81.right, s32[8,128]{1,0:T(8,128)S(1)} %get-tuple-element.106.table, ...), custom_call_target="tpu_custom_call" | custom-call | flops 100663296 | bytes 4194304 | tf_op jit(solution)/shard_map/solve/pallas_call | solution.py:359
  208.9 4.1 %all-to-all-start.12 = ((bf16[32,16,256]{2,1,0:T(8,128)(2,1)}), bf16[32,16,256]{2,1,0:T(8,128)(2,1)S(1)}, u32[]{:S(2)}, u32[]{:S(2)}) async-start(bf16[32,16,256]{2,1,0:T(8,128)(2,1)} %get-tuple-element.83), calls=%async_computation.12 | async-start | bytes 524288 | tf_op jit(solution)/shard_map/all_to_all | solution.py:428
  213.0 6.7 %older.8 = (f32[16,256]{1,0:T(8,128)S(1)}, s32[64]{0:T(128)S(1)}, bf16[10,256,256]{2,1,0:T(8,128)(2,1)S(1)}) custom-call(s32[8,128]{1,0:T(8,128)S(1)} %get-tuple-element.106.table, bf16[8,4,6,256,256]{4,3,2,1,0:T(8,128)(2,1)} %bitcast.80, bf16[32,16,256]{2,1,0:T(8,128)(2,1)S(1)} %all_to_all.92.store.rest_0_.rest_1_.rest_2_.rest_3_), custom_call_target="tpu_custom_call" | custom-call | flops 100663296 | bytes 13631488 | tf_op jit(solution)/shard_map/older/pallas_call | solution.py:248
  219.7 3.7 %all-to-all-done.12.store.rest_0_.rest_1_.rest_2_ = bf16[32,16,256]{2,1,0:T(8,128)(2,1)S(1)} async-done(((bf16[32,16,256]{2,1,0:T(8,128)(2,1)}), bf16[32,16,256]{2,1,0:T(8,128)(2,1)S(1)}, u32[]{:S(2)}, u32[]{:S(2)}) %all-to-all-start.12) | async-done | bytes 262176 | tf_op jit(solution)/shard_map/all_to_all | solution.py:428
  223.4 3.9 %solve.10 = (bf16[16,256]{1,0:T(8,128)(2,1)S(1)}, bf16[32,16,256]{2,1,0:T(8,128)(2,1)}) custom-call(bf16[8,4,6,256,256]{4,3,2,1,0:T(8,128)(2,1)} %bitcast.81, bf16[32,16,256]{2,1,0:T(8,128)(2,1)S(1)} %all-to-all-done.12.store.rest_0_.rest_1_.rest_2_, bf16[16,256]{1,0:T(8,128)(2,1)S(1)} %get-tuple-element.84.right, f32[16,256]{1,0:T(8,128)S(1)} %get-tuple-element.86.before, ...), custom_call_target="tpu_custom_call" | custom-call | flops 100663296 | bytes 4194304 | tf_op jit(solution)/shard_map/solve/pallas_call | solution.py:359
  227.3 4.6 %all-to-all-start.13 = ((bf16[32,16,256]{2,1,0:T(8,128)(2,1)}), bf16[32,16,256]{2,1,0:T(8,128)(2,1)S(1)}, u32[]{:S(2)}, u32[]{:S(2)}) async-start(bf16[32,16,256]{2,1,0:T(8,128)(2,1)} %get-tuple-element.90), calls=%async_computation.13 | async-start | bytes 524288 | tf_op jit(solution)/shard_map/all_to_all | solution.py:428
  232.0 6.5 %older.9 = (f32[16,256]{1,0:T(8,128)S(1)}, s32[64]{0:T(128)S(1)}, bf16[10,256,256]{2,1,0:T(8,128)(2,1)S(1)}) custom-call(s32[8,128]{1,0:T(8,128)S(1)} %get-tuple-element.106.table, bf16[8,2,6,256,256]{4,3,2,1,0:T(8,128)(2,1)} %bitcast.82, bf16[32,16,256]{2,1,0:T(8,128)(2,1)S(1)} %all-to-all-done.12.store.rest_0_.rest_1_.rest_2_, ...), custom_call_target="tpu_custom_call" | custom-call | flops 100663296 | bytes 13631488 | tf_op jit(solution)/shard_map/older/pallas_call | solution.py:248
  238.5 3.9 %all-to-all-done.13.store.rest_0_.rest_1_ = bf16[32,16,256]{2,1,0:T(8,128)(2,1)S(1)} async-done(((bf16[32,16,256]{2,1,0:T(8,128)(2,1)}), bf16[32,16,256]{2,1,0:T(8,128)(2,1)S(1)}, u32[]{:S(2)}, u32[]{:S(2)}) %all-to-all-start.13) | async-done | bytes 262176 | tf_op jit(solution)/shard_map/all_to_all | solution.py:428
  244.7 5.4 %all-to-all-start.14 = ((bf16[32,16,256]{2,1,0:T(8,128)(2,1)}), bf16[32,16,256]{2,1,0:T(8,128)(2,1)S(1)}, u32[]{:S(2)}, u32[]{:S(2)}) async-start(bf16[32,16,256]{2,1,0:T(8,128)(2,1)} %get-tuple-element.97), calls=%async_computation.14 | async-start | bytes 524288 | tf_op jit(solution)/shard_map/all_to_all | solution.py:428
  250.1 6.6 %older.10 = (f32[16,256]{1,0:T(8,128)S(1)}, s32[64]{0:T(128)S(1)}, bf16[10,256,256]{2,1,0:T(8,128)(2,1)S(1)}) custom-call(s32[8,128]{1,0:T(8,128)S(1)} %get-tuple-element.106.table, bf16[8,2,6,256,256]{4,3,2,1,0:T(8,128)(2,1)} %bitcast.84, bf16[32,16,256]{2,1,0:T(8,128)(2,1)S(1)} %all-to-all-done.13.store.rest_0_.rest_1_, ...), custom_call_target="tpu_custom_call" | custom-call | flops 100663296 | bytes 13631488 | tf_op jit(solution)/shard_map/older/pallas_call | solution.py:248
  256.7 3.8 %all-to-all-done.14.store.rest_0_ = bf16[32,16,256]{2,1,0:T(8,128)(2,1)S(1)} async-done(((bf16[32,16,256]{2,1,0:T(8,128)(2,1)}), bf16[32,16,256]{2,1,0:T(8,128)(2,1)S(1)}, u32[]{:S(2)}, u32[]{:S(2)}) %all-to-all-start.14) | async-done | bytes 262176 | tf_op jit(solution)/shard_map/all_to_all | solution.py:428
  263.1 5.0 %all-to-all-start.15 = ((bf16[32,16,256]{2,1,0:T(8,128)(2,1)}), bf16[32,16,256]{2,1,0:T(8,128)(2,1)S(1)}, u32[]{:S(2)}, u32[]{:S(2)}) async-start(bf16[32,16,256]{2,1,0:T(8,128)(2,1)} %get-tuple-element.104), calls=%async_computation.15 | async-start | bytes 524288 | tf_op jit(solution)/shard_map/all_to_all | solution.py:428
  268.6 6.4 %older.11 = (f32[16,256]{1,0:T(8,128)S(1)}, s32[64]{0:T(128)S(1)}, bf16[10,256,256]{2,1,0:T(8,128)(2,1)S(1)}) custom-call(s32[8,128]{1,0:T(8,128)S(1)} %get-tuple-element.106.table, bf16[8,1,6,256,256]{4,3,2,1,0:T(8,128)(2,1)} %bitcast.86, bf16[32,16,256]{2,1,0:T(8,128)(2,1)S(1)} %all-to-all-done.14.store.rest_0_, ...), custom_call_target="tpu_custom_call" | custom-call | flops 100663296 | bytes 13631488 | tf_op jit(solution)/shard_map/older/pallas_call | solution.py:248
  280.1 17.2 %all_to_all.93 = bf16[8,6,16,256]{3,2,1,0:T(8,128)(2,1)S(1)} all-to-all(bf16[8,6,16,256]{3,2,1,0:T(8,128)(2,1)S(1)} %solve.13), channel_id=1, replica_groups=mesh['g'=4,'z'=8,'x'=4,'core'=2] {'x','core'}, dimensions={0} | all-to-all | bytes 786432 | tf_op jit(solution)/shard_map/all_to_all | solution.py:473
  (47 shorter events, 30.7 us)
Async XLA Ops:
  6.5 148.4 %all-gather.11.cloned.1.call-start = ((), (), s32[]{:S(2)}) async-start(), calls=%async_computation.19 | async-start | bytes 28311552 | tf_op jit(solution)/shard_map/all_gather | solution.py:406
  9.5 222.4 %all-gather.9.cloned.1.call-start = ((), (), s32[]{:S(2)}) async-start(), calls=%async_computation.18 | async-start | bytes 14155776 | tf_op jit(solution)/shard_map/all_gather | solution.py:406
  9.6 16.9 %copy-start.5 = (s32[1,5,6]{2,0,1:T(1,128)S(1)}, s32[1,5,6]{2,0,1:T(1,128)}, u32[]{:S(2)}) copy-start(s32[1,5,6]{2,0,1:T(1,128)} %param.13) | copy-start | bytes 364
  9.6 16.9 %copy-start.7 = (s32[1,5,1]{1,2,0:T(1,128)S(1)}, s32[1,5,1]{1,2,0:T(1,128)}, u32[]{:S(2)}) copy-start(s32[1,5,1]{1,2,0:T(1,128)} %param.14) | copy-start | bytes 64
  13.4 31.0 %copy-start.4 = (s32[1,5,6]{2,0,1:T(1,128)S(1)}, s32[1,5,6]{2,0,1:T(1,128)}, u32[]{:S(2)}) copy-start(s32[1,5,6]{2,0,1:T(1,128)} %param.16) | copy-start | bytes 364
  13.4 31.0 %copy-start.6 = (s32[1,5,1]{1,2,0:T(1,128)S(1)}, s32[1,5,1]{1,2,0:T(1,128)}, u32[]{:S(2)}) copy-start(s32[1,5,1]{1,2,0:T(1,128)} %param.17) | copy-start | bytes 64
  13.5 255.1 %all-gather.7.cloned.1.call-start = ((), (), s32[]{:S(2)}) async-start(), calls=%async_computation.17 | async-start | bytes 7077888 | tf_op jit(solution)/shard_map/all_gather | solution.py:406
  14.2 55.0 %copy-start.3 = (bf16[1,6,256,256]{3,2,1,0:T(8,128)(2,1)S(1)}, bf16[1,6,256,256]{3,2,1,0:T(8,128)(2,1)}, u32[]{:S(2)}) copy-start(bf16[1,6,256,256]{3,2,1,0:T(8,128)(2,1)} %rest_0_.8) | copy-start | bytes 2359300
  14.2 23.5 %all-to-all-start = ((bf16[32,16,256]{2,1,0:T(8,128)(2,1)}), bf16[32,16,256]{2,1,0:T(8,128)(2,1)}, u32[]{:S(2)}, u32[]{:S(2)}) async-start(bf16[32,16,256]{2,1,0:T(8,128)(2,1)} %get-tuple-element.62), calls=%async_computation | async-start | bytes 524288 | tf_op jit(solution)/shard_map/all_to_all | solution.py:428
  37.7 16.5 %all-to-all-start.1 = ((bf16[8,4,16,256]{3,2,1,0:T(8,128)(2,1)}), bf16[8,4,16,256]{3,2,1,0:T(8,128)(2,1)S(1)}, u32[]{:S(2)}, u32[]{:S(2)}) async-start(bf16[8,4,16,256]{3,2,1,0:T(8,128)(2,1)} %bitcast.5), calls=%async_computation.1 | async-start | bytes 524288 | tf_op jit(solution)/shard_map/all_to_all | solution.py:431
  54.2 2.2 copy-start
  56.4 42.3 %copy-start.1 = (bf16[1,5,6,256,256]{4,3,2,1,0:T(8,128)(2,1)S(1)}, bf16[1,5,6,256,256]{4,3,2,1,0:T(8,128)(2,1)}, u32[]{:S(2)}) copy-start(bf16[1,5,6,256,256]{4,3,2,1,0:T(8,128)(2,1)} %blocks.5) | copy-start | bytes 11796484
  150.0 15.5 %all-to-all-start.9 = ((bf16[32,16,256]{2,1,0:T(8,128)(2,1)}), bf16[32,16,256]{2,1,0:T(8,128)(2,1)S(1)}, u32[]{:S(2)}, u32[]{:S(2)}) async-start(bf16[32,16,256]{2,1,0:T(8,128)(2,1)} %get-tuple-element.68), calls=%async_computation.9 | async-start | bytes 524288 | tf_op jit(solution)/shard_map/all_to_all | solution.py:428
  168.5 15.8 %all-to-all-start.10 = ((bf16[32,16,256]{2,1,0:T(8,128)(2,1)}), bf16[32,16,256]{2,1,0:T(8,128)(2,1)S(1)}, u32[]{:S(2)}, u32[]{:S(2)}) async-start(bf16[32,16,256]{2,1,0:T(8,128)(2,1)} %get-tuple-element.74), calls=%async_computation.10 | async-start | bytes 524288 | tf_op jit(solution)/shard_map/all_to_all | solution.py:428
  173.9 10.4 %copy-start.2 = (bf16[1,6,256,256]{3,2,1,0:T(8,128)(2,1)S(1)}, bf16[1,6,256,256]{3,2,1,0:T(8,128)(2,1)}, u32[]{:S(2)}) copy-start(bf16[1,6,256,256]{3,2,1,0:T(8,128)(2,1)} %rest_0_.13) | copy-start | bytes 2359300
  208.9 14.5 %all-to-all-start.12 = ((bf16[32,16,256]{2,1,0:T(8,128)(2,1)}), bf16[32,16,256]{2,1,0:T(8,128)(2,1)S(1)}, u32[]{:S(2)}, u32[]{:S(2)}) async-start(bf16[32,16,256]{2,1,0:T(8,128)(2,1)} %get-tuple-element.83), calls=%async_computation.12 | async-start | bytes 524288 | tf_op jit(solution)/shard_map/all_to_all | solution.py:428
  227.3 15.0 %all-to-all-start.13 = ((bf16[32,16,256]{2,1,0:T(8,128)(2,1)}), bf16[32,16,256]{2,1,0:T(8,128)(2,1)S(1)}, u32[]{:S(2)}, u32[]{:S(2)}) async-start(bf16[32,16,256]{2,1,0:T(8,128)(2,1)} %get-tuple-element.90), calls=%async_computation.13 | async-start | bytes 524288 | tf_op jit(solution)/shard_map/all_to_all | solution.py:428
  244.7 15.8 %all-to-all-start.14 = ((bf16[32,16,256]{2,1,0:T(8,128)(2,1)}), bf16[32,16,256]{2,1,0:T(8,128)(2,1)S(1)}, u32[]{:S(2)}, u32[]{:S(2)}) async-start(bf16[32,16,256]{2,1,0:T(8,128)(2,1)} %get-tuple-element.97), calls=%async_computation.14 | async-start | bytes 524288 | tf_op jit(solution)/shard_map/all_to_all | solution.py:428
  263.1 15.4 %all-to-all-start.15 = ((bf16[32,16,256]{2,1,0:T(8,128)(2,1)}), bf16[32,16,256]{2,1,0:T(8,128)(2,1)S(1)}, u32[]{:S(2)}, u32[]{:S(2)}) async-start(bf16[32,16,256]{2,1,0:T(8,128)(2,1)} %get-tuple-element.104), calls=%async_computation.15 | async-start | bytes 524288 | tf_op jit(solution)/shard_map/all_to_all | solution.py:428
Sparse Core Ops, SparseCore 0:
  9.7 138.9 all-gather.10
  150.5 72.2 all-gather.8
  224.6 43.8 all-gather.6

commit v9 on v8

--- a/solution.py
+++ b/solution.py
@@ -22,7 +22,7 @@
 LAST_SPLIT = 3
 RUNS = (4, 2, 1)
 STEP = 4
-READY = (6, 10)
+READY = (12, 12, 20, 20, 16, 14, 10)
 
 
 def dot(x, y):
@@ -212,9 +212,11 @@
 
 def older_kernel(first, line, at, newest, table, blocks, *rest):
     *stores, out, found, ready, room, sems, ready_sems = rest
-    ncol, slots = room.shape[:2]
+    ncol, slots = blocks.shape[0], blocks.shape[2]
     cap = ready.shape[0]
-    copies = run([pltpu.make_async_copy(blocks.at[c, at], room.at[c], sems.at[c]) for c in range(ncol)])
+    copies = []
+    if stores:
+        copies = run([pltpu.make_async_copy(blocks.at[c, at], room.at[c], sems.at[c]) for c in range(ncol)])
     n = jnp.int32(0)
     for i in range(ncol * slots):
         place = table[i // slots, line * slots + i % slots]
@@ -231,8 +233,8 @@
         n = n + jnp.where(hit, 1, 0)
     found[ncol * slots] = n
     total = jnp.zeros(out.shape, F32)
-    for c in range(ncol):
-        copies[c].wait()
+    for c, copy in enumerate(copies):
+        copy.wait()
         for slot in range(slots):
             total += dot(pick(stores, first, table[c, line * slots + slot], row), room[c, slot])
     out[...] = total
@@ -242,9 +244,8 @@
         pltpu.make_async_copy(blocks.at[0, at, 0], ready.at[j], ready_sems.at[j]).wait()
 
 
-def older(ready, first, line, at, newest, table, blocks, stores):
+def older(ready, first, line, at, newest, table, blocks, stores, part):
     ncol, _, slots, size, _ = blocks.shape
-    part = stores[0].shape[1]
     return pl.pallas_call(
         functools.partial(older_kernel, first, line, at, newest),
         out_shape=[
@@ -255,7 +256,7 @@
         in_specs=[SMEM, ANY] + [VMEM] * len(stores),
         out_specs=[VMEM, SMEM, VMEM],
         scratch_shapes=[
-            pltpu.VMEM((ncol, slots, size, size), BF),
+            pltpu.VMEM((ncol if stores else 1, slots, size, size), BF),
             pltpu.SemaphoreType.DMA((ncol,)),
             pltpu.SemaphoreType.DMA((ready,)),
         ],
@@ -265,10 +266,20 @@
     )(table, hbm(blocks), *stores)
 
 
-def finish_row(total, right, level, inverses, levels, rest):
+def fetch_ends(inverses, levels, diag, sems):
+    return run(
+        [
+            pltpu.make_async_copy(ref.at[0, level], diag.at[i], sems.at[i])
+            for i, (ref, level) in enumerate(zip(inverses, levels))
+        ]
+    )
+
+
+def finish_row(total, right, level, ends, diag, rest):
     solved = ((right[level] if len(right.shape) > 2 else right[...]).astype(F32) - total).astype(BF)
-    for i, level in enumerate(levels):
-        solved = dot(solved, inverses[i][0, level]).astype(BF)
+    for i, end in enumerate(ends):
+        end.wait()
+        solved = dot(solved, diag[i]).astype(BF)
     if len(rest) > 2:
         *done, out = rest
         for i in range(out.shape[0]):
@@ -282,25 +293,13 @@
             spread[i] = solved
 
 
-def dense_kernel(newest, line, at, levels, blocks, store, right, table, *rest):
-    m = len(levels)
-    inverses, (*rest, room, sems) = rest[:m], rest[m:]
-    ncol, slots = blocks.shape[0], blocks.shape[2]
-    copies = run([pltpu.make_async_copy(blocks.at[c, at], room.at[c], sems.at[c]) for c in range(ncol)])
-    total = jnp.zeros(store.shape[1:], F32)
-    for c in range(ncol):
-        copies[c].wait()
-        for slot in range(slots):
-            total += dot(pick([store], newest, table[c, line * slots + slot], row), room[c, slot])
-    finish_row(total, right, levels[0], inverses, levels, rest)
-
-
 def sparse_kernel(newest, line, at, levels, blocks, store, right, before, found, ready, *rest):
     m = len(levels)
-    inverses, (*rest, room, sems) = rest[:m], rest[m:]
+    inverses, (*rest, diag, room, sems, end_sems) = rest[:m], rest[m:]
     ncol, slots = blocks.shape[0], blocks.shape[2]
     cap = ready.shape[0]
     n = found[ncol * slots]
+    ends = fetch_ends(inverses, levels, diag, end_sems)
 
     def fetch(j):
         i = found[j] // 32
@@ -335,7 +334,7 @@
     total = lax.fori_loop(
         0, (more + STEP - 1) // STEP, lambda k, total: some(cap, n, lambda j: room[j - cap], k, total), total
     )
-    finish_row(total, right, levels[0], inverses, levels, rest)
+    finish_row(total, right, levels[0], ends, diag, rest)
 
 
 def solve(newest, line, at, levels, table, blocks, store, right, before, inverses, done=()):
@@ -348,24 +347,22 @@
     else:
         out_shape = [jax.ShapeDtypeStruct((part, size), BF), jax.ShapeDtypeStruct((width, part, size), BF)]
         out_specs = [VMEM, VMEM]
-    if before:
-        body, own, own_specs = sparse_kernel, before, [VMEM, SMEM, VMEM]
-        copies = ncol * slots - before[2].shape[0]
-        room = (copies, size, size)
-    else:
-        body, own, own_specs = dense_kernel, [table], [SMEM]
-        room = (ncol, slots, size, size)
-        copies = ncol
-    return pl.pallas_call(
-        functools.partial(body, newest, line, at, levels),
+    copies = ncol * slots - before[2].shape[0]
+    return pl.pallas_call(
+        functools.partial(sparse_kernel, newest, line, at, levels),
         out_shape=out_shape,
-        in_specs=[ANY, VMEM, VMEM] + own_specs + [VMEM] * (len(inverses) + len(done)),
+        in_specs=[ANY, VMEM, VMEM, VMEM, SMEM, VMEM] + [ANY] * len(inverses) + [VMEM] * len(done),
         out_specs=out_specs,
-        scratch_shapes=[pltpu.VMEM(room, BF), pltpu.SemaphoreType.DMA((copies,))],
+        scratch_shapes=[
+            pltpu.VMEM((len(inverses), size, size), BF),
+            pltpu.VMEM((copies, size, size), BF),
+            pltpu.SemaphoreType.DMA((copies,)),
+            pltpu.SemaphoreType.DMA((len(inverses),)),
+        ],
         compiler_params=params(10),
         cost_estimate=pl.CostEstimate(flops=2 * ncol * slots * part * size * size, bytes_accessed=4 << 20, transcendentals=0),
         name="solve",
-    )(hbm(blocks), store, right, *own, *inverses, *done)
+    )(hbm(blocks), store, right, *before, *[hbm(ref) for ref in inverses], *done)
 
 
 def shards(
@@ -442,15 +439,15 @@
         if level < last:
             stores.append(spread(copies))
 
-    def step(ready, line, olds, first, newest, copies):
+    def step(line, olds, first, newest, copies):
         blocks, at = gathered[line]
         copies, tied = lax.optimization_barrier((copies, table))
-        before = older(READY[ready], first, line, at, newest, tied, blocks, olds) if olds else []
+        before = older(READY[line], first, line, at, newest, tied, blocks, olds, part)
         return spread(copies), before
 
     line = 0
     for level in range(last + 1, levels):
-        newest, before = step(0, line, stores, 0, level - 1, copies)
+        newest, before = step(line, stores, 0, level - 1, copies)
         ends = [lower_inverse], [level]
         if level == levels - 1:
             ends = [lower_inverse, upper_inverse], [level, level]
@@ -461,7 +458,7 @@
         line += 1
     result, stores = [solved], []
     for level in range(levels - 2, -1, -1):
-        newest, before = step(1, line, stores, level + 2, level + 1, copies)
+        newest, before = step(line, stores, level + 2, level + 1, copies)
         blocks, at = gathered[line]
         done = result if level == 0 else ()
         solved = solve(level + 1, line, at, [level], table, blocks, newest, own[level], before, [upper_inverse], done)

time: 306 us -> 306 us (level)
  blocking collectives: 123 us -> 106 us
  waiting for transfers between devices: 43.9 us -> 50.9 us
  starting transfers between devices: 48.6 us -> 55.4 us
    all_to_all x3 -> x2, blocking collectives: 44.5 us -> 28.3 us  [spread(): return lax.all_to_all(copies, TURNED, 0, 0, tiled=True)]
    all_to_all x7 -> x8, starting transfers between devices: 41.7 us -> 48.6 us  [spread(): return lax.all_to_all(copies, TURNED, 0, 0, tiled=True)]
    all_to_all x7 -> x8, waiting for transfers between devices: 33.2 us -> 38.9 us  [spread(): return lax.all_to_all(copies, TURNED, 0, 0, tiled=True)]
    pallas_call x6 -> x7, Pallas kernels: 39.9 us -> 43.5 us  [older(): pl.pallas_call(functools.partial(older_kernel, first, line, at, newest),...]
  transfers between devices with their start and end apart: 11 -> 12, of which waited for: 9 -> 10; matrix products, arithmetic and copies ran while one was open for 0% -> 0% of each run, Pallas kernels for 22% -> 23%
where the time goes in v9:
time: 306 us; the launch traced here: 304 us
  blocking collectives  106 us (35%)
  Pallas kernels  74.3 us (24%)
  starting transfers between devices  55.4 us (18%)
  waiting for transfers between devices  50.9 us (17%)
  between operations  13.4 us (4%)
  local copies, waits for them, and re-layouts  3.11 us (1%)
    all_to_all x8, starting transfers between devices, spread(): return lax.all_to_all(copies, TURNED, 0, 0, tiled=True)  48.6 us
    pallas_call x7, Pallas kernels, older(): pl.pallas_call(functools.partial(older_kernel, first, line, at, newest),...  43.5 us
    all_to_all x8, waiting for transfers between devices, spread(): return lax.all_to_all(copies, TURNED, 0, 0, tiled=True)  38.9 us
    all_to_all x2, blocking collectives, by_column(): lax.all_to_all(whole.reshape(ncol, group, part, size), COL, 0, 0, tiled=T...  30.5 us
    all_to_all x3, blocking collectives, shards(): parts = lax.all_to_all(partial, COL, 0, 0, tiled=True)  30.4 us
    all_to_all x2, blocking collectives, spread(): return lax.all_to_all(copies, TURNED, 0, 0, tiled=True)  28.3 us
    pallas_call x7, Pallas kernels, solve(): pl.pallas_call(functools.partial(sparse_kernel, newest, line, at, levels)...  19.8 us
    all_to_all x1, blocking collectives, shards(): whole = lax.all_to_all(solved, COL, 0, 0, tiled=True)  17 us
  transfers between devices with their start and end apart: 12, of which 10 were waited for; matrix products, arithmetic and copies ran while one was open for 0% of the time, Pallas kernels for 23%

profile of v9, /device:TPU:1, one launch (start us, length us, event | category | flops | bytes accessed | tf_op | source)
XLA Modules:
  0.0 303.6 jit_solution(13804557926451577792)
XLA Ops:
  9.6 3.8 %begin.1 = (bf16[2,6,256,256]{3,2,1,0:T(8,128)(2,1)}, bf16[1,6,256,256]{3,2,1,0:T(8,128)(2,1)}, bf16[6,16,256]{2,1,0:T(8,128)(2,1)S(1)}, bf16[16,256]{1,0:T(8,128)(2,1)S(1)}, bf16[32,16,256]{2,1,0:T(8,128)(2,1)}) custom-call(s32[1]{0:T(128)} %bitcast.column, bf16[1,5,6,256,256]{4,3,2,1,0:T(8,128)(2,1)} %blocks.5, bf16[1,5,6,256,256]{4,3,2,1,0:T(8,128)(2,1)} %high_blocks.3, ...), custom_call_target="tpu_custom_call" | custom-call | tf_op jit(solution)/shard_map/begin/pallas_call | solution.py:112
  14.2 12.3 %all-to-all-start = ((bf16[32,16,256]{2,1,0:T(8,128)(2,1)}), bf16[32,16,256]{2,1,0:T(8,128)(2,1)}, u32[]{:S(2)}, u32[]{:S(2)}) async-start(bf16[32,16,256]{2,1,0:T(8,128)(2,1)} %get-tuple-element.66), calls=%async_computation | async-start | bytes 524288 | tf_op jit(solution)/shard_map/all_to_all | solution.py:425
  26.6 11.1 %all-to-all-done.rest_0_ = bf16[32,16,256]{2,1,0:T(8,128)(2,1)} async-done(((bf16[32,16,256]{2,1,0:T(8,128)(2,1)}), bf16[32,16,256]{2,1,0:T(8,128)(2,1)}, u32[]{:S(2)}, u32[]{:S(2)}) %all-to-all-start) | async-done | bytes 262176 | tf_op jit(solution)/shard_map/all_to_all | solution.py:425
  37.7 6.7 %all-to-all-start.1 = ((bf16[8,4,16,256]{3,2,1,0:T(8,128)(2,1)}), bf16[8,4,16,256]{3,2,1,0:T(8,128)(2,1)S(1)}, u32[]{:S(2)}, u32[]{:S(2)}) async-start(bf16[8,4,16,256]{3,2,1,0:T(8,128)(2,1)} %bitcast.5), calls=%async_computation.1 | async-start | bytes 524288 | tf_op jit(solution)/shard_map/all_to_all | solution.py:428
  44.6 9.5 %all-to-all-done.1.rest_0_ = bf16[8,4,16,256]{3,2,1,0:T(8,128)(2,1)S(1)} async-done(((bf16[8,4,16,256]{3,2,1,0:T(8,128)(2,1)}), bf16[8,4,16,256]{3,2,1,0:T(8,128)(2,1)S(1)}, u32[]{:S(2)}, u32[]{:S(2)}) %all-to-all-start.1) | async-done | bytes 262176 | tf_op jit(solution)/shard_map/all_to_all | solution.py:428
  57.4 11.8 %all_to_all.85.parts = f32[8,24,256]{2,1,0:T(8,128)S(1)} all-to-all(f32[8,24,256]{2,1,0:T(8,128)S(1)} %update.3), channel_id=1, replica_groups=mesh['g'=4,'z'=8,'x'=4,'core'=2] {'x','core'}, dimensions={0} | all-to-all | bytes 393216 | tf_op jit(solution)/shard_map/all_to_all | solution.py:434
  69.4 14.2 %all_to_all.86.rest_1_ = bf16[32,16,256]{2,1,0:T(8,128)(2,1)S(1)} all-to-all(bf16[32,16,256]{2,1,0:T(8,128)(2,1)S(1)} %get-tuple-element.68), channel_id=1, replica_groups=mesh['g'=4,'z'=8,'x'=4,'core'=2] {'z','g'}, dimensions={0} | all-to-all | bytes 524288 | tf_op jit(solution)/shard_map/all_to_all | solution.py:425
  83.6 15.1 %all_to_all.87.rest_1_ = bf16[8,4,16,256]{3,2,1,0:T(8,128)(2,1)S(1)} all-to-all(bf16[8,4,16,256]{3,2,1,0:T(8,128)(2,1)S(1)} %bitcast.73), channel_id=1, replica_groups=mesh['g'=4,'z'=8,'x'=4,'core'=2] {'x','core'}, dimensions={0} | all-to-all | bytes 524288 | tf_op jit(solution)/shard_map/all_to_all | solution.py:428
  99.7 10.0 %all_to_all.88.parts = f32[8,16,256]{2,1,0:T(8,128)S(1)} all-to-all(f32[8,16,256]{2,1,0:T(8,128)S(1)} %update.4), channel_id=1, replica_groups=mesh['g'=4,'z'=8,'x'=4,'core'=2] {'x','core'}, dimensions={0} | all-to-all | bytes 262144 | tf_op jit(solution)/shard_map/all_to_all | solution.py:434
  109.9 14.1 %all_to_all.89.rest_2_ = bf16[32,16,256]{2,1,0:T(8,128)(2,1)S(1)} all-to-all(bf16[32,16,256]{2,1,0:T(8,128)(2,1)S(1)} %get-tuple-element.69), channel_id=1, replica_groups=mesh['g'=4,'z'=8,'x'=4,'core'=2] {'z','g'}, dimensions={0} | all-to-all | bytes 524288 | tf_op jit(solution)/shard_map/all_to_all | solution.py:425
  124.0 15.5 %all_to_all.90.rest_2_ = bf16[8,4,16,256]{3,2,1,0:T(8,128)(2,1)S(1)} all-to-all(bf16[8,4,16,256]{3,2,1,0:T(8,128)(2,1)S(1)} %bitcast.74), channel_id=1, replica_groups=mesh['g'=4,'z'=8,'x'=4,'core'=2] {'x','core'}, dimensions={0} | all-to-all | bytes 524288 | tf_op jit(solution)/shard_map/all_to_all | solution.py:428
  140.5 8.6 %all_to_all.91.parts = f32[8,16,256]{2,1,0:T(8,128)S(1)} all-to-all(f32[8,16,256]{2,1,0:T(8,128)S(1)} %update.5), channel_id=1, replica_groups=mesh['g'=4,'z'=8,'x'=4,'core'=2] {'x','core'}, dimensions={0} | all-to-all | bytes 262144 | tf_op jit(solution)/shard_map/all_to_all | solution.py:434
  150.0 5.0 %all-to-all-start.9 = ((bf16[32,16,256]{2,1,0:T(8,128)(2,1)}), bf16[32,16,256]{2,1,0:T(8,128)(2,1)S(1)}, u32[]{:S(2)}, u32[]{:S(2)}) async-start(bf16[32,16,256]{2,1,0:T(8,128)(2,1)} %get-tuple-element.72), calls=%async_computation.9 | async-start | bytes 524288 | tf_op jit(solution)/shard_map/all_to_all | solution.py:425
  155.0 7.0 %older.7 = (f32[16,256]{1,0:T(8,128)S(1)}, s32[64]{0:T(128)S(1)}, bf16[12,256,256]{2,1,0:T(8,128)(2,1)S(1)}) custom-call(s32[8,128]{1,0:T(8,128)S(1)} %get-tuple-element.114.table, bf16[8,4,6,256,256]{4,3,2,1,0:T(8,128)(2,1)} %bitcast.75, bf16[32,16,256]{2,1,0:T(8,128)(2,1)} %all-to-all-done.rest_0_, bf16[32,16,256]{2,1,0:T(8,128)(2,1)S(1)} %all_to_all.86.rest_1_, ...), custom_call_target="tpu_custom_call" | custom-call | flops 100663296 | bytes 13631488 | tf_op jit(solution)/shard_map/older/pallas_call | solution.py:249
  162.0 3.5 %all-to-all-done.9.store.rest_3_ = bf16[32,16,256]{2,1,0:T(8,128)(2,1)S(1)} async-done(((bf16[32,16,256]{2,1,0:T(8,128)(2,1)}), bf16[32,16,256]{2,1,0:T(8,128)(2,1)S(1)}, u32[]{:S(2)}, u32[]{:S(2)}) %all-to-all-start.9) | async-done | bytes 262176 | tf_op jit(solution)/shard_map/all_to_all | solution.py:425
  168.2 5.3 %all-to-all-start.10 = ((bf16[32,16,256]{2,1,0:T(8,128)(2,1)}), bf16[32,16,256]{2,1,0:T(8,128)(2,1)S(1)}, u32[]{:S(2)}, u32[]{:S(2)}) async-start(bf16[32,16,256]{2,1,0:T(8,128)(2,1)} %get-tuple-element.78), calls=%async_computation.10 | async-start | bytes 524288 | tf_op jit(solution)/shard_map/all_to_all | solution.py:425
  173.5 7.0 %older.8 = (f32[16,256]{1,0:T(8,128)S(1)}, s32[64]{0:T(128)S(1)}, bf16[12,256,256]{2,1,0:T(8,128)(2,1)S(1)}) custom-call(s32[8,128]{1,0:T(8,128)S(1)} %get-tuple-element.114.table, bf16[8,4,6,256,256]{4,3,2,1,0:T(8,128)(2,1)} %bitcast.77, bf16[32,16,256]{2,1,0:T(8,128)(2,1)} %all-to-all-done.rest_0_, bf16[32,16,256]{2,1,0:T(8,128)(2,1)S(1)} %all_to_all.86.rest_1_, ...), custom_call_target="tpu_custom_call" | custom-call | flops 100663296 | bytes 13631488 | tf_op jit(solution)/shard_map/older/pallas_call | solution.py:249
  186.8 5.6 %all-to-all-start.11 = ((bf16[32,16,256]{2,1,0:T(8,128)(2,1)}), bf16[32,16,256]{2,1,0:T(8,128)(2,1)S(1)}, u32[]{:S(2)}, u32[]{:S(2)}) async-start(bf16[32,16,256]{2,1,0:T(8,128)(2,1)} %get-tuple-element.84), calls=%async_computation.11 | async-start | bytes 524288 | tf_op jit(solution)/shard_map/all_to_all | solution.py:425
  195.7 7.2 %all-to-all-done.11.store.rest_0_.rest_1_.rest_2_.rest_3_ = bf16[32,16,256]{2,1,0:T(8,128)(2,1)S(1)} async-done(((bf16[32,16,256]{2,1,0:T(8,128)(2,1)}), bf16[32,16,256]{2,1,0:T(8,128)(2,1)S(1)}, u32[]{:S(2)}, u32[]{:S(2)}) %all-to-all-start.11) | async-done | bytes 262176 | tf_op jit(solution)/shard_map/all_to_all | solution.py:425
  202.9 4.1 %solve.9 = (bf16[16,256]{1,0:T(8,128)(2,1)S(1)}, bf16[32,16,256]{2,1,0:T(8,128)(2,1)}) custom-call(bf16[8,4,6,256,256]{4,3,2,1,0:T(8,128)(2,1)} %bitcast.80, bf16[32,16,256]{2,1,0:T(8,128)(2,1)S(1)} %all-to-all-done.11.store.rest_0_.rest_1_.rest_2_.rest_3_, bf16[16,256]{1,0:T(8,128)(2,1)S(1)} %get-tuple-element.85.right, ...), custom_call_target="tpu_custom_call" | custom-call | flops 100663296 | bytes 4194304 | tf_op jit(solution)/shard_map/solve/pallas_call | solution.py:351
  207.1 4.0 %all-to-all-start.12 = ((bf16[32,16,256]{2,1,0:T(8,128)(2,1)}), bf16[32,16,256]{2,1,0:T(8,128)(2,1)S(1)}, u32[]{:S(2)}, u32[]{:S(2)}) async-start(bf16[32,16,256]{2,1,0:T(8,128)(2,1)} %get-tuple-element.91), calls=%async_computation.12 | async-start | bytes 524288 | tf_op jit(solution)/shard_map/all_to_all | solution.py:425
  211.1 7.0 %older.10 = (f32[16,256]{1,0:T(8,128)S(1)}, s32[64]{0:T(128)S(1)}, bf16[20,256,256]{2,1,0:T(8,128)(2,1)S(1)}) custom-call(s32[8,128]{1,0:T(8,128)S(1)} %get-tuple-element.114.table, bf16[8,4,6,256,256]{4,3,2,1,0:T(8,128)(2,1)} %bitcast.81, bf16[32,16,256]{2,1,0:T(8,128)(2,1)S(1)} %all-to-all-done.11.store.rest_0_.rest_1_.rest_2_.rest_3_), custom_call_target="tpu_custom_call" | custom-call | flops 100663296 | bytes 13631488 | tf_op jit(solution)/shard_map/older/pallas_call | solution.py:249
  218.1 3.5 %all-to-all-done.12.store.rest_0_.rest_1_.rest_2_ = bf16[32,16,256]{2,1,0:T(8,128)(2,1)S(1)} async-done(((bf16[32,16,256]{2,1,0:T(8,128)(2,1)}), bf16[32,16,256]{2,1,0:T(8,128)(2,1)S(1)}, u32[]{:S(2)}, u32[]{:S(2)}) %all-to-all-start.12) | async-done | bytes 262176 | tf_op jit(solution)/shard_map/all_to_all | solution.py:425
  224.4 5.8 %all-to-all-start.13 = ((bf16[32,16,256]{2,1,0:T(8,128)(2,1)}), bf16[32,16,256]{2,1,0:T(8,128)(2,1)S(1)}, u32[]{:S(2)}, u32[]{:S(2)}) async-start(bf16[32,16,256]{2,1,0:T(8,128)(2,1)} %get-tuple-element.98), calls=%async_computation.13 | async-start | bytes 524288 | tf_op jit(solution)/shard_map/all_to_all | solution.py:425
  230.3 6.6 %older.11 = (f32[16,256]{1,0:T(8,128)S(1)}, s32[64]{0:T(128)S(1)}, bf16[16,256,256]{2,1,0:T(8,128)(2,1)S(1)}) custom-call(s32[8,128]{1,0:T(8,128)S(1)} %get-tuple-element.114.table, bf16[8,2,6,256,256]{4,3,2,1,0:T(8,128)(2,1)} %bitcast.83, bf16[32,16,256]{2,1,0:T(8,128)(2,1)S(1)} %all-to-all-done.12.store.rest_0_.rest_1_.rest_2_, ...), custom_call_target="tpu_custom_call" | custom-call | flops 100663296 | bytes 13631488 | tf_op jit(solution)/shard_map/older/pallas_call | solution.py:249
  236.9 3.7 %all-to-all-done.13.store.rest_0_.rest_1_ = bf16[32,16,256]{2,1,0:T(8,128)(2,1)S(1)} async-done(((bf16[32,16,256]{2,1,0:T(8,128)(2,1)}), bf16[32,16,256]{2,1,0:T(8,128)(2,1)S(1)}, u32[]{:S(2)}, u32[]{:S(2)}) %all-to-all-start.13) | async-done | bytes 262176 | tf_op jit(solution)/shard_map/all_to_all | solution.py:425
  243.3 5.3 %all-to-all-start.14 = ((bf16[32,16,256]{2,1,0:T(8,128)(2,1)}), bf16[32,16,256]{2,1,0:T(8,128)(2,1)S(1)}, u32[]{:S(2)}, u32[]{:S(2)}) async-start(bf16[32,16,256]{2,1,0:T(8,128)(2,1)} %get-tuple-element.105), calls=%async_computation.14 | async-start | bytes 524288 | tf_op jit(solution)/shard_map/all_to_all | solution.py:425
  248.6 6.4 %older.12 = (f32[16,256]{1,0:T(8,128)S(1)}, s32[64]{0:T(128)S(1)}, bf16[14,256,256]{2,1,0:T(8,128)(2,1)S(1)}) custom-call(s32[8,128]{1,0:T(8,128)S(1)} %get-tuple-element.114.table, bf16[8,2,6,256,256]{4,3,2,1,0:T(8,128)(2,1)} %bitcast.85, bf16[32,16,256]{2,1,0:T(8,128)(2,1)S(1)} %all-to-all-done.13.store.rest_0_.rest_1_, ...), custom_call_target="tpu_custom_call" | custom-call | flops 100663296 | bytes 13631488 | tf_op jit(solution)/shard_map/older/pallas_call | solution.py:249
  255.0 4.0 %all-to-all-done.14.store.rest_0_ = bf16[32,16,256]{2,1,0:T(8,128)(2,1)S(1)} async-done(((bf16[32,16,256]{2,1,0:T(8,128)(2,1)}), bf16[32,16,256]{2,1,0:T(8,128)(2,1)S(1)}, u32[]{:S(2)}, u32[]{:S(2)}) %all-to-all-start.14) | async-done | bytes 262176 | tf_op jit(solution)/shard_map/all_to_all | solution.py:425
  261.7 5.2 %all-to-all-start.15 = ((bf16[32,16,256]{2,1,0:T(8,128)(2,1)}), bf16[32,16,256]{2,1,0:T(8,128)(2,1)S(1)}, u32[]{:S(2)}, u32[]{:S(2)}) async-start(bf16[32,16,256]{2,1,0:T(8,128)(2,1)} %get-tuple-element.112), calls=%async_computation.15 | async-start | bytes 524288 | tf_op jit(solution)/shard_map/all_to_all | solution.py:425
  268.5 6.3 %older.13 = (f32[16,256]{1,0:T(8,128)S(1)}, s32[64]{0:T(128)S(1)}, bf16[10,256,256]{2,1,0:T(8,128)(2,1)S(1)}) custom-call(s32[8,128]{1,0:T(8,128)S(1)} %get-tuple-element.114.table, bf16[8,1,6,256,256]{4,3,2,1,0:T(8,128)(2,1)} %bitcast.87, bf16[32,16,256]{2,1,0:T(8,128)(2,1)S(1)} %all-to-all-done.14.store.rest_0_, ...), custom_call_target="tpu_custom_call" | custom-call | flops 100663296 | bytes 13631488 | tf_op jit(solution)/shard_map/older/pallas_call | solution.py:249
  279.3 17.0 %all_to_all.92 = bf16[8,6,16,256]{3,2,1,0:T(8,128)(2,1)S(1)} all-to-all(bf16[8,6,16,256]{3,2,1,0:T(8,128)(2,1)S(1)} %solve.13), channel_id=1, replica_groups=mesh['g'=4,'z'=8,'x'=4,'core'=2] {'x','core'}, dimensions={0} | all-to-all | bytes 786432 | tf_op jit(solution)/shard_map/all_to_all | solution.py:470
  (47 shorter events, 37.8 us)
Async XLA Ops:
  6.5 148.4 %all-gather.11.cloned.1.call-start = ((), (), s32[]{:S(2)}) async-start(), calls=%async_computation.19 | async-start | bytes 28311552 | tf_op jit(solution)/shard_map/all_gather | solution.py:403
  9.5 220.7 %all-gather.9.cloned.1.call-start = ((), (), s32[]{:S(2)}) async-start(), calls=%async_computation.18 | async-start | bytes 14155776 | tf_op jit(solution)/shard_map/all_gather | solution.py:403
  13.4 13.1 %copy-start.4 = (s32[1,5,6]{2,0,1:T(1,128)S(1)}, s32[1,5,6]{2,0,1:T(1,128)}, u32[]{:S(2)}) copy-start(s32[1,5,6]{2,0,1:T(1,128)} %param.13) | copy-start | bytes 364
  13.4 13.1 %copy-start.6 = (s32[1,5,1]{1,2,0:T(1,128)S(1)}, s32[1,5,1]{1,2,0:T(1,128)}, u32[]{:S(2)}) copy-start(s32[1,5,1]{1,2,0:T(1,128)} %param.14) | copy-start | bytes 64
  13.4 31.0 %copy-start.3 = (s32[1,5,6]{2,0,1:T(1,128)S(1)}, s32[1,5,6]{2,0,1:T(1,128)}, u32[]{:S(2)}) copy-start(s32[1,5,6]{2,0,1:T(1,128)} %param.16) | copy-start | bytes 364
  13.4 31.0 %copy-start.5 = (s32[1,5,1]{1,2,0:T(1,128)S(1)}, s32[1,5,1]{1,2,0:T(1,128)}, u32[]{:S(2)}) copy-start(s32[1,5,1]{1,2,0:T(1,128)} %param.17) | copy-start | bytes 64
  13.4 255.1 %all-gather.7.cloned.1.call-start = ((), (), s32[]{:S(2)}) async-start(), calls=%async_computation.17 | async-start | bytes 7077888 | tf_op jit(solution)/shard_map/all_gather | solution.py:403
  14.2 55.0 %copy-start.2 = (bf16[1,6,256,256]{3,2,1,0:T(8,128)(2,1)S(1)}, bf16[1,6,256,256]{3,2,1,0:T(8,128)(2,1)}, u32[]{:S(2)}) copy-start(bf16[1,6,256,256]{3,2,1,0:T(8,128)(2,1)} %rest_0_.8) | copy-start | bytes 2359300
  14.2 23.5 %all-to-all-start = ((bf16[32,16,256]{2,1,0:T(8,128)(2,1)}), bf16[32,16,256]{2,1,0:T(8,128)(2,1)}, u32[]{:S(2)}, u32[]{:S(2)}) async-start(bf16[32,16,256]{2,1,0:T(8,128)(2,1)} %get-tuple-element.66), calls=%async_computation | async-start | bytes 524288 | tf_op jit(solution)/shard_map/all_to_all | solution.py:425
  37.7 16.5 %all-to-all-start.1 = ((bf16[8,4,16,256]{3,2,1,0:T(8,128)(2,1)}), bf16[8,4,16,256]{3,2,1,0:T(8,128)(2,1)S(1)}, u32[]{:S(2)}, u32[]{:S(2)}) async-start(bf16[8,4,16,256]{3,2,1,0:T(8,128)(2,1)} %bitcast.5), calls=%async_computation.1 | async-start | bytes 524288 | tf_op jit(solution)/shard_map/all_to_all | solution.py:428
  54.2 2.2 copy-start
  56.4 42.3 %copy-start.1 = (bf16[1,5,6,256,256]{4,3,2,1,0:T(8,128)(2,1)S(1)}, bf16[1,5,6,256,256]{4,3,2,1,0:T(8,128)(2,1)}, u32[]{:S(2)}) copy-start(bf16[1,5,6,256,256]{4,3,2,1,0:T(8,128)(2,1)} %blocks.5) | copy-start | bytes 11796484
  150.0 15.5 %all-to-all-start.9 = ((bf16[32,16,256]{2,1,0:T(8,128)(2,1)}), bf16[32,16,256]{2,1,0:T(8,128)(2,1)S(1)}, u32[]{:S(2)}, u32[]{:S(2)}) async-start(bf16[32,16,256]{2,1,0:T(8,128)(2,1)} %get-tuple-element.72), calls=%async_computation.9 | async-start | bytes 524288 | tf_op jit(solution)/shard_map/all_to_all | solution.py:425
  168.2 15.7 %all-to-all-start.10 = ((bf16[32,16,256]{2,1,0:T(8,128)(2,1)}), bf16[32,16,256]{2,1,0:T(8,128)(2,1)S(1)}, u32[]{:S(2)}, u32[]{:S(2)}) async-start(bf16[32,16,256]{2,1,0:T(8,128)(2,1)} %get-tuple-element.78), calls=%async_computation.10 | async-start | bytes 524288 | tf_op jit(solution)/shard_map/all_to_all | solution.py:425
  186.8 16.1 %all-to-all-start.11 = ((bf16[32,16,256]{2,1,0:T(8,128)(2,1)}), bf16[32,16,256]{2,1,0:T(8,128)(2,1)S(1)}, u32[]{:S(2)}, u32[]{:S(2)}) async-start(bf16[32,16,256]{2,1,0:T(8,128)(2,1)} %get-tuple-element.84), calls=%async_computation.11 | async-start | bytes 524288 | tf_op jit(solution)/shard_map/all_to_all | solution.py:425
  207.1 14.5 %all-to-all-start.12 = ((bf16[32,16,256]{2,1,0:T(8,128)(2,1)}), bf16[32,16,256]{2,1,0:T(8,128)(2,1)S(1)}, u32[]{:S(2)}, u32[]{:S(2)}) async-start(bf16[32,16,256]{2,1,0:T(8,128)(2,1)} %get-tuple-element.91), calls=%async_computation.12 | async-start | bytes 524288 | tf_op jit(solution)/shard_map/all_to_all | solution.py:425
  224.4 16.2 %all-to-all-start.13 = ((bf16[32,16,256]{2,1,0:T(8,128)(2,1)}), bf16[32,16,256]{2,1,0:T(8,128)(2,1)S(1)}, u32[]{:S(2)}, u32[]{:S(2)}) async-start(bf16[32,16,256]{2,1,0:T(8,128)(2,1)} %get-tuple-element.98), calls=%async_computation.13 | async-start | bytes 524288 | tf_op jit(solution)/shard_map/all_to_all | solution.py:425
  243.3 15.7 %all-to-all-start.14 = ((bf16[32,16,256]{2,1,0:T(8,128)(2,1)}), bf16[32,16,256]{2,1,0:T(8,128)(2,1)S(1)}, u32[]{:S(2)}, u32[]{:S(2)}) async-start(bf16[32,16,256]{2,1,0:T(8,128)(2,1)} %get-tuple-element.105), calls=%async_computation.14 | async-start | bytes 524288 | tf_op jit(solution)/shard_map/all_to_all | solution.py:425
  261.7 15.6 %all-to-all-start.15 = ((bf16[32,16,256]{2,1,0:T(8,128)(2,1)}), bf16[32,16,256]{2,1,0:T(8,128)(2,1)S(1)}, u32[]{:S(2)}, u32[]{:S(2)}) async-start(bf16[32,16,256]{2,1,0:T(8,128)(2,1)} %get-tuple-element.112), calls=%async_computation.15 | async-start | bytes 524288 | tf_op jit(solution)/shard_map/all_to_all | solution.py:425
Sparse Core Ops, SparseCore 0:
  9.7 138.9 all-gather.10
  150.5 72.2 all-gather.8
  224.6 43.8 all-gather.6

commit v10 on v9

--- a/solution.py
+++ b/solution.py
@@ -210,8 +210,10 @@
     return store[index]
 
 
-def older_kernel(first, line, at, newest, table, blocks, *rest):
-    *stores, out, found, ready, room, sems, ready_sems = rest
+def older_kernel(first, line, at, newest, levels, table, blocks, *rest):
+    inverses, rest = rest[: len(levels)], rest[len(levels) :]
+    *stores, out, found, ready, diag, room, sems, ready_sems, end_sems = rest
+    ends = fetch_ends(inverses, levels, diag, end_sems)
     ncol, slots = blocks.shape[0], blocks.shape[2]
     cap = ready.shape[0]
     copies = []
@@ -243,27 +245,32 @@
     def _(j):
         pltpu.make_async_copy(blocks.at[0, at, 0], ready.at[j], ready_sems.at[j]).wait()
 
-
-def older(ready, first, line, at, newest, table, blocks, stores, part):
+    for end in ends:
+        end.wait()
+
+
+def older(ready, first, line, at, newest, levels, inverses, table, blocks, stores, part):
     ncol, _, slots, size, _ = blocks.shape
     return pl.pallas_call(
-        functools.partial(older_kernel, first, line, at, newest),
+        functools.partial(older_kernel, first, line, at, newest, levels),
         out_shape=[
             pltpu.VMEM((part, size), F32),
             jax.ShapeDtypeStruct((64,), I32),
             pltpu.VMEM((ready, size, size), BF),
+            pltpu.VMEM((len(levels), size, size), BF),
         ],
-        in_specs=[SMEM, ANY] + [VMEM] * len(stores),
-        out_specs=[VMEM, SMEM, VMEM],
+        in_specs=[SMEM, ANY] + [ANY] * len(levels) + [VMEM] * len(stores),
+        out_specs=[VMEM, SMEM, VMEM, VMEM],
         scratch_shapes=[
             pltpu.VMEM((ncol if stores else 1, slots, size, size), BF),
             pltpu.SemaphoreType.DMA((ncol,)),
             pltpu.SemaphoreType.DMA((ready,)),
+            pltpu.SemaphoreType.DMA((len(levels),)),
         ],
         compiler_params=params(10),
         cost_estimate=pl.CostEstimate(flops=2 * ncol * slots * part * size * size, bytes_accessed=13 << 20, transcendentals=0),
         name="older",
-    )(table, hbm(blocks), *stores)
+    )(table, hbm(blocks), *[hbm(ref) for ref in inverses], *stores)
 
 
 def fetch_ends(inverses, levels, diag, sems):
@@ -275,31 +282,21 @@
     )
 
 
-def finish_row(total, right, level, ends, diag, rest):
+def finish_row(total, right, level, diag, rest):
     solved = ((right[level] if len(right.shape) > 2 else right[...]).astype(F32) - total).astype(BF)
-    for i, end in enumerate(ends):
-        end.wait()
+    for i in range(diag.shape[0]):
         solved = dot(solved, diag[i]).astype(BF)
-    if len(rest) > 2:
-        *done, out = rest
-        for i in range(out.shape[0]):
-            out[i, 0] = solved
-            for j, ref in enumerate(done):
-                out[i, j + 1] = ref[...]
-    else:
-        out, spread = rest
-        out[...] = solved
-        for i in range(spread.shape[0]):
-            spread[i] = solved
-
-
-def sparse_kernel(newest, line, at, levels, blocks, store, right, before, found, ready, *rest):
-    m = len(levels)
-    inverses, (*rest, diag, room, sems, end_sems) = rest[:m], rest[m:]
+    for i in range(rest[-1].shape[0]):
+        rest[-1][i] = solved
+    if len(rest) > 1:
+        rest[0][...] = solved
+
+
+def sparse_kernel(at, level, blocks, store, right, before, found, ready, diag, *rest):
+    *rest, room, sems = rest
     ncol, slots = blocks.shape[0], blocks.shape[2]
     cap = ready.shape[0]
     n = found[ncol * slots]
-    ends = fetch_ends(inverses, levels, diag, end_sems)
 
     def fetch(j):
         i = found[j] // 32
@@ -334,35 +331,33 @@
     total = lax.fori_loop(
         0, (more + STEP - 1) // STEP, lambda k, total: some(cap, n, lambda j: room[j - cap], k, total), total
     )
-    finish_row(total, right, levels[0], ends, diag, rest)
-
-
-def solve(newest, line, at, levels, table, blocks, store, right, before, inverses, done=()):
+    finish_row(total, right, level, diag, rest)
+
+
+def solve(at, level, blocks, store, right, before, final=False):
     part, size = right.shape[-2:]
     ncol, slots = blocks.shape[0], blocks.shape[2]
     width = store.shape[0]
-    if done:
-        out_shape = jax.ShapeDtypeStruct((ncol, len(done) + 1, part, size), BF)
+    if final:
+        out_shape = jax.ShapeDtypeStruct((ncol, part, size), BF)
         out_specs = VMEM
     else:
         out_shape = [jax.ShapeDtypeStruct((part, size), BF), jax.ShapeDtypeStruct((width, part, size), BF)]
         out_specs = [VMEM, VMEM]
     copies = ncol * slots - before[2].shape[0]
     return pl.pallas_call(
-        functools.partial(sparse_kernel, newest, line, at, levels),
+        functools.partial(sparse_kernel, at, level),
         out_shape=out_shape,
-        in_specs=[ANY, VMEM, VMEM, VMEM, SMEM, VMEM] + [ANY] * len(inverses) + [VMEM] * len(done),
+        in_specs=[ANY, VMEM, VMEM, VMEM, SMEM, VMEM, VMEM],
         out_specs=out_specs,
         scratch_shapes=[
-            pltpu.VMEM((len(inverses), size, size), BF),
             pltpu.VMEM((copies, size, size), BF),
             pltpu.SemaphoreType.DMA((copies,)),
-            pltpu.SemaphoreType.DMA((len(inverses),)),
         ],
         compiler_params=params(10),
         cost_estimate=pl.CostEstimate(flops=2 * ncol * slots * part * size * size, bytes_accessed=4 << 20, transcendentals=0),
         name="solve",
-    )(hbm(blocks), store, right, *before, *[hbm(ref) for ref in inverses], *done)
+    )(hbm(blocks), store, right, *before)
 
 
 def shards(
@@ -439,36 +434,39 @@
         if level < last:
             stores.append(spread(copies))
 
-    def step(line, olds, first, newest, copies):
+    def step(line, olds, first, newest, levels, inverses, copies):
         blocks, at = gathered[line]
         copies, tied = lax.optimization_barrier((copies, table))
-        before = older(READY[line], first, line, at, newest, tied, blocks, olds, part)
+        before = older(READY[line], first, line, at, newest, levels, inverses, tied, blocks, olds, part)
         return spread(copies), before
 
     line = 0
     for level in range(last + 1, levels):
-        newest, before = step(line, stores, 0, level - 1, copies)
-        ends = [lower_inverse], [level]
+        ends = [level], [lower_inverse]
         if level == levels - 1:
-            ends = [lower_inverse, upper_inverse], [level, level]
+            ends = [level, level], [lower_inverse, upper_inverse]
+        newest, before = step(line, stores, 0, level - 1, *ends, copies)
         blocks, at = gathered[line]
-        solved, copies = solve(level - 1, line, at, ends[1], table, blocks, newest, right, before, ends[0])
+        solved, copies = solve(at, level, blocks, newest, right, before)
         own.append(solved)
         stores.append(newest)
         line += 1
     result, stores = [solved], []
     for level in range(levels - 2, -1, -1):
-        newest, before = step(line, stores, level + 2, level + 1, copies)
+        newest, before = step(line, stores, level + 2, level + 1, [level], [upper_inverse], copies)
         blocks, at = gathered[line]
-        done = result if level == 0 else ()
-        solved = solve(level + 1, line, at, [level], table, blocks, newest, own[level], before, [upper_inverse], done)
-        if level > 0:
-            solved, copies = solved
+        if level == 0:
+            done = jnp.broadcast_to(jnp.stack(result)[None], (4, levels - 1, part, size))
+            done = lax.all_gather(done, COL, axis=0)[:, 0]
+            copies = solve(at, level, blocks, newest, own[level], before, True)
+            whole = lax.all_to_all(copies, COL, 0, 0, tiled=True)
+        else:
+            solved, copies = solve(at, level, blocks, newest, own[level], before)
             result.insert(0, solved)
             stores.insert(0, newest)
         line += 1
-    whole = lax.all_to_all(solved, COL, 0, 0, tiled=True)
-    return jnp.transpose(whole, (1, 0, 2, 3)).reshape(1, levels, nrhs, size)
+    whole = jnp.concatenate([whole[None], jnp.transpose(done, (1, 0, 2, 3))])
+    return whole.reshape(1, levels, nrhs, size)
 
 
 def solution(mesh):

time: 306 us -> 311 us (1.016)
  starting transfers between devices: 55.4 us -> 68.1 us
    all_to_all x1 -> x0, blocking collectives: 17 us -> none  [shards(): whole = lax.all_to_all(solved, COL, 0, 0, tiled=True)]
    all_gather x0 -> x1, blocking collectives: none -> 13.6 us  [shards(): done = lax.all_gather(done, COL, axis=0)[:, 0]]
    all_to_all x0 -> x1, starting transfers between devices: none -> 9.95 us  [shards(): whole = lax.all_to_all(copies, COL, 0, 0, tiled=True)]
  transfers between devices with their start and end apart: 12 -> 13, of which waited for: 10 -> 10; matrix products, arithmetic and copies ran while one was open for 0% -> 0% of each run, Pallas kernels for 23% -> 22%
where the time goes in v10:
time: 311 us
  blocking collectives  103 us (33%)
  Pallas kernels  72.2 us (23%)
  starting transfers between devices  68.1 us (22%)
  waiting for transfers between devices  50.7 us (16%)
  between operations  13.5 us (4%)
    all_to_all x8, starting transfers between devices, spread(): return lax.all_to_all(copies, TURNED, 0, 0, tiled=True)  51.3 us
    pallas_call x7, Pallas kernels, older(): pl.pallas_call(functools.partial(older_kernel, first, line, at, newest, l...  43.7 us
    all_to_all x8, waiting for transfers between devices, spread(): return lax.all_to_all(copies, TURNED, 0, 0, tiled=True)  39.1 us
    all_to_all x2, blocking collectives, by_column(): lax.all_to_all(whole.reshape(ncol, group, part, size), COL, 0, 0, tiled=T...  30.5 us
    all_to_all x3, blocking collectives, shards(): parts = lax.all_to_all(partial, COL, 0, 0, tiled=True)  30.4 us
    all_to_all x2, blocking collectives, spread(): return lax.all_to_all(copies, TURNED, 0, 0, tiled=True)  28.3 us
    pallas_call x7, Pallas kernels, solve(): pl.pallas_call(functools.partial(sparse_kernel, at, level), out_shape=out...  17.6 us
    all_gather x1, blocking collectives, shards(): done = lax.all_gather(done, COL, axis=0)[:, 0]  13.6 us
  transfers between devices with their start and end apart: 13, of which 10 were waited for; matrix products, arithmetic and copies ran while one was open for 0% of the time, Pallas kernels for 22%

profile of v10, /device:TPU:1, one launch (start us, length us, event | category | flops | bytes accessed | tf_op | source)
XLA Modules:
  0.0 310.7 jit_solution(6059457148817996471)
XLA Ops:
  9.6 3.8 %begin.1 = (bf16[2,6,256,256]{3,2,1,0:T(8,128)(2,1)}, bf16[1,6,256,256]{3,2,1,0:T(8,128)(2,1)}, bf16[6,16,256]{2,1,0:T(8,128)(2,1)S(1)}, bf16[16,256]{1,0:T(8,128)(2,1)S(1)}, bf16[32,16,256]{2,1,0:T(8,128)(2,1)}) custom-call(s32[1]{0:T(128)} %bitcast.column, bf16[1,5,6,256,256]{4,3,2,1,0:T(8,128)(2,1)} %blocks.5, bf16[1,5,6,256,256]{4,3,2,1,0:T(8,128)(2,1)} %high_blocks.3, ...), custom_call_target="tpu_custom_call" | custom-call | tf_op jit(solution)/shard_map/begin/pallas_call | solution.py:112
  14.2 12.3 %all-to-all-start = ((bf16[32,16,256]{2,1,0:T(8,128)(2,1)}), bf16[32,16,256]{2,1,0:T(8,128)(2,1)}, u32[]{:S(2)}, u32[]{:S(2)}) async-start(bf16[32,16,256]{2,1,0:T(8,128)(2,1)} %get-tuple-element.73), calls=%async_computation | async-start | bytes 524288 | tf_op jit(solution)/shard_map/all_to_all | solution.py:420
  26.6 11.1 %all-to-all-done.rest_1_.rest_2_ = bf16[32,16,256]{2,1,0:T(8,128)(2,1)} async-done(((bf16[32,16,256]{2,1,0:T(8,128)(2,1)}), bf16[32,16,256]{2,1,0:T(8,128)(2,1)}, u32[]{:S(2)}, u32[]{:S(2)}) %all-to-all-start) | async-done | bytes 262176 | tf_op jit(solution)/shard_map/all_to_all | solution.py:420
  37.7 6.7 %all-to-all-start.1 = ((bf16[8,4,16,256]{3,2,1,0:T(8,128)(2,1)}), bf16[8,4,16,256]{3,2,1,0:T(8,128)(2,1)S(1)}, u32[]{:S(2)}, u32[]{:S(2)}) async-start(bf16[8,4,16,256]{3,2,1,0:T(8,128)(2,1)} %bitcast.5), calls=%async_computation.1 | async-start | bytes 524288 | tf_op jit(solution)/shard_map/all_to_all | solution.py:423
  44.6 9.5 %all-to-all-done.1.rest_0_ = bf16[8,4,16,256]{3,2,1,0:T(8,128)(2,1)S(1)} async-done(((bf16[8,4,16,256]{3,2,1,0:T(8,128)(2,1)}), bf16[8,4,16,256]{3,2,1,0:T(8,128)(2,1)S(1)}, u32[]{:S(2)}, u32[]{:S(2)}) %all-to-all-start.1) | async-done | bytes 262176 | tf_op jit(solution)/shard_map/all_to_all | solution.py:423
  57.3 11.8 %all_to_all.85.parts = f32[8,24,256]{2,1,0:T(8,128)S(1)} all-to-all(f32[8,24,256]{2,1,0:T(8,128)S(1)} %update.3), channel_id=1, replica_groups=mesh['g'=4,'z'=8,'x'=4,'core'=2] {'x','core'}, dimensions={0} | all-to-all | bytes 393216 | tf_op jit(solution)/shard_map/all_to_all | solution.py:429
  69.3 14.2 %all_to_all.86.rest_2_.rest_3_ = bf16[32,16,256]{2,1,0:T(8,128)(2,1)S(1)} all-to-all(bf16[32,16,256]{2,1,0:T(8,128)(2,1)S(1)} %get-tuple-element.75), channel_id=1, replica_groups=mesh['g'=4,'z'=8,'x'=4,'core'=2] {'z','g'}, dimensions={0} | all-to-all | bytes 524288 | tf_op jit(solution)/shard_map/all_to_all | solution.py:420
  83.6 15.1 %all_to_all.87.rest_1_ = bf16[8,4,16,256]{3,2,1,0:T(8,128)(2,1)S(1)} all-to-all(bf16[8,4,16,256]{3,2,1,0:T(8,128)(2,1)S(1)} %bitcast.86), channel_id=1, replica_groups=mesh['g'=4,'z'=8,'x'=4,'core'=2] {'x','core'}, dimensions={0} | all-to-all | bytes 524288 | tf_op jit(solution)/shard_map/all_to_all | solution.py:423
  99.7 10.0 %all_to_all.88.parts = f32[8,16,256]{2,1,0:T(8,128)S(1)} all-to-all(f32[8,16,256]{2,1,0:T(8,128)S(1)} %update.4), channel_id=1, replica_groups=mesh['g'=4,'z'=8,'x'=4,'core'=2] {'x','core'}, dimensions={0} | all-to-all | bytes 262144 | tf_op jit(solution)/shard_map/all_to_all | solution.py:429
  109.9 14.1 %all_to_all.89.rest_3_.rest_4_ = bf16[32,16,256]{2,1,0:T(8,128)(2,1)S(1)} all-to-all(bf16[32,16,256]{2,1,0:T(8,128)(2,1)S(1)} %get-tuple-element.76), channel_id=1, replica_groups=mesh['g'=4,'z'=8,'x'=4,'core'=2] {'z','g'}, dimensions={0} | all-to-all | bytes 524288 | tf_op jit(solution)/shard_map/all_to_all | solution.py:420
  124.0 15.5 %all_to_all.90.rest_2_ = bf16[8,4,16,256]{3,2,1,0:T(8,128)(2,1)S(1)} all-to-all(bf16[8,4,16,256]{3,2,1,0:T(8,128)(2,1)S(1)} %bitcast.87), channel_id=1, replica_groups=mesh['g'=4,'z'=8,'x'=4,'core'=2] {'x','core'}, dimensions={0} | all-to-all | bytes 524288 | tf_op jit(solution)/shard_map/all_to_all | solution.py:423
  140.5 8.6 %all_to_all.91.parts = f32[8,16,256]{2,1,0:T(8,128)S(1)} all-to-all(f32[8,16,256]{2,1,0:T(8,128)S(1)} %update.5), channel_id=1, replica_groups=mesh['g'=4,'z'=8,'x'=4,'core'=2] {'x','core'}, dimensions={0} | all-to-all | bytes 262144 | tf_op jit(solution)/shard_map/all_to_all | solution.py:429
  149.9 5.0 %all-to-all-start.9 = ((bf16[32,16,256]{2,1,0:T(8,128)(2,1)}), bf16[32,16,256]{2,1,0:T(8,128)(2,1)S(1)}, u32[]{:S(2)}, u32[]{:S(2)}) async-start(bf16[32,16,256]{2,1,0:T(8,128)(2,1)} %get-tuple-element.79), calls=%async_computation.9 | async-start | bytes 524288 | tf_op jit(solution)/shard_map/all_to_all | solution.py:420
  154.9 6.8 %older.7 = (f32[16,256]{1,0:T(8,128)S(1)}, s32[64]{0:T(128)S(1)}, bf16[12,256,256]{2,1,0:T(8,128)(2,1)S(1)}, bf16[1,256,256]{2,1,0:T(8,128)(2,1)S(1)}) custom-call(s32[8,128]{1,0:T(8,128)S(1)} %get-tuple-element.127.table, bf16[8,4,6,256,256]{4,3,2,1,0:T(8,128)(2,1)} %bitcast.88, bf16[1,6,256,256]{3,2,1,0:T(8,128)(2,1)} %rest_0_.8, ...), custom_call_target="tpu_custom_call" | custom-call | flops 100663296 | bytes 13631488 | tf_op jit(solution)/shard_map/older/pallas_call | solution.py:254
  161.7 3.8 %all-to-all-done.9.store.rest_5_ = bf16[32,16,256]{2,1,0:T(8,128)(2,1)S(1)} async-done(((bf16[32,16,256]{2,1,0:T(8,128)(2,1)}), bf16[32,16,256]{2,1,0:T(8,128)(2,1)S(1)}, u32[]{:S(2)}, u32[]{:S(2)}) %all-to-all-start.9) | async-done | bytes 262176 | tf_op jit(solution)/shard_map/all_to_all | solution.py:420
  167.8 5.7 %all-to-all-start.10 = ((bf16[32,16,256]{2,1,0:T(8,128)(2,1)}), bf16[32,16,256]{2,1,0:T(8,128)(2,1)S(1)}, u32[]{:S(2)}, u32[]{:S(2)}) async-start(bf16[32,16,256]{2,1,0:T(8,128)(2,1)} %get-tuple-element.86), calls=%async_computation.10 | async-start | bytes 524288 | tf_op jit(solution)/shard_map/all_to_all | solution.py:420
  173.5 6.9 %older.8 = (f32[16,256]{1,0:T(8,128)S(1)}, s32[64]{0:T(128)S(1)}, bf16[12,256,256]{2,1,0:T(8,128)(2,1)S(1)}, bf16[2,256,256]{2,1,0:T(8,128)(2,1)S(1)}) custom-call(s32[8,128]{1,0:T(8,128)S(1)} %get-tuple-element.127.table, bf16[8,4,6,256,256]{4,3,2,1,0:T(8,128)(2,1)} %bitcast.90, bf16[1,6,256,256]{3,2,1,0:T(8,128)(2,1)} %rest_0_.8, ...), custom_call_target="tpu_custom_call" | custom-call | flops 100663296 | bytes 13631488 | tf_op jit(solution)/shard_map/older/pallas_call | solution.py:254
  180.4 3.5 %all-to-all-done.10.store = bf16[32,16,256]{2,1,0:T(8,128)(2,1)S(1)} async-done(((bf16[32,16,256]{2,1,0:T(8,128)(2,1)}), bf16[32,16,256]{2,1,0:T(8,128)(2,1)S(1)}, u32[]{:S(2)}, u32[]{:S(2)}) %all-to-all-start.10) | async-done | bytes 262176 | tf_op jit(solution)/shard_map/all_to_all | solution.py:420
  186.3 5.5 %all-to-all-start.11 = ((bf16[32,16,256]{2,1,0:T(8,128)(2,1)}), bf16[32,16,256]{2,1,0:T(8,128)(2,1)S(1)}, u32[]{:S(2)}, u32[]{:S(2)}) async-start(bf16[32,16,256]{2,1,0:T(8,128)(2,1)} %get-tuple-element.93), calls=%async_computation.11 | async-start | bytes 524288 | tf_op jit(solution)/shard_map/all_to_all | solution.py:420
  195.2 7.2 %all-to-all-done.11.store.rest_1_.rest_2_.rest_3_.rest_4_ = bf16[32,16,256]{2,1,0:T(8,128)(2,1)S(1)} async-done(((bf16[32,16,256]{2,1,0:T(8,128)(2,1)}), bf16[32,16,256]{2,1,0:T(8,128)(2,1)S(1)}, u32[]{:S(2)}, u32[]{:S(2)}) %all-to-all-start.11) | async-done | bytes 262176 | tf_op jit(solution)/shard_map/all_to_all | solution.py:420
  205.7 4.8 %all-to-all-start.12 = ((bf16[32,16,256]{2,1,0:T(8,128)(2,1)}), bf16[32,16,256]{2,1,0:T(8,128)(2,1)S(1)}, u32[]{:S(2)}, u32[]{:S(2)}) async-start(bf16[32,16,256]{2,1,0:T(8,128)(2,1)} %get-tuple-element.101), calls=%async_computation.12 | async-start | bytes 524288 | tf_op jit(solution)/shard_map/all_to_all | solution.py:420
  210.5 6.9 %older.10 = (f32[16,256]{1,0:T(8,128)S(1)}, s32[64]{0:T(128)S(1)}, bf16[20,256,256]{2,1,0:T(8,128)(2,1)S(1)}, bf16[1,256,256]{2,1,0:T(8,128)(2,1)S(1)}) custom-call(s32[8,128]{1,0:T(8,128)S(1)} %get-tuple-element.127.table, bf16[8,4,6,256,256]{4,3,2,1,0:T(8,128)(2,1)} %bitcast.94, bf16[1,6,256,256]{3,2,1,0:T(8,128)(2,1)} %rest_0_.13, ...), custom_call_target="tpu_custom_call" | custom-call | flops 100663296 | bytes 13631488 | tf_op jit(solution)/shard_map/older/pallas_call | solution.py:254
  217.4 3.6 %all-to-all-done.12.store.rest_1_.rest_2_.rest_3_ = bf16[32,16,256]{2,1,0:T(8,128)(2,1)S(1)} async-done(((bf16[32,16,256]{2,1,0:T(8,128)(2,1)}), bf16[32,16,256]{2,1,0:T(8,128)(2,1)S(1)}, u32[]{:S(2)}, u32[]{:S(2)}) %all-to-all-start.12) | async-done | bytes 262176 | tf_op jit(solution)/shard_map/all_to_all | solution.py:420
  223.6 6.9 %all-to-all-start.13 = ((bf16[32,16,256]{2,1,0:T(8,128)(2,1)}), bf16[32,16,256]{2,1,0:T(8,128)(2,1)S(1)}, u32[]{:S(2)}, u32[]{:S(2)}) async-start(bf16[32,16,256]{2,1,0:T(8,128)(2,1)} %get-tuple-element.109), calls=%async_computation.13 | async-start | bytes 524288 | tf_op jit(solution)/shard_map/all_to_all | solution.py:420
  230.5 6.8 %older.11 = (f32[16,256]{1,0:T(8,128)S(1)}, s32[64]{0:T(128)S(1)}, bf16[16,256,256]{2,1,0:T(8,128)(2,1)S(1)}, bf16[1,256,256]{2,1,0:T(8,128)(2,1)S(1)}) custom-call(s32[8,128]{1,0:T(8,128)S(1)} %get-tuple-element.127.table, bf16[8,2,6,256,256]{4,3,2,1,0:T(8,128)(2,1)} %bitcast.96, bf16[1,6,256,256]{3,2,1,0:T(8,128)(2,1)} %rest_0_.13, ...), custom_call_target="tpu_custom_call" | custom-call | flops 100663296 | bytes 13631488 | tf_op jit(solution)/shard_map/older/pallas_call | solution.py:254
  243.4 5.4 %all-to-all-start.14 = ((bf16[32,16,256]{2,1,0:T(8,128)(2,1)}), bf16[32,16,256]{2,1,0:T(8,128)(2,1)S(1)}, u32[]{:S(2)}, u32[]{:S(2)}) async-start(bf16[32,16,256]{2,1,0:T(8,128)(2,1)} %get-tuple-element.117), calls=%async_computation.14 | async-start | bytes 524288 | tf_op jit(solution)/shard_map/all_to_all | solution.py:420
  248.9 6.5 %older.12 = (f32[16,256]{1,0:T(8,128)S(1)}, s32[64]{0:T(128)S(1)}, bf16[14,256,256]{2,1,0:T(8,128)(2,1)S(1)}, bf16[1,256,256]{2,1,0:T(8,128)(2,1)S(1)}) custom-call(s32[8,128]{1,0:T(8,128)S(1)} %get-tuple-element.127.table, bf16[8,2,6,256,256]{4,3,2,1,0:T(8,128)(2,1)} %bitcast.98, bf16[1,6,256,256]{3,2,1,0:T(8,128)(2,1)} %rest_0_.13, ...), custom_call_target="tpu_custom_call" | custom-call | flops 100663296 | bytes 13631488 | tf_op jit(solution)/shard_map/older/pallas_call | solution.py:254
  255.4 3.9 %all-to-all-done.14.store.rest_1_ = bf16[32,16,256]{2,1,0:T(8,128)(2,1)S(1)} async-done(((bf16[32,16,256]{2,1,0:T(8,128)(2,1)}), bf16[32,16,256]{2,1,0:T(8,128)(2,1)S(1)}, u32[]{:S(2)}, u32[]{:S(2)}) %all-to-all-start.14) | async-done | bytes 262176 | tf_op jit(solution)/shard_map/all_to_all | solution.py:420
  261.6 5.6 %all-to-all-start.15 = ((bf16[32,16,256]{2,1,0:T(8,128)(2,1)}), bf16[32,16,256]{2,1,0:T(8,128)(2,1)S(1)}, u32[]{:S(2)}, u32[]{:S(2)}) async-start(bf16[32,16,256]{2,1,0:T(8,128)(2,1)} %get-tuple-element.125), calls=%async_computation.15 | async-start | bytes 524288 | tf_op jit(solution)/shard_map/all_to_all | solution.py:420
  268.5 6.5 %older.13 = (f32[16,256]{1,0:T(8,128)S(1)}, s32[64]{0:T(128)S(1)}, bf16[10,256,256]{2,1,0:T(8,128)(2,1)S(1)}, bf16[1,256,256]{2,1,0:T(8,128)(2,1)S(1)}) custom-call(s32[8,128]{1,0:T(8,128)S(1)} %get-tuple-element.127.table, bf16[8,1,6,256,256]{4,3,2,1,0:T(8,128)(2,1)} %bitcast.100, bf16[1,6,256,256]{3,2,1,0:T(8,128)(2,1)} %rest_0_.13, ...), custom_call_target="tpu_custom_call" | custom-call | flops 100663296 | bytes 13631488 | tf_op jit(solution)/shard_map/older/pallas_call | solution.py:254
  279.8 10.0 %all-to-all-start.16 = ((bf16[8,16,256]{2,1,0:T(8,128)(2,1)}), bf16[8,16,256]{2,1,0:T(8,128)(2,1)S(1)}, u32[]{:S(2)}, u32[]{:S(2)}) async-start(bf16[8,16,256]{2,1,0:T(8,128)(2,1)} %solve.13), calls=%async_computation.16 | async-start | bytes 131072 | tf_op jit(solution)/shard_map/all_to_all | solution.py:462
  289.8 13.6 %all-gather.3 = bf16[40,16,256]{2,1,0:T(8,128)(2,1)S(1)} all-gather(bf16[5,16,256]{2,1,0:T(8,128)(2,1)S(1)} %constant_dynamic-update-slice_fusion), channel_id=6, replica_groups=mesh['g'=4,'z'=8,'x'=4,'core'=2] {'x','core'}, dimensions={0}, use_global_device_ids=true | all-gather | bytes 368640 | tf_op jit(solution)/shard_map/all_gather | solution.py:460
  (55 shorter events, 39.7 us)
Async XLA Ops:
  6.5 148.4 %all-gather.12.cloned.1.call-start = ((), (), s32[]{:S(2)}) async-start(), calls=%async_computation.19 | async-start | bytes 28311552 | tf_op jit(solution)/shard_map/all_gather | solution.py:398
  9.5 221.0 %all-gather.10.cloned.1.call-start = ((), (), s32[]{:S(2)}) async-start(), calls=%async_computation.18 | async-start | bytes 14155776 | tf_op jit(solution)/shard_map/all_gather | solution.py:398
  13.4 13.1 %copy-start.4 = (s32[1,5,6]{2,0,1:T(1,128)S(1)}, s32[1,5,6]{2,0,1:T(1,128)}, u32[]{:S(2)}) copy-start(s32[1,5,6]{2,0,1:T(1,128)} %param.13) | copy-start | bytes 364
  13.4 13.1 %copy-start.6 = (s32[1,5,1]{1,2,0:T(1,128)S(1)}, s32[1,5,1]{1,2,0:T(1,128)}, u32[]{:S(2)}) copy-start(s32[1,5,1]{1,2,0:T(1,128)} %param.14) | copy-start | bytes 64
  13.4 31.0 %copy-start.3 = (s32[1,5,6]{2,0,1:T(1,128)S(1)}, s32[1,5,6]{2,0,1:T(1,128)}, u32[]{:S(2)}) copy-start(s32[1,5,6]{2,0,1:T(1,128)} %param.16) | copy-start | bytes 364
  13.4 31.0 %copy-start.5 = (s32[1,5,1]{1,2,0:T(1,128)S(1)}, s32[1,5,1]{1,2,0:T(1,128)}, u32[]{:S(2)}) copy-start(s32[1,5,1]{1,2,0:T(1,128)} %param.17) | copy-start | bytes 64
  13.4 255.1 %all-gather.8.cloned.1.call-start = ((), (), s32[]{:S(2)}) async-start(), calls=%async_computation.17 | async-start | bytes 7077888 | tf_op jit(solution)/shard_map/all_gather | solution.py:398
  14.2 55.0 %copy-start.2 = (bf16[1,6,256,256]{3,2,1,0:T(8,128)(2,1)S(1)}, bf16[1,6,256,256]{3,2,1,0:T(8,128)(2,1)}, u32[]{:S(2)}) copy-start(bf16[1,6,256,256]{3,2,1,0:T(8,128)(2,1)} %rest_0_.8) | copy-start | bytes 2359300
  14.2 23.5 %all-to-all-start = ((bf16[32,16,256]{2,1,0:T(8,128)(2,1)}), bf16[32,16,256]{2,1,0:T(8,128)(2,1)}, u32[]{:S(2)}, u32[]{:S(2)}) async-start(bf16[32,16,256]{2,1,0:T(8,128)(2,1)} %get-tuple-element.73), calls=%async_computation | async-start | bytes 524288 | tf_op jit(solution)/shard_map/all_to_all | solution.py:420
  37.7 16.5 %all-to-all-start.1 = ((bf16[8,4,16,256]{3,2,1,0:T(8,128)(2,1)}), bf16[8,4,16,256]{3,2,1,0:T(8,128)(2,1)S(1)}, u32[]{:S(2)}, u32[]{:S(2)}) async-start(bf16[8,4,16,256]{3,2,1,0:T(8,128)(2,1)} %bitcast.5), calls=%async_computation.1 | async-start | bytes 524288 | tf_op jit(solution)/shard_map/all_to_all | solution.py:423
  54.2 2.2 copy-start
  56.3 42.3 %copy-start.1 = (bf16[1,5,6,256,256]{4,3,2,1,0:T(8,128)(2,1)S(1)}, bf16[1,5,6,256,256]{4,3,2,1,0:T(8,128)(2,1)}, u32[]{:S(2)}) copy-start(bf16[1,5,6,256,256]{4,3,2,1,0:T(8,128)(2,1)} %blocks.5) | copy-start | bytes 11796484
  149.9 15.5 %all-to-all-start.9 = ((bf16[32,16,256]{2,1,0:T(8,128)(2,1)}), bf16[32,16,256]{2,1,0:T(8,128)(2,1)S(1)}, u32[]{:S(2)}, u32[]{:S(2)}) async-start(bf16[32,16,256]{2,1,0:T(8,128)(2,1)} %get-tuple-element.79), calls=%async_computation.9 | async-start | bytes 524288 | tf_op jit(solution)/shard_map/all_to_all | solution.py:420
  167.8 16.1 %all-to-all-start.10 = ((bf16[32,16,256]{2,1,0:T(8,128)(2,1)}), bf16[32,16,256]{2,1,0:T(8,128)(2,1)S(1)}, u32[]{:S(2)}, u32[]{:S(2)}) async-start(bf16[32,16,256]{2,1,0:T(8,128)(2,1)} %get-tuple-element.86), calls=%async_computation.10 | async-start | bytes 524288 | tf_op jit(solution)/shard_map/all_to_all | solution.py:420
  186.3 16.1 %all-to-all-start.11 = ((bf16[32,16,256]{2,1,0:T(8,128)(2,1)}), bf16[32,16,256]{2,1,0:T(8,128)(2,1)S(1)}, u32[]{:S(2)}, u32[]{:S(2)}) async-start(bf16[32,16,256]{2,1,0:T(8,128)(2,1)} %get-tuple-element.93), calls=%async_computation.11 | async-start | bytes 524288 | tf_op jit(solution)/shard_map/all_to_all | solution.py:420
  205.7 15.3 %all-to-all-start.12 = ((bf16[32,16,256]{2,1,0:T(8,128)(2,1)}), bf16[32,16,256]{2,1,0:T(8,128)(2,1)S(1)}, u32[]{:S(2)}, u32[]{:S(2)}) async-start(bf16[32,16,256]{2,1,0:T(8,128)(2,1)} %get-tuple-element.101), calls=%async_computation.12 | async-start | bytes 524288 | tf_op jit(solution)/shard_map/all_to_all | solution.py:420
  223.6 17.3 %all-to-all-start.13 = ((bf16[32,16,256]{2,1,0:T(8,128)(2,1)}), bf16[32,16,256]{2,1,0:T(8,128)(2,1)S(1)}, u32[]{:S(2)}, u32[]{:S(2)}) async-start(bf16[32,16,256]{2,1,0:T(8,128)(2,1)} %get-tuple-element.109), calls=%async_computation.13 | async-start | bytes 524288 | tf_op jit(solution)/shard_map/all_to_all | solution.py:420
  243.4 15.9 %all-to-all-start.14 = ((bf16[32,16,256]{2,1,0:T(8,128)(2,1)}), bf16[32,16,256]{2,1,0:T(8,128)(2,1)S(1)}, u32[]{:S(2)}, u32[]{:S(2)}) async-start(bf16[32,16,256]{2,1,0:T(8,128)(2,1)} %get-tuple-element.117), calls=%async_computation.14 | async-start | bytes 524288 | tf_op jit(solution)/shard_map/all_to_all | solution.py:420
  261.6 16.0 %all-to-all-start.15 = ((bf16[32,16,256]{2,1,0:T(8,128)(2,1)}), bf16[32,16,256]{2,1,0:T(8,128)(2,1)S(1)}, u32[]{:S(2)}, u32[]{:S(2)}) async-start(bf16[32,16,256]{2,1,0:T(8,128)(2,1)} %get-tuple-element.125), calls=%async_computation.15 | async-start | bytes 524288 | tf_op jit(solution)/shard_map/all_to_all | solution.py:420
  279.8 23.6 %all-to-all-start.16 = ((bf16[8,16,256]{2,1,0:T(8,128)(2,1)}), bf16[8,16,256]{2,1,0:T(8,128)(2,1)S(1)}, u32[]{:S(2)}, u32[]{:S(2)}) async-start(bf16[8,16,256]{2,1,0:T(8,128)(2,1)} %solve.13), calls=%async_computation.16 | async-start | bytes 131072 | tf_op jit(solution)/shard_map/all_to_all | solution.py:462
Sparse Core Ops, SparseCore 0:
  9.7 138.9 all-gather.11
  150.5 72.2 all-gather.9
  224.6 43.8 all-gather.7

commit v11 on v10

--- a/solution.py
+++ b/solution.py
@@ -149,7 +149,7 @@
     total = jnp.zeros((ncol * part, size), F32)
     for slot in range(blocks.shape[2]):
         total += dot(pick(stores, 0, table[level, slot], load), blocks[0, level, slot])
-    out[:, :part] = total.reshape(ncol, part, size)
+    out[:, :part] = total.reshape(ncol, part, size).astype(BF)
     if extra:
         out[:, part:] = jnp.broadcast_to(rest[0][...][None], (ncol, extra, size))
 
@@ -161,7 +161,7 @@
     extra = 0 if late is None else late.shape[0]
     return pl.pallas_call(
         functools.partial(update_kernel, level, n, extra),
-        out_shape=jax.ShapeDtypeStruct((ncol, part + extra, size), F32),
+        out_shape=jax.ShapeDtypeStruct((ncol, part + extra, size), BF),
         in_specs=[SMEM, VMEM] + [VMEM] * (n + (late is not None)),
         out_specs=VMEM,
         compiler_params=params(4),
@@ -174,9 +174,9 @@
     residual = right[level]
     part = residual.shape[0]
     if parts is not None:
-        total = parts[0, :part]
+        total = parts[0, :part].astype(F32)
         for i in range(1, parts.shape[0]):
-            total = total + parts[i, :part]
+            total = total + parts[i, :part].astype(F32)
         residual = (residual.astype(F32) - total).astype(BF)
     solved = dot(residual, inverse[0, level]).astype(BF)
     out[...] = solved
@@ -184,7 +184,7 @@
         spread[i] = solved
     if table:
         for i in range(parts.shape[0]):
-            table[0][i : i + 1] = parts[i, part : part + 1, :128].astype(I32)
+            table[0][i : i + 1] = parts[i, part : part + 1, :128].astype(F32).astype(I32)
 
 
 def finish(level, parts, right, inverse, width):
@@ -286,10 +286,17 @@
     solved = ((right[level] if len(right.shape) > 2 else right[...]).astype(F32) - total).astype(BF)
     for i in range(diag.shape[0]):
         solved = dot(solved, diag[i]).astype(BF)
-    for i in range(rest[-1].shape[0]):
-        rest[-1][i] = solved
-    if len(rest) > 1:
-        rest[0][...] = solved
+    if len(rest) > 2:
+        *done, out = rest
+        for i in range(out.shape[0]):
+            out[i, 0] = solved
+            for j, ref in enumerate(done):
+                out[i, j + 1] = ref[...]
+    else:
+        out, spread = rest
+        out[...] = solved
+        for i in range(spread.shape[0]):
+            spread[i] = solved
 
 
 def sparse_kernel(at, level, blocks, store, right, before, found, ready, diag, *rest):
@@ -334,12 +341,12 @@
     finish_row(total, right, level, diag, rest)
 
 
-def solve(at, level, blocks, store, right, before, final=False):
+def solve(at, level, blocks, store, right, before, done=()):
     part, size = right.shape[-2:]
     ncol, slots = blocks.shape[0], blocks.shape[2]
     width = store.shape[0]
-    if final:
-        out_shape = jax.ShapeDtypeStruct((ncol, part, size), BF)
+    if done:
+        out_shape = jax.ShapeDtypeStruct((ncol, len(done) + 1, part, size), BF)
         out_specs = VMEM
     else:
         out_shape = [jax.ShapeDtypeStruct((part, size), BF), jax.ShapeDtypeStruct((width, part, size), BF)]
@@ -348,7 +355,7 @@
     return pl.pallas_call(
         functools.partial(sparse_kernel, at, level),
         out_shape=out_shape,
-        in_specs=[ANY, VMEM, VMEM, VMEM, SMEM, VMEM, VMEM],
+        in_specs=[ANY, VMEM, VMEM, VMEM, SMEM, VMEM, VMEM] + [VMEM] * len(done),
         out_specs=out_specs,
         scratch_shapes=[
             pltpu.VMEM((copies, size, size), BF),
@@ -357,7 +364,7 @@
         compiler_params=params(10),
         cost_estimate=pl.CostEstimate(flops=2 * ncol * slots * part * size * size, bytes_accessed=4 << 20, transcendentals=0),
         name="solve",
-    )(hbm(blocks), store, right, *before)
+    )(hbm(blocks), store, right, *before, *done)
 
 
 def shards(
@@ -414,7 +421,7 @@
             places(upper_sources, upper_counts, True)[::-1],
         ]
     ).reshape(-1)
-    late = jnp.pad(late.astype(F32)[None], ((0, 7), (0, size - late.shape[0])))
+    late = jnp.pad(late.astype(BF)[None], ((0, 15), (0, size - late.shape[0])))
 
     def spread(copies):
         return lax.all_to_all(copies, TURNED, 0, 0, tiled=True)
@@ -456,17 +463,13 @@
         newest, before = step(line, stores, level + 2, level + 1, [level], [upper_inverse], copies)
         blocks, at = gathered[line]
         if level == 0:
-            done = jnp.broadcast_to(jnp.stack(result)[None], (4, levels - 1, part, size))
-            done = lax.all_gather(done, COL, axis=0)[:, 0]
-            copies = solve(at, level, blocks, newest, own[level], before, True)
-            whole = lax.all_to_all(copies, COL, 0, 0, tiled=True)
+            whole = lax.all_to_all(solve(at, level, blocks, newest, own[level], before, result), COL, 0, 0, tiled=True)
         else:
             solved, copies = solve(at, level, blocks, newest, own[level], before)
             result.insert(0, solved)
             stores.insert(0, newest)
         line += 1
-    whole = jnp.concatenate([whole[None], jnp.transpose(done, (1, 0, 2, 3))])
-    return whole.reshape(1, levels, nrhs, size)
+    return jnp.transpose(whole, (1, 0, 2, 3)).reshape(1, levels, nrhs, size)
 
 
 def solution(mesh):

time: 311 us -> 300 us (0.965)
  starting transfers between devices: 68.1 us -> 55.8 us
    all_to_all x0 -> x1, blocking collectives: none -> 16.7 us  [shards(): lax.all_to_all(solve(at, level, blocks, newest, own[level], before, resul...]
    all_gather x1 -> x0, blocking collectives: 13.6 us -> none  [shards(): done = lax.all_gather(done, COL, axis=0)[:, 0]]
    all_to_all x1 -> x0, starting transfers between devices: 9.95 us -> none  [shards(): whole = lax.all_to_all(copies, COL, 0, 0, tiled=True)]
    all_to_all x3, blocking collectives: 30.4 us -> 27.1 us  [shards(): parts = lax.all_to_all(partial, COL, 0, 0, tiled=True)]
    all_gather x3, waiting for transfers between devices: 1.36 us -> 4.5 us  [shards(): whole = lax.all_gather(part_rows, COL, axis=0)]
  transfers between devices with their start and end apart: 13 -> 12, of which waited for: 10 -> 9; matrix products, arithmetic and copies ran while one was open for 0% -> 0% of each run, Pallas kernels for 22% -> 23%
where the time goes in v11:
time: 300 us; the launch traced here: 298 us
  blocking collectives  103 us (34%)
  Pallas kernels  72 us (24%)
  starting transfers between devices  55.8 us (19%)
  waiting for transfers between devices  51.2 us (17%)
  between operations  13.4 us (4%)
  local copies, waits for them, and re-layouts  3.12 us (1%)
    all_to_all x8, starting transfers between devices, spread(): return lax.all_to_all(copies, TURNED, 0, 0, tiled=True)  49 us
    pallas_call x7, Pallas kernels, older(): pl.pallas_call(functools.partial(older_kernel, first, line, at, newest, l...  43.5 us
    all_to_all x8, waiting for transfers between devices, spread(): return lax.all_to_all(copies, TURNED, 0, 0, tiled=True)  36.5 us
    all_to_all x2, blocking collectives, by_column(): lax.all_to_all(whole.reshape(ncol, group, part, size), COL, 0, 0, tiled=T...  30.8 us
    all_to_all x2, blocking collectives, spread(): return lax.all_to_all(copies, TURNED, 0, 0, tiled=True)  28.1 us
    all_to_all x3, blocking collectives, shards(): parts = lax.all_to_all(partial, COL, 0, 0, tiled=True)  27.1 us
    pallas_call x7, Pallas kernels, solve(): pl.pallas_call(functools.partial(sparse_kernel, at, level), out_shape=out...  17.4 us
    all_to_all x1, blocking collectives, shards(): lax.all_to_all(solve(at, level, blocks, newest, own[level], before, resul...  16.7 us
  transfers between devices with their start and end apart: 12, of which 9 were waited for; matrix products, arithmetic and copies ran while one was open for 0% of the time, Pallas kernels for 23%

profile of v11, /device:TPU:1, one launch (start us, length us, event | category | flops | bytes accessed | tf_op | source)
XLA Modules:
  0.0 298.4 jit_solution(15241727965585664849)
XLA Ops:
  9.6 3.8 %begin.1 = (bf16[2,6,256,256]{3,2,1,0:T(8,128)(2,1)}, bf16[1,6,256,256]{3,2,1,0:T(8,128)(2,1)}, bf16[6,16,256]{2,1,0:T(8,128)(2,1)S(1)}, bf16[16,256]{1,0:T(8,128)(2,1)S(1)}, bf16[32,16,256]{2,1,0:T(8,128)(2,1)}) custom-call(s32[1]{0:T(128)} %bitcast.column, bf16[1,5,6,256,256]{4,3,2,1,0:T(8,128)(2,1)} %blocks.5, bf16[1,5,6,256,256]{4,3,2,1,0:T(8,128)(2,1)} %high_blocks.3, ...), custom_call_target="tpu_custom_call" | custom-call | tf_op jit(solution)/shard_map/begin/pallas_call | solution.py:112
  14.2 12.3 %all-to-all-start = ((bf16[32,16,256]{2,1,0:T(8,128)(2,1)}), bf16[32,16,256]{2,1,0:T(8,128)(2,1)}, u32[]{:S(2)}, u32[]{:S(2)}) async-start(bf16[32,16,256]{2,1,0:T(8,128)(2,1)} %get-tuple-element.73), calls=%async_computation | async-start | bytes 524288 | tf_op jit(solution)/shard_map/all_to_all | solution.py:427
  26.6 11.1 %all-to-all-done.rest_1_.rest_2_ = bf16[32,16,256]{2,1,0:T(8,128)(2,1)} async-done(((bf16[32,16,256]{2,1,0:T(8,128)(2,1)}), bf16[32,16,256]{2,1,0:T(8,128)(2,1)}, u32[]{:S(2)}, u32[]{:S(2)}) %all-to-all-start) | async-done | bytes 262176 | tf_op jit(solution)/shard_map/all_to_all | solution.py:427
  37.7 6.7 %all-to-all-start.1 = ((bf16[8,4,16,256]{3,2,1,0:T(8,128)(2,1)}), bf16[8,4,16,256]{3,2,1,0:T(8,128)(2,1)S(1)}, u32[]{:S(2)}, u32[]{:S(2)}) async-start(bf16[8,4,16,256]{3,2,1,0:T(8,128)(2,1)} %bitcast.5), calls=%async_computation.1 | async-start | bytes 524288 | tf_op jit(solution)/shard_map/all_to_all | solution.py:430
  44.6 9.5 %all-to-all-done.1.rest_0_ = bf16[8,4,16,256]{3,2,1,0:T(8,128)(2,1)S(1)} async-done(((bf16[8,4,16,256]{3,2,1,0:T(8,128)(2,1)}), bf16[8,4,16,256]{3,2,1,0:T(8,128)(2,1)S(1)}, u32[]{:S(2)}, u32[]{:S(2)}) %all-to-all-start.1) | async-done | bytes 262176 | tf_op jit(solution)/shard_map/all_to_all | solution.py:430
  57.4 10.2 %all_to_all.85.parts = bf16[8,32,256]{2,1,0:T(8,128)(2,1)S(1)} all-to-all(bf16[8,32,256]{2,1,0:T(8,128)(2,1)S(1)} %update.3), channel_id=1, replica_groups=mesh['g'=4,'z'=8,'x'=4,'core'=2] {'x','core'}, dimensions={0} | all-to-all | bytes 262144 | tf_op jit(solution)/shard_map/all_to_all | solution.py:436
  67.7 14.0 %all_to_all.86.rest_2_.rest_3_ = bf16[32,16,256]{2,1,0:T(8,128)(2,1)S(1)} all-to-all(bf16[32,16,256]{2,1,0:T(8,128)(2,1)S(1)} %get-tuple-element.75), channel_id=1, replica_groups=mesh['g'=4,'z'=8,'x'=4,'core'=2] {'z','g'}, dimensions={0} | all-to-all | bytes 524288 | tf_op jit(solution)/shard_map/all_to_all | solution.py:427
  81.8 15.5 %all_to_all.87.rest_1_ = bf16[8,4,16,256]{3,2,1,0:T(8,128)(2,1)S(1)} all-to-all(bf16[8,4,16,256]{3,2,1,0:T(8,128)(2,1)S(1)} %bitcast.73), channel_id=1, replica_groups=mesh['g'=4,'z'=8,'x'=4,'core'=2] {'x','core'}, dimensions={0} | all-to-all | bytes 524288 | tf_op jit(solution)/shard_map/all_to_all | solution.py:430
  98.3 8.8 %all_to_all.88.parts = bf16[8,16,256]{2,1,0:T(8,128)(2,1)S(1)} all-to-all(bf16[8,16,256]{2,1,0:T(8,128)(2,1)S(1)} %update.4), channel_id=1, replica_groups=mesh['g'=4,'z'=8,'x'=4,'core'=2] {'x','core'}, dimensions={0} | all-to-all | bytes 131072 | tf_op jit(solution)/shard_map/all_to_all | solution.py:436
  107.3 14.1 %all_to_all.89.rest_3_.rest_4_ = bf16[32,16,256]{2,1,0:T(8,128)(2,1)S(1)} all-to-all(bf16[32,16,256]{2,1,0:T(8,128)(2,1)S(1)} %get-tuple-element.76), channel_id=1, replica_groups=mesh['g'=4,'z'=8,'x'=4,'core'=2] {'z','g'}, dimensions={0} | all-to-all | bytes 524288 | tf_op jit(solution)/shard_map/all_to_all | solution.py:427
  121.3 15.3 %all_to_all.90.rest_2_ = bf16[8,4,16,256]{3,2,1,0:T(8,128)(2,1)S(1)} all-to-all(bf16[8,4,16,256]{3,2,1,0:T(8,128)(2,1)S(1)} %bitcast.74), channel_id=1, replica_groups=mesh['g'=4,'z'=8,'x'=4,'core'=2] {'x','core'}, dimensions={0} | all-to-all | bytes 524288 | tf_op jit(solution)/shard_map/all_to_all | solution.py:430
  137.6 8.2 %all_to_all.91.parts = bf16[8,16,256]{2,1,0:T(8,128)(2,1)S(1)} all-to-all(bf16[8,16,256]{2,1,0:T(8,128)(2,1)S(1)} %update.5), channel_id=1, replica_groups=mesh['g'=4,'z'=8,'x'=4,'core'=2] {'x','core'}, dimensions={0} | all-to-all | bytes 131072 | tf_op jit(solution)/shard_map/all_to_all | solution.py:436
  146.7 4.3 %all-to-all-start.9 = ((bf16[32,16,256]{2,1,0:T(8,128)(2,1)}), bf16[32,16,256]{2,1,0:T(8,128)(2,1)S(1)}, u32[]{:S(2)}, u32[]{:S(2)}) async-start(bf16[32,16,256]{2,1,0:T(8,128)(2,1)} %get-tuple-element.79), calls=%async_computation.9 | async-start | bytes 524288 | tf_op jit(solution)/shard_map/all_to_all | solution.py:427
  151.0 6.9 %older.7 = (f32[16,256]{1,0:T(8,128)S(1)}, s32[64]{0:T(128)S(1)}, bf16[12,256,256]{2,1,0:T(8,128)(2,1)S(1)}, bf16[1,256,256]{2,1,0:T(8,128)(2,1)S(1)}) custom-call(s32[8,128]{1,0:T(8,128)S(1)} %get-tuple-element.127.table, bf16[8,4,6,256,256]{4,3,2,1,0:T(8,128)(2,1)} %bitcast.75, bf16[1,6,256,256]{3,2,1,0:T(8,128)(2,1)} %rest_0_.8, ...), custom_call_target="tpu_custom_call" | custom-call | flops 100663296 | bytes 13631488 | tf_op jit(solution)/shard_map/older/pallas_call | solution.py:254
  157.9 3.7 %all-to-all-done.9.store.rest_5_ = bf16[32,16,256]{2,1,0:T(8,128)(2,1)S(1)} async-done(((bf16[32,16,256]{2,1,0:T(8,128)(2,1)}), bf16[32,16,256]{2,1,0:T(8,128)(2,1)S(1)}, u32[]{:S(2)}, u32[]{:S(2)}) %all-to-all-start.9) | async-done | bytes 262176 | tf_op jit(solution)/shard_map/all_to_all | solution.py:427
  164.0 5.4 %all-to-all-start.10 = ((bf16[32,16,256]{2,1,0:T(8,128)(2,1)}), bf16[32,16,256]{2,1,0:T(8,128)(2,1)S(1)}, u32[]{:S(2)}, u32[]{:S(2)}) async-start(bf16[32,16,256]{2,1,0:T(8,128)(2,1)} %get-tuple-element.86), calls=%async_computation.10 | async-start | bytes 524288 | tf_op jit(solution)/shard_map/all_to_all | solution.py:427
  169.3 6.9 %older.8 = (f32[16,256]{1,0:T(8,128)S(1)}, s32[64]{0:T(128)S(1)}, bf16[12,256,256]{2,1,0:T(8,128)(2,1)S(1)}, bf16[2,256,256]{2,1,0:T(8,128)(2,1)S(1)}) custom-call(s32[8,128]{1,0:T(8,128)S(1)} %get-tuple-element.127.table, bf16[8,4,6,256,256]{4,3,2,1,0:T(8,128)(2,1)} %bitcast.77, bf16[1,6,256,256]{3,2,1,0:T(8,128)(2,1)} %rest_0_.8, ...), custom_call_target="tpu_custom_call" | custom-call | flops 100663296 | bytes 13631488 | tf_op jit(solution)/shard_map/older/pallas_call | solution.py:254
  181.9 5.9 %all-to-all-start.11 = ((bf16[32,16,256]{2,1,0:T(8,128)(2,1)}), bf16[32,16,256]{2,1,0:T(8,128)(2,1)S(1)}, u32[]{:S(2)}, u32[]{:S(2)}) async-start(bf16[32,16,256]{2,1,0:T(8,128)(2,1)} %get-tuple-element.93), calls=%async_computation.11 | async-start | bytes 524288 | tf_op jit(solution)/shard_map/all_to_all | solution.py:427
  191.3 7.0 %all-to-all-done.11.store.rest_1_.rest_2_.rest_3_.rest_4_ = bf16[32,16,256]{2,1,0:T(8,128)(2,1)S(1)} async-done(((bf16[32,16,256]{2,1,0:T(8,128)(2,1)}), bf16[32,16,256]{2,1,0:T(8,128)(2,1)S(1)}, u32[]{:S(2)}, u32[]{:S(2)}) %all-to-all-start.11) | async-done | bytes 262176 | tf_op jit(solution)/shard_map/all_to_all | solution.py:427
  198.2 4.0 %solve.9 = (bf16[16,256]{1,0:T(8,128)(2,1)S(1)}, bf16[32,16,256]{2,1,0:T(8,128)(2,1)}) custom-call(bf16[8,4,6,256,256]{4,3,2,1,0:T(8,128)(2,1)} %bitcast.80, bf16[32,16,256]{2,1,0:T(8,128)(2,1)S(1)} %all-to-all-done.11.store.rest_1_.rest_2_.rest_3_.rest_4_, bf16[16,256]{1,0:T(8,128)(2,1)S(1)} %get-tuple-element.94.right, ...), custom_call_target="tpu_custom_call" | custom-call | flops 100663296 | bytes 4194304 | tf_op jit(solution)/shard_map/solve/pallas_call | solution.py:355
  202.3 3.9 %all-to-all-start.12 = ((bf16[32,16,256]{2,1,0:T(8,128)(2,1)}), bf16[32,16,256]{2,1,0:T(8,128)(2,1)S(1)}, u32[]{:S(2)}, u32[]{:S(2)}) async-start(bf16[32,16,256]{2,1,0:T(8,128)(2,1)} %get-tuple-element.101), calls=%async_computation.12 | async-start | bytes 524288 | tf_op jit(solution)/shard_map/all_to_all | solution.py:427
  206.2 7.1 %older.10 = (f32[16,256]{1,0:T(8,128)S(1)}, s32[64]{0:T(128)S(1)}, bf16[20,256,256]{2,1,0:T(8,128)(2,1)S(1)}, bf16[1,256,256]{2,1,0:T(8,128)(2,1)S(1)}) custom-call(s32[8,128]{1,0:T(8,128)S(1)} %get-tuple-element.127.table, bf16[8,4,6,256,256]{4,3,2,1,0:T(8,128)(2,1)} %bitcast.81, bf16[1,6,256,256]{3,2,1,0:T(8,128)(2,1)} %rest_0_.13, ...), custom_call_target="tpu_custom_call" | custom-call | flops 100663296 | bytes 13631488 | tf_op jit(solution)/shard_map/older/pallas_call | solution.py:254
  219.4 6.0 %all-to-all-start.13 = ((bf16[32,16,256]{2,1,0:T(8,128)(2,1)}), bf16[32,16,256]{2,1,0:T(8,128)(2,1)S(1)}, u32[]{:S(2)}, u32[]{:S(2)}) async-start(bf16[32,16,256]{2,1,0:T(8,128)(2,1)} %get-tuple-element.109), calls=%async_computation.13 | async-start | bytes 524288 | tf_op jit(solution)/shard_map/all_to_all | solution.py:427
  225.4 6.5 %older.11 = (f32[16,256]{1,0:T(8,128)S(1)}, s32[64]{0:T(128)S(1)}, bf16[16,256,256]{2,1,0:T(8,128)(2,1)S(1)}, bf16[1,256,256]{2,1,0:T(8,128)(2,1)S(1)}) custom-call(s32[8,128]{1,0:T(8,128)S(1)} %get-tuple-element.127.table, bf16[8,2,6,256,256]{4,3,2,1,0:T(8,128)(2,1)} %bitcast.83, bf16[1,6,256,256]{3,2,1,0:T(8,128)(2,1)} %rest_0_.13, ...), custom_call_target="tpu_custom_call" | custom-call | flops 100663296 | bytes 13631488 | tf_op jit(solution)/shard_map/older/pallas_call | solution.py:254
  232.0 3.8 %all-to-all-done.13.store.rest_1_.rest_2_ = bf16[32,16,256]{2,1,0:T(8,128)(2,1)S(1)} async-done(((bf16[32,16,256]{2,1,0:T(8,128)(2,1)}), bf16[32,16,256]{2,1,0:T(8,128)(2,1)S(1)}, u32[]{:S(2)}, u32[]{:S(2)}) %all-to-all-start.13) | async-done | bytes 262176 | tf_op jit(solution)/shard_map/all_to_all | solution.py:427
  238.3 5.6 %all-to-all-start.14 = ((bf16[32,16,256]{2,1,0:T(8,128)(2,1)}), bf16[32,16,256]{2,1,0:T(8,128)(2,1)S(1)}, u32[]{:S(2)}, u32[]{:S(2)}) async-start(bf16[32,16,256]{2,1,0:T(8,128)(2,1)} %get-tuple-element.117), calls=%async_computation.14 | async-start | bytes 524288 | tf_op jit(solution)/shard_map/all_to_all | solution.py:427
  244.0 6.3 %older.12 = (f32[16,256]{1,0:T(8,128)S(1)}, s32[64]{0:T(128)S(1)}, bf16[14,256,256]{2,1,0:T(8,128)(2,1)S(1)}, bf16[1,256,256]{2,1,0:T(8,128)(2,1)S(1)}) custom-call(s32[8,128]{1,0:T(8,128)S(1)} %get-tuple-element.127.table, bf16[8,2,6,256,256]{4,3,2,1,0:T(8,128)(2,1)} %bitcast.85, bf16[1,6,256,256]{3,2,1,0:T(8,128)(2,1)} %rest_0_.13, ...), custom_call_target="tpu_custom_call" | custom-call | flops 100663296 | bytes 13631488 | tf_op jit(solution)/shard_map/older/pallas_call | solution.py:254
  250.3 4.1 %all-to-all-done.14.store.rest_1_ = bf16[32,16,256]{2,1,0:T(8,128)(2,1)S(1)} async-done(((bf16[32,16,256]{2,1,0:T(8,128)(2,1)}), bf16[32,16,256]{2,1,0:T(8,128)(2,1)S(1)}, u32[]{:S(2)}, u32[]{:S(2)}) %all-to-all-start.14) | async-done | bytes 262176 | tf_op jit(solution)/shard_map/all_to_all | solution.py:427
  256.4 5.6 %all-to-all-start.15 = ((bf16[32,16,256]{2,1,0:T(8,128)(2,1)}), bf16[32,16,256]{2,1,0:T(8,128)(2,1)S(1)}, u32[]{:S(2)}, u32[]{:S(2)}) async-start(bf16[32,16,256]{2,1,0:T(8,128)(2,1)} %get-tuple-element.125), calls=%async_computation.15 | async-start | bytes 524288 | tf_op jit(solution)/shard_map/all_to_all | solution.py:427
  262.0 4.5 %all-gather.7.cloned.1.call-done = bf16[8,6,256,256]{3,2,1,0:T(8,128)(2,1)} async-done(((bf16[1,6,256,256]{3,2,1,0:T(8,128)(2,1)}), bf16[8,6,256,256]{3,2,1,0:T(8,128)(2,1)}) %all-gather.7.cloned.1.call-update) | async-done | bytes 6291472 | tf_op jit(solution)/shard_map/all_gather | solution.py:405
  266.4 6.4 %older.13 = (f32[16,256]{1,0:T(8,128)S(1)}, s32[64]{0:T(128)S(1)}, bf16[10,256,256]{2,1,0:T(8,128)(2,1)S(1)}, bf16[1,256,256]{2,1,0:T(8,128)(2,1)S(1)}) custom-call(s32[8,128]{1,0:T(8,128)S(1)} %get-tuple-element.127.table, bf16[8,1,6,256,256]{4,3,2,1,0:T(8,128)(2,1)} %bitcast.87, bf16[1,6,256,256]{3,2,1,0:T(8,128)(2,1)} %rest_0_.13, ...), custom_call_target="tpu_custom_call" | custom-call | flops 100663296 | bytes 13631488 | tf_op jit(solution)/shard_map/older/pallas_call | solution.py:254
  274.4 16.7 %all_to_all.92 = bf16[8,6,16,256]{3,2,1,0:T(8,128)(2,1)S(1)} all-to-all(bf16[8,6,16,256]{3,2,1,0:T(8,128)(2,1)S(1)} %solve.13), channel_id=1, replica_groups=mesh['g'=4,'z'=8,'x'=4,'core'=2] {'x','core'}, dimensions={0} | all-to-all | bytes 786432 | tf_op jit(solution)/shard_map/all_to_all | solution.py:466
  (48 shorter events, 35.0 us)
Async XLA Ops:
  6.5 144.5 %all-gather.11.cloned.1.call-start = ((), (), s32[]{:S(2)}) async-start(), calls=%async_computation.19 | async-start | bytes 28311552 | tf_op jit(solution)/shard_map/all_gather | solution.py:405
  9.5 215.9 %all-gather.9.cloned.1.call-start = ((), (), s32[]{:S(2)}) async-start(), calls=%async_computation.18 | async-start | bytes 14155776 | tf_op jit(solution)/shard_map/all_gather | solution.py:405
  13.4 13.1 %copy-start.3 = (s32[1,5,6]{2,0,1:T(1,128)S(1)}, s32[1,5,6]{2,0,1:T(1,128)}, u32[]{:S(2)}) copy-start(s32[1,5,6]{2,0,1:T(1,128)} %param.13) | copy-start | bytes 364
  13.4 13.1 %copy-start.6 = (s32[1,5,1]{1,2,0:T(1,128)S(1)}, s32[1,5,1]{1,2,0:T(1,128)}, u32[]{:S(2)}) copy-start(s32[1,5,1]{1,2,0:T(1,128)} %param.14) | copy-start | bytes 64
  13.4 31.0 %copy-start.4 = (s32[1,5,6]{2,0,1:T(1,128)S(1)}, s32[1,5,6]{2,0,1:T(1,128)}, u32[]{:S(2)}) copy-start(s32[1,5,6]{2,0,1:T(1,128)} %param.16) | copy-start | bytes 364
  13.4 31.0 %copy-start.5 = (s32[1,5,1]{1,2,0:T(1,128)S(1)}, s32[1,5,1]{1,2,0:T(1,128)}, u32[]{:S(2)}) copy-start(s32[1,5,1]{1,2,0:T(1,128)} %param.17) | copy-start | bytes 64
  13.4 253.0 %all-gather.7.cloned.1.call-start = ((), (), s32[]{:S(2)}) async-start(), calls=%async_computation.17 | async-start | bytes 7077888 | tf_op jit(solution)/shard_map/all_gather | solution.py:405
  14.2 53.3 %copy-start.2 = (bf16[1,6,256,256]{3,2,1,0:T(8,128)(2,1)S(1)}, bf16[1,6,256,256]{3,2,1,0:T(8,128)(2,1)}, u32[]{:S(2)}) copy-start(bf16[1,6,256,256]{3,2,1,0:T(8,128)(2,1)} %rest_0_.8) | copy-start | bytes 2359300
  14.2 23.5 %all-to-all-start = ((bf16[32,16,256]{2,1,0:T(8,128)(2,1)}), bf16[32,16,256]{2,1,0:T(8,128)(2,1)}, u32[]{:S(2)}, u32[]{:S(2)}) async-start(bf16[32,16,256]{2,1,0:T(8,128)(2,1)} %get-tuple-element.73), calls=%async_computation | async-start | bytes 524288 | tf_op jit(solution)/shard_map/all_to_all | solution.py:427
  37.7 16.5 %all-to-all-start.1 = ((bf16[8,4,16,256]{3,2,1,0:T(8,128)(2,1)}), bf16[8,4,16,256]{3,2,1,0:T(8,128)(2,1)S(1)}, u32[]{:S(2)}, u32[]{:S(2)}) async-start(bf16[8,4,16,256]{3,2,1,0:T(8,128)(2,1)} %bitcast.5), calls=%async_computation.1 | async-start | bytes 524288 | tf_op jit(solution)/shard_map/all_to_all | solution.py:430
  54.2 2.2 copy-start
  56.4 40.9 %copy-start.1 = (bf16[1,5,6,256,256]{4,3,2,1,0:T(8,128)(2,1)S(1)}, bf16[1,5,6,256,256]{4,3,2,1,0:T(8,128)(2,1)}, u32[]{:S(2)}) copy-start(bf16[1,5,6,256,256]{4,3,2,1,0:T(8,128)(2,1)} %blocks.5) | copy-start | bytes 11796484
  146.7 15.0 %all-to-all-start.9 = ((bf16[32,16,256]{2,1,0:T(8,128)(2,1)}), bf16[32,16,256]{2,1,0:T(8,128)(2,1)S(1)}, u32[]{:S(2)}, u32[]{:S(2)}) async-start(bf16[32,16,256]{2,1,0:T(8,128)(2,1)} %get-tuple-element.79), calls=%async_computation.9 | async-start | bytes 524288 | tf_op jit(solution)/shard_map/all_to_all | solution.py:427
  164.0 15.8 %all-to-all-start.10 = ((bf16[32,16,256]{2,1,0:T(8,128)(2,1)}), bf16[32,16,256]{2,1,0:T(8,128)(2,1)S(1)}, u32[]{:S(2)}, u32[]{:S(2)}) async-start(bf16[32,16,256]{2,1,0:T(8,128)(2,1)} %get-tuple-element.86), calls=%async_computation.10 | async-start | bytes 524288 | tf_op jit(solution)/shard_map/all_to_all | solution.py:427
  181.9 16.3 %all-to-all-start.11 = ((bf16[32,16,256]{2,1,0:T(8,128)(2,1)}), bf16[32,16,256]{2,1,0:T(8,128)(2,1)S(1)}, u32[]{:S(2)}, u32[]{:S(2)}) async-start(bf16[32,16,256]{2,1,0:T(8,128)(2,1)} %get-tuple-element.93), calls=%async_computation.11 | async-start | bytes 524288 | tf_op jit(solution)/shard_map/all_to_all | solution.py:427
  202.3 14.3 %all-to-all-start.12 = ((bf16[32,16,256]{2,1,0:T(8,128)(2,1)}), bf16[32,16,256]{2,1,0:T(8,128)(2,1)S(1)}, u32[]{:S(2)}, u32[]{:S(2)}) async-start(bf16[32,16,256]{2,1,0:T(8,128)(2,1)} %get-tuple-element.101), calls=%async_computation.12 | async-start | bytes 524288 | tf_op jit(solution)/shard_map/all_to_all | solution.py:427
  219.4 16.4 %all-to-all-start.13 = ((bf16[32,16,256]{2,1,0:T(8,128)(2,1)}), bf16[32,16,256]{2,1,0:T(8,128)(2,1)S(1)}, u32[]{:S(2)}, u32[]{:S(2)}) async-start(bf16[32,16,256]{2,1,0:T(8,128)(2,1)} %get-tuple-element.109), calls=%async_computation.13 | async-start | bytes 524288 | tf_op jit(solution)/shard_map/all_to_all | solution.py:427
  238.3 16.0 %all-to-all-start.14 = ((bf16[32,16,256]{2,1,0:T(8,128)(2,1)}), bf16[32,16,256]{2,1,0:T(8,128)(2,1)S(1)}, u32[]{:S(2)}, u32[]{:S(2)}) async-start(bf16[32,16,256]{2,1,0:T(8,128)(2,1)} %get-tuple-element.117), calls=%async_computation.14 | async-start | bytes 524288 | tf_op jit(solution)/shard_map/all_to_all | solution.py:427
  256.4 16.4 %all-to-all-start.15 = ((bf16[32,16,256]{2,1,0:T(8,128)(2,1)}), bf16[32,16,256]{2,1,0:T(8,128)(2,1)S(1)}, u32[]{:S(2)}, u32[]{:S(2)}) async-start(bf16[32,16,256]{2,1,0:T(8,128)(2,1)} %get-tuple-element.125), calls=%async_computation.15 | async-start | bytes 524288 | tf_op jit(solution)/shard_map/all_to_all | solution.py:427
Sparse Core Ops, SparseCore 0:
  9.7 138.3 all-gather.10
  149.9 70.7 all-gather.8
  222.5 43.8 all-gather.6
